TPU v7x, 32 devices: a whole 2x2x4 slice. The times are simulated.
32 devices in a mesh: req: 8 (over y, x, core), tp: 4 (over z).
Axes of the slice: x: 2, y: 2, z: 4, core: 2. Of those that a mesh axis runs over, the one named last changes fastest.
Arguments:
- new_query: bfloat16 [1024, 2560], P('req', 'tp'), may hold values from -64 to 64
- new_keyval: bfloat16 [1024, 1280], P('req', 'tp'), may hold values from -24 to 24
- residual_in: bfloat16 [1024, 2560], P('req'), may hold values from -64 to 64
- leaf_cache: bfloat16 [128, 32, 1280], P('req', None, 'tp'), may hold values from -6 to 6
- leaf_length: int32 [128], P('req'), may hold values from 1 to 32
- new_counts: int32 [8, 16], P('req'), may hold values from 1 to 16, as said below
- request_mid: int32 [128], P('req'), may hold values from 0 to 5
- mid_root: int32 [6], replicated, may hold values from 0 to 1, as said below
- node_length: int32 [8], replicated, may hold values from 1 to 1744, as said below
- prefix_pool: bfloat16 [256, 16, 1280], P('req', None, 'tp'), may hold values from -6 to 6
- page_node: int32 [256], P('req'), may hold values from -1 to 7, as said below
- page_rank: int32 [256], P('req'), may hold values from 0 to 108, as said below
- out_weight: bfloat16 [2560, 2560], P('tp'), may hold values from -0.125 to 0.125
- norm_gain: bfloat16 [2560], replicated, may hold values from 0.5 to 1.5
- gate_weight: bfloat16 [2560, 3584], P(None, 'tp'), may hold values from -0.125 to 0.125
- up_weight: bfloat16 [2560, 3584], P(None, 'tp'), may hold values from -0.125 to 0.125
- down_weight: bfloat16 [3584, 2560], P('tp'), may hold values from -0.09375 to 0.09375
- next_gain: bfloat16 [2560], replicated, may hold values from 0.5 to 1.5
- query_weight: bfloat16 [2560, 2560], P(None, 'tp'), may hold values from -0.125 to 0.125
- keyval_weight: bfloat16 [2560, 1280], P(None, 'tp'), may hold values from -0.125 to 0.125
Outputs:
- attention: bfloat16 [1024, 2560], P('req', 'tp')
- residual_out: bfloat16 [1024, 2560], P(('req', 'tp'))
- next_query: bfloat16 [1024, 2560], P('req', 'tp')
- next_keyval: bfloat16 [1024, 1280], P('req', 'tp')
Inputs may be any that keep to these rules, and one draw needn't show every extreme that they name: `new_counts`: each row sums to 128 and holds one request of exactly 16 new tokens. `mid_root`: each root is the parent of 3 mid-level nodes. `node_length`: A node of k pages has more than 16 * (k - 1) and at most 16 * k prefix tokens; a node with the most pages has exactly 16 * k. `page_node`: every node owns one page or more; 32 pages are free (-1). `page_rank`: the k pages of a node carry the ranks 0 to k - 1, each once; free pages carry 0.
All inputs are finite; a program needn't handle non-finite values.
Results may differ from a plain program's by a relative error of at most 0.015.
Values may be sent and summed in bfloat16 or wider, within the bound.
No kernel may reach another device: no remote copies, remote signals or barrier semaphores. Data moves between devices by JAX's collectives and lax.ppermute only.
A program may use at most 128 MiB of HBM per device.

v0:
```python
import math

import jax
import jax.numpy as jnp
from jax import lax
from jax.sharding import PartitionSpec as P

HD = 80
MAXNEW = 16
ROOTS = 2
MIDS = 6
NODES = 8


MASKED = -1e30
EPSILON = 1e-05


def rms_scale(values_in, gain):
    values = values_in.astype(jnp.float32)
    scale = lax.rsqrt(jnp.mean(values * values, axis=-1, keepdims=True) + EPSILON)
    return (values * scale * gain.astype(jnp.float32)).astype(jnp.bfloat16)


def combine(first, second):
    top_first, total_first, sum_first = first
    top_second, total_second, sum_second = second
    top = jnp.maximum(top_first, top_second)
    factor_first = jnp.exp(top_first - top)
    factor_second = jnp.exp(top_second - top)
    total = total_first * factor_first + total_second * factor_second
    weighted = sum_first * factor_first[..., None] + sum_second * factor_second[..., None]
    return (top, total, weighted)


def attend(queries, keys, values, visible):
    scores = jnp.einsum("nkgd,mkd->nkgm", queries, keys, preferred_element_type=jnp.float32) * (
        1.0 / math.sqrt(HD)
    )
    shown = visible[:, None, None, :]
    scores = jnp.where(shown, scores, MASKED)
    top = jnp.max(scores, axis=-1)
    raised = jnp.where(shown, jnp.exp(scores - top[..., None]), 0.0)
    total = jnp.sum(raised, axis=-1)
    weighted = jnp.einsum(
        "nkgm,mkd->nkgd", raised.astype(jnp.bfloat16), values, preferred_element_type=jnp.float32
    )
    return (top, total, weighted)


def pool_split(pages_in, node_of_page, rank_of_page):
    page_count = pages_in.shape[0]
    page_size = pages_in.shape[1]
    flat = pages_in.reshape(page_count * page_size, pages_in.shape[2] // (2 * HD), 2, HD)
    key_node = jnp.repeat(node_of_page, page_size, total_repeat_length=page_count * page_size)
    key_place = (
        rank_of_page[:, None] * page_size + jnp.arange(page_size, dtype=jnp.int32)[None, :]
    ).reshape(page_count * page_size)
    return (flat[:, :, 0], flat[:, :, 1], key_node, key_place)


def shared_visible(token_info, key_node, key_place):
    root_hit = (key_node[None, :] == token_info[:, 0:1]) & (key_place[None, :] < token_info[:, 2:3])
    mid_hit = (key_node[None, :] == token_info[:, 1:2]) & (key_place[None, :] < token_info[:, 3:4])
    return root_hit | mid_hit


def token_tables(counts, request_mid, mid_root, node_length, row_count):
    requests = counts.shape[0]
    starts = jnp.cumsum(counts) - counts
    index = jnp.arange(row_count, dtype=jnp.int32)
    owner = jnp.sum((index[:, None] >= starts[None, :]).astype(jnp.int32), axis=1) - 1
    pick = (owner[:, None] == jnp.arange(requests, dtype=jnp.int32)[None, :]).astype(jnp.int32)
    offset = index - jnp.sum(pick * starts[None, :], axis=1)
    token_mid = jnp.sum(pick * request_mid[None, :], axis=1)
    mid_pick = (token_mid[:, None] == jnp.arange(MIDS, dtype=jnp.int32)[None, :]).astype(jnp.int32)
    token_root = jnp.sum(mid_pick * mid_root[None, :], axis=1)
    mid_node = token_mid + ROOTS
    node_ids = jnp.arange(NODES, dtype=jnp.int32)
    root_len = jnp.sum(
        (token_root[:, None] == node_ids[None, :]).astype(jnp.int32) * node_length[None, :], axis=1
    )
    mid_len = jnp.sum(
        (mid_node[:, None] == node_ids[None, :]).astype(jnp.int32) * node_length[None, :], axis=1
    )
    token_info = jnp.stack([token_root, mid_node, root_len, mid_len], axis=1)
    return (starts, owner, offset, token_info)


def local_part(
    new_query, new_keyval, leaf_cache, leaf_length, counts, starts, owner, offset, kv_local, group
):
    requests = counts.shape[0]
    leaf_slots = leaf_cache.shape[1]
    slot = jnp.arange(MAXNEW, dtype=jnp.int32)
    row_index = jnp.clip(starts[:, None] + slot[None, :], 0, new_query.shape[0] - 1)
    pad_query = new_query[row_index].reshape(requests, MAXNEW, kv_local, group, HD)
    pad_keyval = new_keyval[row_index]
    joined = jnp.concatenate([leaf_cache, pad_keyval], axis=1).reshape(
        requests, leaf_slots + MAXNEW, kv_local, 2, HD
    )
    leaf_ok = jnp.broadcast_to(
        jnp.arange(leaf_slots, dtype=jnp.int32)[None, None, :] < leaf_length[:, None, None],
        (requests, MAXNEW, leaf_slots),
    )
    causal = jnp.broadcast_to(
        slot[None, None, :] <= slot[None, :, None], (requests, MAXNEW, MAXNEW)
    )
    visible = jnp.concatenate([leaf_ok, causal], axis=2)
    part = jax.vmap(attend)(pad_query, joined[:, :, :, 0], joined[:, :, :, 1], visible)
    flat = owner * MAXNEW + offset
    return tuple((item.reshape((requests * MAXNEW,) + item.shape[2:])[flat] for item in part))


def visit_owners(new_query, token_info, prefix_pool, page_node, page_rank, kv_local, group):
    all_query, all_info = (
        lax.all_gather(new_query, "req", axis=0, tiled=True),
        lax.all_gather(token_info, "req", axis=0, tiled=True),
    )
    total_rows = all_query.shape[0]
    block = math.gcd(total_rows, 512)
    keys, values, key_node, key_place = pool_split(prefix_pool, page_node, page_rank)

    def owner_block(items):
        query_block, info_block = items
        heads = query_block.reshape(block, kv_local, group, HD)
        return attend(heads, keys, values, shared_visible(info_block, key_node, key_place))

    part = lax.map(
        owner_block,
        (
            all_query.reshape(total_rows // block, block, all_query.shape[1]),
            all_info.reshape(total_rows // block, block, 4),
        ),
    )
    holders = lax.axis_size("req")
    row_count = total_rows // holders
    part_top, part_total, part_sum = tuple(
        (item.reshape((holders, row_count) + item.shape[2:]) for item in part)
    )
    tops, totals, sums = (
        lax.all_to_all(part_top, "req", split_axis=0, concat_axis=0, tiled=True),
        lax.all_to_all(part_total, "req", split_axis=0, concat_axis=0, tiled=True),
        lax.all_to_all(part_sum, "req", split_axis=0, concat_axis=0, tiled=True),
    )
    top = jnp.max(tops, axis=0)
    factor = jnp.exp(tops - top[None])
    return (top, jnp.sum(totals * factor, axis=0), jnp.sum(sums * factor[..., None], axis=0))


def per_device(
    new_query,
    new_keyval,
    residual_in,
    leaf_cache,
    leaf_length,
    new_counts,
    request_mid,
    mid_root,
    node_length,
    prefix_pool,
    page_node,
    page_rank,
    out_weight,
    norm_gain,
    gate_weight,
    up_weight,
    down_weight,
    next_gain,
    query_weight,
    keyval_weight,
):
    row_count = new_query.shape[0]
    query_width = new_query.shape[1]
    keyval_width = new_keyval.shape[1]
    kv_local = keyval_width // (2 * HD)
    group = query_width // (kv_local * HD)
    counts = new_counts[0]
    starts, owner, offset, token_info = token_tables(
        counts, request_mid, mid_root, node_length, row_count
    )
    shared = visit_owners(new_query, token_info, prefix_pool, page_node, page_rank, kv_local, group)
    local = local_part(
        new_query,
        new_keyval,
        leaf_cache,
        leaf_length,
        counts,
        starts,
        owner,
        offset,
        kv_local,
        group,
    )
    top, total, weighted = combine(shared, local)
    attention = (weighted / total[..., None]).reshape(row_count, query_width).astype(jnp.bfloat16)
    share = row_count // lax.axis_size("tp")
    mine = lax.axis_index("tp") * share
    attn_proj = lax.psum(jnp.dot(attention, out_weight, preferred_element_type=jnp.float32), "tp")
    mixed = (residual_in.astype(jnp.float32) + attn_proj).astype(jnp.bfloat16)
    normed = rms_scale(mixed, norm_gain)
    gate = jnp.dot(normed, gate_weight, preferred_element_type=jnp.float32)
    upward = jnp.dot(normed, up_weight, preferred_element_type=jnp.float32)
    hidden = (jax.nn.silu(gate) * upward).astype(jnp.bfloat16)
    mlp_proj = lax.psum(jnp.dot(hidden, down_weight, preferred_element_type=jnp.float32), "tp")
    layer_rows = (mixed.astype(jnp.float32) + mlp_proj).astype(jnp.bfloat16)
    residual_out = lax.dynamic_slice_in_dim(layer_rows, mine, share, 0)
    final = rms_scale(layer_rows, next_gain)
    next_query = jnp.dot(final, query_weight, preferred_element_type=jnp.float32).astype(
        jnp.bfloat16
    )
    next_keyval = jnp.dot(final, keyval_weight, preferred_element_type=jnp.float32).astype(
        jnp.bfloat16
    )
    return (attention, residual_out, next_query, next_keyval)


def solution(mesh):
    in_specs = (
        P("req", "tp"),
        P("req", "tp"),
        P("req", None),
        P("req", None, "tp"),
        P("req"),
        P("req", None),
        P("req"),
        P(),
        P(),
        P("req", None, "tp"),
        P("req"),
        P("req"),
        P("tp", None),
        P(),
        P(None, "tp"),
        P(None, "tp"),
        P("tp", None),
        P(),
        P(None, "tp"),
        P(None, "tp"),
    )
    out_specs = (P("req", "tp"), P(("req", "tp"), None), P("req", "tp"), P("req", "tp"))
    return jax.shard_map(
        per_device, mesh=mesh, in_specs=in_specs, out_specs=out_specs, check_vma=False
    )
```

profile of v0, /device:TPU:0, one launch (start us, length us, event | category | flops | bytes accessed | tf_op | source)
XLA Modules:
  0.0 375.2 jit_solution(16658785647169500201)
XLA Ops:
  10.4 2.1 reshape.441
  12.5 3.1 fusion.62
  16.4 1.8 copy.129
  18.2 1.8 copy.128
  20.8 11.4 %all_gather.6 = s32[1024,4]{0,1:T(4,128)} all-gather(s32[128,4]{0,1:T(4,128)S(1)} %pad_add_fusion.1), channel_id=1, replica_groups=mesh['req'=8,'tp'=4] {'req'}, dimensions={0}, use_global_device_ids=true | all-gather | bytes 18432 | tf_op jit(solution)/shard_map/all_gather | solution.py:118
  33.8 4.2 %compare_select_fusion.2 = (s32[512,1]{0,1:T(1,128)S(1)}, s32[512,1]{0,1:T(1,128)S(1)}) fusion(s32[]{:T(128)} %bitcast.29, s32[]{:T(128)} %bitcast.30, s32[]{:T(128)} %bitcast.31, s32[]{:T(128)} %bitcast.32, s32[]{:T(128)} %bitcast.33, s32[]{:T(128)} %bitcast.35, s32[]{:T(128)} %bitcast.34, s32[512,1]{0,1:T(1,128)S(1)} %bitcast.213, s32[512,1]{0,1:T(1,128)S(1)} %bitcast.212), kind=kLoop, calls=%fused_computation.105 | loop fusion | flops 7168 | bytes 8220 | tf_op jit(solution)/shard_map/jit(_take)/gather | solution.py:55
  38.6 16.0 %select_select_fusion = s32[512]{0:T(512)} fusion(pred[512]{0:T(512)(128)(4,1)S(1)} %get-tuple-element.200, pred[512]{0:T(512)(128)(4,1)S(1)} %get-tuple-element.199, pred[512]{0:T(512)(128)(4,1)S(1)} %get-tuple-element.198, pred[512]{0:T(512)(128)(4,1)S(1)} %get-tuple-element.197, pred[512]{0:T(512)(128)(4,1)S(1)} %get-tuple-element.196, ...), kind=kLoop, calls=%fused_computation.129 | loop fusion | flops 17408 | bytes 19060 | tf_op jit(solution)/shard_map/jit(_take)/select_n | solution.py:55
  54.6 100.4 %while.16 = (s32[]{:T(128)}, f32[2,512,2,4]{1,0,3,2:T(2,128)}, f32[2,512,2,4]{1,0,3,2:T(2,128)}, f32[2,512,2,4,80]{1,0,4,3,2:T(2,128)}, s32[512]{0:T(512)}, /*in...) while((s32[]{:T(128)}, f32[2,512,2,4]{1,0,3,2:T(2,128)}, ...), condition=%wide.region_9.10_spmd.clone, body=%wide.region_6.0_spmd.clone.sunk | while | flops 700178944 | bytes 71092600 | solution.py:129
  57.8 2.0 constant_dynamic-slice_fusion.3
  59.8 2.2 copy.193
  62.0 5.8 %bitcast_reduce_fusion.2 = (f32[512,2,4]{0,2,1:T(4,128)S(1)}, f32[2,512,4,512]{1,3,2,0:T(8,128)}) fusion(pred[512,512]{0,1:T(8,128)(4,1)S(1)} %and_or_fusion.2, bf16[512,2,4,80]{0,3,2,1:T(8,128)(2,1)} %bitcast.188, bf16[512,2,80]{0,2,1:T(8,128)(2,1)} %get-tuple-element.391), kind=kOutput, calls=%fused_computation.7.clone.1 | convolution fusion | flops 341831680 | bytes 9486336 | tf_op jit(solution)/shard_map/while/body/eval_jaxpr/nkgd,mkd->nkgm/dot_general | solution.py:37
  69.9 4.6 %fusion.85 = f32[512,2,4]{0,2,1:T(4,128)S(1)} fusion(f32[2,512,4,512]{1,3,2,0:T(8,128)} %get-tuple-element.359, f32[512,2,4]{0,2,1:T(4,128)S(1)} %get-tuple-element.358, pred[512,512]{0,1:T(8,128)(4,1)S(1)} %and_or_fusion.2), kind=kLoop, calls=%fused_computation.12.clone.1 | loop fusion | flops 10481664 | bytes 8683520 | tf_op jit(solution)/shard_map/while/body/eval_jaxpr/reduce_sum | solution.py:44
  75.8 2.3 fusion.86
  78.1 2.4 copy.196
  80.6 24.2 %dynamic_update_slice.19 = f32[2,512,2,4,80]{1,0,4,3,2:T(2,128)} dynamic-update-slice(f32[2,512,2,4,80]{1,0,4,3,2:T(2,128)} %get-tuple-element.375, f32[1,512,2,4,80]{1,0,4,3,2:T(1,128)} %copy.196, s32[]{:T(128)S(6)} %copy.204, s32[]{:T(128)} %constant.138.clone.1..sunk, s32[]{:T(128)} %constant.138.clone.1..sunk, s32[]{:T(128)} %constant.138.clone.1..sunk, s32[]{:T(128)} %constant.138.clone.1..sunk) | dynamic-update-slice | bytes 2621444 | tf_op jit(solution)/shard_map/while/body/jit(dynamic_update_index_in_dim)/dynamic_update_slice | solution.py:129
  108.1 2.0 constant_dynamic-slice_fusion.3
  110.0 2.2 copy.193
  112.2 5.8 %bitcast_reduce_fusion.2 = (f32[512,2,4]{0,2,1:T(4,128)S(1)}, f32[2,512,4,512]{1,3,2,0:T(8,128)}) fusion(pred[512,512]{0,1:T(8,128)(4,1)S(1)} %and_or_fusion.2, bf16[512,2,4,80]{0,3,2,1:T(8,128)(2,1)} %bitcast.188, bf16[512,2,80]{0,2,1:T(8,128)(2,1)} %get-tuple-element.391), kind=kOutput, calls=%fused_computation.7.clone.1 | convolution fusion | flops 341831680 | bytes 9486336 | tf_op jit(solution)/shard_map/while/body/eval_jaxpr/nkgd,mkd->nkgm/dot_general | solution.py:37
  120.1 4.6 %fusion.85 = f32[512,2,4]{0,2,1:T(4,128)S(1)} fusion(f32[2,512,4,512]{1,3,2,0:T(8,128)} %get-tuple-element.359, f32[512,2,4]{0,2,1:T(4,128)S(1)} %get-tuple-element.358, pred[512,512]{0,1:T(8,128)(4,1)S(1)} %and_or_fusion.2), kind=kLoop, calls=%fused_computation.12.clone.1 | loop fusion | flops 10481664 | bytes 8683520 | tf_op jit(solution)/shard_map/while/body/eval_jaxpr/reduce_sum | solution.py:44
  126.0 2.3 fusion.86
  128.3 2.4 copy.196
  130.8 24.2 %dynamic_update_slice.19 = f32[2,512,2,4,80]{1,0,4,3,2:T(2,128)} dynamic-update-slice(f32[2,512,2,4,80]{1,0,4,3,2:T(2,128)} %get-tuple-element.375, f32[1,512,2,4,80]{1,0,4,3,2:T(1,128)} %copy.196, s32[]{:T(128)S(6)} %copy.204, s32[]{:T(128)} %constant.138.clone.1..sunk, s32[]{:T(128)} %constant.138.clone.1..sunk, s32[]{:T(128)} %constant.138.clone.1..sunk, s32[]{:T(128)} %constant.138.clone.1..sunk) | dynamic-update-slice | bytes 2621444 | tf_op jit(solution)/shard_map/while/body/jit(dynamic_update_index_in_dim)/dynamic_update_slice | solution.py:129
  156.5 4.0 %all-to-all-start.1 = ((f32[8,128,2,4]{1,3,2,0:T(4,128)}), f32[8,128,2,4]{1,3,2,0:T(4,128)}, u32[]{:S(2)}, u32[]{:S(2)}) async-start(f32[8,128,2,4]{1,3,2,0:T(4,128)} %copy.135), calls=%async_computation.1 | async-start | bytes 65536 | tf_op jit(solution)/shard_map/all_to_all | solution.py:142
  162.1 1.8 gather_fusion
  165.4 4.1 %all-to-all-start.2 = ((f32[8,128,2,4]{1,3,2,0:T(4,128)}), f32[8,128,2,4]{1,3,2,0:T(4,128)S(1)}, u32[]{:S(2)}, u32[]{:S(2)}) async-start(f32[8,128,2,4]{1,3,2,0:T(4,128)} %copy.150), calls=%async_computation.2 | async-start | bytes 65536 | tf_op jit(solution)/shard_map/all_to_all | solution.py:143
  169.5 2.0 pad_maximum_fusion
  171.4 1.9 gather_fusion.1
  173.4 2.3 reshape.447
  175.7 3.7 reshape.446
  179.4 4.7 %reshape.442 = f32[8,128,2,4,80]{1,0,4,3,2:T(8,128)} reshape(f32[2,512,2,4,80]{1,0,4,3,2:T(2,128)} %get-tuple-element.70) | data formatting | bytes 5242880 | tf_op jit(solution)/shard_map/reshape | solution.py:139
  184.1 3.7 copy.133
  188.5 4.4 %all-to-all-start = ((f32[8,128,2,4,80]{1,4,3,2,0:T(8,128)}), f32[8,128,2,4,80]{1,4,3,2,0:T(8,128)}, u32[]{:S(2)}, u32[]{:S(2)}) async-start(f32[8,128,2,4,80]{1,4,3,2,0:T(8,128)} %copy.133), calls=%async_computation | async-start | bytes 5242880 | tf_op jit(solution)/shard_map/all_to_all | solution.py:144
  193.2 3.7 fusion.61
  199.3 1.9 convolution_bitcast_fusion
  203.0 2.9 gather_fusion.3
  205.9 2.0 copy.148
  207.9 1.7 gather_fusion.2
  209.7 2.5 fusion.30
  217.3 7.9 %all-to-all-done = f32[8,128,2,4,80]{1,4,3,2,0:T(8,128)} async-done(((f32[8,128,2,4,80]{1,4,3,2,0:T(8,128)}), f32[8,128,2,4,80]{1,4,3,2,0:T(8,128)}, u32[]{:S(2)}, u32[]{:S(2)}) %all-to-all-start) | async-done | bytes 2621472 | tf_op jit(solution)/shard_map/all_to_all | solution.py:144
  225.2 2.1 multiply_reduce_fusion
  227.4 1.8 fusion.66
  229.5 59.2 %all-reduce.3.cloned.1.call-done = f32[128,2560]{1,0:T(8,128)} async-done(((f32[128,2560]{1,0:T(8,128)}), f32[128,2560]{1,0:T(8,128)}) %all-reduce.3.cloned.1.call-update) | async-done | bytes 1310736 | tf_op jit(solution)/shard_map/psum | solution.py:199
  288.7 1.8 fusion.24
  291.3 4.0 %fusion.45 = f32[128,896]{1,0:T(8,128)} fusion(bf16[2560,896]{1,0:T(8,128)(2,1)} %param.38, bf16[128,2560]{1,0:T(8,128)(2,1)S(1)} %get-tuple-element.228, f32[2560]{0:T(1024)S(1)} %convert_element_type.63, f32[128]{0:T(128)S(1)} %add_rsqrt_fusion.1), kind=kOutput, calls=%fused_computation.67 | convolution fusion | flops 588513280 | bytes 5712384 | tf_op jit(solution)/shard_map/dot_general | solution.py:202
  295.3 6.7 %fusion.29 = f32[128,2560]{1,0:T(8,128)} fusion(bf16[896,2560]{1,0:T(8,128)(2,1)} %param.40, bf16[2560,896]{1,0:T(8,128)(2,1)} %param.39, f32[128,896]{1,0:T(8,128)} %fusion.45, bf16[128,2560]{1,0:T(8,128)(2,1)} %copy-done.3, f32[2560]{0:T(1024)S(1)} %convert_element_type.63, f32[128]{0:T(128)S(1)} %add_rsqrt_fusion.1), kind=kOutput, calls=%fused_computation.50 | convolution fusion | flops 1176403968 | bytes 11610624 | tf_op jit(solution)/shard_map/dot_general | solution.py:205
  302.9 59.0 %all-reduce.5.cloned.1.call-done = f32[128,2560]{1,0:T(8,128)} async-done(((f32[128,2560]{1,0:T(8,128)}), f32[128,2560]{1,0:T(8,128)}) %all-reduce.5.cloned.1.call-update) | async-done | bytes 1310736 | tf_op jit(solution)/shard_map/psum | solution.py:205
  361.9 1.9 fusion.21
  363.8 2.7 convolution_convert_fusion.1
  (136 shorter events, 38.8 us)
Async XLA Ops:
  7.2 220.2 %copy-start = (bf16[640,2560]{1,0:T(8,128)(2,1)S(1)}, bf16[640,2560]{1,0:T(8,128)(2,1)}, u32[]{:S(2)}) copy-start(bf16[640,2560]{1,0:T(8,128)(2,1)} %param.36) | copy-start | bytes 9830404
  7.2 26.5 %copy-start.11 = (s32[4,128]{1,0:T(4,128)S(1)}, s32[4,128]{1,0:T(4,128)}, u32[]{:S(2)}) copy-start(s32[4,128]{1,0:T(4,128)} %constant.143.clone.1) | copy-start | bytes 6148
  7.2 12.8 %copy-start.14 = (s32[16]{0:T(128)S(1)}, s32[16]{0:T(128)}, u32[]{:S(2)}) copy-start(s32[16]{0:T(128)} %param.30) | copy-start | bytes 196
  7.2 13.4 %copy-start.19 = (s32[6]{0:T(128)S(1)}, s32[6]{0:T(128)}, u32[]{:S(2)}) copy-start(s32[6]{0:T(128)} %param.31) | copy-start | bytes 76
  7.2 13.5 %copy-start.15 = (s32[8]{0:T(128)S(1)}, s32[8]{0:T(128)}, u32[]{:S(2)}) copy-start(s32[8]{0:T(128)} %param.32) | copy-start | bytes 100
  7.2 25.0 %copy-start.5 = (s32[32]{0:T(128)S(1)}, s32[32]{0:T(128)}, u32[]{:S(2)}) copy-start(s32[32]{0:T(128)} %param.34) | copy-start | bytes 388
  7.2 30.9 %copy-start.20 = (s32[32]{0:T(128)S(1)}, s32[32]{0:T(128)}, u32[]{:S(2)}) copy-start(s32[32]{0:T(128)} %param.35) | copy-start | bytes 388
  7.2 47.4 %all-gather.2.cloned.1.call-start = ((), (), s32[]{:S(2)}) async-start(), calls=%async_computation.3 | async-start | bytes 1474560 | tf_op jit(solution)/shard_map/all_gather | solution.py:117
  15.7 5.0 %copy-start.21 = (s32[128]{0:T(128)}, s32[128]{0:T(128)S(1)}, u32[]{:S(2)}) copy-start(s32[128]{0:T(128)S(1)} %convert_reduce_fusion) | copy-start | bytes 1540
  69.9 5.8 %copy-start.1 = (f32[2,512,4,512]{1,3,2,0:T(8,128)S(1)}, f32[2,512,4,512]{1,3,2,0:T(8,128)}, u32[]{:S(2)}) copy-start(f32[2,512,4,512]{1,3,2,0:T(8,128)} %get-tuple-element.359) | copy-start | bytes 25165828 | tf_op jit(solution)/shard_map/while
  69.9 5.8 %copy-start.7 = (bf16[512,2,80]{0,2,1:T(8,128)(2,1)S(1)}, bf16[512,2,80]{0,2,1:T(8,128)(2,1)}, u32[]{:S(2)}) copy-start(bf16[512,2,80]{0,2,1:T(8,128)(2,1)} %get-tuple-element.392) | copy-start | bytes 491524 | tf_op jit(solution)/shard_map/while
  78.1 2.4 copy-start.9
  80.6 24.2 %copy-start.10 = (f32[2,512,2,4]{1,0,3,2:T(2,128)}, f32[2,512,2,4]{1,0,3,2:T(2,128)S(1)}, u32[]{:S(2)}) copy-start(f32[2,512,2,4]{1,0,3,2:T(2,128)S(1)} %dynamic_update_slice.18) | copy-start | bytes 98308 | tf_op jit(solution)/shard_map/while
  120.1 5.8 %copy-start.1 = (f32[2,512,4,512]{1,3,2,0:T(8,128)S(1)}, f32[2,512,4,512]{1,3,2,0:T(8,128)}, u32[]{:S(2)}) copy-start(f32[2,512,4,512]{1,3,2,0:T(8,128)} %get-tuple-element.359) | copy-start | bytes 25165828 | tf_op jit(solution)/shard_map/while
  120.1 5.8 %copy-start.7 = (bf16[512,2,80]{0,2,1:T(8,128)(2,1)S(1)}, bf16[512,2,80]{0,2,1:T(8,128)(2,1)}, u32[]{:S(2)}) copy-start(bf16[512,2,80]{0,2,1:T(8,128)(2,1)} %get-tuple-element.392) | copy-start | bytes 491524 | tf_op jit(solution)/shard_map/while
  128.3 2.4 copy-start.9
  130.8 24.2 %copy-start.10 = (f32[2,512,2,4]{1,0,3,2:T(2,128)}, f32[2,512,2,4]{1,0,3,2:T(2,128)S(1)}, u32[]{:S(2)}) copy-start(f32[2,512,2,4]{1,0,3,2:T(2,128)S(1)} %dynamic_update_slice.18) | copy-start | bytes 98308 | tf_op jit(solution)/shard_map/while
  155.1 16.4 %copy-start.2 = (bf16[128,640]{1,0:T(8,128)(2,1)S(1)}, bf16[128,640]{1,0:T(8,128)(2,1)}, u32[]{:S(2)}) copy-start(bf16[128,640]{1,0:T(8,128)(2,1)} %param.24) | copy-start | bytes 491524
  156.5 8.8 %all-to-all-start.1 = ((f32[8,128,2,4]{1,3,2,0:T(4,128)}), f32[8,128,2,4]{1,3,2,0:T(4,128)}, u32[]{:S(2)}, u32[]{:S(2)}) async-start(f32[8,128,2,4]{1,3,2,0:T(4,128)} %copy.135), calls=%async_computation.1 | async-start | bytes 65536 | tf_op jit(solution)/shard_map/all_to_all | solution.py:142
  165.4 22.5 %all-to-all-start.2 = ((f32[8,128,2,4]{1,3,2,0:T(4,128)}), f32[8,128,2,4]{1,3,2,0:T(4,128)S(1)}, u32[]{:S(2)}, u32[]{:S(2)}) async-start(f32[8,128,2,4]{1,3,2,0:T(4,128)} %copy.150), calls=%async_computation.2 | async-start | bytes 65536 | tf_op jit(solution)/shard_map/all_to_all | solution.py:143
  187.9 5.1 %copy-start.16 = (s32[16]{0:T(128)S(1)}, s32[16]{0:T(128)}, u32[]{:S(2)}) copy-start(s32[16]{0:T(128)} %param.28) | copy-start | bytes 196
  187.9 0.6 copy-start.8
  188.5 36.7 %all-to-all-start = ((f32[8,128,2,4,80]{1,4,3,2,0:T(8,128)}), f32[8,128,2,4,80]{1,4,3,2,0:T(8,128)}, u32[]{:S(2)}, u32[]{:S(2)}) async-start(f32[8,128,2,4,80]{1,4,3,2,0:T(8,128)} %copy.133), calls=%async_computation | async-start | bytes 5242880 | tf_op jit(solution)/shard_map/all_to_all | solution.py:144
  192.9 95.8 %all-reduce.3.cloned.1.call-start = ((), (), s32[]{:S(2)}) async-start(), calls=%async_computation.4 | async-start | bytes 2621440 | tf_op jit(solution)/shard_map/psum | solution.py:199
  193.0 4.0 %copy-start.6 = (bf16[16,16,2,4,80]{4,3,2,1,0:T(4,128)(2,1)S(1)}, bf16[16,16,2,4,80]{4,3,2,1,0:T(4,128)(2,1)}, u32[]{:S(2)}) copy-start(bf16[16,16,2,4,80]{4,3,2,1,0:T(4,128)(2,1)} %reshape.447) | copy-start | bytes 983044
  201.2 1.8 copy-start.17
  201.2 1.8 copy-start.22
  225.2 2.1 copy-start.4
  227.4 2.1 copy-start.12
  229.2 132.7 %all-reduce.5.cloned.1.call-start = ((), (), s32[]{:S(2)}) async-start(), calls=%async_computation.5 | async-start | bytes 2621440 | tf_op jit(solution)/shard_map/psum | solution.py:205
  290.5 0.9 copy-start.3
  295.3 6.8 %copy-start.13 = (bf16[2560]{0:T(1024)(128)(2,1)S(1)}, bf16[2560]{0:T(1024)(128)(2,1)}, u32[]{:S(2)}) copy-start(bf16[2560]{0:T(1024)(128)(2,1)} %param.41) | copy-start | bytes 15364
  361.9 4.7 %copy-start.18 = (bf16[2560,640]{1,0:T(8,128)(2,1)S(1)}, bf16[2560,640]{1,0:T(8,128)(2,1)}, u32[]{:S(2)}) copy-start(bf16[2560,640]{1,0:T(8,128)(2,1)} %param.42) | copy-start | bytes 9830404
Sparse Core Ops, SparseCore 0:
  10.0 27.2 all-gather.1
  229.3 59.3 all-reduce.2
  302.2 59.6 all-reduce.4
where the time goes:
time: 381 us; the launch traced here: 375 us
  waiting for transfers between devices  127 us (33%)
  local copies, waits for them, and re-layouts  125 us (33%)
  other arithmetic  49 us (13%)
  matrix products  36.3 us (10%)
  between operations  14.1 us (4%)
  starting transfers between devices  12.8 us (3%)
  blocking collectives  11.4 us (3%)
    psum x1, waiting for transfers between devices, per_device(): lax.psum(jnp.dot(attention, out_weight, preferred_element_type=jnp.float3...  59.2 us
    psum x1, waiting for transfers between devices, per_device(): lax.psum(jnp.dot(hidden, down_weight, preferred_element_type=jnp.float32)...  59 us
    dynamic_update_slice x12, local copies, waits for them, and re-layouts, visit_owners(): lax.map(owner_block, (all_query.reshape(total_rows // block, block, all_q...  57.6 us
    select_n x1, other arithmetic, pool_split(): jnp.repeat(node_of_page, page_size, total_repeat_length=page_count * page...  16 us
    dot_general x3, matrix products, attend(): jnp.einsum('nkgd,mkd->nkgm', queries, keys, preferred_element_type=jnp.fl...  13.1 us
    reduce_sum x3, other arithmetic, attend(): total = jnp.sum(raised, axis=-1)  11.8 us
    all_gather x1, blocking collectives, visit_owners(): lax.all_gather(token_info, 'req', axis=0, tiled=True)  11.4 us
    reshape x6, local copies, waits for them, and re-layouts, visit_owners(): item.reshape((holders, row_count) + item.shape[2:])  11.4 us
  transfers between devices with their start and end apart: 6, of which 3 were waited for; matrix products, arithmetic and copies ran while one was open for 22% of the time, Pallas kernels for 0%

commit v1 on v0

v1 whole, which is shorter than its diff:
```python
import functools
import math

import jax
import jax.numpy as jnp
from jax import lax
from jax.experimental import pallas as pl
from jax.experimental.pallas import tpu as pltpu
from jax.sharding import PartitionSpec as P

HD = 80
ROOTS = 2
MIDS = 6
LANES = 128
MASKED = -1e30
EPSILON = 1e-05
RATE = math.log2(math.e) / math.sqrt(HD)

bf16 = jnp.bfloat16
f32 = jnp.float32
i32 = jnp.int32
VMEM = pl.BlockSpec(memory_space=pltpu.VMEM)
SMEM = pl.BlockSpec(memory_space=pltpu.SMEM)
PARAMS = pltpu.CompilerParams(vmem_limit_bytes=48 * 1024 * 1024)


def padded(width):
    return -(-width // LANES) * LANES


def key_start(c):
    return c * 2 * HD // LANES * LANES


def key_shift(c):
    return c * 2 * HD % LANES


def value_start(c):
    return (c * 2 * HD + HD) // LANES * LANES


def value_shift(c):
    return (c * 2 * HD + HD) % LANES


def key_window(ref, c):
    first = ref[:, key_start(c) : key_start(c) + LANES]
    last = ref[:, ref.shape[1] - LANES :]
    return jnp.concatenate([first, last], axis=1)


def value_window(ref, c):
    stop = min(value_start(c) + 2 * LANES, ref.shape[1])
    return ref[:, value_start(c) : stop]


def scores_of(query, keys):
    return lax.dot_general(query, keys, (((1,), (1,)), ((), ())), preferred_element_type=f32)


def prep_kernel(node_ref, rank_ref, length_ref, root_ref, pool_ref, out_ref):
    pages, size, width = pool_ref.shape
    free = out_ref.shape[1] - width
    lane = lax.broadcasted_iota(i32, (size, free), 1)
    slot = lax.broadcasted_iota(i32, (size, free), 0)
    root = jnp.full((size, free), -2, i32)
    for m in range(MIDS):
        root = jnp.where(lane == m, root_ref[m], root)
    hidden = jnp.where(lane < MIDS, MASKED, 0.0)
    for p in range(pages):
        node = node_ref[p]
        left = length_ref[jnp.maximum(node, 0)] - size * rank_ref[p]
        seen = ((root == node) | (lane + ROOTS == node)) & (slot < left)
        rows = slice(p * size, (p + 1) * size)
        out_ref[rows, :width] = pool_ref[p]
        out_ref[rows, width:] = jnp.where(seen, 0.0, hidden).astype(bf16)


def prepare(page_node, page_rank, node_length, mid_root, prefix_pool):
    pages, size, width = prefix_pool.shape
    return pl.pallas_call(
        prep_kernel,
        out_shape=jax.ShapeDtypeStruct((pages * size, padded(width + MIDS)), bf16),
        in_specs=[SMEM, SMEM, SMEM, SMEM, VMEM],
        out_specs=VMEM,
        compiler_params=PARAMS,
        name="pool_rows",
    )(page_node, page_rank, node_length, mid_root, prefix_pool)


def fold(scores, values, state):
    top = functools.reduce(jnp.maximum, [jnp.max(s, axis=1, keepdims=True) for s in scores])
    if state is not None:
        top = jnp.maximum(top, state[0])
    total, weighted = None, None
    for s, v in zip(scores, values):
        raised = jnp.exp2((s - top) * RATE)
        part = jnp.sum(raised, axis=1, keepdims=True)
        mixed = jnp.dot(raised.astype(bf16), v, preferred_element_type=f32)
        total = part if total is None else total + part
        if weighted is None:
            weighted = mixed
        else:
            weighted = weighted + mixed
    if state is not None:
        factor = jnp.exp2((state[0] - top) * RATE)
        total = total + state[1] * factor
        weighted = weighted + state[2] * factor
    return top, total, weighted


def pack(top, total, weighted):
    lane = lax.broadcasted_iota(i32, weighted.shape, 1)
    return jnp.where(lane == 0, top, jnp.where(lane == 1, total, weighted))


def unpack(state):
    return state[:, 0:1], state[:, 1:2], state


def write_out(out_ref, state, c, group, rows):
    _, total, weighted = state
    shift = value_shift(c)
    result = (weighted[:, shift : shift + HD] / total).astype(bf16)
    for g in range(group):
        h = c * group + g
        out_ref[:, h * HD : (h + 1) * HD] = result[g * rows : (g + 1) * rows]


def local_kernel(count_ref, mid_ref, leaf_len_ref, query_ref, keyval_ref, leaf_ref, *refs, chunks):
    pool_refs, (aug_ref, state_ref) = refs[:chunks], refs[chunks:]
    rows = query_ref.shape[0]
    width = keyval_ref.shape[1]
    requests, slots, _ = leaf_ref.shape
    kv_local = width // (2 * HD)
    group = query_ref.shape[1] // (kv_local * HD)
    row = lax.broadcasted_iota(i32, (rows, LANES), 0)
    lane = lax.broadcasted_iota(i32, (rows, LANES), 1)
    zero = jnp.zeros((rows, LANES), i32)
    start, low, high, mid = zero, zero, zero, zero
    begin = jnp.int32(0)
    for r in range(requests):
        here = row >= begin
        start = jnp.where(here, begin, start)
        low = jnp.where(here, r * slots, low)
        high = jnp.where(here, r * slots + leaf_len_ref[r], high)
        mid = jnp.where(here, mid_ref[r], mid)
        begin = begin + count_ref[0, r]
    chosen = jnp.where(lane == width % LANES + mid, 1.0, 0.0).astype(bf16)

    leaf_all = leaf_ref[...].reshape(requests * slots, width)
    leaf_at = lax.broadcasted_iota(i32, (rows, requests * slots), 1)
    leaf_ok = (leaf_at >= low[:, 0:1]) & (leaf_at < high[:, 0:1])
    new_ok = (lane >= start) & (lane <= row)
    for c in range(kv_local):
        base = c * group * rows
        key0, val0 = key_start(c), value_start(c)
        shift = key_shift(c)
        for g in range(group):
            h = c * group + g
            at = slice(base + g * rows, base + (g + 1) * rows)
            aug_ref[at, :LANES] = jnp.zeros((rows, LANES), bf16)
            aug_ref[at, shift : shift + HD] = query_ref[:, h * HD : (h + 1) * HD]
            aug_ref[at, LANES:] = chosen
        query = aug_ref[base : base + group * rows, :]
        narrow = query[:, :LANES]
        s_leaf = scores_of(narrow, leaf_all[:, key0 : key0 + LANES])
        s_leaf = jnp.where(leaf_ok[None], s_leaf.reshape(group, rows, -1), MASKED)
        s_new = scores_of(narrow, keyval_ref[:, key0 : key0 + LANES])
        s_new = jnp.where(new_ok[None], s_new.reshape(group, rows, -1), MASKED)
        scores = [s_leaf.reshape(group * rows, -1), s_new.reshape(group * rows, -1)]
        stop = min(val0 + 2 * LANES, width)
        fill = val0 + 2 * LANES - stop
        values = [leaf_all[:, val0:stop], keyval_ref[:, val0:stop]]
        if fill:
            values = [
                jnp.concatenate([v, jnp.zeros((v.shape[0], fill), bf16)], axis=1) for v in values
            ]
        for ref in pool_refs:
            scores.append(scores_of(query, key_window(ref, c)))
            values.append(value_window(ref, c))
        state_ref[base : base + group * rows, :] = pack(*fold(scores, values, None))


def chunk_kernel(*refs, last, kv_local, rows):
    aug_ref, state_ref = refs[:2]
    pool_refs, out_ref = refs[2:-1], refs[-1]
    block = aug_ref.shape[0] // kv_local
    for c in range(kv_local):
        at = slice(c * block, (c + 1) * block)
        query = aug_ref[at, :]
        scores = [scores_of(query, key_window(ref, c)) for ref in pool_refs]
        values = [value_window(ref, c) for ref in pool_refs]
        state = fold(scores, values, unpack(state_ref[at, :]))
        if last:
            write_out(out_ref, state, c, block // rows, rows)
        else:
            out_ref[at, :] = pack(*state)


def start_attention(new_query, new_keyval, leaf, leaf_length, counts, request_mid, pools):
    rows, query_width = new_query.shape
    heads = query_width // HD
    return pl.pallas_call(
        functools.partial(local_kernel, chunks=len(pools)),
        out_shape=(
            jax.ShapeDtypeStruct((heads * rows, 2 * LANES), bf16),
            jax.ShapeDtypeStruct((heads * rows, 2 * LANES), f32),
        ),
        in_specs=[SMEM] * 3 + [VMEM] * (3 + len(pools)),
        out_specs=(VMEM, VMEM),
        compiler_params=PARAMS,
        name="attend_local",
    )(counts, request_mid, leaf_length, new_query, new_keyval, leaf, *pools)


def extend_attention(aug, state, pools, last, kv_local, rows):
    if last:
        shape = jax.ShapeDtypeStruct((rows, aug.shape[0] // rows * HD), bf16)
    else:
        shape = jax.ShapeDtypeStruct(state.shape, f32)
    return pl.pallas_call(
        functools.partial(chunk_kernel, last=last, kv_local=kv_local, rows=rows),
        out_shape=shape,
        in_specs=[VMEM] * (2 + len(pools)),
        out_specs=VMEM,
        compiler_params=PARAMS,
        name="attend_pages",
    )(aug, state, *pools)


def trade(value, axis, bit):
    size = lax.axis_size(axis)
    return lax.ppermute(value, axis, [(i, i ^ bit) for i in range(size)])


def total_over_tp(partial):
    if lax.axis_size("tp") != 4:
        return lax.psum(partial, "tp")
    half = partial.shape[1] // 2
    first, second = partial[:, :half].astype(bf16), partial[:, half:].astype(bf16)
    first_in, second_in = trade(first, "tp", 3), trade(second, "tp", 1)
    first = (first.astype(f32) + first_in.astype(f32)).astype(bf16)
    second = (second.astype(f32) + second_in.astype(f32)).astype(bf16)
    first_in, second_in = trade(first, "tp", 1), trade(second, "tp", 3)
    first = first.astype(f32) + first_in.astype(f32)
    second = second.astype(f32) + second_in.astype(f32)
    return jnp.concatenate([first, second], axis=1)


def rms_scale(values_in, gain):
    values = values_in.astype(f32)
    scale = lax.rsqrt(jnp.mean(values * values, axis=-1, keepdims=True) + EPSILON)
    return (values * scale * gain.astype(f32)).astype(bf16)


def per_device(
    new_query,
    new_keyval,
    residual_in,
    leaf_cache,
    leaf_length,
    new_counts,
    request_mid,
    mid_root,
    node_length,
    prefix_pool,
    page_node,
    page_rank,
    out_weight,
    norm_gain,
    gate_weight,
    up_weight,
    down_weight,
    next_gain,
    query_weight,
    keyval_weight,
):
    row_count = new_query.shape[0]
    kv_local = new_keyval.shape[1] // (2 * HD)
    pool = prepare(page_node, page_rank, node_length, mid_root, prefix_pool)
    local_args = (new_query, new_keyval, leaf_cache, leaf_length, new_counts, request_mid)
    if lax.axis_size("req") == 8:
        far = [trade(pool, "req", bit) for bit in (2, 4, 6)]
        beside = trade(pool, "req", 1)
        aug, state = start_attention(*local_args, [pool, beside])
        other = [trade(item, "req", 1) for item in far]
        state = extend_attention(aug, state, far, False, kv_local, row_count)
        attention = extend_attention(aug, state, other, True, kv_local, row_count)
    else:
        every = lax.all_gather(pool, "req", axis=0)
        aug, state = start_attention(*local_args, [])
        step = 4
        for i in range(0, every.shape[0], step):
            chunk = [every[i : i + step].reshape(-1, pool.shape[1])]
            last = i + step >= every.shape[0]
            state = extend_attention(aug, state, chunk, last, kv_local, row_count)
        attention = state

    share = row_count // lax.axis_size("tp")
    mine = lax.axis_index("tp") * share
    attn_proj = total_over_tp(jnp.dot(attention, out_weight, preferred_element_type=f32))
    mixed = (residual_in.astype(f32) + attn_proj).astype(bf16)
    normed = rms_scale(mixed, norm_gain)
    gate = jnp.dot(normed, gate_weight, preferred_element_type=f32)
    upward = jnp.dot(normed, up_weight, preferred_element_type=f32)
    hidden = (jax.nn.silu(gate) * upward).astype(bf16)
    mlp_proj = total_over_tp(jnp.dot(hidden, down_weight, preferred_element_type=f32))
    layer_rows = (mixed.astype(f32) + mlp_proj).astype(bf16)
    residual_out = lax.dynamic_slice_in_dim(layer_rows, mine, share, 0)
    final = rms_scale(layer_rows, next_gain)
    next_query = jnp.dot(final, query_weight, preferred_element_type=f32).astype(bf16)
    next_keyval = jnp.dot(final, keyval_weight, preferred_element_type=f32).astype(bf16)
    return (attention, residual_out, next_query, next_keyval)


def solution(mesh):
    in_specs = (
        P("req", "tp"),
        P("req", "tp"),
        P("req", None),
        P("req", None, "tp"),
        P("req"),
        P("req", None),
        P("req"),
        P(),
        P(),
        P("req", None, "tp"),
        P("req"),
        P("req"),
        P("tp", None),
        P(),
        P(None, "tp"),
        P(None, "tp"),
        P("tp", None),
        P(),
        P(None, "tp"),
        P(None, "tp"),
    )
    out_specs = (P("req", "tp"), P(("req", "tp"), None), P("req", "tp"), P("req", "tp"))
    return jax.shard_map(
        per_device, mesh=mesh, in_specs=in_specs, out_specs=out_specs, check_vma=False
    )
```

time: 381 us -> 136 us (0.36); the launches traced: 375 us -> 135 us
  local copies, waits for them, and re-layouts: 125 us -> 12.5 us
  waiting for transfers between devices: 127 us -> 74.6 us
  other arithmetic: 49 us -> 3.12 us
  matrix products: 36.3 us -> 12.7 us
  Pallas kernels: 0 us -> 15.4 us
  between operations: 14.1 us -> 0.9 us
  blocking collectives: 11.4 us -> 0 us
    psum x2 -> x0, waiting for transfers between devices: 118 us -> none  [the longest x1 59.2 us: per_device(): lax.psum(jnp.dot(attention, out_weight, preferred_element_type=jnp.float3...]
    ppermute x0 -> x15, waiting for transfers between devices: none -> 74.6 us  [trade(): return lax.ppermute(value, axis, [(i, i ^ bit) for i in range(size)])]
    dynamic_update_slice x12 -> x0, local copies, waits for them, and re-layouts: 57.6 us -> none  [visit_owners(): lax.map(owner_block, (all_query.reshape(total_rows // block, block, all_q...]
    dot_general x11 -> x5, matrix products: 36.3 us -> 12.7 us  [the longest x1 6.51 us: per_device(): jnp.dot(hidden, down_weight, preferred_element_type=f32)]
    reshape x11 -> x0, local copies, waits for them, and re-layouts: 22.1 us -> none  [the longest x6 11.4 us: visit_owners(): item.reshape((holders, row_count) + item.shape[2:])]
    select_n x3 -> x0, other arithmetic: 16.1 us -> none  [the longest x1 16 us: pool_split(): jnp.repeat(node_of_page, page_size, total_repeat_length=page_count * page...]
    ppermute x0 -> x15, starting transfers between devices: none -> 16.1 us  [trade(): return lax.ppermute(value, axis, [(i, i ^ bit) for i in range(size)])]
    reduce_sum x9 -> x0, other arithmetic: 15.5 us -> none  [the longest x3 11.8 us: attend(): total = jnp.sum(raised, axis=-1)]
  transfers between devices with their start and end apart: 6 -> 15, of which waited for: 3 -> 8; matrix products, arithmetic and copies ran while one was open for 22% -> 2% of each run, Pallas kernels for 0% -> 6%
where the time goes in v1:
time: 136 us; the launch traced here: 135 us
  waiting for transfers between devices  74.6 us (55%)
  starting transfers between devices  16.1 us (12%)
  Pallas kernels  15.4 us (11%)
  matrix products  12.7 us (9%)
  local copies, waits for them, and re-layouts  12.5 us (9%)
  other arithmetic  3.12 us (2%)
    ppermute x15, waiting for transfers between devices, trade(): return lax.ppermute(value, axis, [(i, i ^ bit) for i in range(size)])  74.6 us
    ppermute x15, starting transfers between devices, trade(): return lax.ppermute(value, axis, [(i, i ^ bit) for i in range(size)])  16.1 us
    unnamed x45, local copies, waits for them, and re-layouts  10.6 us
    pallas_call x2, Pallas kernels, extend_attention(): pl.pallas_call(functools.partial(chunk_kernel, last=last, kv_local=kv_loc...  9.91 us
    dot_general x1, matrix products, per_device(): jnp.dot(hidden, down_weight, preferred_element_type=f32)  6.51 us
    pallas_call x1, Pallas kernels, start_attention(): pl.pallas_call(functools.partial(local_kernel, chunks=len(pools)), out_sh...  4.04 us
  transfers between devices with their start and end apart: 15, of which 8 were waited for; matrix products, arithmetic and copies ran while one was open for 2% of the time, Pallas kernels for 6%

profile of v1, /device:TPU:0, one launch (start us, length us, event | category | flops | bytes accessed | tf_op | source)
XLA Modules:
  0.0 135.3 jit_solution(2043498431452399017)
XLA Ops:
  0.7 1.1 copy-done.1
  1.8 0.7 copy-done.4
  2.5 0.7 copy-done.5
  3.1 0.7 copy-done.6
  3.8 0.7 copy-done.7
  4.4 1.5 %pool_rows.1.refs_0_ = bf16[512,384]{1,0:T(8,128)(2,1)} custom-call(s32[32]{0:T(128)S(1)} %copy-done.4, s32[32]{0:T(128)S(1)} %copy-done.5, s32[8]{0:T(128)S(1)} %copy-done.6, s32[6]{0:T(128)S(1)} %copy-done.7, bf16[32,16,320]{2,1,0:T(8,128)(2,1)S(1)} %copy-done.1), custom_call_target="tpu_custom_call" | custom-call | tf_op jit(solution)/shard_map/pool_rows/pallas_call | solution.py:82
  5.9 2.9 %collective-permute-start.1 = (bf16[512,384]{1,0:T(8,128)(2,1)}, bf16[512,384]{1,0:T(8,128)(2,1)}, u32[]{:S(2)}, u32[]{:S(2)}) collective-permute-start(bf16[512,384]{1,0:T(8,128)(2,1)} %pool_rows.1.refs_0_), channel_id=1, source_target_pairs={{0,8},{4,12},{8,0},{12,4},{16,24},{20,28},{24,16},{28,20},{1,9},{5... | collective-permute-start | bytes 1179656 | tf_op jit(solution)/shard_map/ppermute | solution.py:235
  8.8 1.5 %collective-permute-start.2 = (bf16[512,384]{1,0:T(8,128)(2,1)}, bf16[512,384]{1,0:T(8,128)(2,1)}, u32[]{:S(2)}, u32[]{:S(2)}) collective-permute-start(bf16[512,384]{1,0:T(8,128)(2,1)} %pool_rows.1.refs_0_), channel_id=1, source_target_pairs={{0,16},{4,20},{8,24},{12,28},{16,0},{20,4},{24,8},{28,12},{1,17},{... | collective-permute-start | bytes 1179656 | tf_op jit(solution)/shard_map/ppermute | solution.py:235
  10.3 8.7 %collective-permute-done.1.refs_2_ = bf16[512,384]{1,0:T(8,128)(2,1)} collective-permute-done((bf16[512,384]{1,0:T(8,128)(2,1)}, bf16[512,384]{1,0:T(8,128)(2,1)}, u32[]{:S(2)}, u32[]{:S(2)}) %collective-permute-start.1) | collective-permute-done | bytes 393248 | tf_op jit(solution)/shard_map/ppermute | solution.py:235
  19.1 9.1 %collective-permute-done.2.refs_3_ = bf16[512,384]{1,0:T(8,128)(2,1)} collective-permute-done((bf16[512,384]{1,0:T(8,128)(2,1)}, bf16[512,384]{1,0:T(8,128)(2,1)}, u32[]{:S(2)}, u32[]{:S(2)}) %collective-permute-start.2) | collective-permute-done | bytes 393248 | tf_op jit(solution)/shard_map/ppermute | solution.py:235
  28.1 0.5 collective-permute-start.6
  28.6 1.0 copy.24.keyval_ref
  29.7 1.0 copy-done.2
  30.7 0.9 copy-done.3
  31.6 0.7 copy-done.8
  32.2 0.7 copy-done.9
  32.9 0.7 copy-done.10
  33.5 4.0 %attend_local.1 = (bf16[1024,256]{1,0:T(8,128)(2,1)S(1)}, f32[1024,256]{1,0:T(8,128)S(1)}) custom-call(s32[1,16]{1,0:T(1,128)S(1)} %copy-done.8, s32[16]{0:T(128)S(1)} %copy-done.9, s32[16]{0:T(128)S(1)} %copy-done.10, bf16[128,640]{1,0:T(8,128)(2,1)S(1)} %copy-done.3, bf16[128,320]{1,0:T(8,128)(2,1)S(1)} %copy.24.keyval_ref, ...), custom_call_target="tpu_custom_call" | custom-call | tf_op jit(solution)/shard_map/attend_local/pallas_call | solution.py:205
  37.6 4.6 %attend_pages.2.refs_1_ = f32[1024,256]{1,0:T(8,128)S(1)} custom-call(bf16[1024,256]{1,0:T(8,128)(2,1)S(1)} %get-tuple-element.6.refs_0_, f32[1024,256]{1,0:T(8,128)S(1)} %get-tuple-element.7.refs_1_, bf16[512,384]{1,0:T(8,128)(2,1)} %collective-permute-done.1.refs_2_, bf16[512,384]{1,0:T(8,128)(2,1)} %collective-permute-done.2.refs_3_, ...), custom_call_target="tpu_custom_call" | custom-call | tf_op jit(solution)/shard_map/attend_pages/pallas_call | solution.py:223
  42.2 5.4 %attend_pages.3 = bf16[128,640]{1,0:T(8,128)(2,1)} custom-call(bf16[1024,256]{1,0:T(8,128)(2,1)S(1)} %get-tuple-element.6.refs_0_, f32[1024,256]{1,0:T(8,128)S(1)} %attend_pages.2.refs_1_, bf16[512,384]{1,0:T(8,128)(2,1)} %collective-permute-done.4.refs_2_, bf16[512,384]{1,0:T(8,128)(2,1)} %collective-permute-done.5.refs_3_, ...), custom_call_target="tpu_custom_call" | custom-call | tf_op jit(solution)/shard_map/attend_pages/pallas_call | solution.py:223
  47.6 1.6 %convolution_convert_fusion = bf16[128,2560]{1,0:T(8,128)(2,1)S(1)} fusion(bf16[128,640]{1,0:T(8,128)(2,1)} %attend_pages.3, bf16[640,2560]{1,0:T(8,128)(2,1)S(1)} %copy-done), kind=kOutput, calls=%fused_computation | convolution fusion | flops 419758080 | bytes 4096000 | tf_op jit(solution)/shard_map/dot_general | solution.py:303
  49.2 3.7 %collective-permute-start.7 = (bf16[128,1280]{1,0:T(8,128)(2,1)S(1)}, bf16[128,1280]{1,0:T(8,128)(2,1)S(1)}, u32[]{:S(2)}, u32[]{:S(2)}) collective-permute-start(bf16[128,1280]{1,0:T(8,128)(2,1)S(1)} %get-tuple-element.18), channel_id=1, source_target_pairs={{0,3},{1,2},{2,1},{3,0},{4,7},{5,6},{6,5},{7,4},{8,11},{9,10},{10,... | collective-permute-start | bytes 983048 | tf_op jit(solution)/shard_map/ppermute | solution.py:235
  52.9 8.9 %collective-permute-done.7 = bf16[128,1280]{1,0:T(8,128)(2,1)S(1)} collective-permute-done((bf16[128,1280]{1,0:T(8,128)(2,1)S(1)}, bf16[128,1280]{1,0:T(8,128)(2,1)S(1)}, u32[]{:S(2)}, u32[]{:S(2)}) %collective-permute-start.7) | collective-permute-done | bytes 327712 | tf_op jit(solution)/shard_map/ppermute | solution.py:235
  61.8 6.1 %collective-permute-done.9 = bf16[128,1280]{1,0:T(8,128)(2,1)S(1)} collective-permute-done((bf16[128,1280]{1,0:T(8,128)(2,1)S(1)}, bf16[128,1280]{1,0:T(8,128)(2,1)S(1)}, u32[]{:S(2)}, u32[]{:S(2)}) %collective-permute-start.9) | collective-permute-done | bytes 327712 | tf_op jit(solution)/shard_map/ppermute | solution.py:235
  67.9 0.2 add_convert_fusion.3
  68.1 1.7 %collective-permute-start.8 = (bf16[128,1280]{1,0:T(8,128)(2,1)S(1)}, bf16[128,1280]{1,0:T(8,128)(2,1)S(1)}, u32[]{:S(2)}, u32[]{:S(2)}) collective-permute-start(bf16[128,1280]{1,0:T(8,128)(2,1)S(1)} %get-tuple-element.16), channel_id=1, source_target_pairs={{0,1},{1,0},{2,3},{3,2},{4,5},{5,4},{6,7},{7,6},{8,9},{9,8},{10,11... | collective-permute-start | bytes 983048 | tf_op jit(solution)/shard_map/ppermute | solution.py:235
  69.8 0.5 collective-permute-start.10
  70.3 14.5 %collective-permute-done.8 = bf16[128,1280]{1,0:T(8,128)(2,1)S(1)} collective-permute-done((bf16[128,1280]{1,0:T(8,128)(2,1)S(1)}, bf16[128,1280]{1,0:T(8,128)(2,1)S(1)}, u32[]{:S(2)}, u32[]{:S(2)}) %collective-permute-start.8) | collective-permute-done | bytes 327712 | tf_op jit(solution)/shard_map/ppermute | solution.py:235
  84.9 0.1 convert_add_fusion.3
  85.0 0.3 fusion.3
  85.3 0.8 copy-done.11
  86.1 1.9 %fusion.17 = f32[128,896]{1,0:T(8,128)} fusion(bf16[2560,896]{1,0:T(8,128)(2,1)S(1)} %bitcast.8, bf16[128,2560]{1,0:T(8,128)(2,1)S(1)} %get-tuple-element.11, f32[2560]{0:T(1024)S(1)} %convert_element_type.114, f32[128]{0:T(128)S(1)} %add_rsqrt_fusion.1), kind=kOutput, calls=%fused_computation.34 | convolution fusion | flops 588513280 | bytes 5712384 | tf_op jit(solution)/shard_map/dot_general | solution.py:306
  88.0 6.5 %convolution_convert_fusion.1 = bf16[128,2560]{1,0:T(8,128)(2,1)} fusion(bf16[896,2560]{1,0:T(8,128)(2,1)} %param.36, bf16[2560,896]{1,0:T(8,128)(2,1)} %param.35, f32[128,896]{1,0:T(8,128)} %fusion.17, bf16[128,2560]{1,0:T(8,128)(2,1)} %copy-done.11, f32[2560]{0:T(1024)S(1)} %convert_element_type.114, f32[128]{0:T(128)S(1)} %add_rsqrt_fusion.1), kind=kOutput, calls=%fused_computation.1 | convolution fusion | flops 1176731648 | bytes 10955264 | tf_op jit(solution)/shard_map/dot_general | solution.py:309
  94.5 1.2 fusion.24
  95.7 2.6 %collective-permute-start.11 = (bf16[128,1280]{1,0:T(8,128)(2,1)S(1)}, bf16[128,1280]{1,0:T(8,128)(2,1)S(1)}, u32[]{:S(2)}, u32[]{:S(2)}) collective-permute-start(bf16[128,1280]{1,0:T(8,128)(2,1)S(1)} %get-tuple-element.14), channel_id=1, source_target_pairs={{0,3},{1,2},{2,1},{3,0},{4,7},{5,6},{6,5},{7,4},{8,11},{9,10},{10,... | collective-permute-start | bytes 983048 | tf_op jit(solution)/shard_map/ppermute | solution.py:235
  98.4 9.8 %collective-permute-done.11 = bf16[128,1280]{1,0:T(8,128)(2,1)S(1)} collective-permute-done((bf16[128,1280]{1,0:T(8,128)(2,1)S(1)}, bf16[128,1280]{1,0:T(8,128)(2,1)S(1)}, u32[]{:S(2)}, u32[]{:S(2)}) %collective-permute-start.11) | collective-permute-done | bytes 327712 | tf_op jit(solution)/shard_map/ppermute | solution.py:235
  108.2 3.5 %collective-permute-done.13 = bf16[128,1280]{1,0:T(8,128)(2,1)S(1)} collective-permute-done((bf16[128,1280]{1,0:T(8,128)(2,1)S(1)}, bf16[128,1280]{1,0:T(8,128)(2,1)S(1)}, u32[]{:S(2)}, u32[]{:S(2)}) %collective-permute-start.13) | collective-permute-done | bytes 327712 | tf_op jit(solution)/shard_map/ppermute | solution.py:235
  111.7 1.0 add_convert_fusion.1
  112.7 1.6 %collective-permute-start.12 = (bf16[128,1280]{1,0:T(8,128)(2,1)}, bf16[128,1280]{1,0:T(8,128)(2,1)}, u32[]{:S(2)}, u32[]{:S(2)}) collective-permute-start(bf16[128,1280]{1,0:T(8,128)(2,1)} %get-tuple-element.12), channel_id=1, source_target_pairs={{0,1},{1,0},{2,3},{3,2},{4,5},{5,4},{6,7},{7,6},{8,9},{9,8},{10,11... | collective-permute-start | bytes 983048 | tf_op jit(solution)/shard_map/ppermute | solution.py:235
  114.3 1.0 collective-permute-start.14
  115.3 14.0 %collective-permute-done.12 = bf16[128,1280]{1,0:T(8,128)(2,1)} collective-permute-done((bf16[128,1280]{1,0:T(8,128)(2,1)}, bf16[128,1280]{1,0:T(8,128)(2,1)}, u32[]{:S(2)}, u32[]{:S(2)}) %collective-permute-start.12) | collective-permute-done | bytes 327712 | tf_op jit(solution)/shard_map/ppermute | solution.py:235
  129.3 1.1 convert_add_fusion.2
  130.5 0.1 convert_add_fusion.1
  130.6 0.3 fusion
  130.9 1.0 copy-done.19
  131.9 1.3 convolution_convert_fusion.3
  133.2 1.4 %convolution_convert_fusion.2 = bf16[128,640]{1,0:T(8,128)(2,1)} fusion(bf16[2560,640]{1,0:T(8,128)(2,1)S(1)} %copy-done.18, bf16[128,2560]{1,0:T(8,128)(2,1)S(1)} %get-tuple-element.9, f32[2560]{0:T(1024)S(1)} %convert_element_type.129, f32[128]{0:T(128)S(1)} %add_rsqrt_fusion), kind=kOutput, calls=%fused_computation.18 | convolution fusion | flops 420823040 | bytes 4106752 | tf_op jit(solution)/shard_map/dot_general | solution.py:313
  134.6 0.7 constant_dynamic-slice_fusion
  (52 shorter events, 0.2 us)
Async XLA Ops:
  0.6 46.9 %copy-start = (bf16[640,2560]{1,0:T(8,128)(2,1)S(1)}, bf16[640,2560]{1,0:T(8,128)(2,1)}, u32[]{:S(2)}) copy-start(bf16[640,2560]{1,0:T(8,128)(2,1)} %param.32) | copy-start | bytes 9830404
  0.6 1.1 copy-start.1
  1.8 0.7 copy-start.4
  2.5 0.7 copy-start.5
  3.1 0.7 copy-start.6
  3.8 0.7 copy-start.7
  5.9 13.2 %collective-permute-start.1 = (bf16[512,384]{1,0:T(8,128)(2,1)}, bf16[512,384]{1,0:T(8,128)(2,1)}, u32[]{:S(2)}, u32[]{:S(2)}) collective-permute-start(bf16[512,384]{1,0:T(8,128)(2,1)} %pool_rows.1.refs_0_), channel_id=1, source_target_pairs={{0,8},{4,12},{8,0},{12,4},{16,24},{20,28},{24,16},{28,20},{1,9},{5... | collective-permute-start | bytes 1179656 | tf_op jit(solution)/shard_map/ppermute | solution.py:235
  8.8 19.3 %collective-permute-start.2 = (bf16[512,384]{1,0:T(8,128)(2,1)}, bf16[512,384]{1,0:T(8,128)(2,1)}, u32[]{:S(2)}, u32[]{:S(2)}) collective-permute-start(bf16[512,384]{1,0:T(8,128)(2,1)} %pool_rows.1.refs_0_), channel_id=1, source_target_pairs={{0,16},{4,20},{8,24},{12,28},{16,0},{20,4},{24,8},{28,12},{1,17},{... | collective-permute-start | bytes 1179656 | tf_op jit(solution)/shard_map/ppermute | solution.py:235
  10.3 17.8 %collective-permute-start.3 = (bf16[512,384]{1,0:T(8,128)(2,1)}, bf16[512,384]{1,0:T(8,128)(2,1)}, u32[]{:S(2)}, u32[]{:S(2)}) collective-permute-start(bf16[512,384]{1,0:T(8,128)(2,1)} %pool_rows.1.refs_0_), channel_id=1, source_target_pairs={{0,24},{4,28},{8,16},{12,20},{16,8},{20,12},{24,0},{28,4},{1,25},{... | collective-permute-start | bytes 1179656 | tf_op jit(solution)/shard_map/ppermute | solution.py:235
  10.3 19.3 %collective-permute-start = (bf16[512,384]{1,0:T(8,128)(2,1)}, bf16[512,384]{1,0:T(8,128)(2,1)}, u32[]{:S(2)}, u32[]{:S(2)}) collective-permute-start(bf16[512,384]{1,0:T(8,128)(2,1)} %pool_rows.1.refs_0_), channel_id=1, source_target_pairs={{0,4},{4,0},{8,12},{12,8},{16,20},{20,16},{24,28},{28,24},{1,5},{5... | collective-permute-start | bytes 1179656 | tf_op jit(solution)/shard_map/ppermute | solution.py:235
  19.1 23.1 %collective-permute-start.4 = (bf16[512,384]{1,0:T(8,128)(2,1)}, bf16[512,384]{1,0:T(8,128)(2,1)}, u32[]{:S(2)}, u32[]{:S(2)}) collective-permute-start(bf16[512,384]{1,0:T(8,128)(2,1)} %collective-permute-done.1.refs_2_), channel_id=1, source_target_pairs={{0,4},{4,0},{8,12},{12,8},{16,20},{20,16},{24,28},{28,24},{1,5},{5... | collective-permute-start | bytes 1179656 | tf_op jit(solution)/shard_map/ppermute | solution.py:235
  28.1 14.0 %collective-permute-start.5 = (bf16[512,384]{1,0:T(8,128)(2,1)}, bf16[512,384]{1,0:T(8,128)(2,1)}, u32[]{:S(2)}, u32[]{:S(2)}) collective-permute-start(bf16[512,384]{1,0:T(8,128)(2,1)} %collective-permute-done.2.refs_3_), channel_id=1, source_target_pairs={{0,4},{4,0},{8,12},{12,8},{16,20},{20,16},{24,28},{28,24},{1,5},{5... | collective-permute-start | bytes 1179656 | tf_op jit(solution)/shard_map/ppermute | solution.py:235
  28.1 14.0 %collective-permute-start.6 = (bf16[512,384]{1,0:T(8,128)(2,1)}, bf16[512,384]{1,0:T(8,128)(2,1)}, u32[]{:S(2)}, u32[]{:S(2)}) collective-permute-start(bf16[512,384]{1,0:T(8,128)(2,1)} %collective-permute-done.3.refs_4_), channel_id=1, source_target_pairs={{0,4},{4,0},{8,12},{12,8},{16,20},{20,16},{24,28},{28,24},{1,5},{5... | collective-permute-start | bytes 1179656 | tf_op jit(solution)/shard_map/ppermute | solution.py:235
  29.7 1.0 copy-start.2
  30.7 0.9 copy-start.3
  31.6 0.7 copy-start.8
  32.2 0.7 copy-start.9
  32.9 0.7 copy-start.10
  42.2 43.9 %slice-start = ((s8[4587520]{0:T(1024)(128)(4,1)}), s8[393216]{0:T(1024)(128)(4,1)S(1)}, s32[]{:S(2)}) async-start(s8[4587520]{0:T(1024)(128)(4,1)} %bitcast.7), calls=%async_computation | async-start | bytes 786432
  47.6 22.2 %copy-start.16 = (bf16[2560]{0:T(1024)(128)(2,1)S(1)}, bf16[2560]{0:T(1024)(128)(2,1)}, u32[]{:S(2)}) copy-start(bf16[2560]{0:T(1024)(128)(2,1)} %param.33) | copy-start | bytes 15364
  49.2 37.0 %slice-start.1 = ((s8[4587520]{0:T(1024)(128)(4,1)}), s8[4194304]{0:T(1024)(128)(4,1)S(1)}, s32[]{:S(2)}) async-start(s8[4587520]{0:T(1024)(128)(4,1)} %bitcast.7), calls=%async_computation.1 | async-start | bytes 8388608
  49.2 12.5 %collective-permute-start.7 = (bf16[128,1280]{1,0:T(8,128)(2,1)S(1)}, bf16[128,1280]{1,0:T(8,128)(2,1)S(1)}, u32[]{:S(2)}, u32[]{:S(2)}) collective-permute-start(bf16[128,1280]{1,0:T(8,128)(2,1)S(1)} %get-tuple-element.18), channel_id=1, source_target_pairs={{0,3},{1,2},{2,1},{3,0},{4,7},{5,6},{6,5},{7,4},{8,11},{9,10},{10,... | collective-permute-start | bytes 983048 | tf_op jit(solution)/shard_map/ppermute | solution.py:235
  52.9 15.0 %collective-permute-start.9 = (bf16[128,1280]{1,0:T(8,128)(2,1)S(1)}, bf16[128,1280]{1,0:T(8,128)(2,1)S(1)}, u32[]{:S(2)}, u32[]{:S(2)}) collective-permute-start(bf16[128,1280]{1,0:T(8,128)(2,1)S(1)} %get-tuple-element.19), channel_id=1, source_target_pairs={{0,1},{1,0},{2,3},{3,2},{4,5},{5,4},{6,7},{7,6},{8,9},{9,8},{10,11... | collective-permute-start | bytes 983048 | tf_op jit(solution)/shard_map/ppermute | solution.py:235
  68.1 16.7 %collective-permute-start.8 = (bf16[128,1280]{1,0:T(8,128)(2,1)S(1)}, bf16[128,1280]{1,0:T(8,128)(2,1)S(1)}, u32[]{:S(2)}, u32[]{:S(2)}) collective-permute-start(bf16[128,1280]{1,0:T(8,128)(2,1)S(1)} %get-tuple-element.16), channel_id=1, source_target_pairs={{0,1},{1,0},{2,3},{3,2},{4,5},{5,4},{6,7},{7,6},{8,9},{9,8},{10,11... | collective-permute-start | bytes 983048 | tf_op jit(solution)/shard_map/ppermute | solution.py:235
  69.8 15.1 %copy-start.15 = (bf16[128,2560]{1,0:T(8,128)(2,1)S(1)}, bf16[128,2560]{1,0:T(8,128)(2,1)}, u32[]{:S(2)}) copy-start(bf16[128,2560]{1,0:T(8,128)(2,1)} %param.22) | copy-start | bytes 1966084
  69.8 15.0 %collective-permute-start.10 = (bf16[128,1280]{1,0:T(8,128)(2,1)S(1)}, bf16[128,1280]{1,0:T(8,128)(2,1)S(1)}, u32[]{:S(2)}, u32[]{:S(2)}) collective-permute-start(bf16[128,1280]{1,0:T(8,128)(2,1)S(1)} %get-tuple-element.17), channel_id=1, source_target_pairs={{0,3},{1,2},{2,1},{3,0},{4,7},{5,6},{6,5},{7,4},{8,11},{9,10},{10,... | collective-permute-start | bytes 983048 | tf_op jit(solution)/shard_map/ppermute | solution.py:235
  85.3 0.9 copy-start.11
  94.5 17.2 %copy-start.13 = (bf16[128,2560]{1,0:T(8,128)(2,1)S(1)}, bf16[128,2560]{1,0:T(8,128)(2,1)}, u32[]{:S(2)}) copy-start(bf16[128,2560]{1,0:T(8,128)(2,1)} %convolution_convert_fusion.1) | copy-start | bytes 1966084
  95.7 18.6 %copy-start.17 = (bf16[2560]{0:T(1024)(128)(2,1)S(1)}, bf16[2560]{0:T(1024)(128)(2,1)}, u32[]{:S(2)}) copy-start(bf16[2560]{0:T(1024)(128)(2,1)} %param.37) | copy-start | bytes 15364
  95.7 12.4 %collective-permute-start.11 = (bf16[128,1280]{1,0:T(8,128)(2,1)S(1)}, bf16[128,1280]{1,0:T(8,128)(2,1)S(1)}, u32[]{:S(2)}, u32[]{:S(2)}) collective-permute-start(bf16[128,1280]{1,0:T(8,128)(2,1)S(1)} %get-tuple-element.14), channel_id=1, source_target_pairs={{0,3},{1,2},{2,1},{3,0},{4,7},{5,6},{6,5},{7,4},{8,11},{9,10},{10,... | collective-permute-start | bytes 983048 | tf_op jit(solution)/shard_map/ppermute | solution.py:235
  98.4 13.3 %collective-permute-start.13 = (bf16[128,1280]{1,0:T(8,128)(2,1)S(1)}, bf16[128,1280]{1,0:T(8,128)(2,1)S(1)}, u32[]{:S(2)}, u32[]{:S(2)}) collective-permute-start(bf16[128,1280]{1,0:T(8,128)(2,1)S(1)} %get-tuple-element.15), channel_id=1, source_target_pairs={{0,1},{1,0},{2,3},{3,2},{4,5},{5,4},{6,7},{7,6},{8,9},{9,8},{10,11... | collective-permute-start | bytes 983048 | tf_op jit(solution)/shard_map/ppermute | solution.py:235
  112.7 16.6 %collective-permute-start.12 = (bf16[128,1280]{1,0:T(8,128)(2,1)}, bf16[128,1280]{1,0:T(8,128)(2,1)}, u32[]{:S(2)}, u32[]{:S(2)}) collective-permute-start(bf16[128,1280]{1,0:T(8,128)(2,1)} %get-tuple-element.12), channel_id=1, source_target_pairs={{0,1},{1,0},{2,3},{3,2},{4,5},{5,4},{6,7},{7,6},{8,9},{9,8},{10,11... | collective-permute-start | bytes 983048 | tf_op jit(solution)/shard_map/ppermute | solution.py:235
  114.3 16.2 %copy-start.14 = (bf16[128,1280]{1,0:T(8,128)(2,1)S(1)}, bf16[128,1280]{1,0:T(8,128)(2,1)}, u32[]{:S(2)}) copy-start(bf16[128,1280]{1,0:T(8,128)(2,1)} %get-tuple-element.13) | copy-start | bytes 983044
  114.3 16.3 %copy-start.12 = (bf16[128,2560]{1,0:T(8,128)(2,1)S(1)}, bf16[128,2560]{1,0:T(8,128)(2,1)}, u32[]{:S(2)}) copy-start(bf16[128,2560]{1,0:T(8,128)(2,1)} %copy-done.11) | copy-start | bytes 1966084
  114.3 16.2 %collective-permute-start.14 = (bf16[128,1280]{1,0:T(8,128)(2,1)}, bf16[128,1280]{1,0:T(8,128)(2,1)S(1)}, u32[]{:S(2)}, u32[]{:S(2)}) collective-permute-start(bf16[128,1280]{1,0:T(8,128)(2,1)} %get-tuple-element.13), channel_id=1, source_target_pairs={{0,3},{1,2},{2,1},{3,0},{4,7},{5,6},{6,5},{7,4},{8,11},{9,10},{10,... | collective-permute-start | bytes 983048 | tf_op jit(solution)/shard_map/ppermute | solution.py:235
  130.5 1.4 %copy-start.19 = (bf16[2560,320]{0,1:T(8,128)(2,1)S(1)}, bf16[2560,320]{0,1:T(8,128)(2,1)}, u32[]{:S(2)}) copy-start(bf16[2560,320]{0,1:T(8,128)(2,1)} %param.39) | copy-start | bytes 4915204
  130.6 2.6 %copy-start.18 = (bf16[2560,640]{1,0:T(8,128)(2,1)S(1)}, bf16[2560,640]{1,0:T(8,128)(2,1)}, u32[]{:S(2)}) copy-start(bf16[2560,640]{1,0:T(8,128)(2,1)} %param.38) | copy-start | bytes 9830404

commit v2 on v1

v2 whole, which is shorter than its diff:
```python
import functools
import math

import jax
import jax.numpy as jnp
from jax import lax
from jax.experimental import pallas as pl
from jax.experimental.pallas import tpu as pltpu
from jax.sharding import PartitionSpec as P

HD = 80
ROOTS = 2
MIDS = 6
LANES = 128
MASKED = -1e30
EPSILON = 1e-05
RATE = math.log2(math.e) / math.sqrt(HD)

bf16 = jnp.bfloat16
f32 = jnp.float32
i32 = jnp.int32
ANY = pl.BlockSpec(memory_space=pl.ANY)
VMEM = pl.BlockSpec(memory_space=pltpu.VMEM)
SMEM = pl.BlockSpec(memory_space=pltpu.SMEM)
PARAMS = pltpu.CompilerParams(vmem_limit_bytes=48 * 1024 * 1024)


def padded(width):
    return -(-width // LANES) * LANES


def key_start(c):
    return c * 2 * HD // LANES * LANES


def key_shift(c):
    return c * 2 * HD % LANES


def value_start(c):
    return (c * 2 * HD + HD) // LANES * LANES


def value_shift(c):
    return (c * 2 * HD + HD) % LANES


def key_window(ref, c):
    first = ref[:, key_start(c) : key_start(c) + LANES]
    last = ref[:, ref.shape[1] - LANES :]
    return jnp.concatenate([first, last], axis=1)


def value_window(ref, c):
    stop = min(value_start(c) + 2 * LANES, ref.shape[1])
    return ref[:, value_start(c) : stop]


def scores_of(query, keys):
    return lax.dot_general(query, keys, (((1,), (1,)), ((), ())), preferred_element_type=f32)


def fetch(pairs, sems):
    copies = [pltpu.make_async_copy(a, b, sems.at[i]) for i, (a, b) in enumerate(pairs)]
    for copy in copies:
        copy.start()
    return copies


def prep_kernel(
    node_hbm, rank_hbm, length_hbm, root_hbm, pool_ref, out_ref, node_ref, rank_ref, length_ref, root_ref, sems
):
    pairs = ((node_hbm, node_ref), (rank_hbm, rank_ref), (length_hbm, length_ref), (root_hbm, root_ref))
    for copy in fetch(pairs, sems):
        copy.wait()
    pages, size, width = pool_ref.shape
    free = out_ref.shape[1] - width
    lane = lax.broadcasted_iota(i32, (size, free), 1)
    slot = lax.broadcasted_iota(i32, (size, free), 0)
    root = jnp.full((size, free), -2, i32)
    for m in range(MIDS):
        root = jnp.where(lane == m, root_ref[m], root)
    hidden = jnp.where(lane < MIDS, MASKED, 0.0)
    for p in range(pages):
        node = node_ref[p]
        left = length_ref[jnp.maximum(node, 0)] - size * rank_ref[p]
        seen = ((root == node) | (lane + ROOTS == node)) & (slot < left)
        rows = slice(p * size, (p + 1) * size)
        out_ref[rows, :width] = pool_ref[p]
        out_ref[rows, width:] = jnp.where(seen, 0.0, hidden).astype(bf16)


def prepare(page_node, page_rank, node_length, mid_root, prefix_pool):
    pages, size, width = prefix_pool.shape
    tables = (page_node, page_rank, node_length, mid_root)
    return pl.pallas_call(
        prep_kernel,
        out_shape=jax.ShapeDtypeStruct((pages * size, padded(width + MIDS)), bf16),
        in_specs=[ANY] * 4 + [VMEM],
        out_specs=VMEM,
        scratch_shapes=[pltpu.SMEM(t.shape, i32) for t in tables] + [pltpu.SemaphoreType.DMA((4,))],
        compiler_params=PARAMS,
        name="pool_rows",
    )(*tables, prefix_pool)


def half_start(rows, half):
    parity = lax.rem(lax.axis_index("tp"), 2)
    return (parity if half else 1 - parity) * (rows // 2)


def fold(scores, values, state):
    top = functools.reduce(jnp.maximum, [jnp.max(s, axis=1, keepdims=True) for s in scores])
    if state is not None:
        top = jnp.maximum(top, state[0])
    total, weighted = None, None
    for s, v in zip(scores, values):
        raised = jnp.exp2((s - top) * RATE)
        part = jnp.sum(raised, axis=1, keepdims=True)
        mixed = jnp.dot(raised.astype(bf16), v, preferred_element_type=f32)
        total = part if total is None else total + part
        weighted = mixed if weighted is None else weighted + mixed
    if state is not None:
        factor = jnp.exp2((state[0] - top) * RATE)
        total = total + state[1] * factor
        weighted = weighted + state[2] * factor
    return top, total, weighted


def pack(top, total, weighted):
    lane = lax.broadcasted_iota(i32, weighted.shape, 1)
    return jnp.where(lane == 0, top, jnp.where(lane == 1, total, weighted))


def unpack(state):
    return state[:, 0:1], state[:, 1:2], state


def local_kernel(
    count_hbm, mid_hbm, leaf_len_hbm, query_ref, keyval_ref, leaf_ref, pool_ref, aug_ref, state_ref,
    count_ref, mid_ref, leaf_len_ref, sems,
):
    pairs = ((count_hbm, count_ref), (mid_hbm, mid_ref), (leaf_len_hbm, leaf_len_ref))
    for copy in fetch(pairs, sems):
        copy.wait()
    rows = query_ref.shape[0]
    part = rows // 2
    width = keyval_ref.shape[1]
    requests, slots, _ = leaf_ref.shape
    kv_local = width // (2 * HD)
    group = query_ref.shape[1] // (kv_local * HD)
    lane = lax.broadcasted_iota(i32, (part, LANES), 1)
    zero = jnp.zeros((part, LANES), i32)
    leaf_all = leaf_ref[...].reshape(requests * slots, width)
    leaf_at = lax.broadcasted_iota(i32, (part, requests * slots), 1)
    for half in range(2):
        first = half_start(rows, half)
        row = lax.broadcasted_iota(i32, (part, LANES), 0) + first
        start, low, high, mid = zero, zero, zero, zero
        begin = jnp.int32(0)
        for r in range(requests):
            here = row >= begin
            start = jnp.where(here, begin, start)
            low = jnp.where(here, r * slots, low)
            high = jnp.where(here, r * slots + leaf_len_ref[r], high)
            mid = jnp.where(here, mid_ref[r], mid)
            begin = begin + count_ref[0, r]
        chosen = jnp.where(lane == width % LANES + mid, 1.0, 0.0).astype(bf16)
        leaf_ok = (leaf_at >= low[:, 0:1]) & (leaf_at < high[:, 0:1])
        new_ok = (lane >= start) & (lane <= row)
        tokens = query_ref[pl.ds(pl.multiple_of(first, part), part), :]
        for c in range(kv_local):
            base = (half * kv_local + c) * group * part
            block = slice(base, base + group * part)
            key0, val0 = key_start(c), value_start(c)
            shift = key_shift(c)
            for g in range(group):
                h = c * group + g
                at = slice(base + g * part, base + (g + 1) * part)
                aug_ref[at, :LANES] = jnp.zeros((part, LANES), bf16)
                aug_ref[at, shift : shift + HD] = tokens[:, h * HD : (h + 1) * HD]
                aug_ref[at, LANES:] = chosen
            query = aug_ref[block, :]
            narrow = query[:, :LANES]
            s_leaf = scores_of(narrow, leaf_all[:, key0 : key0 + LANES])
            s_leaf = jnp.where(leaf_ok[None], s_leaf.reshape(group, part, -1), MASKED)
            s_new = scores_of(narrow, keyval_ref[:, key0 : key0 + LANES])
            s_new = jnp.where(new_ok[None], s_new.reshape(group, part, -1), MASKED)
            scores = [s_leaf.reshape(group * part, -1), s_new.reshape(group * part, -1)]
            stop = min(val0 + 2 * LANES, width)
            fill = val0 + 2 * LANES - stop
            values = [leaf_all[:, val0:stop], keyval_ref[:, val0:stop]]
            if fill:
                values = [
                    jnp.concatenate([v, jnp.zeros((v.shape[0], fill), bf16)], axis=1) for v in values
                ]
            scores.append(scores_of(query, key_window(pool_ref, c)))
            values.append(value_window(pool_ref, c))
            state_ref[block, :] = pack(*fold(scores, values, None))


def start_attention(new_query, new_keyval, leaf, leaf_length, counts, request_mid, pool):
    rows, query_width = new_query.shape
    heads = query_width // HD
    tables = (counts, request_mid, leaf_length)
    keys = leaf.shape[0] * leaf.shape[1] + rows + pool.shape[0]
    return pl.pallas_call(
        local_kernel,
        out_shape=(
            jax.ShapeDtypeStruct((heads * rows, 2 * LANES), bf16),
            jax.ShapeDtypeStruct((heads * rows, 2 * LANES), f32),
        ),
        in_specs=[ANY] * 3 + [VMEM] * 4,
        out_specs=(VMEM, VMEM),
        scratch_shapes=[pltpu.SMEM(t.shape, i32) for t in tables] + [pltpu.SemaphoreType.DMA((3,))],
        compiler_params=PARAMS,
        cost_estimate=attention_cost(heads * rows, keys),
        name="attend_local",
    )(*tables, new_query, new_keyval, leaf, pool)


def attention_cost(rows, keys):
    return pl.CostEstimate(
        flops=8 * LANES * rows * keys, bytes_accessed=8 * rows * 2 * LANES, transcendentals=rows * keys
    )


def extended(query, state, pool_refs, c):
    scores = [scores_of(query, key_window(ref, c)) for ref in pool_refs]
    values = [value_window(ref, c) for ref in pool_refs]
    return fold(scores, values, unpack(state))


def chunk_kernel(*refs, blocks):
    aug_ref, state_ref = refs[:2]
    pool_refs, out_ref = refs[2:-1], refs[-1]
    size = aug_ref.shape[0] // blocks
    for b in range(blocks):
        at = slice(b * size, (b + 1) * size)
        state = extended(aug_ref[at, :], state_ref[at, :], pool_refs, b % (blocks // 2))
        out_ref[at, :] = pack(*state)


def extend_attention(aug, state, pools, kv_local):
    keys = sum(item.shape[0] for item in pools)
    return pl.pallas_call(
        functools.partial(chunk_kernel, blocks=2 * kv_local),
        out_shape=jax.ShapeDtypeStruct(state.shape, f32),
        in_specs=[VMEM] * (2 + len(pools)),
        out_specs=VMEM,
        compiler_params=PARAMS,
        cost_estimate=attention_cost(aug.shape[0], keys),
        name="attend_pages",
    )(aug, state, *pools)


def finish_kernel(*refs, half, kv_local, chunks, width):
    aug_ref, state_ref = refs[:2]
    pool_refs = refs[2 : 2 + chunks]
    weight_hbm = refs[2 + chunks]
    part = aug_ref.shape[0] // (2 * width // HD)
    rest = refs[3 + chunks :]
    if half:
        other_ref, att_ref, proj_ref, weight_ref, mine_ref, sem = rest
    else:
        att_ref, proj_ref, weight_ref, mine_ref, sem = rest
    copy = pltpu.make_async_copy(weight_hbm, weight_ref, sem)
    copy.start()
    group = width // (kv_local * HD)
    size = group * part
    for c in range(kv_local):
        at = slice((half * kv_local + c) * size, (half * kv_local + c + 1) * size)
        if chunks:
            state = extended(aug_ref[at, :], state_ref[at, :], pool_refs, c)
        else:
            state = unpack(state_ref[at, :])
        shift = value_shift(c)
        result = (state[2][:, shift : shift + HD] / state[1]).astype(bf16)
        for g in range(group):
            h = c * group + g
            mine_ref[:, h * HD : (h + 1) * HD] = result[g * part : (g + 1) * part]
    if half:
        mine = pl.multiple_of(half_start(2 * part, 1), part)
        theirs = pl.multiple_of(half_start(2 * part, 0), part)
        att_ref[pl.ds(mine, part), :] = mine_ref[...]
        att_ref[pl.ds(theirs, part), :] = other_ref[...]
    else:
        att_ref[...] = mine_ref[...]
    copy.wait()
    proj = jnp.dot(mine_ref[...], weight_ref[...], preferred_element_type=f32)
    proj_ref[...] = proj.astype(proj_ref.dtype)


def finish_attention(aug, state, pools, out_weight, half, kv_local, rows, other):
    width = out_weight.shape[0]
    part = rows // 2
    keys = sum(item.shape[0] for item in pools)
    return pl.pallas_call(
        functools.partial(
            finish_kernel, half=half, kv_local=kv_local, chunks=len(pools), width=width
        ),
        out_shape=(
            jax.ShapeDtypeStruct((rows if half else part, width), bf16),
            jax.ShapeDtypeStruct((part, out_weight.shape[1]), f32 if half else bf16),
        ),
        in_specs=[VMEM] * (2 + len(pools)) + [ANY] + [VMEM] * half,
        out_specs=(VMEM, VMEM),
        scratch_shapes=[
            pltpu.VMEM(out_weight.shape, bf16),
            pltpu.VMEM((part, width), bf16),
            pltpu.SemaphoreType.DMA,
        ],
        compiler_params=PARAMS,
        cost_estimate=attention_cost(aug.shape[0] // 2, keys + 512),
        name="attend_finish",
    )(aug, state, *pools, out_weight, *other)


def normalized(values_in, gain):
    values = values_in.astype(f32)
    scale = lax.rsqrt(jnp.mean(values * values, axis=-1, keepdims=True) + EPSILON)
    return (values * scale * gain.astype(f32)).astype(bf16)


def block_width(width):
    return LANES if width % LANES == 0 else width


def mlp_kernel(rows_ref, gain_ref, gate_ref, up_ref, down_ref, out_ref, normed_ref, sum_ref):
    step = pl.program_id(0)

    @pl.when(step == 0)
    def _():
        normed_ref[...] = normalized(rows_ref[...], gain_ref[...])
        sum_ref[...] = jnp.zeros_like(sum_ref)

    normed = normed_ref[...]
    gate = jnp.dot(normed, gate_ref[...], preferred_element_type=f32)
    upward = jnp.dot(normed, up_ref[...], preferred_element_type=f32)
    hidden = (jax.nn.silu(gate) * upward).astype(bf16)
    sum_ref[...] += jnp.dot(hidden, down_ref[...], preferred_element_type=f32)

    @pl.when(step == pl.num_programs(0) - 1)
    def _():
        out_ref[...] = sum_ref[...].astype(out_ref.dtype)


def feed_forward(rows, gain, gate_weight, up_weight, down_weight, dtype):
    count, depth = rows.shape
    width = gate_weight.shape[1]
    step = block_width(width)
    return pl.pallas_call(
        mlp_kernel,
        out_shape=jax.ShapeDtypeStruct((count, depth), dtype),
        grid=(width // step,),
        in_specs=[
            pl.BlockSpec((count, depth), lambda i: (0, 0)),
            pl.BlockSpec((1, depth), lambda i: (0, 0)),
            pl.BlockSpec((depth, step), lambda i: (0, i)),
            pl.BlockSpec((depth, step), lambda i: (0, i)),
            pl.BlockSpec((step, depth), lambda i: (i, 0)),
        ],
        out_specs=pl.BlockSpec((count, depth), lambda i: (0, 0)),
        scratch_shapes=[pltpu.VMEM((count, depth), bf16), pltpu.VMEM((count, depth), f32)],
        compiler_params=PARAMS,
        cost_estimate=pl.CostEstimate(
            flops=6 * count * depth * width, bytes_accessed=6 * depth * width, transcendentals=0
        ),
        name="feed_forward",
    )(rows, gain.reshape(1, depth), gate_weight, up_weight, down_weight)


def next_kernel(rows_ref, gain_ref, query_ref, keyval_ref, *refs, half):
    if half:
        query_in, keyval_in, query_out, keyval_out, normed_ref, query_sum, keyval_sum = refs
    else:
        query_out, keyval_out, normed_ref, query_sum, keyval_sum = refs
    step = pl.program_id(0)
    depth = query_ref.shape[0]

    @pl.when(step == 0)
    def _():
        normed = normalized(rows_ref[...], gain_ref[...])
        for k in range(normed_ref.shape[0]):
            normed_ref[k] = normed[:, k * depth : (k + 1) * depth]
        query_sum[...] = jnp.zeros_like(query_sum)
        keyval_sum[...] = jnp.zeros_like(keyval_sum)

    normed = normed_ref[step]
    query_sum[...] += jnp.dot(normed, query_ref[...], preferred_element_type=f32)
    keyval_sum[...] += jnp.dot(normed, keyval_ref[...], preferred_element_type=f32)

    @pl.when(step == pl.num_programs(0) - 1)
    def _():
        query, keyval = query_sum[...].astype(bf16), keyval_sum[...].astype(bf16)
        if half:
            part = query.shape[0]
            mine = pl.multiple_of(half_start(2 * part, 1), part)
            theirs = pl.multiple_of(half_start(2 * part, 0), part)
            query_out[pl.ds(mine, part), :] = query
            query_out[pl.ds(theirs, part), :] = query_in[...]
            keyval_out[pl.ds(mine, part), :] = keyval
            keyval_out[pl.ds(theirs, part), :] = keyval_in[...]
        else:
            query_out[...] = query
            keyval_out[...] = keyval


def next_projections(rows, gain, query_weight, keyval_weight, other):
    count, depth = rows.shape
    steps = 5
    block = depth // steps
    widths = (query_weight.shape[1], keyval_weight.shape[1])
    half = len(other) > 0
    out_rows = 2 * count if half else count
    return pl.pallas_call(
        functools.partial(next_kernel, half=half),
        out_shape=tuple(jax.ShapeDtypeStruct((out_rows, w), bf16) for w in widths),
        grid=(steps,),
        in_specs=[
            pl.BlockSpec((count, depth), lambda i: (0, 0)),
            pl.BlockSpec((1, depth), lambda i: (0, 0)),
        ]
        + [pl.BlockSpec((block, w), lambda i: (i, 0)) for w in widths]
        + [pl.BlockSpec(item.shape, lambda i: (0, 0)) for item in other],
        out_specs=tuple(pl.BlockSpec((out_rows, w), lambda i: (0, 0)) for w in widths),
        scratch_shapes=[pltpu.VMEM((steps, count, block), bf16)]
        + [pltpu.VMEM((count, w), f32) for w in widths],
        compiler_params=PARAMS,
        cost_estimate=pl.CostEstimate(
            flops=2 * count * depth * sum(widths),
            bytes_accessed=2 * depth * sum(widths),
            transcendentals=0,
        ),
        name="next_layer",
    )(rows, gain.reshape(1, depth), query_weight, keyval_weight, *other)


def trade(value, axis, bit):
    size = lax.axis_size(axis)
    return lax.ppermute(value, axis, [(i, i ^ bit) for i in range(size)])


def cross(value, even_bit, odd_bit):
    size = lax.axis_size("req")
    pairs = [(i, i ^ (odd_bit if i % 2 else even_bit)) for i in range(size)]
    return lax.ppermute(value, "req", pairs)


def wide(value):
    return value.astype(f32)


def per_device(
    new_query,
    new_keyval,
    residual_in,
    leaf_cache,
    leaf_length,
    new_counts,
    request_mid,
    mid_root,
    node_length,
    prefix_pool,
    page_node,
    page_rank,
    out_weight,
    norm_gain,
    gate_weight,
    up_weight,
    down_weight,
    next_gain,
    query_weight,
    keyval_weight,
):
    rows = new_query.shape[0]
    part = rows // 2
    kv_local = new_keyval.shape[1] // (2 * HD)
    pool = prepare(page_node, page_rank, node_length, mid_root, prefix_pool)
    local_args = (new_query, new_keyval, leaf_cache, leaf_length, new_counts, request_mid, pool)
    if lax.axis_size("req") == 8:
        first = cross(pool, 2, 4)
        second = cross(pool, 4, 2)
        beside = trade(pool, "req", 1)
        aug, state = start_attention(*local_args)
        corner = cross(first, 4, 2)
        first_other = trade(first, "req", 1)
        second_other = trade(second, "req", 1)
        state = extend_attention(aug, state, [beside, first, second], kv_local)
        state = extend_attention(aug, state, [first_other, second_other], kv_local)
        corner_other = trade(corner, "req", 1)
        state = extend_attention(aug, state, [corner], kv_local)
        pools = [corner_other]
    else:
        every = lax.all_gather(pool, "req", axis=0)
        holders = every.shape[0]
        aug, state = start_attention(*local_args)
        places = (lax.axis_index("req") + 1 + jnp.arange(holders - 1)) % holders
        step = 4
        for i in range(0, holders - 1, step):
            chunk = every[places[i : i + step]].reshape(-1, pool.shape[1])
            state = extend_attention(aug, state, [chunk], kv_local)
        pools = []

    theirs_att, theirs_proj = finish_attention(
        aug, state, pools, out_weight, 0, kv_local, rows, ()
    )
    attention, mine_proj = finish_attention(
        aug, state, pools, out_weight, 1, kv_local, rows, (theirs_att,)
    )

    mine = half_start(rows, 1)
    theirs = half_start(rows, 0)
    share = rows // lax.axis_size("tp")
    place = lax.axis_index("tp") * share
    res_mine = lax.dynamic_slice_in_dim(residual_in, mine, part, 0)
    if lax.axis_size("tp") == 4:
        got = trade(theirs_proj, "tp", 1)
        pair = (mine_proj + wide(got)).astype(bf16)
        got = trade(pair, "tp", 2)
        mixed_mine = (wide(res_mine) + (wide(pair) + wide(got))).astype(bf16)
        mixed_theirs = trade(mixed_mine, "tp", 1)
        mlp = (norm_gain, gate_weight, up_weight, down_weight)
        mlp_mine = feed_forward(mixed_mine, *mlp, bf16)
        got = trade(mlp_mine, "tp", 1)
        mlp_theirs = feed_forward(mixed_theirs, *mlp, f32)
        pair = (mlp_theirs + wide(got)).astype(bf16)
        got = trade(pair, "tp", 2)
        layer_theirs = (wide(mixed_theirs) + (wide(pair) + wide(got))).astype(bf16)
        layer_mine = trade(layer_theirs, "tp", 1)
    else:
        res_theirs = lax.dynamic_slice_in_dim(residual_in, theirs, part, 0)
        order = jnp.where(mine == 0, 1, 0)

        def in_order(theirs_part, mine_part):
            both = jnp.stack([theirs_part, mine_part])
            return jnp.where(order == 1, both[::-1], both).reshape(rows, -1)

        total = lax.psum(in_order(wide(theirs_proj), mine_proj), "tp")
        mixed = (wide(in_order(res_theirs, res_mine)) + total).astype(bf16)
        mlp = feed_forward(mixed, norm_gain, gate_weight, up_weight, down_weight, f32)
        layer = (wide(mixed) + lax.psum(mlp, "tp")).astype(bf16)
        layer_mine = lax.dynamic_slice_in_dim(layer, mine, part, 0)
        layer_theirs = lax.dynamic_slice_in_dim(layer, theirs, part, 0)
    weights = (next_gain, query_weight, keyval_weight)
    other = next_projections(layer_theirs, *weights, ())
    next_query, next_keyval = next_projections(layer_mine, *weights, other)
    at = lax.rem(place, part)
    held = (place >= mine) & (place < mine + part)
    residual_out = jnp.where(
        held,
        lax.dynamic_slice_in_dim(layer_mine, at, share, 0),
        lax.dynamic_slice_in_dim(layer_theirs, at, share, 0),
    )
    return (attention, residual_out, next_query, next_keyval)


def solution(mesh):
    in_specs = (
        P("req", "tp"),
        P("req", "tp"),
        P("req", None),
        P("req", None, "tp"),
        P("req"),
        P("req", None),
        P("req"),
        P(),
        P(),
        P("req", None, "tp"),
        P("req"),
        P("req"),
        P("tp", None),
        P(),
        P(None, "tp"),
        P(None, "tp"),
        P("tp", None),
        P(),
        P(None, "tp"),
        P(None, "tp"),
    )
    out_specs = (P("req", "tp"), P(("req", "tp"), None), P("req", "tp"), P("req", "tp"))
    return jax.shard_map(
        per_device, mesh=mesh, in_specs=in_specs, out_specs=out_specs, check_vma=False
    )
```

time: 136 us -> 124 us (0.912)
  waiting for transfers between devices: 74.6 us -> 48.5 us
  Pallas kernels: 15.4 us -> 36.8 us
  matrix products: 12.7 us -> 0 us
  local copies, waits for them, and re-layouts: 12.5 us -> 19.4 us
  other arithmetic: 3.12 us -> 1.06 us
    ppermute x15 -> x10, waiting for transfers between devices: 74.6 us -> 36 us  [trade(): return lax.ppermute(value, axis, [(i, i ^ bit) for i in range(size)])]
    pallas_call x3 -> x10, Pallas kernels: 14 us -> 36 us  [the longest x2 16.5 us: feed_forward(): pl.pallas_call(mlp_kernel, out_shape=jax.ShapeDtypeStruct((count, depth),...]
    dot_general x5 -> x0, matrix products: 12.7 us -> none  [the longest x1 6.51 us: per_device(): jnp.dot(hidden, down_weight, preferred_element_type=f32)]
    ppermute x0 -> x3, waiting for transfers between devices: none -> 12.6 us  [cross(): return lax.ppermute(value, 'req', pairs)]
    unnamed x45 -> x37, local copies, waits for them, and re-layouts: 10.6 us -> 19.4 us
    ppermute x0 -> x3, starting transfers between devices: none -> 6.09 us  [cross(): return lax.ppermute(value, 'req', pairs)]
    ppermute x15 -> x10, starting transfers between devices: 16.1 us -> 11 us  [trade(): return lax.ppermute(value, axis, [(i, i ^ bit) for i in range(size)])]
    add x4 -> x0, other arithmetic: 1.37 us -> none  [the longest x2 1.2 us: total_over_tp(): first = first.astype(f32) + first_in.astype(f32)]
  transfers between devices with their start and end apart: 15 -> 13, of which waited for: 8 -> 6; matrix products, arithmetic and copies ran while one was open for 2% -> 4% of each run, Pallas kernels for 6% -> 25%
where the time goes in v2:
time: 124 us
  waiting for transfers between devices  48.5 us (39%)
  Pallas kernels  36.8 us (30%)
  local copies, waits for them, and re-layouts  19.4 us (16%)
  starting transfers between devices  17.1 us (14%)
    ppermute x10, waiting for transfers between devices, trade(): return lax.ppermute(value, axis, [(i, i ^ bit) for i in range(size)])  36 us
    unnamed x37, local copies, waits for them, and re-layouts  19.4 us
    pallas_call x2, Pallas kernels, feed_forward(): pl.pallas_call(mlp_kernel, out_shape=jax.ShapeDtypeStruct((count, depth),...  16.5 us
    ppermute x3, waiting for transfers between devices, cross(): return lax.ppermute(value, 'req', pairs)  12.6 us
    ppermute x10, starting transfers between devices, trade(): return lax.ppermute(value, axis, [(i, i ^ bit) for i in range(size)])  11 us
    pallas_call x3, Pallas kernels, extend_attention(): pl.pallas_call(functools.partial(chunk_kernel, blocks=2 * kv_local), out_...  7.56 us
    ppermute x3, starting transfers between devices, cross(): return lax.ppermute(value, 'req', pairs)  6.09 us
    pallas_call x2, Pallas kernels, finish_attention(): pl.pallas_call(functools.partial(finish_kernel, half=half, kv_local=kv_lo...  5.03 us
  transfers between devices with their start and end apart: 13, of which 6 were waited for; matrix products, arithmetic and copies ran while one was open for 4% of the time, Pallas kernels for 25%

profile of v2, /device:TPU:0, one launch (start us, length us, event | category | flops | bytes accessed | tf_op | source)
XLA Modules:
  0.0 123.7 jit_solution(437472396127810844)
XLA Ops:
  0.6 1.0 copy-done.4
  1.6 0.7 copy-done.5
  2.3 0.7 copy-done.6
  2.9 0.7 copy-done.7
  3.6 0.7 copy-done.8
  4.3 0.7 pool_rows.1.pool_ref
  5.0 3.0 %collective-permute-start.1 = (bf16[512,384]{1,0:T(8,128)(2,1)S(1)}, bf16[512,384]{1,0:T(8,128)(2,1)S(1)}, u32[]{:S(2)}, u32[]{:S(2)}) collective-permute-start(bf16[512,384]{1,0:T(8,128)(2,1)S(1)} %pool_rows.1.pool_ref), channel_id=1, source_target_pairs={{0,8},{4,20},{8,0},{12,28},{16,24},{20,4},{24,16},{28,12},{1,9},{5... | collective-permute-start | bytes 1179656 | tf_op jit(solution)/shard_map/ppermute | solution.py:447
  8.0 1.5 %collective-permute-start.2 = (bf16[512,384]{1,0:T(8,128)(2,1)S(1)}, bf16[512,384]{1,0:T(8,128)(2,1)S(1)}, u32[]{:S(2)}, u32[]{:S(2)}) collective-permute-start(bf16[512,384]{1,0:T(8,128)(2,1)S(1)} %pool_rows.1.pool_ref), channel_id=1, source_target_pairs={{0,16},{4,12},{8,24},{12,4},{16,0},{20,28},{24,8},{28,20},{1,17},{... | collective-permute-start | bytes 1179656 | tf_op jit(solution)/shard_map/ppermute | solution.py:447
  9.5 7.9 %collective-permute-done.1.refs_3_ = bf16[512,384]{1,0:T(8,128)(2,1)S(1)} collective-permute-done((bf16[512,384]{1,0:T(8,128)(2,1)S(1)}, bf16[512,384]{1,0:T(8,128)(2,1)S(1)}, u32[]{:S(2)}, u32[]{:S(2)}) %collective-permute-start.1) | collective-permute-done | bytes 393248 | tf_op jit(solution)/shard_map/ppermute | solution.py:447
  17.4 1.6 %collective-permute-start.5 = (bf16[512,384]{1,0:T(8,128)(2,1)S(1)}, bf16[512,384]{1,0:T(8,128)(2,1)S(1)}, u32[]{:S(2)}, u32[]{:S(2)}) collective-permute-start(bf16[512,384]{1,0:T(8,128)(2,1)S(1)} %collective-permute-done.1.refs_3_), channel_id=1, source_target_pairs={{0,16},{4,12},{8,24},{12,4},{16,0},{20,28},{24,8},{28,20},{1,17},{... | collective-permute-start | bytes 1179656 | tf_op jit(solution)/shard_map/ppermute | solution.py:447
  19.0 0.5 collective-permute-start.3
  19.5 1.0 copy.24.keyval_ref
  20.5 4.7 %collective-permute-done.5.refs_2_ = bf16[512,384]{1,0:T(8,128)(2,1)S(1)} collective-permute-done((bf16[512,384]{1,0:T(8,128)(2,1)S(1)}, bf16[512,384]{1,0:T(8,128)(2,1)S(1)}, u32[]{:S(2)}, u32[]{:S(2)}) %collective-permute-start.5) | collective-permute-done | bytes 393248 | tf_op jit(solution)/shard_map/ppermute | solution.py:447
  25.2 1.0 copy-done.9
  26.2 0.9 copy-done.10
  27.1 0.7 copy-done.11
  27.8 0.7 copy-done.12
  28.4 0.7 copy-done.13
  29.1 2.9 %attend_local.1 = (bf16[1024,256]{1,0:T(8,128)(2,1)S(1)}, f32[1024,256]{1,0:T(8,128)S(1)}) custom-call(s32[1,16]{1,0:T(1,128)S(1)} %copy-done.11, s32[16]{0:T(128)S(1)} %copy-done.12, s32[16]{0:T(128)S(1)} %copy-done.13, bf16[128,640]{1,0:T(8,128)(2,1)S(1)} %copy-done.10, bf16[128,320]{1,0:T(8,128)(2,1)S(1)} %copy.24.keyval_ref, ...), custom_call_target="tpu_custom_call" | custom-call | flops 1207959552 | bytes 2097152 | tf_op jit(solution)/shard_map/attend_local/pallas_call | solution.py:207
  32.0 3.0 %attend_pages.3.refs_1_ = f32[1024,256]{1,0:T(8,128)S(1)} custom-call(bf16[1024,256]{1,0:T(8,128)(2,1)S(1)} %get-tuple-element.14.refs_0_, f32[1024,256]{1,0:T(8,128)S(1)} %get-tuple-element.15.refs_1_, bf16[512,384]{1,0:T(8,128)(2,1)S(1)} %collective-permute-done.refs_2_, bf16[512,384]{1,0:T(8,128)(2,1)S(1)} %collective-permute-done.1.refs_3_, ...), custom_call_target="tpu_custom_call" | custom-call | flops 1610612736 | bytes 2097152 | tf_op jit(solution)/shard_map/attend_pages/pallas_call | solution.py:246
  35.0 2.8 %attend_pages.4.refs_1_ = f32[1024,256]{1,0:T(8,128)S(1)} custom-call(bf16[1024,256]{1,0:T(8,128)(2,1)S(1)} %get-tuple-element.14.refs_0_, f32[1024,256]{1,0:T(8,128)S(1)} %attend_pages.3.refs_1_, bf16[512,384]{1,0:T(8,128)(2,1)S(1)} %collective-permute-done.3.refs_2_, bf16[512,384]{1,0:T(8,128)(2,1)S(1)} %collective-permute-done.4.refs_3_), custom_call_target="tpu_custom_call" | custom-call | flops 1073741824 | bytes 2097152 | tf_op jit(solution)/shard_map/attend_pages/pallas_call | solution.py:246
  37.8 1.8 %attend_pages.5.refs_1_ = f32[1024,256]{1,0:T(8,128)S(1)} custom-call(bf16[1024,256]{1,0:T(8,128)(2,1)S(1)} %get-tuple-element.14.refs_0_, f32[1024,256]{1,0:T(8,128)S(1)} %attend_pages.4.refs_1_, bf16[512,384]{1,0:T(8,128)(2,1)S(1)} %collective-permute-done.5.refs_2_), custom_call_target="tpu_custom_call" | custom-call | flops 536870912 | bytes 2097152 | tf_op jit(solution)/shard_map/attend_pages/pallas_call | solution.py:246
  39.6 2.7 %attend_finish.2 = (bf16[64,640]{1,0:T(8,128)(2,1)S(1)}, bf16[64,2560]{1,0:T(8,128)(2,1)S(1)}) custom-call(bf16[1024,256]{1,0:T(8,128)(2,1)S(1)} %get-tuple-element.14.refs_0_, f32[1024,256]{1,0:T(8,128)S(1)} %attend_pages.5.refs_1_, bf16[512,384]{1,0:T(8,128)(2,1)S(1)} %collective-permute-done.6.refs_2_, bf16[640,2560]{1,0:T(8,128)(2,1)S(1)} %copy-done.2), custom_call_target="tpu_custom_call" | custom-call | flops 536870912 | bytes 1048576 | tf_op jit(solution)/shard_map/attend_finish/pallas_call | solution.py:298
  42.3 2.6 %collective-permute-start.7 = (bf16[64,2560]{1,0:T(8,128)(2,1)S(1)}, bf16[64,2560]{1,0:T(8,128)(2,1)S(1)}, u32[]{:S(2)}, u32[]{:S(2)}) collective-permute-start(bf16[64,2560]{1,0:T(8,128)(2,1)S(1)} %get-tuple-element.19), channel_id=1, source_target_pairs={{0,1},{1,0},{2,3},{3,2},{4,5},{5,4},{6,7},{7,6},{8,9},{9,8},{10,11... | collective-permute-start | bytes 983048 | tf_op jit(solution)/shard_map/ppermute | solution.py:441
  44.9 2.3 %attend_finish.3 = (bf16[128,640]{1,0:T(8,128)(2,1)}, f32[64,2560]{1,0:T(8,128)S(1)}) custom-call(bf16[1024,256]{1,0:T(8,128)(2,1)S(1)} %get-tuple-element.14.refs_0_, f32[1024,256]{1,0:T(8,128)S(1)} %attend_pages.5.refs_1_, bf16[512,384]{1,0:T(8,128)(2,1)S(1)} %collective-permute-done.6.refs_2_, bf16[640,2560]{1,0:T(8,128)(2,1)S(1)} %copy-done.2, ...), custom_call_target="tpu_custom_call" | custom-call | flops 536870912 | bytes 1048576 | tf_op jit(solution)/shard_map/attend_finish/pallas_call | solution.py:298
  47.3 6.0 %collective-permute-done.7 = bf16[64,2560]{1,0:T(8,128)(2,1)S(1)} collective-permute-done((bf16[64,2560]{1,0:T(8,128)(2,1)S(1)}, bf16[64,2560]{1,0:T(8,128)(2,1)S(1)}, u32[]{:S(2)}, u32[]{:S(2)}) %collective-permute-start.7) | collective-permute-done | bytes 327712 | tf_op jit(solution)/shard_map/ppermute | solution.py:441
  53.3 0.1 add_convert_fusion.3
  53.4 2.8 %collective-permute-start.8 = (bf16[64,2560]{1,0:T(8,128)(2,1)S(1)}, bf16[64,2560]{1,0:T(8,128)(2,1)S(1)}, u32[]{:S(2)}, u32[]{:S(2)}) collective-permute-start(bf16[64,2560]{1,0:T(8,128)(2,1)S(1)} %add_convert_fusion.3), channel_id=1, source_target_pairs={{0,2},{1,3},{2,0},{3,1},{4,6},{5,7},{6,4},{7,5},{8,10},{9,11},{10,... | collective-permute-start | bytes 983048 | tf_op jit(solution)/shard_map/ppermute | solution.py:441
  56.2 14.7 %collective-permute-done.8 = bf16[64,2560]{1,0:T(8,128)(2,1)S(1)} collective-permute-done((bf16[64,2560]{1,0:T(8,128)(2,1)S(1)}, bf16[64,2560]{1,0:T(8,128)(2,1)S(1)}, u32[]{:S(2)}, u32[]{:S(2)}) %collective-permute-start.8) | collective-permute-done | bytes 327712 | tf_op jit(solution)/shard_map/ppermute | solution.py:441
  70.9 0.1 add_convert_fusion.2.rows_ref
  71.0 0.7 collective-permute-start.9
  71.7 2.3 %copy-done = bf16[2560,896]{1,0:T(8,128)(2,1)S(1)} copy-done((bf16[2560,896]{1,0:T(8,128)(2,1)S(1)}, bf16[2560,896]{1,0:T(8,128)(2,1)}, u32[]{:S(2)}) %copy-start) | copy-done | bytes 4587544
  74.0 8.2 %feed_forward.3 = bf16[64,2560]{1,0:T(8,128)(2,1)S(1)} custom-call(bf16[64,2560]{1,0:T(8,128)(2,1)S(1)} %add_convert_fusion.2.rows_ref, bf16[1,2560]{1,0:T(2,128)(2,1)S(1)} %reshape.16.gain_ref, bf16[2560,896]{1,0:T(8,128)(2,1)S(1)} %copy-done, bf16[2560,896]{1,0:T(8,128)(2,1)} %up_ref.3, bf16[896,2560]{1,0:T(8,128)(2,1)} %down_ref.3), custom_call_target="tpu_custom_call" | custom-call | flops 880803840 | bytes 13762560 | tf_op jit(solution)/shard_map/feed_forward/pallas_call | solution.py:352
  82.2 1.5 %collective-permute-start.10 = (bf16[64,2560]{1,0:T(8,128)(2,1)S(1)}, bf16[64,2560]{1,0:T(8,128)(2,1)S(1)}, u32[]{:S(2)}, u32[]{:S(2)}) collective-permute-start(bf16[64,2560]{1,0:T(8,128)(2,1)S(1)} %feed_forward.3), channel_id=1, source_target_pairs={{0,1},{1,0},{2,3},{3,2},{4,5},{5,4},{6,7},{7,6},{8,9},{9,8},{10,11... | collective-permute-start | bytes 983048 | tf_op jit(solution)/shard_map/ppermute | solution.py:441
  83.7 2.3 %copy-done.1 = bf16[2560,896]{1,0:T(8,128)(2,1)S(1)} copy-done((bf16[2560,896]{1,0:T(8,128)(2,1)S(1)}, bf16[2560,896]{1,0:T(8,128)(2,1)}, u32[]{:S(2)}) %copy-start.1) | copy-done | bytes 4587544
  86.0 8.2 %feed_forward.2 = f32[64,2560]{1,0:T(8,128)S(1)} custom-call(bf16[64,2560]{1,0:T(8,128)(2,1)S(1)} %collective-permute-done.9.rows_ref, bf16[1,2560]{1,0:T(2,128)(2,1)S(1)} %reshape.16.gain_ref, bf16[2560,896]{1,0:T(8,128)(2,1)S(1)} %copy-done.1, bf16[2560,896]{1,0:T(8,128)(2,1)} %up_ref.3, bf16[896,2560]{1,0:T(8,128)(2,1)} %down_ref.3), custom_call_target="tpu_custom_call" | custom-call | flops 880803840 | bytes 13762560 | tf_op jit(solution)/shard_map/feed_forward/pallas_call | solution.py:352
  94.3 0.1 add_convert_fusion.1
  94.4 2.1 %collective-permute-start.11 = (bf16[64,2560]{1,0:T(8,128)(2,1)S(1)}, bf16[64,2560]{1,0:T(8,128)(2,1)S(1)}, u32[]{:S(2)}, u32[]{:S(2)}) collective-permute-start(bf16[64,2560]{1,0:T(8,128)(2,1)S(1)} %add_convert_fusion.1), channel_id=1, source_target_pairs={{0,2},{1,3},{2,0},{3,1},{4,6},{5,7},{6,4},{7,5},{8,10},{9,11},{10,... | collective-permute-start | bytes 983048 | tf_op jit(solution)/shard_map/ppermute | solution.py:441
  96.4 14.6 %collective-permute-done.11 = bf16[64,2560]{1,0:T(8,128)(2,1)S(1)} collective-permute-done((bf16[64,2560]{1,0:T(8,128)(2,1)S(1)}, bf16[64,2560]{1,0:T(8,128)(2,1)S(1)}, u32[]{:S(2)}, u32[]{:S(2)}) %collective-permute-start.11) | collective-permute-done | bytes 327712 | tf_op jit(solution)/shard_map/ppermute | solution.py:441
  111.1 0.1 add_convert_fusion.rows_ref
  111.2 0.8 collective-permute-start.12
  112.0 3.6 %copy.26.keyval_ref = bf16[2560,320]{1,0:T(8,128)(2,1)S(1)} copy(bf16[2560,320]{0,1:T(8,128)(2,1)} %param.39) | data formatting | bytes 3276800 | tf_op args[19]
  115.6 1.9 %copy-done.3 = bf16[2560,640]{1,0:T(8,128)(2,1)S(1)} copy-done((bf16[2560,640]{1,0:T(8,128)(2,1)S(1)}, bf16[2560,640]{1,0:T(8,128)(2,1)}, u32[]{:S(2)}) %copy-start.3) | copy-done | bytes 3276824
  117.5 1.7 %next_layer.2 = (bf16[64,640]{1,0:T(8,128)(2,1)S(1)}, bf16[64,320]{1,0:T(8,128)(2,1)S(1)}) custom-call(bf16[64,2560]{1,0:T(8,128)(2,1)S(1)} %add_convert_fusion.rows_ref, bf16[1,2560]{1,0:T(2,128)(2,1)S(1)} %reshape.17.gain_ref, bf16[2560,640]{1,0:T(8,128)(2,1)S(1)} %copy-done.3, bf16[2560,320]{1,0:T(8,128)(2,1)S(1)} %copy.26.keyval_ref), custom_call_target="tpu_custom_call" | custom-call | flops 314572800 | bytes 4915200 | tf_op jit(solution)/shard_map/next_layer/pallas_call | solution.py:416
  119.2 0.6 collective-permute-done.12.rows_ref
  119.9 2.4 %next_layer.3 = (bf16[128,640]{1,0:T(8,128)(2,1)}, bf16[128,320]{1,0:T(8,128)(2,1)S(1)}) custom-call(bf16[64,2560]{1,0:T(8,128)(2,1)S(1)} %collective-permute-done.12.rows_ref, bf16[1,2560]{1,0:T(2,128)(2,1)S(1)} %reshape.17.gain_ref, bf16[2560,640]{1,0:T(8,128)(2,1)S(1)} %copy-done.3, bf16[2560,320]{1,0:T(8,128)(2,1)S(1)} %copy.26.keyval_ref, ...), custom_call_target="tpu_custom_call" | custom-call | flops 314572800 | bytes 4915200 | tf_op jit(solution)/shard_map/next_layer/pallas_call | solution.py:416
  122.2 0.7 copy.27
  123.0 0.7 dynamic-slice_select_fusion
  (33 shorter events, 0.1 us)
Async XLA Ops:
  0.6 1.0 copy-start.4
  1.6 0.7 copy-start.5
  2.3 0.7 copy-start.6
  2.9 0.7 copy-start.7
  3.6 0.7 copy-start.8
  5.0 12.4 %collective-permute-start.1 = (bf16[512,384]{1,0:T(8,128)(2,1)S(1)}, bf16[512,384]{1,0:T(8,128)(2,1)S(1)}, u32[]{:S(2)}, u32[]{:S(2)}) collective-permute-start(bf16[512,384]{1,0:T(8,128)(2,1)S(1)} %pool_rows.1.pool_ref), channel_id=1, source_target_pairs={{0,8},{4,20},{8,0},{12,28},{16,24},{20,4},{24,16},{28,12},{1,9},{5... | collective-permute-start | bytes 1179656 | tf_op jit(solution)/shard_map/ppermute | solution.py:447
  8.0 11.5 %collective-permute-start.2 = (bf16[512,384]{1,0:T(8,128)(2,1)S(1)}, bf16[512,384]{1,0:T(8,128)(2,1)S(1)}, u32[]{:S(2)}, u32[]{:S(2)}) collective-permute-start(bf16[512,384]{1,0:T(8,128)(2,1)S(1)} %pool_rows.1.pool_ref), channel_id=1, source_target_pairs={{0,16},{4,12},{8,24},{12,4},{16,0},{20,28},{24,8},{28,20},{1,17},{... | collective-permute-start | bytes 1179656 | tf_op jit(solution)/shard_map/ppermute | solution.py:447
  17.4 7.8 %collective-permute-start.5 = (bf16[512,384]{1,0:T(8,128)(2,1)S(1)}, bf16[512,384]{1,0:T(8,128)(2,1)S(1)}, u32[]{:S(2)}, u32[]{:S(2)}) collective-permute-start(bf16[512,384]{1,0:T(8,128)(2,1)S(1)} %collective-permute-done.1.refs_3_), channel_id=1, source_target_pairs={{0,16},{4,12},{8,24},{12,4},{16,0},{20,28},{24,8},{28,20},{1,17},{... | collective-permute-start | bytes 1179656 | tf_op jit(solution)/shard_map/ppermute | solution.py:447
  19.0 13.0 %collective-permute-start = (bf16[512,384]{1,0:T(8,128)(2,1)S(1)}, bf16[512,384]{1,0:T(8,128)(2,1)S(1)}, u32[]{:S(2)}, u32[]{:S(2)}) collective-permute-start(bf16[512,384]{1,0:T(8,128)(2,1)S(1)} %pool_rows.1.pool_ref), channel_id=1, source_target_pairs={{0,4},{4,0},{8,12},{12,8},{16,20},{20,16},{24,28},{28,24},{1,5},{5... | collective-permute-start | bytes 1179656 | tf_op jit(solution)/shard_map/ppermute | solution.py:441
  19.0 16.0 %collective-permute-start.3 = (bf16[512,384]{1,0:T(8,128)(2,1)S(1)}, bf16[512,384]{1,0:T(8,128)(2,1)S(1)}, u32[]{:S(2)}, u32[]{:S(2)}) collective-permute-start(bf16[512,384]{1,0:T(8,128)(2,1)S(1)} %collective-permute-done.1.refs_3_), channel_id=1, source_target_pairs={{0,4},{4,0},{8,12},{12,8},{16,20},{20,16},{24,28},{28,24},{1,5},{5... | collective-permute-start | bytes 1179656 | tf_op jit(solution)/shard_map/ppermute | solution.py:441
  19.5 15.5 %collective-permute-start.4 = (bf16[512,384]{1,0:T(8,128)(2,1)S(1)}, bf16[512,384]{1,0:T(8,128)(2,1)S(1)}, u32[]{:S(2)}, u32[]{:S(2)}) collective-permute-start(bf16[512,384]{1,0:T(8,128)(2,1)S(1)} %collective-permute-done.2.refs_4_), channel_id=1, source_target_pairs={{0,4},{4,0},{8,12},{12,8},{16,20},{20,16},{24,28},{28,24},{1,5},{5... | collective-permute-start | bytes 1179656 | tf_op jit(solution)/shard_map/ppermute | solution.py:441
  25.2 14.4 %collective-permute-start.6 = (bf16[512,384]{1,0:T(8,128)(2,1)S(1)}, bf16[512,384]{1,0:T(8,128)(2,1)S(1)}, u32[]{:S(2)}, u32[]{:S(2)}) collective-permute-start(bf16[512,384]{1,0:T(8,128)(2,1)S(1)} %collective-permute-done.5.refs_2_), channel_id=1, source_target_pairs={{0,4},{4,0},{8,12},{12,8},{16,20},{20,16},{24,28},{28,24},{1,5},{5... | collective-permute-start | bytes 1179656 | tf_op jit(solution)/shard_map/ppermute | solution.py:441
  25.2 1.0 copy-start.9
  26.2 0.9 copy-start.10
  27.1 0.7 copy-start.11
  27.8 0.7 copy-start.12
  28.4 0.7 copy-start.13
  34.9 4.6 %copy-start.2 = (bf16[640,2560]{1,0:T(8,128)(2,1)S(1)}, bf16[640,2560]{1,0:T(8,128)(2,1)}, u32[]{:S(2)}) copy-start(bf16[640,2560]{1,0:T(8,128)(2,1)} %refs_3_.3) | copy-start | bytes 9830404
  42.3 11.0 %collective-permute-start.7 = (bf16[64,2560]{1,0:T(8,128)(2,1)S(1)}, bf16[64,2560]{1,0:T(8,128)(2,1)S(1)}, u32[]{:S(2)}, u32[]{:S(2)}) collective-permute-start(bf16[64,2560]{1,0:T(8,128)(2,1)S(1)} %get-tuple-element.19), channel_id=1, source_target_pairs={{0,1},{1,0},{2,3},{3,2},{4,5},{5,4},{6,7},{7,6},{8,9},{9,8},{10,11... | collective-permute-start | bytes 983048 | tf_op jit(solution)/shard_map/ppermute | solution.py:441
  44.9 11.3 %copy-start.15 = (bf16[2560]{0:T(1024)(128)(2,1)S(1)}, bf16[2560]{0:T(1024)(128)(2,1)}, u32[]{:S(2)}) copy-start(bf16[2560]{0:T(1024)(128)(2,1)} %param.33) | copy-start | bytes 15364
  44.9 26.0 %copy-start.14 = (bf16[128,2560]{1,0:T(8,128)(2,1)S(1)}, bf16[128,2560]{1,0:T(8,128)(2,1)}, u32[]{:S(2)}) copy-start(bf16[128,2560]{1,0:T(8,128)(2,1)} %param.22) | copy-start | bytes 1966084
  53.4 17.5 %collective-permute-start.8 = (bf16[64,2560]{1,0:T(8,128)(2,1)S(1)}, bf16[64,2560]{1,0:T(8,128)(2,1)S(1)}, u32[]{:S(2)}, u32[]{:S(2)}) collective-permute-start(bf16[64,2560]{1,0:T(8,128)(2,1)S(1)} %add_convert_fusion.3), channel_id=1, source_target_pairs={{0,2},{1,3},{2,0},{3,1},{4,6},{5,7},{6,4},{7,5},{8,10},{9,11},{10,... | collective-permute-start | bytes 983048 | tf_op jit(solution)/shard_map/ppermute | solution.py:441
  71.0 12.7 %collective-permute-start.9 = (bf16[64,2560]{1,0:T(8,128)(2,1)S(1)}, bf16[64,2560]{1,0:T(8,128)(2,1)S(1)}, u32[]{:S(2)}, u32[]{:S(2)}) collective-permute-start(bf16[64,2560]{1,0:T(8,128)(2,1)S(1)} %add_convert_fusion.2.rows_ref), channel_id=1, source_target_pairs={{0,1},{1,0},{2,3},{3,2},{4,5},{5,4},{6,7},{7,6},{8,9},{9,8},{10,11... | collective-permute-start | bytes 983048 | tf_op jit(solution)/shard_map/ppermute | solution.py:441
  71.7 2.3 %copy-start = (bf16[2560,896]{1,0:T(8,128)(2,1)S(1)}, bf16[2560,896]{1,0:T(8,128)(2,1)}, u32[]{:S(2)}) copy-start(bf16[2560,896]{1,0:T(8,128)(2,1)} %gate_ref.3) | copy-start | bytes 13762564
  82.2 12.0 %collective-permute-start.10 = (bf16[64,2560]{1,0:T(8,128)(2,1)S(1)}, bf16[64,2560]{1,0:T(8,128)(2,1)S(1)}, u32[]{:S(2)}, u32[]{:S(2)}) collective-permute-start(bf16[64,2560]{1,0:T(8,128)(2,1)S(1)} %feed_forward.3), channel_id=1, source_target_pairs={{0,1},{1,0},{2,3},{3,2},{4,5},{5,4},{6,7},{7,6},{8,9},{9,8},{10,11... | collective-permute-start | bytes 983048 | tf_op jit(solution)/shard_map/ppermute | solution.py:441
  83.7 2.3 %copy-start.1 = (bf16[2560,896]{1,0:T(8,128)(2,1)S(1)}, bf16[2560,896]{1,0:T(8,128)(2,1)}, u32[]{:S(2)}) copy-start(bf16[2560,896]{1,0:T(8,128)(2,1)} %gate_ref.3) | copy-start | bytes 13762564
  94.3 21.3 %copy-start.16 = (bf16[2560]{0:T(1024)(128)(2,1)S(1)}, bf16[2560]{0:T(1024)(128)(2,1)}, u32[]{:S(2)}) copy-start(bf16[2560]{0:T(1024)(128)(2,1)} %param.37) | copy-start | bytes 15364
  94.4 16.7 %collective-permute-start.11 = (bf16[64,2560]{1,0:T(8,128)(2,1)S(1)}, bf16[64,2560]{1,0:T(8,128)(2,1)S(1)}, u32[]{:S(2)}, u32[]{:S(2)}) collective-permute-start(bf16[64,2560]{1,0:T(8,128)(2,1)S(1)} %add_convert_fusion.1), channel_id=1, source_target_pairs={{0,2},{1,3},{2,0},{3,1},{4,6},{5,7},{6,4},{7,5},{8,10},{9,11},{10,... | collective-permute-start | bytes 983048 | tf_op jit(solution)/shard_map/ppermute | solution.py:441
  111.2 8.7 %collective-permute-start.12 = (bf16[64,2560]{1,0:T(8,128)(2,1)S(1)}, bf16[64,2560]{1,0:T(8,128)(2,1)S(1)}, u32[]{:S(2)}, u32[]{:S(2)}) collective-permute-start(bf16[64,2560]{1,0:T(8,128)(2,1)S(1)} %add_convert_fusion.rows_ref), channel_id=1, source_target_pairs={{0,1},{1,0},{2,3},{3,2},{4,5},{5,4},{6,7},{7,6},{8,9},{9,8},{10,11... | collective-permute-start | bytes 983048 | tf_op jit(solution)/shard_map/ppermute | solution.py:441
  115.6 1.9 %copy-start.3 = (bf16[2560,640]{1,0:T(8,128)(2,1)S(1)}, bf16[2560,640]{1,0:T(8,128)(2,1)}, u32[]{:S(2)}) copy-start(bf16[2560,640]{1,0:T(8,128)(2,1)} %query_ref.5) | copy-start | bytes 9830404

commit v3 on v2

--- a/solution.py
+++ b/solution.py
@@ -19,10 +19,10 @@
 bf16 = jnp.bfloat16
 f32 = jnp.float32
 i32 = jnp.int32
-ANY = pl.BlockSpec(memory_space=pl.ANY)
+HBM = pl.BlockSpec(memory_space=pltpu.HBM)
 VMEM = pl.BlockSpec(memory_space=pltpu.VMEM)
 SMEM = pl.BlockSpec(memory_space=pltpu.SMEM)
-PARAMS = pltpu.CompilerParams(vmem_limit_bytes=48 * 1024 * 1024)
+PARAMS = pltpu.CompilerParams(vmem_limit_bytes=24 * 1024 * 1024)
 
 
 def padded(width):
@@ -65,6 +65,14 @@
     for copy in copies:
         copy.start()
     return copies
+
+
+def in_hbm(values):
+    return [pltpu.with_memory_space_constraint(value, pltpu.HBM) for value in values]
+
+
+def in_vmem(values):
+    return [pltpu.with_memory_space_constraint(value, pltpu.VMEM) for value in values]
 
 
 def prep_kernel(
@@ -96,12 +104,12 @@
     return pl.pallas_call(
         prep_kernel,
         out_shape=jax.ShapeDtypeStruct((pages * size, padded(width + MIDS)), bf16),
-        in_specs=[ANY] * 4 + [VMEM],
+        in_specs=[HBM] * 4 + [VMEM],
         out_specs=VMEM,
         scratch_shapes=[pltpu.SMEM(t.shape, i32) for t in tables] + [pltpu.SemaphoreType.DMA((4,))],
         compiler_params=PARAMS,
         name="pool_rows",
-    )(*tables, prefix_pool)
+    )(*in_hbm(tables), prefix_pool)
 
 
 def half_start(rows, half):
@@ -137,9 +145,10 @@
 
 
 def local_kernel(
-    count_hbm, mid_hbm, leaf_len_hbm, query_ref, keyval_ref, leaf_ref, pool_ref, aug_ref, state_ref,
-    count_ref, mid_ref, leaf_len_ref, sems,
+    count_hbm, mid_hbm, leaf_len_hbm, query_ref, keyval_ref, leaf_ref, *refs, chunks
 ):
+    pool_refs = refs[:chunks]
+    aug_ref, state_ref, count_ref, mid_ref, leaf_len_ref, sems = refs[chunks:]
     pairs = ((count_hbm, count_ref), (mid_hbm, mid_ref), (leaf_len_hbm, leaf_len_ref))
     for copy in fetch(pairs, sems):
         copy.wait()
@@ -194,29 +203,30 @@
                 values = [
                     jnp.concatenate([v, jnp.zeros((v.shape[0], fill), bf16)], axis=1) for v in values
                 ]
-            scores.append(scores_of(query, key_window(pool_ref, c)))
-            values.append(value_window(pool_ref, c))
+            for pool_ref in pool_refs:
+                scores.append(scores_of(query, key_window(pool_ref, c)))
+                values.append(value_window(pool_ref, c))
             state_ref[block, :] = pack(*fold(scores, values, None))
 
 
-def start_attention(new_query, new_keyval, leaf, leaf_length, counts, request_mid, pool):
+def start_attention(new_query, new_keyval, leaf, leaf_length, counts, request_mid, pools):
     rows, query_width = new_query.shape
     heads = query_width // HD
     tables = (counts, request_mid, leaf_length)
-    keys = leaf.shape[0] * leaf.shape[1] + rows + pool.shape[0]
-    return pl.pallas_call(
-        local_kernel,
+    keys = leaf.shape[0] * leaf.shape[1] + rows + sum(item.shape[0] for item in pools)
+    return pl.pallas_call(
+        functools.partial(local_kernel, chunks=len(pools)),
         out_shape=(
             jax.ShapeDtypeStruct((heads * rows, 2 * LANES), bf16),
             jax.ShapeDtypeStruct((heads * rows, 2 * LANES), f32),
         ),
-        in_specs=[ANY] * 3 + [VMEM] * 4,
+        in_specs=[HBM] * 3 + [VMEM] * (3 + len(pools)),
         out_specs=(VMEM, VMEM),
         scratch_shapes=[pltpu.SMEM(t.shape, i32) for t in tables] + [pltpu.SemaphoreType.DMA((3,))],
         compiler_params=PARAMS,
         cost_estimate=attention_cost(heads * rows, keys),
         name="attend_local",
-    )(*tables, new_query, new_keyval, leaf, pool)
+    )(*in_hbm(tables), new_query, new_keyval, leaf, *pools)
 
 
 def attention_cost(rows, keys):
@@ -257,15 +267,13 @@
 def finish_kernel(*refs, half, kv_local, chunks, width):
     aug_ref, state_ref = refs[:2]
     pool_refs = refs[2 : 2 + chunks]
-    weight_hbm = refs[2 + chunks]
+    weight_ref = refs[2 + chunks]
     part = aug_ref.shape[0] // (2 * width // HD)
     rest = refs[3 + chunks :]
     if half:
-        other_ref, att_ref, proj_ref, weight_ref, mine_ref, sem = rest
+        other_ref, att_ref, proj_ref, mine_ref = rest
     else:
-        att_ref, proj_ref, weight_ref, mine_ref, sem = rest
-    copy = pltpu.make_async_copy(weight_hbm, weight_ref, sem)
-    copy.start()
+        att_ref, proj_ref, mine_ref = rest
     group = width // (kv_local * HD)
     size = group * part
     for c in range(kv_local):
@@ -286,7 +294,6 @@
         att_ref[pl.ds(theirs, part), :] = other_ref[...]
     else:
         att_ref[...] = mine_ref[...]
-    copy.wait()
     proj = jnp.dot(mine_ref[...], weight_ref[...], preferred_element_type=f32)
     proj_ref[...] = proj.astype(proj_ref.dtype)
 
@@ -303,13 +310,9 @@
             jax.ShapeDtypeStruct((rows if half else part, width), bf16),
             jax.ShapeDtypeStruct((part, out_weight.shape[1]), f32 if half else bf16),
         ),
-        in_specs=[VMEM] * (2 + len(pools)) + [ANY] + [VMEM] * half,
+        in_specs=[VMEM] * (3 + len(pools) + half),
         out_specs=(VMEM, VMEM),
-        scratch_shapes=[
-            pltpu.VMEM(out_weight.shape, bf16),
-            pltpu.VMEM((part, width), bf16),
-            pltpu.SemaphoreType.DMA,
-        ],
+        scratch_shapes=[pltpu.VMEM((part, width), bf16)],
         compiler_params=PARAMS,
         cost_estimate=attention_cost(aug.shape[0] // 2, keys + 512),
         name="attend_finish",
@@ -322,110 +325,95 @@
     return (values * scale * gain.astype(f32)).astype(bf16)
 
 
-def block_width(width):
-    return LANES if width % LANES == 0 else width
-
-
-def mlp_kernel(rows_ref, gain_ref, gate_ref, up_ref, down_ref, out_ref, normed_ref, sum_ref):
-    step = pl.program_id(0)
-
-    @pl.when(step == 0)
-    def _():
-        normed_ref[...] = normalized(rows_ref[...], gain_ref[...])
-        sum_ref[...] = jnp.zeros_like(sum_ref)
-
-    normed = normed_ref[...]
+def stage_kernel(*refs):
+    count = len(refs) // 2
+    for copy in fetch(zip(refs[:count], refs[count : 2 * count]), refs[-1]):
+        copy.wait()
+
+
+def stage(weights):
+    return pl.pallas_call(
+        stage_kernel,
+        out_shape=tuple(pltpu.VMEM(w.shape, w.dtype) for w in weights),
+        in_specs=[HBM] * len(weights),
+        out_specs=(VMEM,) * len(weights),
+        scratch_shapes=[pltpu.SemaphoreType.DMA((len(weights),))],
+        compiler_params=pltpu.CompilerParams(vmem_limit_bytes=1024 * 1024),
+        cost_estimate=pl.CostEstimate(
+            flops=0, bytes_accessed=sum(2 * w.size for w in weights), transcendentals=0
+        ),
+        name="stage",
+    )(*in_hbm(weights))
+
+
+def mlp_kernel(rows_ref, gain_ref, gate_ref, up_ref, down_ref, out_ref):
+    normed = normalized(rows_ref[...], gain_ref[...])
     gate = jnp.dot(normed, gate_ref[...], preferred_element_type=f32)
     upward = jnp.dot(normed, up_ref[...], preferred_element_type=f32)
     hidden = (jax.nn.silu(gate) * upward).astype(bf16)
-    sum_ref[...] += jnp.dot(hidden, down_ref[...], preferred_element_type=f32)
-
-    @pl.when(step == pl.num_programs(0) - 1)
-    def _():
-        out_ref[...] = sum_ref[...].astype(out_ref.dtype)
+    out_ref[...] = jnp.dot(hidden, down_ref[...], preferred_element_type=f32).astype(out_ref.dtype)
 
 
 def feed_forward(rows, gain, gate_weight, up_weight, down_weight, dtype):
     count, depth = rows.shape
     width = gate_weight.shape[1]
-    step = block_width(width)
     return pl.pallas_call(
         mlp_kernel,
         out_shape=jax.ShapeDtypeStruct((count, depth), dtype),
-        grid=(width // step,),
-        in_specs=[
-            pl.BlockSpec((count, depth), lambda i: (0, 0)),
-            pl.BlockSpec((1, depth), lambda i: (0, 0)),
-            pl.BlockSpec((depth, step), lambda i: (0, i)),
-            pl.BlockSpec((depth, step), lambda i: (0, i)),
-            pl.BlockSpec((step, depth), lambda i: (i, 0)),
-        ],
-        out_specs=pl.BlockSpec((count, depth), lambda i: (0, 0)),
-        scratch_shapes=[pltpu.VMEM((count, depth), bf16), pltpu.VMEM((count, depth), f32)],
+        in_specs=[VMEM] * 5,
+        out_specs=VMEM,
         compiler_params=PARAMS,
         cost_estimate=pl.CostEstimate(
             flops=6 * count * depth * width, bytes_accessed=6 * depth * width, transcendentals=0
         ),
         name="feed_forward",
-    )(rows, gain.reshape(1, depth), gate_weight, up_weight, down_weight)
-
-
-def next_kernel(rows_ref, gain_ref, query_ref, keyval_ref, *refs, half):
-    if half:
-        query_in, keyval_in, query_out, keyval_out, normed_ref, query_sum, keyval_sum = refs
-    else:
-        query_out, keyval_out, normed_ref, query_sum, keyval_sum = refs
-    step = pl.program_id(0)
-    depth = query_ref.shape[0]
-
-    @pl.when(step == 0)
+    )(rows, gain.reshape(1, depth), *in_vmem((gate_weight, up_weight, down_weight)))
+
+
+def next_kernel(rows_ref, gain_ref, query_ref, keyval_hbm, *refs):
+    refs, (keyval_ref, sem) = refs[:-2], refs[-2:]
+    copy = pltpu.make_async_copy(keyval_hbm, keyval_ref, sem)
+    copy.start()
+    normed = normalized(rows_ref[...], gain_ref[...])
+    query = jnp.dot(normed, query_ref[...], preferred_element_type=f32).astype(bf16)
+    copy.wait()
+    keyval = scores_of(keyval_ref[...], normed).astype(bf16)
+    if len(refs) == 2:
+        query_out, keyval_out = refs
+        query_out[...] = query
+        keyval_out[...] = keyval
+        return
+    query_in, keyval_in, query_out, keyval_out = refs
+    part = query.shape[0]
+    mine = pl.multiple_of(half_start(2 * part, 1), part)
+    theirs = pl.multiple_of(half_start(2 * part, 0), part)
+    query_out[pl.ds(mine, part), :] = query
+    query_out[pl.ds(theirs, part), :] = query_in[...]
+
+    @pl.when(mine == 0)
     def _():
-        normed = normalized(rows_ref[...], gain_ref[...])
-        for k in range(normed_ref.shape[0]):
-            normed_ref[k] = normed[:, k * depth : (k + 1) * depth]
-        query_sum[...] = jnp.zeros_like(query_sum)
-        keyval_sum[...] = jnp.zeros_like(keyval_sum)
-
-    normed = normed_ref[step]
-    query_sum[...] += jnp.dot(normed, query_ref[...], preferred_element_type=f32)
-    keyval_sum[...] += jnp.dot(normed, keyval_ref[...], preferred_element_type=f32)
-
-    @pl.when(step == pl.num_programs(0) - 1)
+        keyval_out[:, :part] = keyval
+        keyval_out[:, part:] = keyval_in[...]
+
+    @pl.when(mine != 0)
     def _():
-        query, keyval = query_sum[...].astype(bf16), keyval_sum[...].astype(bf16)
-        if half:
-            part = query.shape[0]
-            mine = pl.multiple_of(half_start(2 * part, 1), part)
-            theirs = pl.multiple_of(half_start(2 * part, 0), part)
-            query_out[pl.ds(mine, part), :] = query
-            query_out[pl.ds(theirs, part), :] = query_in[...]
-            keyval_out[pl.ds(mine, part), :] = keyval
-            keyval_out[pl.ds(theirs, part), :] = keyval_in[...]
-        else:
-            query_out[...] = query
-            keyval_out[...] = keyval
+        keyval_out[:, :part] = keyval_in[...]
+        keyval_out[:, part:] = keyval
 
 
 def next_projections(rows, gain, query_weight, keyval_weight, other):
     count, depth = rows.shape
-    steps = 5
-    block = depth // steps
-    widths = (query_weight.shape[1], keyval_weight.shape[1])
-    half = len(other) > 0
-    out_rows = 2 * count if half else count
-    return pl.pallas_call(
-        functools.partial(next_kernel, half=half),
-        out_shape=tuple(jax.ShapeDtypeStruct((out_rows, w), bf16) for w in widths),
-        grid=(steps,),
-        in_specs=[
-            pl.BlockSpec((count, depth), lambda i: (0, 0)),
-            pl.BlockSpec((1, depth), lambda i: (0, 0)),
-        ]
-        + [pl.BlockSpec((block, w), lambda i: (i, 0)) for w in widths]
-        + [pl.BlockSpec(item.shape, lambda i: (0, 0)) for item in other],
-        out_specs=tuple(pl.BlockSpec((out_rows, w), lambda i: (0, 0)) for w in widths),
-        scratch_shapes=[pltpu.VMEM((steps, count, block), bf16)]
-        + [pltpu.VMEM((count, w), f32) for w in widths],
+    widths = (query_weight.shape[1], keyval_weight.shape[0])
+    out_rows = 2 * count if other else count
+    return pl.pallas_call(
+        next_kernel,
+        out_shape=(
+            jax.ShapeDtypeStruct((out_rows, widths[0]), bf16),
+            jax.ShapeDtypeStruct((widths[1], out_rows), bf16),
+        ),
+        in_specs=[VMEM] * 3 + [HBM] + [VMEM] * len(other),
+        out_specs=(VMEM, VMEM),
+        scratch_shapes=[pltpu.VMEM(keyval_weight.shape, bf16), pltpu.SemaphoreType.DMA],
         compiler_params=PARAMS,
         cost_estimate=pl.CostEstimate(
             flops=2 * count * depth * sum(widths),
@@ -433,7 +421,7 @@
             transcendentals=0,
         ),
         name="next_layer",
-    )(rows, gain.reshape(1, depth), query_weight, keyval_weight, *other)
+    )(rows, gain.reshape(1, depth), *in_vmem([query_weight]), *in_hbm([keyval_weight]), *other)
 
 
 def trade(value, axis, bit):
@@ -477,24 +465,24 @@
     part = rows // 2
     kv_local = new_keyval.shape[1] // (2 * HD)
     pool = prepare(page_node, page_rank, node_length, mid_root, prefix_pool)
-    local_args = (new_query, new_keyval, leaf_cache, leaf_length, new_counts, request_mid, pool)
+    local_args = (new_query, new_keyval, leaf_cache, leaf_length, new_counts, request_mid)
     if lax.axis_size("req") == 8:
         first = cross(pool, 2, 4)
         second = cross(pool, 4, 2)
         beside = trade(pool, "req", 1)
-        aug, state = start_attention(*local_args)
+        aug, state = start_attention(*local_args, [pool, beside])
+        first, second, aug, state = lax.optimization_barrier((first, second, aug, state))
         corner = cross(first, 4, 2)
         first_other = trade(first, "req", 1)
         second_other = trade(second, "req", 1)
-        state = extend_attention(aug, state, [beside, first, second], kv_local)
-        state = extend_attention(aug, state, [first_other, second_other], kv_local)
-        corner_other = trade(corner, "req", 1)
-        state = extend_attention(aug, state, [corner], kv_local)
-        pools = [corner_other]
+        near = [first, second, first_other, second_other]
+        state = extend_attention(aug, state, near, kv_local)
+        corner, aug, state = lax.optimization_barrier((corner, aug, state))
+        pools = [corner, trade(corner, "req", 1)]
     else:
         every = lax.all_gather(pool, "req", axis=0)
         holders = every.shape[0]
-        aug, state = start_attention(*local_args)
+        aug, state = start_attention(*local_args, [pool])
         places = (lax.axis_index("req") + 1 + jnp.arange(holders - 1)) % holders
         step = 4
         for i in range(0, holders - 1, step):
@@ -517,15 +505,18 @@
     if lax.axis_size("tp") == 4:
         got = trade(theirs_proj, "tp", 1)
         pair = (mine_proj + wide(got)).astype(bf16)
+        pair, *mlp = lax.optimization_barrier((pair, gate_weight, up_weight, down_weight))
         got = trade(pair, "tp", 2)
+        got, *mlp = lax.optimization_barrier((got, *stage(mlp)))
         mixed_mine = (wide(res_mine) + (wide(pair) + wide(got))).astype(bf16)
         mixed_theirs = trade(mixed_mine, "tp", 1)
-        mlp = (norm_gain, gate_weight, up_weight, down_weight)
-        mlp_mine = feed_forward(mixed_mine, *mlp, bf16)
+        mlp_mine = feed_forward(mixed_mine, norm_gain, *mlp, bf16)
         got = trade(mlp_mine, "tp", 1)
-        mlp_theirs = feed_forward(mixed_theirs, *mlp, f32)
+        mlp_theirs = feed_forward(mixed_theirs, norm_gain, *mlp, f32)
         pair = (mlp_theirs + wide(got)).astype(bf16)
+        pair, query_weight = lax.optimization_barrier((pair, query_weight))
         got = trade(pair, "tp", 2)
+        got, query_weight = lax.optimization_barrier((got, *stage([query_weight])))
         layer_theirs = (wide(mixed_theirs) + (wide(pair) + wide(got))).astype(bf16)
         layer_mine = trade(layer_theirs, "tp", 1)
     else:
@@ -542,7 +533,7 @@
         layer = (wide(mixed) + lax.psum(mlp, "tp")).astype(bf16)
         layer_mine = lax.dynamic_slice_in_dim(layer, mine, part, 0)
         layer_theirs = lax.dynamic_slice_in_dim(layer, theirs, part, 0)
-    weights = (next_gain, query_weight, keyval_weight)
+    weights = [next_gain, query_weight, keyval_weight.T]
     other = next_projections(layer_theirs, *weights, ())
     next_query, next_keyval = next_projections(layer_mine, *weights, other)
     at = lax.rem(place, part)
@@ -552,7 +543,7 @@
         lax.dynamic_slice_in_dim(layer_mine, at, share, 0),
         lax.dynamic_slice_in_dim(layer_theirs, at, share, 0),
     )
-    return (attention, residual_out, next_query, next_keyval)
+    return (attention, residual_out, next_query, next_keyval.T)
 
 
 def solution(mesh):

time: 124 us -> 106 us (0.85)
  local copies, waits for them, and re-layouts: 19.4 us -> 3.93 us
  waiting for transfers between devices: 48.5 us -> 45.3 us
  Pallas kernels: 36.8 us -> 34.3 us
  other arithmetic: 1.06 us -> 2.8 us
    unnamed x37 -> x15, local copies, waits for them, and re-layouts: 19.4 us -> 3.92 us
    pallas_call x3 -> x5, Pallas kernels: 6.96 us -> 18.8 us  [the longest x2 8.02 us: next_projections(): pl.pallas_call(next_kernel, out_shape=(jax.ShapeDtypeStruct((out_rows, wi...]
    pallas_call x2, Pallas kernels: 16.5 us -> 5.2 us  [feed_forward(): pl.pallas_call(mlp_kernel, out_shape=jax.ShapeDtypeStruct((count, depth),...]
    ppermute x3, waiting for transfers between devices: 12.6 us -> 3.94 us  [cross(): return lax.ppermute(value, 'req', pairs)]
    ppermute x10, waiting for transfers between devices: 36 us -> 41.3 us  [trade(): return lax.ppermute(value, axis, [(i, i ^ bit) for i in range(size)])]
    pallas_call x3 -> x1, Pallas kernels: 7.56 us -> 3.56 us  [extend_attention(): pl.pallas_call(functools.partial(chunk_kernel, blocks=2 * kv_local), out_...]
  transfers between devices with their start and end apart: 13 -> 13, of which waited for: 6 -> 10; matrix products, arithmetic and copies ran while one was open for 4% -> 1% of each run, Pallas kernels for 25% -> 25%
where the time goes in v3:
time: 106 us; the launch traced here: 105 us
  waiting for transfers between devices  45.3 us (43%)
  Pallas kernels  34.3 us (32%)
  starting transfers between devices  18 us (17%)
  local copies, waits for them, and re-layouts  3.93 us (4%)
  other arithmetic  2.8 us (3%)
    ppermute x10, waiting for transfers between devices, trade(): return lax.ppermute(value, axis, [(i, i ^ bit) for i in range(size)])  41.3 us
    ppermute x10, starting transfers between devices, trade(): return lax.ppermute(value, axis, [(i, i ^ bit) for i in range(size)])  12.2 us
    pallas_call x2, Pallas kernels, next_projections(): pl.pallas_call(next_kernel, out_shape=(jax.ShapeDtypeStruct((out_rows, wi...  8.02 us
    pallas_call x2, Pallas kernels, stage(): pl.pallas_call(stage_kernel, out_shape=tuple((pltpu.VMEM(w.shape, w.dtype...  7.01 us
    pallas_call x2, Pallas kernels, finish_attention(): pl.pallas_call(functools.partial(finish_kernel, half=half, kv_local=kv_lo...  5.92 us
    ppermute x3, starting transfers between devices, cross(): return lax.ppermute(value, 'req', pairs)  5.83 us
    pallas_call x2, Pallas kernels, feed_forward(): pl.pallas_call(mlp_kernel, out_shape=jax.ShapeDtypeStruct((count, depth),...  5.2 us
    ppermute x3, waiting for transfers between devices, cross(): return lax.ppermute(value, 'req', pairs)  3.94 us
  transfers between devices with their start and end apart: 13, of which 10 were waited for; matrix products, arithmetic and copies ran while one was open for 1% of the time, Pallas kernels for 25%

profile of v3, /device:TPU:0, one launch (start us, length us, event | category | flops | bytes accessed | tf_op | source)
XLA Modules:
  0.0 105.2 jit_solution(17997382527715651882)
XLA Ops:
  0.6 1.0 copy-done.1
  1.6 0.9 pool_rows.1.refs_0_
  2.5 0.5 collective-permute-start.2
  3.0 2.6 %collective-permute-start = (bf16[512,384]{1,0:T(8,128)(2,1)S(1)}, bf16[512,384]{1,0:T(8,128)(2,1)S(1)}, u32[]{:S(2)}, u32[]{:S(2)}) collective-permute-start(bf16[512,384]{1,0:T(8,128)(2,1)S(1)} %pool_rows.1.refs_0_), channel_id=1, source_target_pairs={{0,8},{4,20},{8,0},{12,28},{16,24},{20,4},{24,16},{28,12},{1,9},{5... | collective-permute-start | bytes 1179656 | tf_op jit(solution)/shard_map/ppermute | solution.py:435
  5.6 1.5 %collective-permute-start.1 = (bf16[512,384]{1,0:T(8,128)(2,1)S(1)}, bf16[512,384]{1,0:T(8,128)(2,1)S(1)}, u32[]{:S(2)}, u32[]{:S(2)}) collective-permute-start(bf16[512,384]{1,0:T(8,128)(2,1)S(1)} %pool_rows.1.refs_0_), channel_id=1, source_target_pairs={{0,16},{4,12},{8,24},{12,4},{16,0},{20,28},{24,8},{28,20},{1,17},{... | collective-permute-start | bytes 1179656 | tf_op jit(solution)/shard_map/ppermute | solution.py:435
  7.1 1.0 copy.24.keyval_ref
  8.1 0.0 copy-start.2
  8.1 1.0 copy-done.2
  9.1 0.9 copy-done.3
  10.0 3.8 %attend_local.1 = (bf16[1024,256]{1,0:T(8,128)(2,1)S(1)}, f32[1024,256]{1,0:T(8,128)S(1)}) custom-call(s32[1,16]{1,0:T(1,128)} %count_hbm.1, s32[16]{0:T(128)} %mid_hbm.1, s32[16]{0:T(128)} %leaf_len_hbm.1, bf16[128,640]{1,0:T(8,128)(2,1)S(1)} %copy-done.3, bf16[128,320]{1,0:T(8,128)(2,1)S(1)} %copy.24.keyval_ref, bf16[16,32,320]{2,1,0:T(8,128)(2,1)S(1)} %copy-done.2, ...), custom_call_target="tpu_custom_call" | custom-call | flops 1744830464 | bytes 2097152 | tf_op jit(solution)/shard_map/attend_local/pallas_call | solution.py:217
  13.8 0.0 copy-start
  13.8 0.6 collective-permute-done.refs_2_
  14.4 0.9 collective-permute-done.1.refs_3_
  15.3 0.1 collective-permute-start.4
  15.4 0.4 collective-permute-start.5
  15.8 1.8 %collective-permute-start.3 = (bf16[512,384]{1,0:T(8,128)(2,1)S(1)}, bf16[512,384]{1,0:T(8,128)(2,1)S(1)}, u32[]{:S(2)}, u32[]{:S(2)}) collective-permute-start(bf16[512,384]{1,0:T(8,128)(2,1)S(1)} %collective-permute-done.refs_2_), channel_id=1, source_target_pairs={{0,16},{4,12},{8,24},{12,4},{16,0},{20,28},{24,8},{28,20},{1,17},{... | collective-permute-start | bytes 1179656 | tf_op jit(solution)/shard_map/ppermute | solution.py:435
  17.6 0.0 collective-permute-done.5.refs_5_
  17.6 3.6 %attend_pages.1.refs_1_ = f32[1024,256]{1,0:T(8,128)S(1)} custom-call(bf16[1024,256]{1,0:T(8,128)(2,1)S(1)} %get-tuple-element.42.refs_0_, f32[1024,256]{1,0:T(8,128)S(1)} %get-tuple-element.40.refs_1_, bf16[512,384]{1,0:T(8,128)(2,1)S(1)} %collective-permute-done.refs_2_, bf16[512,384]{1,0:T(8,128)(2,1)S(1)} %collective-permute-done.1.refs_3_, ...), custom_call_target="tpu_custom_call" | custom-call | flops 2147483648 | bytes 2097152 | tf_op jit(solution)/shard_map/attend_pages/pallas_call | solution.py:256
  21.2 2.4 %collective-permute-done.3.refs_2_ = bf16[512,384]{1,0:T(8,128)(2,1)S(1)} collective-permute-done((bf16[512,384]{1,0:T(8,128)(2,1)S(1)}, bf16[512,384]{1,0:T(8,128)(2,1)S(1)}, u32[]{:S(2)}, u32[]{:S(2)}) %collective-permute-start.3) | collective-permute-done | bytes 393248 | tf_op jit(solution)/shard_map/ppermute | solution.py:435
  23.6 1.7 %collective-permute-done.6.refs_3_ = bf16[512,384]{1,0:T(8,128)(2,1)S(1)} collective-permute-done((bf16[512,384]{1,0:T(8,128)(2,1)S(1)}, bf16[512,384]{1,0:T(8,128)(2,1)S(1)}, u32[]{:S(2)}, u32[]{:S(2)}) %collective-permute-start.6) | collective-permute-done | bytes 393248 | tf_op jit(solution)/shard_map/ppermute | solution.py:429
  25.3 2.9 %attend_finish.2 = (bf16[64,640]{1,0:T(8,128)(2,1)S(1)}, bf16[64,2560]{1,0:T(8,128)(2,1)S(1)}) custom-call(bf16[1024,256]{1,0:T(8,128)(2,1)S(1)} %get-tuple-element.42.refs_0_, f32[1024,256]{1,0:T(8,128)S(1)} %attend_pages.1.refs_1_, bf16[512,384]{1,0:T(8,128)(2,1)S(1)} %collective-permute-done.3.refs_2_, ...), custom_call_target="tpu_custom_call" | custom-call | flops 805306368 | bytes 1048576 | tf_op jit(solution)/shard_map/attend_finish/pallas_call | solution.py:305
  28.3 0.0 copy-start.5
  28.3 1.9 %collective-permute-start.7 = (bf16[64,2560]{1,0:T(8,128)(2,1)S(1)}, bf16[64,2560]{1,0:T(8,128)(2,1)S(1)}, u32[]{:S(2)}, u32[]{:S(2)}) collective-permute-start(bf16[64,2560]{1,0:T(8,128)(2,1)S(1)} %get-tuple-element.48), channel_id=1, source_target_pairs={{0,1},{1,0},{2,3},{3,2},{4,5},{5,4},{6,7},{7,6},{8,9},{9,8},{10,11... | collective-permute-start | bytes 983048 | tf_op jit(solution)/shard_map/ppermute | solution.py:429
  30.2 3.0 %attend_finish.3 = (bf16[128,640]{1,0:T(8,128)(2,1)}, f32[64,2560]{1,0:T(8,128)S(1)}) custom-call(bf16[1024,256]{1,0:T(8,128)(2,1)S(1)} %get-tuple-element.42.refs_0_, f32[1024,256]{1,0:T(8,128)S(1)} %attend_pages.1.refs_1_, bf16[512,384]{1,0:T(8,128)(2,1)S(1)} %collective-permute-done.3.refs_2_, bf16[512,384]{1,0:T(8,128)(2,1)S(1)} %collective-permute-done.6.refs_3_, ...), custom_call_target="tpu_custom_call" | custom-call | flops 805306368 | bytes 1048576 | tf_op jit(solution)/shard_map/attend_finish/pallas_call | solution.py:305
  33.2 5.0 %collective-permute-done.7 = bf16[64,2560]{1,0:T(8,128)(2,1)S(1)} collective-permute-done((bf16[64,2560]{1,0:T(8,128)(2,1)S(1)}, bf16[64,2560]{1,0:T(8,128)(2,1)S(1)}, u32[]{:S(2)}, u32[]{:S(2)}) %collective-permute-start.7) | collective-permute-done | bytes 327712 | tf_op jit(solution)/shard_map/ppermute | solution.py:429
  38.2 0.1 add_convert_fusion.3
  38.2 2.8 %collective-permute-start.8 = (bf16[64,2560]{1,0:T(8,128)(2,1)S(1)}, bf16[64,2560]{1,0:T(8,128)(2,1)S(1)}, u32[]{:S(2)}, u32[]{:S(2)}) collective-permute-start(bf16[64,2560]{1,0:T(8,128)(2,1)S(1)} %add_convert_fusion.3), channel_id=1, source_target_pairs={{0,2},{1,3},{2,0},{3,1},{4,6},{5,7},{6,4},{7,5},{8,10},{9,11},{10,... | collective-permute-start | bytes 983048 | tf_op jit(solution)/shard_map/ppermute | solution.py:429
  41.1 0.0 copy-start.4
  41.1 5.1 %stage.2 = (bf16[2560,896]{1,0:T(8,128)(2,1)S(1)}, bf16[2560,896]{1,0:T(8,128)(2,1)S(1)}, bf16[896,2560]{1,0:T(8,128)(2,1)S(1)}) custom-call(bf16[2560,896]{1,0:T(8,128)(2,1)} %refs_0_, bf16[2560,896]{1,0:T(8,128)(2,1)} %refs_1_, bf16[896,2560]{1,0:T(8,128)(2,1)} %refs_2_), custom_call_target="tpu_custom_call" | custom-call | bytes 13762560 | tf_op jit(solution)/shard_map/stage/pallas_call | solution.py:335
  46.2 9.1 %collective-permute-done.8 = bf16[64,2560]{1,0:T(8,128)(2,1)S(1)} collective-permute-done((bf16[64,2560]{1,0:T(8,128)(2,1)S(1)}, bf16[64,2560]{1,0:T(8,128)(2,1)S(1)}, u32[]{:S(2)}, u32[]{:S(2)}) %collective-permute-start.8) | collective-permute-done | bytes 327712 | tf_op jit(solution)/shard_map/ppermute | solution.py:429
  55.3 0.1 add_convert_fusion.2.rows_ref
  55.4 1.0 collective-permute-start.9
  56.4 2.6 %feed_forward.3 = bf16[64,2560]{1,0:T(8,128)(2,1)S(1)} custom-call(bf16[64,2560]{1,0:T(8,128)(2,1)S(1)} %add_convert_fusion.2.rows_ref, bf16[1,2560]{1,0:T(2,128)(2,1)S(1)} %reshape.16.gain_ref, bf16[2560,896]{1,0:T(8,128)(2,1)S(1)} %get-tuple-element.57.gate_ref, bf16[2560,896]{1,0:T(8,128)(2,1)S(1)} %get-tuple-element.58.up_ref, ...), custom_call_target="tpu_custom_call" | custom-call | flops 880803840 | bytes 13762560 | tf_op jit(solution)/shard_map/feed_forward/pallas_call | solution.py:360
  59.0 1.4 %collective-permute-start.10 = (bf16[64,2560]{1,0:T(8,128)(2,1)S(1)}, bf16[64,2560]{1,0:T(8,128)(2,1)S(1)}, u32[]{:S(2)}, u32[]{:S(2)}) collective-permute-start(bf16[64,2560]{1,0:T(8,128)(2,1)S(1)} %feed_forward.3), channel_id=1, source_target_pairs={{0,1},{1,0},{2,3},{3,2},{4,5},{5,4},{6,7},{7,6},{8,9},{9,8},{10,11... | collective-permute-start | bytes 983048 | tf_op jit(solution)/shard_map/ppermute | solution.py:429
  60.3 6.0 %collective-permute-done.9.rows_ref = bf16[64,2560]{1,0:T(8,128)(2,1)S(1)} collective-permute-done((bf16[64,2560]{1,0:T(8,128)(2,1)S(1)}, bf16[64,2560]{1,0:T(8,128)(2,1)S(1)}, u32[]{:S(2)}, u32[]{:S(2)}) %collective-permute-start.9) | collective-permute-done | bytes 327712 | tf_op jit(solution)/shard_map/ppermute | solution.py:429
  66.3 2.6 %feed_forward.2 = f32[64,2560]{1,0:T(8,128)S(1)} custom-call(bf16[64,2560]{1,0:T(8,128)(2,1)S(1)} %collective-permute-done.9.rows_ref, bf16[1,2560]{1,0:T(2,128)(2,1)S(1)} %reshape.16.gain_ref, bf16[2560,896]{1,0:T(8,128)(2,1)S(1)} %get-tuple-element.57.gate_ref, bf16[2560,896]{1,0:T(8,128)(2,1)S(1)} %get-tuple-element.58.up_ref, ...), custom_call_target="tpu_custom_call" | custom-call | flops 880803840 | bytes 13762560 | tf_op jit(solution)/shard_map/feed_forward/pallas_call | solution.py:360
  68.9 0.0 copy-start.6
  68.9 2.4 %collective-permute-done.10 = bf16[64,2560]{1,0:T(8,128)(2,1)S(1)} collective-permute-done((bf16[64,2560]{1,0:T(8,128)(2,1)S(1)}, bf16[64,2560]{1,0:T(8,128)(2,1)S(1)}, u32[]{:S(2)}, u32[]{:S(2)}) %collective-permute-start.10) | collective-permute-done | bytes 327712 | tf_op jit(solution)/shard_map/ppermute | solution.py:429
  71.3 0.1 add_convert_fusion.1
  71.3 3.4 %collective-permute-start.11 = (bf16[64,2560]{1,0:T(8,128)(2,1)S(1)}, bf16[64,2560]{1,0:T(8,128)(2,1)S(1)}, u32[]{:S(2)}, u32[]{:S(2)}) collective-permute-start(bf16[64,2560]{1,0:T(8,128)(2,1)S(1)} %add_convert_fusion.1), channel_id=1, source_target_pairs={{0,2},{1,3},{2,0},{3,1},{4,6},{5,7},{6,4},{7,5},{8,10},{9,11},{10,... | collective-permute-start | bytes 983048 | tf_op jit(solution)/shard_map/ppermute | solution.py:429
  74.8 1.9 %stage.3.query_ref = bf16[2560,640]{1,0:T(8,128)(2,1)S(1)} custom-call(bf16[2560,640]{1,0:T(8,128)(2,1)} %refs_0_.1), custom_call_target="tpu_custom_call" | custom-call | bytes 3276800 | tf_op jit(solution)/shard_map/stage/pallas_call | solution.py:335
  76.7 12.4 %collective-permute-done.11 = bf16[64,2560]{1,0:T(8,128)(2,1)S(1)} collective-permute-done((bf16[64,2560]{1,0:T(8,128)(2,1)S(1)}, bf16[64,2560]{1,0:T(8,128)(2,1)S(1)}, u32[]{:S(2)}, u32[]{:S(2)}) %collective-permute-start.11) | collective-permute-done | bytes 327712 | tf_op jit(solution)/shard_map/ppermute | solution.py:429
  89.2 0.8 add_convert_fusion.rows_ref
  90.0 0.7 collective-permute-start.12
  90.7 3.6 %next_layer.2 = (bf16[64,640]{1,0:T(8,128)(2,1)S(1)}, bf16[320,64]{1,0:T(8,128)(2,1)S(1)}) custom-call(bf16[64,2560]{1,0:T(8,128)(2,1)} %add_convert_fusion.rows_ref, bf16[1,2560]{1,0:T(2,128)(2,1)S(1)} %reshape.17.gain_ref, bf16[2560,640]{1,0:T(8,128)(2,1)S(1)} %stage.3.query_ref, bf16[320,2560]{1,0:T(8,128)(2,1)} %bitcast.2), custom_call_target="tpu_custom_call" | custom-call | flops 314572800 | bytes 4915200 | tf_op jit(solution)/shard_map/next_layer/pallas_call | solution.py:408
  94.4 4.7 %collective-permute-done.12.rows_ref = bf16[64,2560]{1,0:T(8,128)(2,1)} collective-permute-done((bf16[64,2560]{1,0:T(8,128)(2,1)}, bf16[64,2560]{1,0:T(8,128)(2,1)}, u32[]{:S(2)}, u32[]{:S(2)}) %collective-permute-start.12) | collective-permute-done | bytes 327712 | tf_op jit(solution)/shard_map/ppermute | solution.py:429
  99.1 4.4 %next_layer.3 = (bf16[128,640]{1,0:T(8,128)(2,1)}, bf16[320,128]{1,0:T(8,128)(2,1)}) custom-call(bf16[64,2560]{1,0:T(8,128)(2,1)} %collective-permute-done.12.rows_ref, bf16[1,2560]{1,0:T(2,128)(2,1)S(1)} %reshape.17.gain_ref, bf16[2560,640]{1,0:T(8,128)(2,1)S(1)} %stage.3.query_ref, bf16[320,2560]{1,0:T(8,128)(2,1)} %bitcast.3, ...), custom_call_target="tpu_custom_call" | custom-call | flops 314572800 | bytes 4915200 | tf_op jit(solution)/shard_map/next_layer/pallas_call | solution.py:408
  103.5 1.7 %dynamic-slice_select_fusion = bf16[32,2560]{1,0:T(8,128)(2,1)} fusion(bf16[64,2560]{1,0:T(8,128)(2,1)} %add_convert_fusion.rows_ref, s32[]{:T(128)S(6)} %select_n.17, bf16[64,2560]{1,0:T(8,128)(2,1)} %collective-permute-done.12.rows_ref, pred[]{:T(512)S(6)} %and.6), kind=kLoop, calls=%fused_computation.4 | loop fusion | flops 81920 | bytes 491525 | tf_op jit(solution)/shard_map/jit(_where)/select_n | solution.py:541
  (11 shorter events, 0.0 us)
Async XLA Ops:
  0.6 1.0 copy-start.1
  2.5 5.6 %collective-permute-start.2 = (bf16[512,384]{1,0:T(8,128)(2,1)S(1)}, bf16[512,384]{1,0:T(8,128)(2,1)S(1)}, u32[]{:S(2)}, u32[]{:S(2)}) collective-permute-start(bf16[512,384]{1,0:T(8,128)(2,1)S(1)} %pool_rows.1.refs_0_), channel_id=1, source_target_pairs={{0,4},{4,0},{8,12},{12,8},{16,20},{20,16},{24,28},{28,24},{1,5},{5... | collective-permute-start | bytes 1179656 | tf_op jit(solution)/shard_map/ppermute | solution.py:429
  3.0 11.4 %collective-permute-start = (bf16[512,384]{1,0:T(8,128)(2,1)S(1)}, bf16[512,384]{1,0:T(8,128)(2,1)S(1)}, u32[]{:S(2)}, u32[]{:S(2)}) collective-permute-start(bf16[512,384]{1,0:T(8,128)(2,1)S(1)} %pool_rows.1.refs_0_), channel_id=1, source_target_pairs={{0,8},{4,20},{8,0},{12,28},{16,24},{20,4},{24,16},{28,12},{1,9},{5... | collective-permute-start | bytes 1179656 | tf_op jit(solution)/shard_map/ppermute | solution.py:435
  5.6 9.7 %collective-permute-start.1 = (bf16[512,384]{1,0:T(8,128)(2,1)S(1)}, bf16[512,384]{1,0:T(8,128)(2,1)S(1)}, u32[]{:S(2)}, u32[]{:S(2)}) collective-permute-start(bf16[512,384]{1,0:T(8,128)(2,1)S(1)} %pool_rows.1.refs_0_), channel_id=1, source_target_pairs={{0,16},{4,12},{8,24},{12,4},{16,0},{20,28},{24,8},{28,20},{1,17},{... | collective-permute-start | bytes 1179656 | tf_op jit(solution)/shard_map/ppermute | solution.py:435
  8.1 1.0 copy-start.2
  9.1 0.9 copy-start.3
  13.8 11.5 %copy-start = (bf16[640,2560]{1,0:T(8,128)(2,1)S(1)}, bf16[640,2560]{1,0:T(8,128)(2,1)}, u32[]{:S(2)}) copy-start(bf16[640,2560]{1,0:T(8,128)(2,1)} %refs_4_.3) | copy-start | bytes 9830404
  15.3 2.3 %collective-permute-start.4 = (bf16[512,384]{1,0:T(8,128)(2,1)S(1)}, bf16[512,384]{1,0:T(8,128)(2,1)S(1)}, u32[]{:S(2)}, u32[]{:S(2)}) collective-permute-start(bf16[512,384]{1,0:T(8,128)(2,1)S(1)} %collective-permute-done.refs_2_), channel_id=1, source_target_pairs={{0,4},{4,0},{8,12},{12,8},{16,20},{20,16},{24,28},{28,24},{1,5},{5... | collective-permute-start | bytes 1179656 | tf_op jit(solution)/shard_map/ppermute | solution.py:429
  15.4 2.2 %collective-permute-start.5 = (bf16[512,384]{1,0:T(8,128)(2,1)S(1)}, bf16[512,384]{1,0:T(8,128)(2,1)S(1)}, u32[]{:S(2)}, u32[]{:S(2)}) collective-permute-start(bf16[512,384]{1,0:T(8,128)(2,1)S(1)} %collective-permute-done.1.refs_3_), channel_id=1, source_target_pairs={{0,4},{4,0},{8,12},{12,8},{16,20},{20,16},{24,28},{28,24},{1,5},{5... | collective-permute-start | bytes 1179656 | tf_op jit(solution)/shard_map/ppermute | solution.py:429
  15.8 7.8 %collective-permute-start.3 = (bf16[512,384]{1,0:T(8,128)(2,1)S(1)}, bf16[512,384]{1,0:T(8,128)(2,1)S(1)}, u32[]{:S(2)}, u32[]{:S(2)}) collective-permute-start(bf16[512,384]{1,0:T(8,128)(2,1)S(1)} %collective-permute-done.refs_2_), channel_id=1, source_target_pairs={{0,16},{4,12},{8,24},{12,4},{16,0},{20,28},{24,8},{28,20},{1,17},{... | collective-permute-start | bytes 1179656 | tf_op jit(solution)/shard_map/ppermute | solution.py:435
  23.6 1.7 %collective-permute-start.6 = (bf16[512,384]{1,0:T(8,128)(2,1)S(1)}, bf16[512,384]{1,0:T(8,128)(2,1)S(1)}, u32[]{:S(2)}, u32[]{:S(2)}) collective-permute-start(bf16[512,384]{1,0:T(8,128)(2,1)S(1)} %collective-permute-done.3.refs_2_), channel_id=1, source_target_pairs={{0,4},{4,0},{8,12},{12,8},{16,20},{20,16},{24,28},{28,24},{1,5},{5... | collective-permute-start | bytes 1179656 | tf_op jit(solution)/shard_map/ppermute | solution.py:429
  28.3 12.8 %copy-start.5 = (bf16[2560]{0:T(1024)(128)(2,1)S(1)}, bf16[2560]{0:T(1024)(128)(2,1)}, u32[]{:S(2)}) copy-start(bf16[2560]{0:T(1024)(128)(2,1)} %param.33) | copy-start | bytes 15364
  28.3 9.9 %collective-permute-start.7 = (bf16[64,2560]{1,0:T(8,128)(2,1)S(1)}, bf16[64,2560]{1,0:T(8,128)(2,1)S(1)}, u32[]{:S(2)}, u32[]{:S(2)}) collective-permute-start(bf16[64,2560]{1,0:T(8,128)(2,1)S(1)} %get-tuple-element.48), channel_id=1, source_target_pairs={{0,1},{1,0},{2,3},{3,2},{4,5},{5,4},{6,7},{7,6},{8,9},{9,8},{10,11... | collective-permute-start | bytes 983048 | tf_op jit(solution)/shard_map/ppermute | solution.py:429
  38.2 17.0 %collective-permute-start.8 = (bf16[64,2560]{1,0:T(8,128)(2,1)S(1)}, bf16[64,2560]{1,0:T(8,128)(2,1)S(1)}, u32[]{:S(2)}, u32[]{:S(2)}) collective-permute-start(bf16[64,2560]{1,0:T(8,128)(2,1)S(1)} %add_convert_fusion.3), channel_id=1, source_target_pairs={{0,2},{1,3},{2,0},{3,1},{4,6},{5,7},{6,4},{7,5},{8,10},{9,11},{10,... | collective-permute-start | bytes 983048 | tf_op jit(solution)/shard_map/ppermute | solution.py:429
  41.1 14.2 %copy-start.4 = (bf16[128,2560]{1,0:T(8,128)(2,1)S(1)}, bf16[128,2560]{1,0:T(8,128)(2,1)}, u32[]{:S(2)}) copy-start(bf16[128,2560]{1,0:T(8,128)(2,1)} %param.22) | copy-start | bytes 1966084
  55.4 10.9 %collective-permute-start.9 = (bf16[64,2560]{1,0:T(8,128)(2,1)S(1)}, bf16[64,2560]{1,0:T(8,128)(2,1)S(1)}, u32[]{:S(2)}, u32[]{:S(2)}) collective-permute-start(bf16[64,2560]{1,0:T(8,128)(2,1)S(1)} %add_convert_fusion.2.rows_ref), channel_id=1, source_target_pairs={{0,1},{1,0},{2,3},{3,2},{4,5},{5,4},{6,7},{7,6},{8,9},{9,8},{10,11... | collective-permute-start | bytes 983048 | tf_op jit(solution)/shard_map/ppermute | solution.py:429
  59.0 12.3 %collective-permute-start.10 = (bf16[64,2560]{1,0:T(8,128)(2,1)S(1)}, bf16[64,2560]{1,0:T(8,128)(2,1)S(1)}, u32[]{:S(2)}, u32[]{:S(2)}) collective-permute-start(bf16[64,2560]{1,0:T(8,128)(2,1)S(1)} %feed_forward.3), channel_id=1, source_target_pairs={{0,1},{1,0},{2,3},{3,2},{4,5},{5,4},{6,7},{7,6},{8,9},{9,8},{10,11... | collective-permute-start | bytes 983048 | tf_op jit(solution)/shard_map/ppermute | solution.py:429
  68.9 21.8 %copy-start.6 = (bf16[2560]{0:T(1024)(128)(2,1)S(1)}, bf16[2560]{0:T(1024)(128)(2,1)}, u32[]{:S(2)}) copy-start(bf16[2560]{0:T(1024)(128)(2,1)} %param.37) | copy-start | bytes 15364
  71.3 17.8 %collective-permute-start.11 = (bf16[64,2560]{1,0:T(8,128)(2,1)S(1)}, bf16[64,2560]{1,0:T(8,128)(2,1)S(1)}, u32[]{:S(2)}, u32[]{:S(2)}) collective-permute-start(bf16[64,2560]{1,0:T(8,128)(2,1)S(1)} %add_convert_fusion.1), channel_id=1, source_target_pairs={{0,2},{1,3},{2,0},{3,1},{4,6},{5,7},{6,4},{7,5},{8,10},{9,11},{10,... | collective-permute-start | bytes 983048 | tf_op jit(solution)/shard_map/ppermute | solution.py:429
  90.0 9.1 %collective-permute-start.12 = (bf16[64,2560]{1,0:T(8,128)(2,1)}, bf16[64,2560]{1,0:T(8,128)(2,1)}, u32[]{:S(2)}, u32[]{:S(2)}) collective-permute-start(bf16[64,2560]{1,0:T(8,128)(2,1)} %add_convert_fusion.rows_ref), channel_id=1, source_target_pairs={{0,1},{1,0},{2,3},{3,2},{4,5},{5,4},{6,7},{7,6},{8,9},{9,8},{10,11... | collective-permute-start | bytes 983048 | tf_op jit(solution)/shard_map/ppermute | solution.py:429

commit v4 on v3

--- a/solution.py
+++ b/solution.py
@@ -16,6 +16,8 @@
 EPSILON = 1e-05
 RATE = math.log2(math.e) / math.sqrt(HD)
 
+PIECES = 2
+
 bf16 = jnp.bfloat16
 f32 = jnp.float32
 i32 = jnp.int32
@@ -65,6 +67,19 @@
     for copy in copies:
         copy.start()
     return copies
+
+
+def piece(width, k):
+    step = width // PIECES
+    return slice(k * step, (k + 1) * step)
+
+
+def pieces_of(rows, width, dtype):
+    return tuple(jax.ShapeDtypeStruct((rows, width // PIECES), dtype) for _ in range(PIECES))
+
+
+def joined(refs):
+    return jnp.concatenate([ref[...] for ref in refs], axis=1)
 
 
 def in_hbm(values):
@@ -270,10 +285,8 @@
     weight_ref = refs[2 + chunks]
     part = aug_ref.shape[0] // (2 * width // HD)
     rest = refs[3 + chunks :]
-    if half:
-        other_ref, att_ref, proj_ref, mine_ref = rest
-    else:
-        att_ref, proj_ref, mine_ref = rest
+    att_ref, *proj_refs, mine_ref = rest[2 * half :]
+    proj_refs, res_refs = proj_refs[:PIECES], proj_refs[PIECES:]
     group = width // (kv_local * HD)
     size = group * part
     for c in range(kv_local):
@@ -291,11 +304,15 @@
         mine = pl.multiple_of(half_start(2 * part, 1), part)
         theirs = pl.multiple_of(half_start(2 * part, 0), part)
         att_ref[pl.ds(mine, part), :] = mine_ref[...]
-        att_ref[pl.ds(theirs, part), :] = other_ref[...]
+        att_ref[pl.ds(theirs, part), :] = rest[0][...]
+        for k, res_ref in enumerate(res_refs):
+            res_ref[...] = rest[1][pl.ds(mine, part), piece(rest[1].shape[1], k)]
     else:
         att_ref[...] = mine_ref[...]
-    proj = jnp.dot(mine_ref[...], weight_ref[...], preferred_element_type=f32)
-    proj_ref[...] = proj.astype(proj_ref.dtype)
+    for k, proj_ref in enumerate(proj_refs):
+        weight = weight_ref[:, piece(weight_ref.shape[1], k)]
+        proj = jnp.dot(mine_ref[...], weight, preferred_element_type=f32)
+        proj_ref[...] = proj.astype(proj_ref.dtype)
 
 
 def finish_attention(aug, state, pools, out_weight, half, kv_local, rows, other):
@@ -308,10 +325,11 @@
         ),
         out_shape=(
             jax.ShapeDtypeStruct((rows if half else part, width), bf16),
-            jax.ShapeDtypeStruct((part, out_weight.shape[1]), f32 if half else bf16),
+            *pieces_of(part, out_weight.shape[1], f32 if half else bf16),
+            *(pieces_of(part, out_weight.shape[1], bf16) if half else ()),
         ),
-        in_specs=[VMEM] * (3 + len(pools) + half),
-        out_specs=(VMEM, VMEM),
+        in_specs=[VMEM] * (3 + len(pools) + len(other)),
+        out_specs=(VMEM,) * (1 + PIECES + half * PIECES),
         scratch_shapes=[pltpu.VMEM((part, width), bf16)],
         compiler_params=PARAMS,
         cost_estimate=attention_cost(aug.shape[0] // 2, keys + 512),
@@ -346,44 +364,48 @@
     )(*in_hbm(weights))
 
 
-def mlp_kernel(rows_ref, gain_ref, gate_ref, up_ref, down_ref, out_ref):
-    normed = normalized(rows_ref[...], gain_ref[...])
+def mlp_kernel(*refs):
+    row_refs, (gain_ref, gate_ref, up_ref, down_ref) = refs[:PIECES], refs[PIECES : PIECES + 4]
+    normed = normalized(joined(row_refs), gain_ref[...])
     gate = jnp.dot(normed, gate_ref[...], preferred_element_type=f32)
     upward = jnp.dot(normed, up_ref[...], preferred_element_type=f32)
     hidden = (jax.nn.silu(gate) * upward).astype(bf16)
-    out_ref[...] = jnp.dot(hidden, down_ref[...], preferred_element_type=f32).astype(out_ref.dtype)
+    for k, out_ref in enumerate(refs[PIECES + 4 :]):
+        weight = down_ref[:, piece(down_ref.shape[1], k)]
+        result = jnp.dot(hidden, weight, preferred_element_type=f32)
+        out_ref[...] = result.astype(out_ref.dtype)
 
 
 def feed_forward(rows, gain, gate_weight, up_weight, down_weight, dtype):
-    count, depth = rows.shape
-    width = gate_weight.shape[1]
+    count = rows[0].shape[0]
+    depth, width = gate_weight.shape
     return pl.pallas_call(
         mlp_kernel,
-        out_shape=jax.ShapeDtypeStruct((count, depth), dtype),
-        in_specs=[VMEM] * 5,
-        out_specs=VMEM,
+        out_shape=pieces_of(count, depth, dtype),
+        in_specs=[VMEM] * (PIECES + 4),
+        out_specs=(VMEM,) * PIECES,
         compiler_params=PARAMS,
         cost_estimate=pl.CostEstimate(
             flops=6 * count * depth * width, bytes_accessed=6 * depth * width, transcendentals=0
         ),
         name="feed_forward",
-    )(rows, gain.reshape(1, depth), *in_vmem((gate_weight, up_weight, down_weight)))
-
-
-def next_kernel(rows_ref, gain_ref, query_ref, keyval_hbm, *refs):
-    refs, (keyval_ref, sem) = refs[:-2], refs[-2:]
-    copy = pltpu.make_async_copy(keyval_hbm, keyval_ref, sem)
-    copy.start()
-    normed = normalized(rows_ref[...], gain_ref[...])
+    )(*rows, gain.reshape(1, depth), *in_vmem((gate_weight, up_weight, down_weight)))
+
+
+def next_kernel(*refs, half):
+    row_refs, refs = refs[:PIECES], refs[PIECES:]
+    gain_ref, query_ref, keyval_ref = refs[:3]
+    rows = joined(row_refs)
+    normed = normalized(rows, gain_ref[...])
     query = jnp.dot(normed, query_ref[...], preferred_element_type=f32).astype(bf16)
-    copy.wait()
     keyval = scores_of(keyval_ref[...], normed).astype(bf16)
-    if len(refs) == 2:
-        query_out, keyval_out = refs
+    if not half:
+        query_out, keyval_out = refs[3:]
         query_out[...] = query
         keyval_out[...] = keyval
         return
-    query_in, keyval_in, query_out, keyval_out = refs
+    query_in, keyval_in = refs[3:5]
+    query_out, keyval_out, residual_out = refs[5 + PIECES :]
     part = query.shape[0]
     mine = pl.multiple_of(half_start(2 * part, 1), part)
     theirs = pl.multiple_of(half_start(2 * part, 0), part)
@@ -400,20 +422,30 @@
         keyval_out[:, :part] = keyval_in[...]
         keyval_out[:, part:] = keyval
 
+    share = residual_out.shape[0]
+    place = lax.axis_index("tp") * share
+    at = pl.multiple_of(lax.rem(place, part), share)
+    held = (place >= mine) & (place < mine + part)
+    for k in range(PIECES):
+        ours = row_refs[k][pl.ds(at, share), :]
+        others = refs[5 + k][pl.ds(at, share), :]
+        residual_out[:, piece(rows.shape[1], k)] = jnp.where(held, ours, others)
+
 
 def next_projections(rows, gain, query_weight, keyval_weight, other):
-    count, depth = rows.shape
+    count = rows[0].shape[0]
+    depth = query_weight.shape[0]
     widths = (query_weight.shape[1], keyval_weight.shape[0])
-    out_rows = 2 * count if other else count
+    half = len(other) > 0
+    out_rows = 2 * count if half else count
+    shapes = [(out_rows, widths[0]), (widths[1], out_rows)]
+    if half:
+        shapes.append((out_rows // lax.axis_size("tp"), depth))
     return pl.pallas_call(
-        next_kernel,
-        out_shape=(
-            jax.ShapeDtypeStruct((out_rows, widths[0]), bf16),
-            jax.ShapeDtypeStruct((widths[1], out_rows), bf16),
-        ),
-        in_specs=[VMEM] * 3 + [HBM] + [VMEM] * len(other),
-        out_specs=(VMEM, VMEM),
-        scratch_shapes=[pltpu.VMEM(keyval_weight.shape, bf16), pltpu.SemaphoreType.DMA],
+        functools.partial(next_kernel, half=half),
+        out_shape=tuple(jax.ShapeDtypeStruct(shape, bf16) for shape in shapes),
+        in_specs=[VMEM] * (PIECES + 3 + len(other)),
+        out_specs=(VMEM,) * len(shapes),
         compiler_params=PARAMS,
         cost_estimate=pl.CostEstimate(
             flops=2 * count * depth * sum(widths),
@@ -421,7 +453,7 @@
             transcendentals=0,
         ),
         name="next_layer",
-    )(rows, gain.reshape(1, depth), *in_vmem([query_weight]), *in_hbm([keyval_weight]), *other)
+    )(*rows, gain.reshape(1, depth), *in_vmem([query_weight]), keyval_weight, *other)
 
 
 def trade(value, axis, bit):
@@ -433,6 +465,22 @@
     size = lax.axis_size("req")
     pairs = [(i, i ^ (odd_bit if i % 2 else even_bit)) for i in range(size)]
     return lax.ppermute(value, "req", pairs)
+
+
+def trades(values, bit):
+    return [trade(value, "tp", bit) for value in values]
+
+
+def each(join, *pieces):
+    return [join(*items) for items in zip(*pieces)]
+
+
+def add_pair(mine, got):
+    return (mine + wide(got)).astype(bf16)
+
+
+def add_rows(pair, rows, got):
+    return (wide(rows) + (wide(pair) + wide(got))).astype(bf16)
 
 
 def wide(value):
@@ -490,58 +538,56 @@
             state = extend_attention(aug, state, [chunk], kv_local)
         pools = []
 
-    theirs_att, theirs_proj = finish_attention(
+    theirs_att, *theirs_proj = finish_attention(
         aug, state, pools, out_weight, 0, kv_local, rows, ()
     )
-    attention, mine_proj = finish_attention(
-        aug, state, pools, out_weight, 1, kv_local, rows, (theirs_att,)
+    attention, *mine_proj = finish_attention(
+        aug, state, pools, out_weight, 1, kv_local, rows, (theirs_att, residual_in)
     )
+    mine_proj, res_mine = mine_proj[:PIECES], mine_proj[PIECES:]
 
     mine = half_start(rows, 1)
     theirs = half_start(rows, 0)
-    share = rows // lax.axis_size("tp")
-    place = lax.axis_index("tp") * share
-    res_mine = lax.dynamic_slice_in_dim(residual_in, mine, part, 0)
+    depth = residual_in.shape[1]
     if lax.axis_size("tp") == 4:
-        got = trade(theirs_proj, "tp", 1)
-        pair = (mine_proj + wide(got)).astype(bf16)
-        pair, *mlp = lax.optimization_barrier((pair, gate_weight, up_weight, down_weight))
-        got = trade(pair, "tp", 2)
-        got, *mlp = lax.optimization_barrier((got, *stage(mlp)))
-        mixed_mine = (wide(res_mine) + (wide(pair) + wide(got))).astype(bf16)
-        mixed_theirs = trade(mixed_mine, "tp", 1)
-        mlp_mine = feed_forward(mixed_mine, norm_gain, *mlp, bf16)
-        got = trade(mlp_mine, "tp", 1)
+        got = trades(theirs_proj, 1)
+        pair = each(add_pair, mine_proj, got)
+        pair[0], *mlp = lax.optimization_barrier((pair[0], gate_weight, up_weight, down_weight))
+        got = trades(pair, 2)
+        got[-1], *mlp = lax.optimization_barrier((got[-1], *stage(mlp)))
+        mixed_mine = each(add_rows, pair, res_mine, got)
+        mixed_theirs = trades(mixed_mine, 1)
+        got = trades(feed_forward(mixed_mine, norm_gain, *mlp, bf16), 1)
         mlp_theirs = feed_forward(mixed_theirs, norm_gain, *mlp, f32)
-        pair = (mlp_theirs + wide(got)).astype(bf16)
-        pair, query_weight = lax.optimization_barrier((pair, query_weight))
-        got = trade(pair, "tp", 2)
-        got, query_weight = lax.optimization_barrier((got, *stage([query_weight])))
-        layer_theirs = (wide(mixed_theirs) + (wide(pair) + wide(got))).astype(bf16)
-        layer_mine = trade(layer_theirs, "tp", 1)
+        pair = each(add_pair, mlp_theirs, got)
+        pair[0], query_weight = lax.optimization_barrier((pair[0], query_weight))
+        got = trades(pair, 2)
+        got[-1], query_weight = lax.optimization_barrier((got[-1], stage([query_weight])[0]))
+        layer_theirs = each(add_rows, pair, mixed_theirs, got)
+        layer_mine = trades(layer_theirs, 1)
     else:
+        res_mine = jnp.concatenate(res_mine, axis=1)
         res_theirs = lax.dynamic_slice_in_dim(residual_in, theirs, part, 0)
-        order = jnp.where(mine == 0, 1, 0)
 
         def in_order(theirs_part, mine_part):
             both = jnp.stack([theirs_part, mine_part])
-            return jnp.where(order == 1, both[::-1], both).reshape(rows, -1)
-
-        total = lax.psum(in_order(wide(theirs_proj), mine_proj), "tp")
+            return jnp.where(mine == 0, both[::-1], both).reshape(rows, -1)
+
+        theirs_proj = jnp.concatenate([wide(item) for item in theirs_proj], axis=1)
+        mine_proj = jnp.concatenate(mine_proj, axis=1)
+        total = lax.psum(in_order(theirs_proj, mine_proj), "tp")
         mixed = (wide(in_order(res_theirs, res_mine)) + total).astype(bf16)
-        mlp = feed_forward(mixed, norm_gain, gate_weight, up_weight, down_weight, f32)
-        layer = (wide(mixed) + lax.psum(mlp, "tp")).astype(bf16)
-        layer_mine = lax.dynamic_slice_in_dim(layer, mine, part, 0)
-        layer_theirs = lax.dynamic_slice_in_dim(layer, theirs, part, 0)
-    weights = [next_gain, query_weight, keyval_weight.T]
+        mixed_pieces = [mixed[:, piece(depth, k)] for k in range(PIECES)]
+        mlp = feed_forward(mixed_pieces, norm_gain, gate_weight, up_weight, down_weight, f32)
+        mlp = lax.psum(jnp.concatenate(mlp, axis=1), "tp")
+        layer = (wide(mixed) + mlp).astype(bf16)
+        layer = [layer[:, piece(depth, k)] for k in range(PIECES)]
+        layer_mine = [lax.dynamic_slice_in_dim(item, mine, part, 0) for item in layer]
+        layer_theirs = [lax.dynamic_slice_in_dim(item, theirs, part, 0) for item in layer]
+    weights = (next_gain, query_weight, keyval_weight.T)
     other = next_projections(layer_theirs, *weights, ())
-    next_query, next_keyval = next_projections(layer_mine, *weights, other)
-    at = lax.rem(place, part)
-    held = (place >= mine) & (place < mine + part)
-    residual_out = jnp.where(
-        held,
-        lax.dynamic_slice_in_dim(layer_mine, at, share, 0),
-        lax.dynamic_slice_in_dim(layer_theirs, at, share, 0),
+    next_query, next_keyval, residual_out = next_projections(
+        layer_mine, *weights, (*other, *layer_theirs)
     )
     return (attention, residual_out, next_query, next_keyval.T)
 

time: 106 us -> 88 us (0.83)
  waiting for transfers between devices: 45.3 us -> 33.8 us
  Pallas kernels: 34.3 us -> 29.4 us
  other arithmetic: 2.8 us -> 0.58 us
  starting transfers between devices: 18 us -> 19.1 us
    ppermute x10 -> x16, waiting for transfers between devices: 41.3 us -> 29.9 us  [trade(): return lax.ppermute(value, axis, [(i, i ^ bit) for i in range(size)])]
    pallas_call x4, Pallas kernels: 13.2 us -> 8.37 us  [the longest x2 5.12 us: feed_forward(): pl.pallas_call(mlp_kernel, out_shape=pieces_of(count, depth, dtype), in_s...]
    select_n x1 -> x0, other arithmetic: 1.71 us -> none  [per_device(): jnp.where(held, lax.dynamic_slice_in_dim(layer_mine, at, share, 0), lax.d...]
    ppermute x10 -> x16, starting transfers between devices: 12.2 us -> 13.2 us  [trade(): return lax.ppermute(value, axis, [(i, i ^ bit) for i in range(size)])]
    unnamed x15 -> x17, local copies, waits for them, and re-layouts: 3.92 us -> 3.91 us
  transfers between devices with their start and end apart: 13 -> 19, of which waited for: 10 -> 15; matrix products, arithmetic and copies ran while one was open for 1% -> 2% of each run, Pallas kernels for 25% -> 27%
where the time goes in v4:
time: 88 us; the launch traced here: 87.7 us
  waiting for transfers between devices  33.8 us (38%)
  Pallas kernels  29.4 us (33%)
  starting transfers between devices  19.1 us (22%)
  local copies, waits for them, and re-layouts  3.93 us (4%)
    ppermute x16, waiting for transfers between devices, trade(): return lax.ppermute(value, axis, [(i, i ^ bit) for i in range(size)])  29.9 us
    ppermute x16, starting transfers between devices, trade(): return lax.ppermute(value, axis, [(i, i ^ bit) for i in range(size)])  13.2 us
    pallas_call x2, Pallas kernels, stage(): pl.pallas_call(stage_kernel, out_shape=tuple((pltpu.VMEM(w.shape, w.dtype...  6.97 us
    pallas_call x2, Pallas kernels, finish_attention(): pl.pallas_call(functools.partial(finish_kernel, half=half, kv_local=kv_lo...  5.92 us
    ppermute x3, starting transfers between devices, cross(): return lax.ppermute(value, 'req', pairs)  5.83 us
    pallas_call x2, Pallas kernels, feed_forward(): pl.pallas_call(mlp_kernel, out_shape=pieces_of(count, depth, dtype), in_s...  5.12 us
    ppermute x3, waiting for transfers between devices, cross(): return lax.ppermute(value, 'req', pairs)  3.93 us
    unnamed x17, local copies, waits for them, and re-layouts  3.91 us
  transfers between devices with their start and end apart: 19, of which 15 were waited for; matrix products, arithmetic and copies ran while one was open for 2% of the time, Pallas kernels for 27%

profile of v4, /device:TPU:0, one launch (start us, length us, event | category | flops | bytes accessed | tf_op | source)
XLA Modules:
  0.0 87.7 jit_solution(11151394514380045867)
XLA Ops:
  0.6 1.0 %copy-done.3 = bf16[32,16,320]{2,1,0:T(8,128)(2,1)S(1)} copy-done((bf16[32,16,320]{2,1,0:T(8,128)(2,1)S(1)}, bf16[32,16,320]{2,1,0:T(8,128)(2,1)}, u32[]{:S(2)}) %copy-start.3) | copy-done | bytes 327704
  1.6 0.9 pool_rows.1.refs_0_
  2.5 0.5 collective-permute-start.2
  3.0 2.6 %collective-permute-start = (bf16[512,384]{1,0:T(8,128)(2,1)S(1)}, bf16[512,384]{1,0:T(8,128)(2,1)S(1)}, u32[]{:S(2)}, u32[]{:S(2)}) collective-permute-start(bf16[512,384]{1,0:T(8,128)(2,1)S(1)} %pool_rows.1.refs_0_), channel_id=1, source_target_pairs={{0,8},{4,20},{8,0},{12,28},{16,24},{20,4},{24,16},{28,12},{1,9},{5... | collective-permute-start | bytes 1179656 | tf_op jit(solution)/shard_map/ppermute | solution.py:467
  5.6 1.5 %collective-permute-start.1 = (bf16[512,384]{1,0:T(8,128)(2,1)S(1)}, bf16[512,384]{1,0:T(8,128)(2,1)S(1)}, u32[]{:S(2)}, u32[]{:S(2)}) collective-permute-start(bf16[512,384]{1,0:T(8,128)(2,1)S(1)} %pool_rows.1.refs_0_), channel_id=1, source_target_pairs={{0,16},{4,12},{8,24},{12,4},{16,0},{20,28},{24,8},{28,20},{1,17},{... | collective-permute-start | bytes 1179656 | tf_op jit(solution)/shard_map/ppermute | solution.py:467
  7.1 1.0 %copy.24.keyval_ref = bf16[128,320]{1,0:T(8,128)(2,1)S(1)} copy(bf16[128,320]{0,1:T(8,128)(2,1)} %param.21) | data formatting | bytes 163840 | tf_op args[1]
  8.1 1.0 %copy-done.4 = bf16[16,32,320]{2,1,0:T(8,128)(2,1)S(1)} copy-done((bf16[16,32,320]{2,1,0:T(8,128)(2,1)S(1)}, bf16[16,32,320]{2,1,0:T(8,128)(2,1)}, u32[]{:S(2)}) %copy-start.4) | copy-done | bytes 327704
  9.1 0.9 %copy-done.5 = bf16[128,640]{1,0:T(8,128)(2,1)S(1)} copy-done((bf16[128,640]{1,0:T(8,128)(2,1)S(1)}, bf16[128,640]{1,0:T(8,128)(2,1)}, u32[]{:S(2)}) %copy-start.5) | copy-done | bytes 163864
  10.0 3.8 %attend_local.1 = (bf16[1024,256]{1,0:T(8,128)(2,1)S(1)}, f32[1024,256]{1,0:T(8,128)S(1)}) custom-call(s32[1,16]{1,0:T(1,128)} %count_hbm.1, s32[16]{0:T(128)} %mid_hbm.1, s32[16]{0:T(128)} %leaf_len_hbm.1, bf16[128,640]{1,0:T(8,128)(2,1)S(1)} %copy-done.5, bf16[128,320]{1,0:T(8,128)(2,1)S(1)} %copy.24.keyval_ref, bf16[16,32,320]{2,1,0:T(8,128)(2,1)S(1)} %copy-done.4, ...), custom_call_target="tpu_custom_call" | custom-call | flops 1744830464 | bytes 2097152 | tf_op jit(solution)/shard_map/attend_local/pallas_call | solution.py:232
  13.8 0.6 collective-permute-done.refs_2_
  14.4 0.9 %collective-permute-done.1.refs_3_ = bf16[512,384]{1,0:T(8,128)(2,1)S(1)} collective-permute-done((bf16[512,384]{1,0:T(8,128)(2,1)S(1)}, bf16[512,384]{1,0:T(8,128)(2,1)S(1)}, u32[]{:S(2)}, u32[]{:S(2)}) %collective-permute-start.1) | collective-permute-done | bytes 393248 | tf_op jit(solution)/shard_map/ppermute | solution.py:467
  15.3 0.1 collective-permute-start.4
  15.4 0.4 collective-permute-start.5
  15.8 1.8 %collective-permute-start.3 = (bf16[512,384]{1,0:T(8,128)(2,1)S(1)}, bf16[512,384]{1,0:T(8,128)(2,1)S(1)}, u32[]{:S(2)}, u32[]{:S(2)}) collective-permute-start(bf16[512,384]{1,0:T(8,128)(2,1)S(1)} %collective-permute-done.refs_2_), channel_id=1, source_target_pairs={{0,16},{4,12},{8,24},{12,4},{16,0},{20,28},{24,8},{28,20},{1,17},{... | collective-permute-start | bytes 1179656 | tf_op jit(solution)/shard_map/ppermute | solution.py:467
  17.6 3.6 %attend_pages.1.refs_1_ = f32[1024,256]{1,0:T(8,128)S(1)} custom-call(bf16[1024,256]{1,0:T(8,128)(2,1)S(1)} %get-tuple-element.51.refs_0_, f32[1024,256]{1,0:T(8,128)S(1)} %get-tuple-element.49.refs_1_, bf16[512,384]{1,0:T(8,128)(2,1)S(1)} %collective-permute-done.refs_2_, bf16[512,384]{1,0:T(8,128)(2,1)S(1)} %collective-permute-done.1.refs_3_, ...), custom_call_target="tpu_custom_call" | custom-call | flops 2147483648 | bytes 2097152 | tf_op jit(solution)/shard_map/attend_pages/pallas_call | solution.py:271
  21.2 2.4 %collective-permute-done.3.refs_2_ = bf16[512,384]{1,0:T(8,128)(2,1)S(1)} collective-permute-done((bf16[512,384]{1,0:T(8,128)(2,1)S(1)}, bf16[512,384]{1,0:T(8,128)(2,1)S(1)}, u32[]{:S(2)}, u32[]{:S(2)}) %collective-permute-start.3) | collective-permute-done | bytes 393248 | tf_op jit(solution)/shard_map/ppermute | solution.py:467
  23.6 1.7 %collective-permute-done.6.refs_3_ = bf16[512,384]{1,0:T(8,128)(2,1)S(1)} collective-permute-done((bf16[512,384]{1,0:T(8,128)(2,1)S(1)}, bf16[512,384]{1,0:T(8,128)(2,1)S(1)}, u32[]{:S(2)}, u32[]{:S(2)}) %collective-permute-start.6) | collective-permute-done | bytes 393248 | tf_op jit(solution)/shard_map/ppermute | solution.py:461
  25.3 2.9 %attend_finish.2 = (bf16[64,640]{1,0:T(8,128)(2,1)S(1)}, bf16[64,1280]{1,0:T(8,128)(2,1)S(1)}, bf16[64,1280]{1,0:T(8,128)(2,1)S(1)}) custom-call(bf16[1024,256]{1,0:T(8,128)(2,1)S(1)} %get-tuple-element.51.refs_0_, f32[1024,256]{1,0:T(8,128)S(1)} %attend_pages.1.refs_1_, bf16[512,384]{1,0:T(8,128)(2,1)S(1)} %collective-permute-done.3.refs_2_, ...), custom_call_target="tpu_custom_call" | custom-call | flops 805306368 | bytes 1048576 | tf_op jit(solution)/shard_map/attend_finish/pallas_call | solution.py:322
  28.3 1.9 %collective-permute-start.10 = (bf16[64,1280]{1,0:T(8,128)(2,1)S(1)}, bf16[64,1280]{1,0:T(8,128)(2,1)S(1)}, u32[]{:S(2)}, u32[]{:S(2)}) collective-permute-start(bf16[64,1280]{1,0:T(8,128)(2,1)S(1)} %get-tuple-element.62), channel_id=1, source_target_pairs={{0,1},{1,0},{2,3},{3,2},{4,5},{5,4},{6,7},{7,6},{8,9},{9,8},{10,11... | collective-permute-start | bytes 491528 | tf_op jit(solution)/shard_map/ppermute | solution.py:461
  30.2 0.3 collective-permute-start.7
  30.5 3.0 %attend_finish.3 = (bf16[128,640]{1,0:T(8,128)(2,1)}, f32[64,1280]{1,0:T(8,128)S(1)}, f32[64,1280]{1,0:T(8,128)S(1)}, bf16[64,1280]{1,0:T(8,128)(2,1)S(1)}, bf16[64,1280]{1,0:T(8,128)(2,1)S(1)}) custom-call(bf16[1024,256]{1,0:T(8,128)(2,1)S(1)} %get-tuple-element.51.refs_0_, f32[1024,256]{1,0:T(8,128)S(1)} %attend_pages.1.refs_1_, ...), custom_call_target="tpu_custom_call" | custom-call | flops 805306368 | bytes 1048576 | tf_op jit(solution)/shard_map/attend_finish/pallas_call | solution.py:322
  33.4 1.9 %collective-permute-done.10 = bf16[64,1280]{1,0:T(8,128)(2,1)S(1)} collective-permute-done((bf16[64,1280]{1,0:T(8,128)(2,1)S(1)}, bf16[64,1280]{1,0:T(8,128)(2,1)S(1)}, u32[]{:S(2)}, u32[]{:S(2)}) %collective-permute-start.10) | collective-permute-done | bytes 163872 | tf_op jit(solution)/shard_map/ppermute | solution.py:461
  35.4 2.9 %collective-permute-start.11 = (bf16[64,1280]{1,0:T(8,128)(2,1)S(1)}, bf16[64,1280]{1,0:T(8,128)(2,1)S(1)}, u32[]{:S(2)}, u32[]{:S(2)}) collective-permute-start(bf16[64,1280]{1,0:T(8,128)(2,1)S(1)} %add_convert_fusion.5), channel_id=1, source_target_pairs={{0,2},{1,3},{2,0},{3,1},{4,6},{5,7},{6,4},{7,5},{8,10},{9,11},{10,... | collective-permute-start | bytes 491528 | tf_op jit(solution)/shard_map/ppermute | solution.py:461
  38.3 1.6 %collective-permute-done.7 = bf16[64,1280]{1,0:T(8,128)(2,1)S(1)} collective-permute-done((bf16[64,1280]{1,0:T(8,128)(2,1)S(1)}, bf16[64,1280]{1,0:T(8,128)(2,1)S(1)}, u32[]{:S(2)}, u32[]{:S(2)}) %collective-permute-start.7) | collective-permute-done | bytes 163872 | tf_op jit(solution)/shard_map/ppermute | solution.py:461
  40.0 1.9 %collective-permute-start.8 = (bf16[64,1280]{1,0:T(8,128)(2,1)S(1)}, bf16[64,1280]{1,0:T(8,128)(2,1)S(1)}, u32[]{:S(2)}, u32[]{:S(2)}) collective-permute-start(bf16[64,1280]{1,0:T(8,128)(2,1)S(1)} %add_convert_fusion.7), channel_id=1, source_target_pairs={{0,2},{1,3},{2,0},{3,1},{4,6},{5,7},{6,4},{7,5},{8,10},{9,11},{10,... | collective-permute-start | bytes 491528 | tf_op jit(solution)/shard_map/ppermute | solution.py:461
  41.8 5.0 %stage.2 = (bf16[2560,896]{1,0:T(8,128)(2,1)S(1)}, bf16[2560,896]{1,0:T(8,128)(2,1)S(1)}, bf16[896,2560]{1,0:T(8,128)(2,1)S(1)}) custom-call(bf16[2560,896]{1,0:T(8,128)(2,1)} %refs_0_, bf16[2560,896]{1,0:T(8,128)(2,1)} %refs_1_, bf16[896,2560]{1,0:T(8,128)(2,1)} %refs_2_), custom_call_target="tpu_custom_call" | custom-call | bytes 13762560 | tf_op jit(solution)/shard_map/stage/pallas_call | solution.py:353
  46.9 2.8 %collective-permute-done.11 = bf16[64,1280]{1,0:T(8,128)(2,1)S(1)} collective-permute-done((bf16[64,1280]{1,0:T(8,128)(2,1)S(1)}, bf16[64,1280]{1,0:T(8,128)(2,1)S(1)}, u32[]{:S(2)}, u32[]{:S(2)}) %collective-permute-start.11) | collective-permute-done | bytes 163872 | tf_op jit(solution)/shard_map/ppermute | solution.py:461
  49.6 0.2 add_convert_fusion.4.refs_1_
  49.9 0.1 collective-permute-start.12
  50.0 2.1 %collective-permute-done.8 = bf16[64,1280]{1,0:T(8,128)(2,1)S(1)} collective-permute-done((bf16[64,1280]{1,0:T(8,128)(2,1)S(1)}, bf16[64,1280]{1,0:T(8,128)(2,1)S(1)}, u32[]{:S(2)}, u32[]{:S(2)}) %collective-permute-start.8) | collective-permute-done | bytes 163872 | tf_op jit(solution)/shard_map/ppermute | solution.py:461
  52.2 0.4 collective-permute-start.9
  52.6 2.6 %feed_forward.3 = (bf16[64,1280]{1,0:T(8,128)(2,1)S(1)}, bf16[64,1280]{1,0:T(8,128)(2,1)S(1)}) custom-call(bf16[64,1280]{1,0:T(8,128)(2,1)S(1)} %add_convert_fusion.6.refs_0_, bf16[64,1280]{1,0:T(8,128)(2,1)S(1)} %add_convert_fusion.4.refs_1_, bf16[1,2560]{1,0:T(2,128)(2,1)S(1)} %reshape.16.refs_2_, bf16[2560,896]{1,0:T(8,128)(2,1)S(1)} %get-tuple-element.70.refs_3_, ...), custom_call_target="tpu_custom_call" | custom-call | flops 880803840 | bytes 13762560 | tf_op jit(solution)/shard_map/feed_forward/pallas_call | solution.py:382
  55.2 1.7 %collective-permute-start.16 = (bf16[64,1280]{1,0:T(8,128)(2,1)S(1)}, bf16[64,1280]{1,0:T(8,128)(2,1)S(1)}, u32[]{:S(2)}, u32[]{:S(2)}) collective-permute-start(bf16[64,1280]{1,0:T(8,128)(2,1)S(1)} %get-tuple-element.77), channel_id=1, source_target_pairs={{0,1},{1,0},{2,3},{3,2},{4,5},{5,4},{6,7},{7,6},{8,9},{9,8},{10,11... | collective-permute-start | bytes 491528 | tf_op jit(solution)/shard_map/ppermute | solution.py:461
  56.9 0.4 collective-permute-start.13
  57.3 3.3 %collective-permute-done.9.refs_0_ = bf16[64,1280]{1,0:T(8,128)(2,1)S(1)} collective-permute-done((bf16[64,1280]{1,0:T(8,128)(2,1)S(1)}, bf16[64,1280]{1,0:T(8,128)(2,1)S(1)}, u32[]{:S(2)}, u32[]{:S(2)}) %collective-permute-start.9) | collective-permute-done | bytes 163872 | tf_op jit(solution)/shard_map/ppermute | solution.py:461
  60.6 2.6 %feed_forward.2 = (f32[64,1280]{1,0:T(8,128)S(1)}, f32[64,1280]{1,0:T(8,128)S(1)}) custom-call(bf16[64,1280]{1,0:T(8,128)(2,1)S(1)} %collective-permute-done.9.refs_0_, bf16[64,1280]{1,0:T(8,128)(2,1)S(1)} %collective-permute-done.12.refs_1_, bf16[1,2560]{1,0:T(2,128)(2,1)S(1)} %reshape.16.refs_2_, bf16[2560,896]{1,0:T(8,128)(2,1)S(1)} %get-tuple-element.70.refs_3_, ...), custom_call_target="tpu_custom_call" | custom-call | flops 880803840 | bytes 13762560 | tf_op jit(solution)/shard_map/feed_forward/pallas_call | solution.py:382
  63.2 0.9 %collective-permute-done.16 = bf16[64,1280]{1,0:T(8,128)(2,1)S(1)} collective-permute-done((bf16[64,1280]{1,0:T(8,128)(2,1)S(1)}, bf16[64,1280]{1,0:T(8,128)(2,1)S(1)}, u32[]{:S(2)}, u32[]{:S(2)}) %collective-permute-start.16) | collective-permute-done | bytes 163872 | tf_op jit(solution)/shard_map/ppermute | solution.py:461
  64.2 1.6 %collective-permute-start.17 = (bf16[64,1280]{1,0:T(8,128)(2,1)S(1)}, bf16[64,1280]{1,0:T(8,128)(2,1)S(1)}, u32[]{:S(2)}, u32[]{:S(2)}) collective-permute-start(bf16[64,1280]{1,0:T(8,128)(2,1)S(1)} %add_convert_fusion.1), channel_id=1, source_target_pairs={{0,2},{1,3},{2,0},{3,1},{4,6},{5,7},{6,4},{7,5},{8,10},{9,11},{10,... | collective-permute-start | bytes 491528 | tf_op jit(solution)/shard_map/ppermute | solution.py:461
  65.8 2.1 %collective-permute-done.13 = bf16[64,1280]{1,0:T(8,128)(2,1)S(1)} collective-permute-done((bf16[64,1280]{1,0:T(8,128)(2,1)S(1)}, bf16[64,1280]{1,0:T(8,128)(2,1)S(1)}, u32[]{:S(2)}, u32[]{:S(2)}) %collective-permute-start.13) | collective-permute-done | bytes 163872 | tf_op jit(solution)/shard_map/ppermute | solution.py:461
  67.9 1.9 %stage.3.refs_3_ = bf16[2560,640]{1,0:T(8,128)(2,1)S(1)} custom-call(bf16[2560,640]{1,0:T(8,128)(2,1)} %refs_0_.1), custom_call_target="tpu_custom_call" | custom-call | bytes 3276800 | tf_op jit(solution)/shard_map/stage/pallas_call | solution.py:353
  69.8 0.6 collective-permute-start.14
  70.4 6.9 %collective-permute-done.17 = bf16[64,1280]{1,0:T(8,128)(2,1)S(1)} collective-permute-done((bf16[64,1280]{1,0:T(8,128)(2,1)S(1)}, bf16[64,1280]{1,0:T(8,128)(2,1)S(1)}, u32[]{:S(2)}, u32[]{:S(2)}) %collective-permute-start.17) | collective-permute-done | bytes 163872 | tf_op jit(solution)/shard_map/ppermute | solution.py:461
  77.5 1.7 %collective-permute-done.14 = bf16[64,1280]{1,0:T(8,128)(2,1)S(1)} collective-permute-done((bf16[64,1280]{1,0:T(8,128)(2,1)S(1)}, bf16[64,1280]{1,0:T(8,128)(2,1)S(1)}, u32[]{:S(2)}, u32[]{:S(2)}) %collective-permute-start.14) | collective-permute-done | bytes 163872 | tf_op jit(solution)/shard_map/ppermute | solution.py:461
  79.2 0.4 collective-permute-start.15
  79.6 1.2 %next_layer.2 = (bf16[64,640]{1,0:T(8,128)(2,1)S(1)}, bf16[320,64]{1,0:T(8,128)(2,1)S(1)}) custom-call(bf16[64,1280]{1,0:T(8,128)(2,1)S(1)} %add_convert_fusion.2.refs_0_.refs_7_, bf16[64,1280]{1,0:T(8,128)(2,1)S(1)} %add_convert_fusion.refs_1_.refs_8_, bf16[1,2560]{1,0:T(2,128)(2,1)S(1)} %reshape.17.refs_2_, bf16[2560,640]{1,0:T(8,128)(2,1)S(1)} %stage.3.refs_3_, ...), custom_call_target="tpu_custom_call" | custom-call | flops 314572800 | bytes 4915200 | tf_op jit(solution)/shard_map/next_layer/pallas_call | solution.py:444
  80.8 3.0 %collective-permute-done.18.refs_1_ = bf16[64,1280]{1,0:T(8,128)(2,1)S(1)} collective-permute-done((bf16[64,1280]{1,0:T(8,128)(2,1)S(1)}, bf16[64,1280]{1,0:T(8,128)(2,1)S(1)}, u32[]{:S(2)}, u32[]{:S(2)}) %collective-permute-start.18) | collective-permute-done | bytes 163872 | tf_op jit(solution)/shard_map/ppermute | solution.py:461
  83.9 1.8 %collective-permute-done.15.refs_0_ = bf16[64,1280]{1,0:T(8,128)(2,1)S(1)} collective-permute-done((bf16[64,1280]{1,0:T(8,128)(2,1)S(1)}, bf16[64,1280]{1,0:T(8,128)(2,1)S(1)}, u32[]{:S(2)}, u32[]{:S(2)}) %collective-permute-start.15) | collective-permute-done | bytes 163872 | tf_op jit(solution)/shard_map/ppermute | solution.py:461
  85.6 2.1 %next_layer.3 = (bf16[128,640]{1,0:T(8,128)(2,1)}, bf16[320,128]{1,0:T(8,128)(2,1)}, bf16[32,2560]{1,0:T(8,128)(2,1)}) custom-call(bf16[64,1280]{1,0:T(8,128)(2,1)S(1)} %collective-permute-done.15.refs_0_, bf16[64,1280]{1,0:T(8,128)(2,1)S(1)} %collective-permute-done.18.refs_1_, bf16[1,2560]{1,0:T(2,128)(2,1)S(1)} %reshape.17.refs_2_, ...), custom_call_target="tpu_custom_call" | custom-call | flops 314572800 | bytes 4915200 | tf_op jit(solution)/shard_map/next_layer/pallas_call | solution.py:444
  (28 shorter events, 0.5 us)
Async XLA Ops:
  0.6 1.0 %copy-start.3 = (bf16[32,16,320]{2,1,0:T(8,128)(2,1)S(1)}, bf16[32,16,320]{2,1,0:T(8,128)(2,1)}, u32[]{:S(2)}) copy-start(bf16[32,16,320]{2,1,0:T(8,128)(2,1)} %pool_ref.1) | copy-start | bytes 983044
  2.5 5.6 %collective-permute-start.2 = (bf16[512,384]{1,0:T(8,128)(2,1)S(1)}, bf16[512,384]{1,0:T(8,128)(2,1)S(1)}, u32[]{:S(2)}, u32[]{:S(2)}) collective-permute-start(bf16[512,384]{1,0:T(8,128)(2,1)S(1)} %pool_rows.1.refs_0_), channel_id=1, source_target_pairs={{0,4},{4,0},{8,12},{12,8},{16,20},{20,16},{24,28},{28,24},{1,5},{5... | collective-permute-start | bytes 1179656 | tf_op jit(solution)/shard_map/ppermute | solution.py:461
  3.0 11.4 %collective-permute-start = (bf16[512,384]{1,0:T(8,128)(2,1)S(1)}, bf16[512,384]{1,0:T(8,128)(2,1)S(1)}, u32[]{:S(2)}, u32[]{:S(2)}) collective-permute-start(bf16[512,384]{1,0:T(8,128)(2,1)S(1)} %pool_rows.1.refs_0_), channel_id=1, source_target_pairs={{0,8},{4,20},{8,0},{12,28},{16,24},{20,4},{24,16},{28,12},{1,9},{5... | collective-permute-start | bytes 1179656 | tf_op jit(solution)/shard_map/ppermute | solution.py:467
  5.6 9.7 %collective-permute-start.1 = (bf16[512,384]{1,0:T(8,128)(2,1)S(1)}, bf16[512,384]{1,0:T(8,128)(2,1)S(1)}, u32[]{:S(2)}, u32[]{:S(2)}) collective-permute-start(bf16[512,384]{1,0:T(8,128)(2,1)S(1)} %pool_rows.1.refs_0_), channel_id=1, source_target_pairs={{0,16},{4,12},{8,24},{12,4},{16,0},{20,28},{24,8},{28,20},{1,17},{... | collective-permute-start | bytes 1179656 | tf_op jit(solution)/shard_map/ppermute | solution.py:467
  8.1 1.0 %copy-start.4 = (bf16[16,32,320]{2,1,0:T(8,128)(2,1)S(1)}, bf16[16,32,320]{2,1,0:T(8,128)(2,1)}, u32[]{:S(2)}) copy-start(bf16[16,32,320]{2,1,0:T(8,128)(2,1)} %leaf_ref.1) | copy-start | bytes 983044
  9.1 0.9 %copy-start.5 = (bf16[128,640]{1,0:T(8,128)(2,1)S(1)}, bf16[128,640]{1,0:T(8,128)(2,1)}, u32[]{:S(2)}) copy-start(bf16[128,640]{1,0:T(8,128)(2,1)} %query_ref.1) | copy-start | bytes 491524
  13.8 11.5 %copy-start = (bf16[640,2560]{1,0:T(8,128)(2,1)S(1)}, bf16[640,2560]{1,0:T(8,128)(2,1)}, u32[]{:S(2)}) copy-start(bf16[640,2560]{1,0:T(8,128)(2,1)} %refs_4_.3) | copy-start | bytes 9830404
  15.3 2.3 %collective-permute-start.4 = (bf16[512,384]{1,0:T(8,128)(2,1)S(1)}, bf16[512,384]{1,0:T(8,128)(2,1)S(1)}, u32[]{:S(2)}, u32[]{:S(2)}) collective-permute-start(bf16[512,384]{1,0:T(8,128)(2,1)S(1)} %collective-permute-done.refs_2_), channel_id=1, source_target_pairs={{0,4},{4,0},{8,12},{12,8},{16,20},{20,16},{24,28},{28,24},{1,5},{5... | collective-permute-start | bytes 1179656 | tf_op jit(solution)/shard_map/ppermute | solution.py:461
  15.4 2.2 %collective-permute-start.5 = (bf16[512,384]{1,0:T(8,128)(2,1)S(1)}, bf16[512,384]{1,0:T(8,128)(2,1)S(1)}, u32[]{:S(2)}, u32[]{:S(2)}) collective-permute-start(bf16[512,384]{1,0:T(8,128)(2,1)S(1)} %collective-permute-done.1.refs_3_), channel_id=1, source_target_pairs={{0,4},{4,0},{8,12},{12,8},{16,20},{20,16},{24,28},{28,24},{1,5},{5... | collective-permute-start | bytes 1179656 | tf_op jit(solution)/shard_map/ppermute | solution.py:461
  15.8 7.8 %collective-permute-start.3 = (bf16[512,384]{1,0:T(8,128)(2,1)S(1)}, bf16[512,384]{1,0:T(8,128)(2,1)S(1)}, u32[]{:S(2)}, u32[]{:S(2)}) collective-permute-start(bf16[512,384]{1,0:T(8,128)(2,1)S(1)} %collective-permute-done.refs_2_), channel_id=1, source_target_pairs={{0,16},{4,12},{8,24},{12,4},{16,0},{20,28},{24,8},{28,20},{1,17},{... | collective-permute-start | bytes 1179656 | tf_op jit(solution)/shard_map/ppermute | solution.py:467
  21.2 9.0 %copy-start.6 = (bf16[2560]{0:T(1024)(128)(2,1)S(1)}, bf16[2560]{0:T(1024)(128)(2,1)}, u32[]{:S(2)}) copy-start(bf16[2560]{0:T(1024)(128)(2,1)} %param.33) | copy-start | bytes 15364
  21.2 9.3 %copy-start.2 = (bf16[128,2560]{1,0:T(8,128)(2,1)S(1)}, bf16[128,2560]{1,0:T(8,128)(2,1)}, u32[]{:S(2)}) copy-start(bf16[128,2560]{1,0:T(8,128)(2,1)} %refs_6_.1) | copy-start | bytes 1966084
  23.6 1.7 %collective-permute-start.6 = (bf16[512,384]{1,0:T(8,128)(2,1)S(1)}, bf16[512,384]{1,0:T(8,128)(2,1)S(1)}, u32[]{:S(2)}, u32[]{:S(2)}) collective-permute-start(bf16[512,384]{1,0:T(8,128)(2,1)S(1)} %collective-permute-done.3.refs_2_), channel_id=1, source_target_pairs={{0,4},{4,0},{8,12},{12,8},{16,20},{20,16},{24,28},{28,24},{1,5},{5... | collective-permute-start | bytes 1179656 | tf_op jit(solution)/shard_map/ppermute | solution.py:461
  28.3 7.1 %collective-permute-start.10 = (bf16[64,1280]{1,0:T(8,128)(2,1)S(1)}, bf16[64,1280]{1,0:T(8,128)(2,1)S(1)}, u32[]{:S(2)}, u32[]{:S(2)}) collective-permute-start(bf16[64,1280]{1,0:T(8,128)(2,1)S(1)} %get-tuple-element.62), channel_id=1, source_target_pairs={{0,1},{1,0},{2,3},{3,2},{4,5},{5,4},{6,7},{7,6},{8,9},{9,8},{10,11... | collective-permute-start | bytes 491528 | tf_op jit(solution)/shard_map/ppermute | solution.py:461
  30.2 9.8 %collective-permute-start.7 = (bf16[64,1280]{1,0:T(8,128)(2,1)S(1)}, bf16[64,1280]{1,0:T(8,128)(2,1)S(1)}, u32[]{:S(2)}, u32[]{:S(2)}) collective-permute-start(bf16[64,1280]{1,0:T(8,128)(2,1)S(1)} %get-tuple-element.58), channel_id=1, source_target_pairs={{0,1},{1,0},{2,3},{3,2},{4,5},{5,4},{6,7},{7,6},{8,9},{9,8},{10,11... | collective-permute-start | bytes 491528 | tf_op jit(solution)/shard_map/ppermute | solution.py:461
  35.4 14.2 %collective-permute-start.11 = (bf16[64,1280]{1,0:T(8,128)(2,1)S(1)}, bf16[64,1280]{1,0:T(8,128)(2,1)S(1)}, u32[]{:S(2)}, u32[]{:S(2)}) collective-permute-start(bf16[64,1280]{1,0:T(8,128)(2,1)S(1)} %add_convert_fusion.5), channel_id=1, source_target_pairs={{0,2},{1,3},{2,0},{3,1},{4,6},{5,7},{6,4},{7,5},{8,10},{9,11},{10,... | collective-permute-start | bytes 491528 | tf_op jit(solution)/shard_map/ppermute | solution.py:461
  40.0 12.2 %collective-permute-start.8 = (bf16[64,1280]{1,0:T(8,128)(2,1)S(1)}, bf16[64,1280]{1,0:T(8,128)(2,1)S(1)}, u32[]{:S(2)}, u32[]{:S(2)}) collective-permute-start(bf16[64,1280]{1,0:T(8,128)(2,1)S(1)} %add_convert_fusion.7), channel_id=1, source_target_pairs={{0,2},{1,3},{2,0},{3,1},{4,6},{5,7},{6,4},{7,5},{8,10},{9,11},{10,... | collective-permute-start | bytes 491528 | tf_op jit(solution)/shard_map/ppermute | solution.py:461
  49.9 7.4 %collective-permute-start.12 = (bf16[64,1280]{1,0:T(8,128)(2,1)S(1)}, bf16[64,1280]{1,0:T(8,128)(2,1)S(1)}, u32[]{:S(2)}, u32[]{:S(2)}) collective-permute-start(bf16[64,1280]{1,0:T(8,128)(2,1)S(1)} %add_convert_fusion.4.refs_1_), channel_id=1, source_target_pairs={{0,1},{1,0},{2,3},{3,2},{4,5},{5,4},{6,7},{7,6},{8,9},{9,8},{10,11... | collective-permute-start | bytes 491528 | tf_op jit(solution)/shard_map/ppermute | solution.py:461
  52.2 8.4 %collective-permute-start.9 = (bf16[64,1280]{1,0:T(8,128)(2,1)S(1)}, bf16[64,1280]{1,0:T(8,128)(2,1)S(1)}, u32[]{:S(2)}, u32[]{:S(2)}) collective-permute-start(bf16[64,1280]{1,0:T(8,128)(2,1)S(1)} %add_convert_fusion.6.refs_0_), channel_id=1, source_target_pairs={{0,1},{1,0},{2,3},{3,2},{4,5},{5,4},{6,7},{7,6},{8,9},{9,8},{10,11... | collective-permute-start | bytes 491528 | tf_op jit(solution)/shard_map/ppermute | solution.py:461
  55.2 8.9 %collective-permute-start.16 = (bf16[64,1280]{1,0:T(8,128)(2,1)S(1)}, bf16[64,1280]{1,0:T(8,128)(2,1)S(1)}, u32[]{:S(2)}, u32[]{:S(2)}) collective-permute-start(bf16[64,1280]{1,0:T(8,128)(2,1)S(1)} %get-tuple-element.77), channel_id=1, source_target_pairs={{0,1},{1,0},{2,3},{3,2},{4,5},{5,4},{6,7},{7,6},{8,9},{9,8},{10,11... | collective-permute-start | bytes 491528 | tf_op jit(solution)/shard_map/ppermute | solution.py:461
  56.9 10.9 %collective-permute-start.13 = (bf16[64,1280]{1,0:T(8,128)(2,1)S(1)}, bf16[64,1280]{1,0:T(8,128)(2,1)S(1)}, u32[]{:S(2)}, u32[]{:S(2)}) collective-permute-start(bf16[64,1280]{1,0:T(8,128)(2,1)S(1)} %get-tuple-element.74), channel_id=1, source_target_pairs={{0,1},{1,0},{2,3},{3,2},{4,5},{5,4},{6,7},{7,6},{8,9},{9,8},{10,11... | collective-permute-start | bytes 491528 | tf_op jit(solution)/shard_map/ppermute | solution.py:461
  64.1 15.5 %copy-start.7 = (bf16[2560]{0:T(1024)(128)(2,1)S(1)}, bf16[2560]{0:T(1024)(128)(2,1)}, u32[]{:S(2)}) copy-start(bf16[2560]{0:T(1024)(128)(2,1)} %param.37) | copy-start | bytes 15364
  64.1 15.5 %copy-start.1 = (bf16[2560,320]{0,1:T(8,128)(2,1)S(1)}, bf16[2560,320]{0,1:T(8,128)(2,1)}, u32[]{:S(2)}) copy-start(bf16[2560,320]{0,1:T(8,128)(2,1)} %param.39) | copy-start | bytes 4915204
  64.2 13.2 %collective-permute-start.17 = (bf16[64,1280]{1,0:T(8,128)(2,1)S(1)}, bf16[64,1280]{1,0:T(8,128)(2,1)S(1)}, u32[]{:S(2)}, u32[]{:S(2)}) collective-permute-start(bf16[64,1280]{1,0:T(8,128)(2,1)S(1)} %add_convert_fusion.1), channel_id=1, source_target_pairs={{0,2},{1,3},{2,0},{3,1},{4,6},{5,7},{6,4},{7,5},{8,10},{9,11},{10,... | collective-permute-start | bytes 491528 | tf_op jit(solution)/shard_map/ppermute | solution.py:461
  69.8 9.3 %collective-permute-start.14 = (bf16[64,1280]{1,0:T(8,128)(2,1)S(1)}, bf16[64,1280]{1,0:T(8,128)(2,1)S(1)}, u32[]{:S(2)}, u32[]{:S(2)}) collective-permute-start(bf16[64,1280]{1,0:T(8,128)(2,1)S(1)} %add_convert_fusion.3), channel_id=1, source_target_pairs={{0,2},{1,3},{2,0},{3,1},{4,6},{5,7},{6,4},{7,5},{8,10},{9,11},{10,... | collective-permute-start | bytes 491528 | tf_op jit(solution)/shard_map/ppermute | solution.py:461
  77.4 6.5 %collective-permute-start.18 = (bf16[64,1280]{1,0:T(8,128)(2,1)S(1)}, bf16[64,1280]{1,0:T(8,128)(2,1)S(1)}, u32[]{:S(2)}, u32[]{:S(2)}) collective-permute-start(bf16[64,1280]{1,0:T(8,128)(2,1)S(1)} %add_convert_fusion.refs_1_.refs_8_), channel_id=1, source_target_pairs={{0,1},{1,0},{2,3},{3,2},{4,5},{5,4},{6,7},{7,6},{8,9},{9,8},{10,11... | collective-permute-start | bytes 491528 | tf_op jit(solution)/shard_map/ppermute | solution.py:461
  79.2 6.4 %collective-permute-start.15 = (bf16[64,1280]{1,0:T(8,128)(2,1)S(1)}, bf16[64,1280]{1,0:T(8,128)(2,1)S(1)}, u32[]{:S(2)}, u32[]{:S(2)}) collective-permute-start(bf16[64,1280]{1,0:T(8,128)(2,1)S(1)} %add_convert_fusion.2.refs_0_.refs_7_), channel_id=1, source_target_pairs={{0,1},{1,0},{2,3},{3,2},{4,5},{5,4},{6,7},{7,6},{8,9},{9,8},{10,11... | collective-permute-start | bytes 491528 | tf_op jit(solution)/shard_map/ppermute | solution.py:461

commit v5 on v4

--- a/solution.py
+++ b/solution.py
@@ -519,14 +519,18 @@
         second = cross(pool, 4, 2)
         beside = trade(pool, "req", 1)
         aug, state = start_attention(*local_args, [pool, beside])
-        first, second, aug, state = lax.optimization_barrier((first, second, aug, state))
+        first, aug, state = lax.optimization_barrier((first, aug, state))
         corner = cross(first, 4, 2)
-        first_other = trade(first, "req", 1)
-        second_other = trade(second, "req", 1)
-        near = [first, second, first_other, second_other]
+        first, second = lax.optimization_barrier((first, second))
+        near = [first, second, trade(first, "req", 1), trade(second, "req", 1)]
         state = extend_attention(aug, state, near, kv_local)
-        corner, aug, state = lax.optimization_barrier((corner, aug, state))
-        pools = [corner, trade(corner, "req", 1)]
+        state, down_weight = lax.optimization_barrier((state, down_weight))
+        corner, state, down_weight = lax.optimization_barrier(
+            (corner, state, *stage([down_weight]))
+        )
+        corner_other = trade(corner, "req", 1)
+        state = extend_attention(aug, state, [corner], kv_local)
+        pools = [corner_other]
     else:
         every = lax.all_gather(pool, "req", axis=0)
         holders = every.shape[0]
@@ -551,18 +555,22 @@
     depth = residual_in.shape[1]
     if lax.axis_size("tp") == 4:
         got = trades(theirs_proj, 1)
-        pair = each(add_pair, mine_proj, got)
-        pair[0], *mlp = lax.optimization_barrier((pair[0], gate_weight, up_weight, down_weight))
+        last = add_pair(mine_proj[-1], got[-1])
+        last, gate_weight, up_weight = lax.optimization_barrier((last, gate_weight, up_weight))
+        staged = stage([gate_weight, up_weight])
+        got[:-1], gate_weight, up_weight = lax.optimization_barrier((got[:-1], *staged))
+        mlp = (gate_weight, up_weight, down_weight)
+        pair = [*each(add_pair, mine_proj[:-1], got[:-1]), last]
         got = trades(pair, 2)
-        got[-1], *mlp = lax.optimization_barrier((got[-1], *stage(mlp)))
         mixed_mine = each(add_rows, pair, res_mine, got)
         mixed_theirs = trades(mixed_mine, 1)
         got = trades(feed_forward(mixed_mine, norm_gain, *mlp, bf16), 1)
         mlp_theirs = feed_forward(mixed_theirs, norm_gain, *mlp, f32)
-        pair = each(add_pair, mlp_theirs, got)
-        pair[0], query_weight = lax.optimization_barrier((pair[0], query_weight))
+        last = add_pair(mlp_theirs[-1], got[-1])
+        last, query_weight = lax.optimization_barrier((last, query_weight))
+        got[:-1], query_weight = lax.optimization_barrier((got[:-1], *stage([query_weight])))
+        pair = [*each(add_pair, mlp_theirs[:-1], got[:-1]), last]
         got = trades(pair, 2)
-        got[-1], query_weight = lax.optimization_barrier((got[-1], stage([query_weight])[0]))
         layer_theirs = each(add_rows, pair, mixed_theirs, got)
         layer_mine = trades(layer_theirs, 1)
     else:

time: 88 us -> 89.1 us (1.012)
  waiting for transfers between devices: 33.8 us -> 31.9 us
  starting transfers between devices: 19.1 us -> 20.7 us
  Pallas kernels: 29.4 us -> 30.9 us
    ppermute x3, waiting for transfers between devices: 3.93 us -> 1.51 us  [cross(): return lax.ppermute(value, 'req', pairs)]
    pallas_call x1 -> x2, Pallas kernels: 3.56 us -> 5.36 us  [extend_attention(): pl.pallas_call(functools.partial(chunk_kernel, blocks=2 * kv_local), out_...]
    ppermute x16, starting transfers between devices: 13.2 us -> 14.9 us  [trade(): return lax.ppermute(value, axis, [(i, i ^ bit) for i in range(size)])]
    pallas_call x2, Pallas kernels: 5.92 us -> 4.45 us  [finish_attention(): pl.pallas_call(functools.partial(finish_kernel, half=half, kv_local=kv_lo...]
    pallas_call x2 -> x3, Pallas kernels: 6.97 us -> 8.11 us  [stage(): pl.pallas_call(stage_kernel, out_shape=tuple((pltpu.VMEM(w.shape, w.dtype...]
  transfers between devices with their start and end apart: 19 -> 19, of which waited for: 15 -> 11; matrix products, arithmetic and copies ran while one was open for 2% -> 2% of each run, Pallas kernels for 27% -> 29%
where the time goes in v5:
time: 89.1 us; the launch traced here: 88.8 us
  waiting for transfers between devices  31.9 us (36%)
  Pallas kernels  30.9 us (35%)
  starting transfers between devices  20.7 us (23%)
  local copies, waits for them, and re-layouts  3.93 us (4%)
  between operations  0.9 us (1%)
    ppermute x16, waiting for transfers between devices, trade(): return lax.ppermute(value, axis, [(i, i ^ bit) for i in range(size)])  30.4 us
    ppermute x16, starting transfers between devices, trade(): return lax.ppermute(value, axis, [(i, i ^ bit) for i in range(size)])  14.9 us
    pallas_call x3, Pallas kernels, stage(): pl.pallas_call(stage_kernel, out_shape=tuple((pltpu.VMEM(w.shape, w.dtype...  8.11 us
    ppermute x3, starting transfers between devices, cross(): return lax.ppermute(value, 'req', pairs)  5.83 us
    pallas_call x2, Pallas kernels, extend_attention(): pl.pallas_call(functools.partial(chunk_kernel, blocks=2 * kv_local), out_...  5.36 us
    pallas_call x2, Pallas kernels, feed_forward(): pl.pallas_call(mlp_kernel, out_shape=pieces_of(count, depth, dtype), in_s...  5.11 us
    pallas_call x2, Pallas kernels, finish_attention(): pl.pallas_call(functools.partial(finish_kernel, half=half, kv_local=kv_lo...  4.45 us
    unnamed x17, local copies, waits for them, and re-layouts  3.92 us
  transfers between devices with their start and end apart: 19, of which 11 were waited for; matrix products, arithmetic and copies ran while one was open for 2% of the time, Pallas kernels for 29%

profile of v5, /device:TPU:0, one launch (start us, length us, event | category | flops | bytes accessed | tf_op | source)
XLA Modules:
  0.0 88.8 jit_solution(1698296376596762504)
XLA Ops:
  0.6 1.0 %copy-done.3 = bf16[32,16,320]{2,1,0:T(8,128)(2,1)S(1)} copy-done((bf16[32,16,320]{2,1,0:T(8,128)(2,1)S(1)}, bf16[32,16,320]{2,1,0:T(8,128)(2,1)}, u32[]{:S(2)}) %copy-start.3) | copy-done | bytes 327704
  1.6 0.9 pool_rows.1.refs_0_
  2.5 0.5 collective-permute-start.1
  3.0 2.6 %collective-permute-start = (bf16[512,384]{1,0:T(8,128)(2,1)S(1)}, bf16[512,384]{1,0:T(8,128)(2,1)S(1)}, u32[]{:S(2)}, u32[]{:S(2)}) collective-permute-start(bf16[512,384]{1,0:T(8,128)(2,1)S(1)} %pool_rows.1.refs_0_), channel_id=1, source_target_pairs={{0,8},{4,20},{8,0},{12,28},{16,24},{20,4},{24,16},{28,12},{1,9},{5... | collective-permute-start | bytes 1179656 | tf_op jit(solution)/shard_map/ppermute | solution.py:467
  5.6 1.5 %collective-permute-start.3 = (bf16[512,384]{1,0:T(8,128)(2,1)S(1)}, bf16[512,384]{1,0:T(8,128)(2,1)S(1)}, u32[]{:S(2)}, u32[]{:S(2)}) collective-permute-start(bf16[512,384]{1,0:T(8,128)(2,1)S(1)} %pool_rows.1.refs_0_), channel_id=1, source_target_pairs={{0,16},{4,12},{8,24},{12,4},{16,0},{20,28},{24,8},{28,20},{1,17},{... | collective-permute-start | bytes 1179656 | tf_op jit(solution)/shard_map/ppermute | solution.py:467
  7.1 1.0 %copy.24.keyval_ref = bf16[128,320]{1,0:T(8,128)(2,1)S(1)} copy(bf16[128,320]{0,1:T(8,128)(2,1)} %param.21) | data formatting | bytes 163840 | tf_op args[1]
  8.1 1.0 %copy-done.4 = bf16[16,32,320]{2,1,0:T(8,128)(2,1)S(1)} copy-done((bf16[16,32,320]{2,1,0:T(8,128)(2,1)S(1)}, bf16[16,32,320]{2,1,0:T(8,128)(2,1)}, u32[]{:S(2)}) %copy-start.4) | copy-done | bytes 327704
  9.1 0.9 %copy-done.5 = bf16[128,640]{1,0:T(8,128)(2,1)S(1)} copy-done((bf16[128,640]{1,0:T(8,128)(2,1)S(1)}, bf16[128,640]{1,0:T(8,128)(2,1)}, u32[]{:S(2)}) %copy-start.5) | copy-done | bytes 163864
  10.0 3.8 %attend_local.1 = (bf16[1024,256]{1,0:T(8,128)(2,1)S(1)}, f32[1024,256]{1,0:T(8,128)S(1)}) custom-call(s32[1,16]{1,0:T(1,128)} %count_hbm.1, s32[16]{0:T(128)} %mid_hbm.1, s32[16]{0:T(128)} %leaf_len_hbm.1, bf16[128,640]{1,0:T(8,128)(2,1)S(1)} %copy-done.5, bf16[128,320]{1,0:T(8,128)(2,1)S(1)} %copy.24.keyval_ref, bf16[16,32,320]{2,1,0:T(8,128)(2,1)S(1)} %copy-done.4, ...), custom_call_target="tpu_custom_call" | custom-call | flops 1744830464 | bytes 2097152 | tf_op jit(solution)/shard_map/attend_local/pallas_call | solution.py:232
  13.8 0.6 collective-permute-done.refs_2_
  14.4 0.9 collective-permute-done.3.refs_3_
  15.3 0.1 collective-permute-start.4
  15.4 0.4 collective-permute-start.5
  15.8 1.8 %collective-permute-start.2 = (bf16[512,384]{1,0:T(8,128)(2,1)S(1)}, bf16[512,384]{1,0:T(8,128)(2,1)S(1)}, u32[]{:S(2)}, u32[]{:S(2)}) collective-permute-start(bf16[512,384]{1,0:T(8,128)(2,1)S(1)} %collective-permute-done.refs_2_), channel_id=1, source_target_pairs={{0,16},{4,12},{8,24},{12,4},{16,0},{20,28},{24,8},{28,20},{1,17},{... | collective-permute-start | bytes 1179656 | tf_op jit(solution)/shard_map/ppermute | solution.py:467
  17.6 3.6 %attend_pages.2.refs_1_ = f32[1024,256]{1,0:T(8,128)S(1)} custom-call(bf16[1024,256]{1,0:T(8,128)(2,1)S(1)} %get-tuple-element.47.refs_0_, f32[1024,256]{1,0:T(8,128)S(1)} %get-tuple-element.49.refs_1_, bf16[512,384]{1,0:T(8,128)(2,1)S(1)} %collective-permute-done.refs_2_, bf16[512,384]{1,0:T(8,128)(2,1)S(1)} %collective-permute-done.3.refs_3_, ...), custom_call_target="tpu_custom_call" | custom-call | flops 2147483648 | bytes 2097152 | tf_op jit(solution)/shard_map/attend_pages/pallas_call | solution.py:271
  21.2 2.5 %stage.3.refs_5_ = bf16[896,2560]{1,0:T(8,128)(2,1)S(1)} custom-call(bf16[896,2560]{1,0:T(8,128)(2,1)} %refs_0_), custom_call_target="tpu_custom_call" | custom-call | bytes 4587520 | tf_op jit(solution)/shard_map/stage/pallas_call | solution.py:353
  23.7 0.2 collective-permute-start.6
  23.9 1.8 %attend_pages.3.refs_1_ = f32[1024,256]{1,0:T(8,128)S(1)} custom-call(bf16[1024,256]{1,0:T(8,128)(2,1)S(1)} %get-tuple-element.47.refs_0_, f32[1024,256]{1,0:T(8,128)S(1)} %attend_pages.2.refs_1_, bf16[512,384]{1,0:T(8,128)(2,1)S(1)} %collective-permute-done.2.refs_2_), custom_call_target="tpu_custom_call" | custom-call | flops 536870912 | bytes 2097152 | tf_op jit(solution)/shard_map/attend_pages/pallas_call | solution.py:271
  25.7 2.2 %attend_finish.2 = (bf16[64,640]{1,0:T(8,128)(2,1)S(1)}, bf16[64,1280]{1,0:T(8,128)(2,1)S(1)}, bf16[64,1280]{1,0:T(8,128)(2,1)S(1)}) custom-call(bf16[1024,256]{1,0:T(8,128)(2,1)S(1)} %get-tuple-element.47.refs_0_, f32[1024,256]{1,0:T(8,128)S(1)} %attend_pages.3.refs_1_, bf16[512,384]{1,0:T(8,128)(2,1)S(1)} %collective-permute-done.6.refs_2_, ...), custom_call_target="tpu_custom_call" | custom-call | flops 536870912 | bytes 1048576 | tf_op jit(solution)/shard_map/attend_finish/pallas_call | solution.py:322
  27.9 2.1 %collective-permute-start.8 = (bf16[64,1280]{1,0:T(8,128)(2,1)S(1)}, bf16[64,1280]{1,0:T(8,128)(2,1)S(1)}, u32[]{:S(2)}, u32[]{:S(2)}) collective-permute-start(bf16[64,1280]{1,0:T(8,128)(2,1)S(1)} %get-tuple-element.62), channel_id=1, source_target_pairs={{0,1},{1,0},{2,3},{3,2},{4,5},{5,4},{6,7},{7,6},{8,9},{9,8},{10,11... | collective-permute-start | bytes 491528 | tf_op jit(solution)/shard_map/ppermute | solution.py:461
  30.0 0.1 collective-permute-start.7
  30.1 2.3 %attend_finish.3 = (bf16[128,640]{1,0:T(8,128)(2,1)}, f32[64,1280]{1,0:T(8,128)S(1)}, f32[64,1280]{1,0:T(8,128)S(1)}, bf16[64,1280]{1,0:T(8,128)(2,1)S(1)}, bf16[64,1280]{1,0:T(8,128)(2,1)S(1)}) custom-call(bf16[1024,256]{1,0:T(8,128)(2,1)S(1)} %get-tuple-element.47.refs_0_, f32[1024,256]{1,0:T(8,128)S(1)} %attend_pages.3.refs_1_, ...), custom_call_target="tpu_custom_call" | custom-call | flops 536870912 | bytes 1048576 | tf_op jit(solution)/shard_map/attend_finish/pallas_call | solution.py:322
  32.4 2.6 %collective-permute-done.8 = bf16[64,1280]{1,0:T(8,128)(2,1)S(1)} collective-permute-done((bf16[64,1280]{1,0:T(8,128)(2,1)S(1)}, bf16[64,1280]{1,0:T(8,128)(2,1)S(1)}, u32[]{:S(2)}, u32[]{:S(2)}) %collective-permute-start.8) | collective-permute-done | bytes 163872 | tf_op jit(solution)/shard_map/ppermute | solution.py:461
  35.0 3.1 %collective-permute-start.11 = (bf16[64,1280]{1,0:T(8,128)(2,1)S(1)}, bf16[64,1280]{1,0:T(8,128)(2,1)S(1)}, u32[]{:S(2)}, u32[]{:S(2)}) collective-permute-start(bf16[64,1280]{1,0:T(8,128)(2,1)S(1)} %add_convert_fusion.7), channel_id=1, source_target_pairs={{0,2},{1,3},{2,0},{3,1},{4,6},{5,7},{6,4},{7,5},{8,10},{9,11},{10,... | collective-permute-start | bytes 491528 | tf_op jit(solution)/shard_map/ppermute | solution.py:461
  38.1 3.7 %stage.4 = (bf16[2560,896]{1,0:T(8,128)(2,1)S(1)}, bf16[2560,896]{1,0:T(8,128)(2,1)S(1)}) custom-call(bf16[2560,896]{1,0:T(8,128)(2,1)} %refs_0_.1, bf16[2560,896]{1,0:T(8,128)(2,1)} %refs_1_), custom_call_target="tpu_custom_call" | custom-call | bytes 9175040 | tf_op jit(solution)/shard_map/stage/pallas_call | solution.py:353
  41.9 0.1 collective-permute-start.9
  42.0 5.5 %collective-permute-done.11 = bf16[64,1280]{1,0:T(8,128)(2,1)S(1)} collective-permute-done((bf16[64,1280]{1,0:T(8,128)(2,1)S(1)}, bf16[64,1280]{1,0:T(8,128)(2,1)S(1)}, u32[]{:S(2)}, u32[]{:S(2)}) %collective-permute-start.11) | collective-permute-done | bytes 163872 | tf_op jit(solution)/shard_map/ppermute | solution.py:461
  47.6 2.1 %collective-permute-start.12 = (bf16[64,1280]{1,0:T(8,128)(2,1)S(1)}, bf16[64,1280]{1,0:T(8,128)(2,1)S(1)}, u32[]{:S(2)}, u32[]{:S(2)}) collective-permute-start(bf16[64,1280]{1,0:T(8,128)(2,1)S(1)} %add_convert_fusion.4.refs_1_), channel_id=1, source_target_pairs={{0,1},{1,0},{2,3},{3,2},{4,5},{5,4},{6,7},{7,6},{8,9},{9,8},{10,11... | collective-permute-start | bytes 491528 | tf_op jit(solution)/shard_map/ppermute | solution.py:461
  49.7 2.3 %collective-permute-done.9 = bf16[64,1280]{1,0:T(8,128)(2,1)S(1)} collective-permute-done((bf16[64,1280]{1,0:T(8,128)(2,1)S(1)}, bf16[64,1280]{1,0:T(8,128)(2,1)S(1)}, u32[]{:S(2)}, u32[]{:S(2)}) %collective-permute-start.9) | collective-permute-done | bytes 163872 | tf_op jit(solution)/shard_map/ppermute | solution.py:461
  51.9 0.1 add_convert_fusion.5.refs_0_
  52.0 0.5 collective-permute-start.10
  52.5 2.6 %feed_forward.3 = (bf16[64,1280]{1,0:T(8,128)(2,1)S(1)}, bf16[64,1280]{1,0:T(8,128)(2,1)S(1)}) custom-call(bf16[64,1280]{1,0:T(8,128)(2,1)S(1)} %add_convert_fusion.5.refs_0_, bf16[64,1280]{1,0:T(8,128)(2,1)S(1)} %add_convert_fusion.4.refs_1_, bf16[1,2560]{1,0:T(2,128)(2,1)S(1)} %reshape.16.refs_2_, bf16[2560,896]{1,0:T(8,128)(2,1)S(1)} %get-tuple-element.70.refs_3_, ...), custom_call_target="tpu_custom_call" | custom-call | flops 880803840 | bytes 13762560 | tf_op jit(solution)/shard_map/feed_forward/pallas_call | solution.py:382
  55.1 1.7 %collective-permute-start.14 = (bf16[64,1280]{1,0:T(8,128)(2,1)S(1)}, bf16[64,1280]{1,0:T(8,128)(2,1)S(1)}, u32[]{:S(2)}, u32[]{:S(2)}) collective-permute-start(bf16[64,1280]{1,0:T(8,128)(2,1)S(1)} %get-tuple-element.76), channel_id=1, source_target_pairs={{0,1},{1,0},{2,3},{3,2},{4,5},{5,4},{6,7},{7,6},{8,9},{9,8},{10,11... | collective-permute-start | bytes 491528 | tf_op jit(solution)/shard_map/ppermute | solution.py:461
  56.7 0.4 collective-permute-start.13
  57.2 2.0 %collective-permute-done.10.refs_0_ = bf16[64,1280]{1,0:T(8,128)(2,1)S(1)} collective-permute-done((bf16[64,1280]{1,0:T(8,128)(2,1)S(1)}, bf16[64,1280]{1,0:T(8,128)(2,1)S(1)}, u32[]{:S(2)}, u32[]{:S(2)}) %collective-permute-start.10) | collective-permute-done | bytes 163872 | tf_op jit(solution)/shard_map/ppermute | solution.py:461
  59.2 2.6 %feed_forward.2 = (f32[64,1280]{1,0:T(8,128)S(1)}, f32[64,1280]{1,0:T(8,128)S(1)}) custom-call(bf16[64,1280]{1,0:T(8,128)(2,1)S(1)} %collective-permute-done.10.refs_0_, bf16[64,1280]{1,0:T(8,128)(2,1)S(1)} %collective-permute-done.12.refs_1_, bf16[1,2560]{1,0:T(2,128)(2,1)S(1)} %reshape.16.refs_2_, bf16[2560,896]{1,0:T(8,128)(2,1)S(1)} %get-tuple-element.70.refs_3_, ...), custom_call_target="tpu_custom_call" | custom-call | flops 880803840 | bytes 13762560 | tf_op jit(solution)/shard_map/feed_forward/pallas_call | solution.py:382
  61.8 1.0 %collective-permute-done.14 = bf16[64,1280]{1,0:T(8,128)(2,1)S(1)} collective-permute-done((bf16[64,1280]{1,0:T(8,128)(2,1)S(1)}, bf16[64,1280]{1,0:T(8,128)(2,1)S(1)}, u32[]{:S(2)}, u32[]{:S(2)}) %collective-permute-start.14) | collective-permute-done | bytes 163872 | tf_op jit(solution)/shard_map/ppermute | solution.py:461
  62.8 2.9 %collective-permute-start.17 = (bf16[64,1280]{1,0:T(8,128)(2,1)S(1)}, bf16[64,1280]{1,0:T(8,128)(2,1)S(1)}, u32[]{:S(2)}, u32[]{:S(2)}) collective-permute-start(bf16[64,1280]{1,0:T(8,128)(2,1)S(1)} %add_convert_fusion.3), channel_id=1, source_target_pairs={{0,2},{1,3},{2,0},{3,1},{4,6},{5,7},{6,4},{7,5},{8,10},{9,11},{10,... | collective-permute-start | bytes 491528 | tf_op jit(solution)/shard_map/ppermute | solution.py:461
  65.7 1.9 %stage.5.refs_3_ = bf16[2560,640]{1,0:T(8,128)(2,1)S(1)} custom-call(bf16[2560,640]{1,0:T(8,128)(2,1)} %refs_0_.2), custom_call_target="tpu_custom_call" | custom-call | bytes 3276800 | tf_op jit(solution)/shard_map/stage/pallas_call | solution.py:353
  67.7 0.6 collective-permute-start.15
  68.2 9.0 %collective-permute-done.17 = bf16[64,1280]{1,0:T(8,128)(2,1)S(1)} collective-permute-done((bf16[64,1280]{1,0:T(8,128)(2,1)S(1)}, bf16[64,1280]{1,0:T(8,128)(2,1)S(1)}, u32[]{:S(2)}, u32[]{:S(2)}) %collective-permute-start.17) | collective-permute-done | bytes 163872 | tf_op jit(solution)/shard_map/ppermute | solution.py:461
  77.3 0.1 collective-permute-start.18
  77.4 2.5 %collective-permute-done.15 = bf16[64,1280]{1,0:T(8,128)(2,1)S(1)} collective-permute-done((bf16[64,1280]{1,0:T(8,128)(2,1)S(1)}, bf16[64,1280]{1,0:T(8,128)(2,1)S(1)}, u32[]{:S(2)}, u32[]{:S(2)}) %collective-permute-start.15) | collective-permute-done | bytes 163872 | tf_op jit(solution)/shard_map/ppermute | solution.py:461
  79.9 0.1 collective-permute-start.16
  80.0 1.2 %next_layer.2 = (bf16[64,640]{1,0:T(8,128)(2,1)S(1)}, bf16[320,64]{1,0:T(8,128)(2,1)S(1)}) custom-call(bf16[64,1280]{1,0:T(8,128)(2,1)S(1)} %add_convert_fusion.1.refs_0_.refs_7_, bf16[64,1280]{1,0:T(8,128)(2,1)S(1)} %add_convert_fusion.refs_1_.refs_8_, bf16[1,2560]{1,0:T(2,128)(2,1)S(1)} %reshape.17.refs_2_, bf16[2560,640]{1,0:T(8,128)(2,1)S(1)} %stage.5.refs_3_, ...), custom_call_target="tpu_custom_call" | custom-call | flops 314572800 | bytes 4915200 | tf_op jit(solution)/shard_map/next_layer/pallas_call | solution.py:444
  81.2 3.3 %collective-permute-done.18.refs_1_ = bf16[64,1280]{1,0:T(8,128)(2,1)S(1)} collective-permute-done((bf16[64,1280]{1,0:T(8,128)(2,1)S(1)}, bf16[64,1280]{1,0:T(8,128)(2,1)S(1)}, u32[]{:S(2)}, u32[]{:S(2)}) %collective-permute-start.18) | collective-permute-done | bytes 163872 | tf_op jit(solution)/shard_map/ppermute | solution.py:461
  84.5 2.3 %collective-permute-done.16.refs_0_ = bf16[64,1280]{1,0:T(8,128)(2,1)S(1)} collective-permute-done((bf16[64,1280]{1,0:T(8,128)(2,1)S(1)}, bf16[64,1280]{1,0:T(8,128)(2,1)S(1)}, u32[]{:S(2)}, u32[]{:S(2)}) %collective-permute-start.16) | collective-permute-done | bytes 163872 | tf_op jit(solution)/shard_map/ppermute | solution.py:461
  86.8 2.1 %next_layer.3 = (bf16[128,640]{1,0:T(8,128)(2,1)}, bf16[320,128]{1,0:T(8,128)(2,1)}, bf16[32,2560]{1,0:T(8,128)(2,1)}) custom-call(bf16[64,1280]{1,0:T(8,128)(2,1)S(1)} %collective-permute-done.16.refs_0_, bf16[64,1280]{1,0:T(8,128)(2,1)S(1)} %collective-permute-done.18.refs_1_, bf16[1,2560]{1,0:T(2,128)(2,1)S(1)} %reshape.17.refs_2_, ...), custom_call_target="tpu_custom_call" | custom-call | flops 314572800 | bytes 4915200 | tf_op jit(solution)/shard_map/next_layer/pallas_call | solution.py:444
  (30 shorter events, 0.4 us)
Async XLA Ops:
  0.6 1.0 %copy-start.3 = (bf16[32,16,320]{2,1,0:T(8,128)(2,1)S(1)}, bf16[32,16,320]{2,1,0:T(8,128)(2,1)}, u32[]{:S(2)}) copy-start(bf16[32,16,320]{2,1,0:T(8,128)(2,1)} %pool_ref.1) | copy-start | bytes 983044
  2.5 5.6 %collective-permute-start.1 = (bf16[512,384]{1,0:T(8,128)(2,1)S(1)}, bf16[512,384]{1,0:T(8,128)(2,1)S(1)}, u32[]{:S(2)}, u32[]{:S(2)}) collective-permute-start(bf16[512,384]{1,0:T(8,128)(2,1)S(1)} %pool_rows.1.refs_0_), channel_id=1, source_target_pairs={{0,4},{4,0},{8,12},{12,8},{16,20},{20,16},{24,28},{28,24},{1,5},{5... | collective-permute-start | bytes 1179656 | tf_op jit(solution)/shard_map/ppermute | solution.py:461
  3.0 11.4 %collective-permute-start = (bf16[512,384]{1,0:T(8,128)(2,1)S(1)}, bf16[512,384]{1,0:T(8,128)(2,1)S(1)}, u32[]{:S(2)}, u32[]{:S(2)}) collective-permute-start(bf16[512,384]{1,0:T(8,128)(2,1)S(1)} %pool_rows.1.refs_0_), channel_id=1, source_target_pairs={{0,8},{4,20},{8,0},{12,28},{16,24},{20,4},{24,16},{28,12},{1,9},{5... | collective-permute-start | bytes 1179656 | tf_op jit(solution)/shard_map/ppermute | solution.py:467
  5.6 9.7 %collective-permute-start.3 = (bf16[512,384]{1,0:T(8,128)(2,1)S(1)}, bf16[512,384]{1,0:T(8,128)(2,1)S(1)}, u32[]{:S(2)}, u32[]{:S(2)}) collective-permute-start(bf16[512,384]{1,0:T(8,128)(2,1)S(1)} %pool_rows.1.refs_0_), channel_id=1, source_target_pairs={{0,16},{4,12},{8,24},{12,4},{16,0},{20,28},{24,8},{28,20},{1,17},{... | collective-permute-start | bytes 1179656 | tf_op jit(solution)/shard_map/ppermute | solution.py:467
  8.1 1.0 %copy-start.4 = (bf16[16,32,320]{2,1,0:T(8,128)(2,1)S(1)}, bf16[16,32,320]{2,1,0:T(8,128)(2,1)}, u32[]{:S(2)}) copy-start(bf16[16,32,320]{2,1,0:T(8,128)(2,1)} %leaf_ref.1) | copy-start | bytes 983044
  9.1 0.9 %copy-start.5 = (bf16[128,640]{1,0:T(8,128)(2,1)S(1)}, bf16[128,640]{1,0:T(8,128)(2,1)}, u32[]{:S(2)}) copy-start(bf16[128,640]{1,0:T(8,128)(2,1)} %query_ref.1) | copy-start | bytes 491524
  15.3 2.3 %collective-permute-start.4 = (bf16[512,384]{1,0:T(8,128)(2,1)S(1)}, bf16[512,384]{1,0:T(8,128)(2,1)S(1)}, u32[]{:S(2)}, u32[]{:S(2)}) collective-permute-start(bf16[512,384]{1,0:T(8,128)(2,1)S(1)} %collective-permute-done.refs_2_), channel_id=1, source_target_pairs={{0,4},{4,0},{8,12},{12,8},{16,20},{20,16},{24,28},{28,24},{1,5},{5... | collective-permute-start | bytes 1179656 | tf_op jit(solution)/shard_map/ppermute | solution.py:461
  15.4 2.2 %collective-permute-start.5 = (bf16[512,384]{1,0:T(8,128)(2,1)S(1)}, bf16[512,384]{1,0:T(8,128)(2,1)S(1)}, u32[]{:S(2)}, u32[]{:S(2)}) collective-permute-start(bf16[512,384]{1,0:T(8,128)(2,1)S(1)} %collective-permute-done.3.refs_3_), channel_id=1, source_target_pairs={{0,4},{4,0},{8,12},{12,8},{16,20},{20,16},{24,28},{28,24},{1,5},{5... | collective-permute-start | bytes 1179656 | tf_op jit(solution)/shard_map/ppermute | solution.py:461
  15.8 7.8 %collective-permute-start.2 = (bf16[512,384]{1,0:T(8,128)(2,1)S(1)}, bf16[512,384]{1,0:T(8,128)(2,1)S(1)}, u32[]{:S(2)}, u32[]{:S(2)}) collective-permute-start(bf16[512,384]{1,0:T(8,128)(2,1)S(1)} %collective-permute-done.refs_2_), channel_id=1, source_target_pairs={{0,16},{4,12},{8,24},{12,4},{16,0},{20,28},{24,8},{28,20},{1,17},{... | collective-permute-start | bytes 1179656 | tf_op jit(solution)/shard_map/ppermute | solution.py:467
  21.2 4.5 %copy-start = (bf16[640,2560]{1,0:T(8,128)(2,1)S(1)}, bf16[640,2560]{1,0:T(8,128)(2,1)}, u32[]{:S(2)}) copy-start(bf16[640,2560]{1,0:T(8,128)(2,1)} %refs_3_.3) | copy-start | bytes 9830404
  23.6 6.3 %copy-start.6 = (bf16[2560]{0:T(1024)(128)(2,1)S(1)}, bf16[2560]{0:T(1024)(128)(2,1)}, u32[]{:S(2)}) copy-start(bf16[2560]{0:T(1024)(128)(2,1)} %param.33) | copy-start | bytes 15364
  23.7 6.4 %copy-start.2 = (bf16[128,2560]{1,0:T(8,128)(2,1)S(1)}, bf16[128,2560]{1,0:T(8,128)(2,1)}, u32[]{:S(2)}) copy-start(bf16[128,2560]{1,0:T(8,128)(2,1)} %refs_5_.1) | copy-start | bytes 1966084
  23.7 2.0 %collective-permute-start.6 = (bf16[512,384]{1,0:T(8,128)(2,1)S(1)}, bf16[512,384]{1,0:T(8,128)(2,1)S(1)}, u32[]{:S(2)}, u32[]{:S(2)}) collective-permute-start(bf16[512,384]{1,0:T(8,128)(2,1)S(1)} %collective-permute-done.2.refs_2_), channel_id=1, source_target_pairs={{0,4},{4,0},{8,12},{12,8},{16,20},{20,16},{24,28},{28,24},{1,5},{5... | collective-permute-start | bytes 1179656 | tf_op jit(solution)/shard_map/ppermute | solution.py:461
  27.9 7.1 %collective-permute-start.8 = (bf16[64,1280]{1,0:T(8,128)(2,1)S(1)}, bf16[64,1280]{1,0:T(8,128)(2,1)S(1)}, u32[]{:S(2)}, u32[]{:S(2)}) collective-permute-start(bf16[64,1280]{1,0:T(8,128)(2,1)S(1)} %get-tuple-element.62), channel_id=1, source_target_pairs={{0,1},{1,0},{2,3},{3,2},{4,5},{5,4},{6,7},{7,6},{8,9},{9,8},{10,11... | collective-permute-start | bytes 491528 | tf_op jit(solution)/shard_map/ppermute | solution.py:461
  30.0 11.9 %collective-permute-start.7 = (bf16[64,1280]{1,0:T(8,128)(2,1)S(1)}, bf16[64,1280]{1,0:T(8,128)(2,1)S(1)}, u32[]{:S(2)}, u32[]{:S(2)}) collective-permute-start(bf16[64,1280]{1,0:T(8,128)(2,1)S(1)} %get-tuple-element.60), channel_id=1, source_target_pairs={{0,1},{1,0},{2,3},{3,2},{4,5},{5,4},{6,7},{7,6},{8,9},{9,8},{10,11... | collective-permute-start | bytes 491528 | tf_op jit(solution)/shard_map/ppermute | solution.py:461
  35.0 12.5 %collective-permute-start.11 = (bf16[64,1280]{1,0:T(8,128)(2,1)S(1)}, bf16[64,1280]{1,0:T(8,128)(2,1)S(1)}, u32[]{:S(2)}, u32[]{:S(2)}) collective-permute-start(bf16[64,1280]{1,0:T(8,128)(2,1)S(1)} %add_convert_fusion.7), channel_id=1, source_target_pairs={{0,2},{1,3},{2,0},{3,1},{4,6},{5,7},{6,4},{7,5},{8,10},{9,11},{10,... | collective-permute-start | bytes 491528 | tf_op jit(solution)/shard_map/ppermute | solution.py:461
  41.9 10.0 %collective-permute-start.9 = (bf16[64,1280]{1,0:T(8,128)(2,1)S(1)}, bf16[64,1280]{1,0:T(8,128)(2,1)S(1)}, u32[]{:S(2)}, u32[]{:S(2)}) collective-permute-start(bf16[64,1280]{1,0:T(8,128)(2,1)S(1)} %add_convert_fusion.6), channel_id=1, source_target_pairs={{0,2},{1,3},{2,0},{3,1},{4,6},{5,7},{6,4},{7,5},{8,10},{9,11},{10,... | collective-permute-start | bytes 491528 | tf_op jit(solution)/shard_map/ppermute | solution.py:461
  47.6 9.6 %collective-permute-start.12 = (bf16[64,1280]{1,0:T(8,128)(2,1)S(1)}, bf16[64,1280]{1,0:T(8,128)(2,1)S(1)}, u32[]{:S(2)}, u32[]{:S(2)}) collective-permute-start(bf16[64,1280]{1,0:T(8,128)(2,1)S(1)} %add_convert_fusion.4.refs_1_), channel_id=1, source_target_pairs={{0,1},{1,0},{2,3},{3,2},{4,5},{5,4},{6,7},{7,6},{8,9},{9,8},{10,11... | collective-permute-start | bytes 491528 | tf_op jit(solution)/shard_map/ppermute | solution.py:461
  52.0 7.2 %collective-permute-start.10 = (bf16[64,1280]{1,0:T(8,128)(2,1)S(1)}, bf16[64,1280]{1,0:T(8,128)(2,1)S(1)}, u32[]{:S(2)}, u32[]{:S(2)}) collective-permute-start(bf16[64,1280]{1,0:T(8,128)(2,1)S(1)} %add_convert_fusion.5.refs_0_), channel_id=1, source_target_pairs={{0,1},{1,0},{2,3},{3,2},{4,5},{5,4},{6,7},{7,6},{8,9},{9,8},{10,11... | collective-permute-start | bytes 491528 | tf_op jit(solution)/shard_map/ppermute | solution.py:461
  55.1 7.6 %collective-permute-start.14 = (bf16[64,1280]{1,0:T(8,128)(2,1)S(1)}, bf16[64,1280]{1,0:T(8,128)(2,1)S(1)}, u32[]{:S(2)}, u32[]{:S(2)}) collective-permute-start(bf16[64,1280]{1,0:T(8,128)(2,1)S(1)} %get-tuple-element.76), channel_id=1, source_target_pairs={{0,1},{1,0},{2,3},{3,2},{4,5},{5,4},{6,7},{7,6},{8,9},{9,8},{10,11... | collective-permute-start | bytes 491528 | tf_op jit(solution)/shard_map/ppermute | solution.py:461
  56.7 10.9 %collective-permute-start.13 = (bf16[64,1280]{1,0:T(8,128)(2,1)S(1)}, bf16[64,1280]{1,0:T(8,128)(2,1)S(1)}, u32[]{:S(2)}, u32[]{:S(2)}) collective-permute-start(bf16[64,1280]{1,0:T(8,128)(2,1)S(1)} %get-tuple-element.74), channel_id=1, source_target_pairs={{0,1},{1,0},{2,3},{3,2},{4,5},{5,4},{6,7},{7,6},{8,9},{9,8},{10,11... | collective-permute-start | bytes 491528 | tf_op jit(solution)/shard_map/ppermute | solution.py:461
  62.7 17.3 %copy-start.7 = (bf16[2560]{0:T(1024)(128)(2,1)S(1)}, bf16[2560]{0:T(1024)(128)(2,1)}, u32[]{:S(2)}) copy-start(bf16[2560]{0:T(1024)(128)(2,1)} %param.37) | copy-start | bytes 15364
  62.7 17.3 %copy-start.1 = (bf16[2560,320]{0,1:T(8,128)(2,1)S(1)}, bf16[2560,320]{0,1:T(8,128)(2,1)}, u32[]{:S(2)}) copy-start(bf16[2560,320]{0,1:T(8,128)(2,1)} %param.39) | copy-start | bytes 4915204
  62.8 14.5 %collective-permute-start.17 = (bf16[64,1280]{1,0:T(8,128)(2,1)S(1)}, bf16[64,1280]{1,0:T(8,128)(2,1)S(1)}, u32[]{:S(2)}, u32[]{:S(2)}) collective-permute-start(bf16[64,1280]{1,0:T(8,128)(2,1)S(1)} %add_convert_fusion.3), channel_id=1, source_target_pairs={{0,2},{1,3},{2,0},{3,1},{4,6},{5,7},{6,4},{7,5},{8,10},{9,11},{10,... | collective-permute-start | bytes 491528 | tf_op jit(solution)/shard_map/ppermute | solution.py:461
  67.7 12.2 %collective-permute-start.15 = (bf16[64,1280]{1,0:T(8,128)(2,1)S(1)}, bf16[64,1280]{1,0:T(8,128)(2,1)S(1)}, u32[]{:S(2)}, u32[]{:S(2)}) collective-permute-start(bf16[64,1280]{1,0:T(8,128)(2,1)S(1)} %add_convert_fusion.2), channel_id=1, source_target_pairs={{0,2},{1,3},{2,0},{3,1},{4,6},{5,7},{6,4},{7,5},{8,10},{9,11},{10,... | collective-permute-start | bytes 491528 | tf_op jit(solution)/shard_map/ppermute | solution.py:461
  77.3 7.2 %collective-permute-start.18 = (bf16[64,1280]{1,0:T(8,128)(2,1)S(1)}, bf16[64,1280]{1,0:T(8,128)(2,1)S(1)}, u32[]{:S(2)}, u32[]{:S(2)}) collective-permute-start(bf16[64,1280]{1,0:T(8,128)(2,1)S(1)} %add_convert_fusion.refs_1_.refs_8_), channel_id=1, source_target_pairs={{0,1},{1,0},{2,3},{3,2},{4,5},{5,4},{6,7},{7,6},{8,9},{9,8},{10,11... | collective-permute-start | bytes 491528 | tf_op jit(solution)/shard_map/ppermute | solution.py:461
  79.9 6.9 %collective-permute-start.16 = (bf16[64,1280]{1,0:T(8,128)(2,1)S(1)}, bf16[64,1280]{1,0:T(8,128)(2,1)S(1)}, u32[]{:S(2)}, u32[]{:S(2)}) collective-permute-start(bf16[64,1280]{1,0:T(8,128)(2,1)S(1)} %add_convert_fusion.1.refs_0_.refs_7_), channel_id=1, source_target_pairs={{0,1},{1,0},{2,3},{3,2},{4,5},{5,4},{6,7},{7,6},{8,9},{9,8},{10,11... | collective-permute-start | bytes 491528 | tf_op jit(solution)/shard_map/ppermute | solution.py:461

commit v6 on v5

--- a/solution.py
+++ b/solution.py
@@ -91,10 +91,18 @@
 
 
 def prep_kernel(
-    node_hbm, rank_hbm, length_hbm, root_hbm, pool_ref, out_ref, node_ref, rank_ref, length_ref, root_ref, sems
+    node_hbm, rank_hbm, length_hbm, root_hbm, pool_hbm, out_ref,
+    node_ref, rank_ref, length_ref, root_ref, pool_ref, sems,
 ):
-    pairs = ((node_hbm, node_ref), (rank_hbm, rank_ref), (length_hbm, length_ref), (root_hbm, root_ref))
-    for copy in fetch(pairs, sems):
+    pairs = (
+        (pool_hbm, pool_ref),
+        (node_hbm, node_ref),
+        (rank_hbm, rank_ref),
+        (length_hbm, length_ref),
+        (root_hbm, root_ref),
+    )
+    pool_copy, *copies = fetch(pairs, sems)
+    for copy in copies:
         copy.wait()
     pages, size, width = pool_ref.shape
     free = out_ref.shape[1] - width
@@ -109,8 +117,9 @@
         left = length_ref[jnp.maximum(node, 0)] - size * rank_ref[p]
         seen = ((root == node) | (lane + ROOTS == node)) & (slot < left)
         rows = slice(p * size, (p + 1) * size)
-        out_ref[rows, :width] = pool_ref[p]
         out_ref[rows, width:] = jnp.where(seen, 0.0, hidden).astype(bf16)
+    pool_copy.wait()
+    out_ref[:, :width] = pool_ref[...].reshape(pages * size, width)
 
 
 def prepare(page_node, page_rank, node_length, mid_root, prefix_pool):
@@ -119,12 +128,13 @@
     return pl.pallas_call(
         prep_kernel,
         out_shape=jax.ShapeDtypeStruct((pages * size, padded(width + MIDS)), bf16),
-        in_specs=[HBM] * 4 + [VMEM],
+        in_specs=[HBM] * 5,
         out_specs=VMEM,
-        scratch_shapes=[pltpu.SMEM(t.shape, i32) for t in tables] + [pltpu.SemaphoreType.DMA((4,))],
+        scratch_shapes=[pltpu.SMEM(t.shape, i32) for t in tables]
+        + [pltpu.VMEM(prefix_pool.shape, bf16), pltpu.SemaphoreType.DMA((5,))],
         compiler_params=PARAMS,
         name="pool_rows",
-    )(*in_hbm(tables), prefix_pool)
+    )(*in_hbm((*tables, prefix_pool)))
 
 
 def half_start(rows, half):
@@ -279,6 +289,13 @@
     )(aug, state, *pools)
 
 
+def project(out_refs, rows, weight_ref, places):
+    for out_ref, k in zip(out_refs, places):
+        weight = weight_ref[:, piece(weight_ref.shape[1], k)]
+        result = jnp.dot(rows, weight, preferred_element_type=f32)
+        out_ref[...] = result.astype(out_ref.dtype)
+
+
 def finish_kernel(*refs, half, kv_local, chunks, width):
     aug_ref, state_ref = refs[:2]
     pool_refs = refs[2 : 2 + chunks]
@@ -286,7 +303,10 @@
     part = aug_ref.shape[0] // (2 * width // HD)
     rest = refs[3 + chunks :]
     att_ref, *proj_refs, mine_ref = rest[2 * half :]
-    proj_refs, res_refs = proj_refs[:PIECES], proj_refs[PIECES:]
+    if half:
+        send_refs, proj_refs = proj_refs[: PIECES - 1], proj_refs[PIECES - 1 :]
+        proj_refs, res_refs = proj_refs[:PIECES], proj_refs[PIECES:]
+        project(send_refs, rest[0][...], weight_ref, range(1, PIECES))
     group = width // (kv_local * HD)
     size = group * part
     for c in range(kv_local):
@@ -309,27 +329,26 @@
             res_ref[...] = rest[1][pl.ds(mine, part), piece(rest[1].shape[1], k)]
     else:
         att_ref[...] = mine_ref[...]
-    for k, proj_ref in enumerate(proj_refs):
-        weight = weight_ref[:, piece(weight_ref.shape[1], k)]
-        proj = jnp.dot(mine_ref[...], weight, preferred_element_type=f32)
-        proj_ref[...] = proj.astype(proj_ref.dtype)
+    project(proj_refs, mine_ref[...], weight_ref, range(PIECES if half else 1))
 
 
 def finish_attention(aug, state, pools, out_weight, half, kv_local, rows, other):
     width = out_weight.shape[0]
     part = rows // 2
     keys = sum(item.shape[0] for item in pools)
+    depth = out_weight.shape[1]
+    sent = pieces_of(part, depth, bf16)
+    if half:
+        shapes = (*sent[:-1], *pieces_of(part, depth, f32), *pieces_of(part, depth, bf16))
+    else:
+        shapes = sent[-1:]
     return pl.pallas_call(
         functools.partial(
             finish_kernel, half=half, kv_local=kv_local, chunks=len(pools), width=width
         ),
-        out_shape=(
-            jax.ShapeDtypeStruct((rows if half else part, width), bf16),
-            *pieces_of(part, out_weight.shape[1], f32 if half else bf16),
-            *(pieces_of(part, out_weight.shape[1], bf16) if half else ()),
-        ),
+        out_shape=(jax.ShapeDtypeStruct((rows if half else part, width), bf16), *shapes),
         in_specs=[VMEM] * (3 + len(pools) + len(other)),
-        out_specs=(VMEM,) * (1 + PIECES + half * PIECES),
+        out_specs=(VMEM,) * (1 + len(shapes)),
         scratch_shapes=[pltpu.VMEM((part, width), bf16)],
         compiler_params=PARAMS,
         cost_estimate=attention_cost(aug.shape[0] // 2, keys + 512),
@@ -364,32 +383,41 @@
     )(*in_hbm(weights))
 
 
-def mlp_kernel(*refs):
+def mlp_kernel(*refs, second):
     row_refs, (gain_ref, gate_ref, up_ref, down_ref) = refs[:PIECES], refs[PIECES : PIECES + 4]
+    refs = refs[PIECES + 4 :]
+    if second:
+        project(refs[1:PIECES], refs[0][...], down_ref, range(PIECES - 1))
     normed = normalized(joined(row_refs), gain_ref[...])
     gate = jnp.dot(normed, gate_ref[...], preferred_element_type=f32)
     upward = jnp.dot(normed, up_ref[...], preferred_element_type=f32)
     hidden = (jax.nn.silu(gate) * upward).astype(bf16)
-    for k, out_ref in enumerate(refs[PIECES + 4 :]):
-        weight = down_ref[:, piece(down_ref.shape[1], k)]
-        result = jnp.dot(hidden, weight, preferred_element_type=f32)
-        out_ref[...] = result.astype(out_ref.dtype)
-
-
-def feed_forward(rows, gain, gate_weight, up_weight, down_weight, dtype):
+    if second:
+        project(refs[PIECES:], hidden, down_ref, range(PIECES))
+    else:
+        refs[0][...] = hidden
+        project(refs[1:], hidden, down_ref, [PIECES - 1])
+
+
+def feed_forward(rows, gain, gate_weight, up_weight, down_weight, other=()):
     count = rows[0].shape[0]
     depth, width = gate_weight.shape
+    sent = pieces_of(count, depth, bf16)
+    if other:
+        shapes = (*sent[:-1], *pieces_of(count, depth, f32))
+    else:
+        shapes = (jax.ShapeDtypeStruct((count, width), bf16), sent[-1])
     return pl.pallas_call(
-        mlp_kernel,
-        out_shape=pieces_of(count, depth, dtype),
-        in_specs=[VMEM] * (PIECES + 4),
-        out_specs=(VMEM,) * PIECES,
+        functools.partial(mlp_kernel, second=len(other) > 0),
+        out_shape=shapes,
+        in_specs=[VMEM] * (PIECES + 4 + len(other)),
+        out_specs=(VMEM,) * len(shapes),
         compiler_params=PARAMS,
         cost_estimate=pl.CostEstimate(
             flops=6 * count * depth * width, bytes_accessed=6 * depth * width, transcendentals=0
         ),
         name="feed_forward",
-    )(*rows, gain.reshape(1, depth), *in_vmem((gate_weight, up_weight, down_weight)))
+    )(*rows, gain.reshape(1, depth), *in_vmem((gate_weight, up_weight, down_weight)), *other)
 
 
 def next_kernel(*refs, half):
@@ -477,6 +505,12 @@
 
 def add_pair(mine, got):
     return (mine + wide(got)).astype(bf16)
+
+
+def pairs_in_turn(mine, got, weights):
+    last = add_pair(mine[-1], got[-1])
+    _, rest, weights = lax.optimization_barrier((last, got[:-1], weights))
+    return [*each(add_pair, mine[:-1], rest), last], weights
 
 
 def add_rows(pair, rows, got):
@@ -548,29 +582,31 @@
     attention, *mine_proj = finish_attention(
         aug, state, pools, out_weight, 1, kv_local, rows, (theirs_att, residual_in)
     )
-    mine_proj, res_mine = mine_proj[:PIECES], mine_proj[PIECES:]
+    theirs_proj = theirs_proj + mine_proj[: PIECES - 1]
+    mine_proj, res_mine = mine_proj[PIECES - 1 : -PIECES], mine_proj[-PIECES:]
 
     mine = half_start(rows, 1)
     theirs = half_start(rows, 0)
     depth = residual_in.shape[1]
     if lax.axis_size("tp") == 4:
         got = trades(theirs_proj, 1)
-        last = add_pair(mine_proj[-1], got[-1])
-        last, gate_weight, up_weight = lax.optimization_barrier((last, gate_weight, up_weight))
-        staged = stage([gate_weight, up_weight])
-        got[:-1], gate_weight, up_weight = lax.optimization_barrier((got[:-1], *staged))
-        mlp = (gate_weight, up_weight, down_weight)
-        pair = [*each(add_pair, mine_proj[:-1], got[:-1]), last]
+        pair, (gate_weight, up_weight) = pairs_in_turn(
+            mine_proj[::-1], got[::-1], (gate_weight, up_weight)
+        )
+        pair = pair[::-1]
         got = trades(pair, 2)
+        got[-1], *staged = lax.optimization_barrier((got[-1], *stage([gate_weight, up_weight])))
+        mlp = (*staged, down_weight)
         mixed_mine = each(add_rows, pair, res_mine, got)
         mixed_theirs = trades(mixed_mine, 1)
-        got = trades(feed_forward(mixed_mine, norm_gain, *mlp, bf16), 1)
-        mlp_theirs = feed_forward(mixed_theirs, norm_gain, *mlp, f32)
-        last = add_pair(mlp_theirs[-1], got[-1])
-        last, query_weight = lax.optimization_barrier((last, query_weight))
-        got[:-1], query_weight = lax.optimization_barrier((got[:-1], *stage([query_weight])))
-        pair = [*each(add_pair, mlp_theirs[:-1], got[:-1]), last]
+        hidden, last = feed_forward(mixed_mine, norm_gain, *mlp)
+        last = trade(last, "tp", 1)
+        result = feed_forward(mixed_theirs, norm_gain, *mlp, [hidden])
+        got = [*trades(result[: PIECES - 1], 1), last]
+        mlp_theirs = result[PIECES - 1 :]
+        pair, (query_weight,) = pairs_in_turn(mlp_theirs, got, (query_weight,))
         got = trades(pair, 2)
+        got[-1], query_weight = lax.optimization_barrier((got[-1], *stage([query_weight])))
         layer_theirs = each(add_rows, pair, mixed_theirs, got)
         layer_mine = trades(layer_theirs, 1)
     else:
@@ -585,9 +621,16 @@
         mine_proj = jnp.concatenate(mine_proj, axis=1)
         total = lax.psum(in_order(theirs_proj, mine_proj), "tp")
         mixed = (wide(in_order(res_theirs, res_mine)) + total).astype(bf16)
-        mixed_pieces = [mixed[:, piece(depth, k)] for k in range(PIECES)]
-        mlp = feed_forward(mixed_pieces, norm_gain, gate_weight, up_weight, down_weight, f32)
-        mlp = lax.psum(jnp.concatenate(mlp, axis=1), "tp")
+        mixed_halves = [
+            [mixed[h * part : (h + 1) * part, piece(depth, k)] for k in range(PIECES)]
+            for h in range(2)
+        ]
+        mlp_weights = (gate_weight, up_weight, down_weight)
+        hidden, last = feed_forward(mixed_halves[0], norm_gain, *mlp_weights)
+        result = feed_forward(mixed_halves[1], norm_gain, *mlp_weights, [hidden])
+        halves = [[*result[: PIECES - 1], last], result[PIECES - 1 :]]
+        mlp = [jnp.concatenate([wide(item) for item in half], axis=1) for half in halves]
+        mlp = lax.psum(jnp.concatenate(mlp, axis=0), "tp")
         layer = (wide(mixed) + mlp).astype(bf16)
         layer = [layer[:, piece(depth, k)] for k in range(PIECES)]
         layer_mine = [lax.dynamic_slice_in_dim(item, mine, part, 0) for item in layer]

time: 89.1 us -> 87.3 us (0.980)
  waiting for transfers between devices: 31.9 us -> 30.2 us
  local copies, waits for them, and re-layouts: 3.93 us -> 2.95 us
  starting transfers between devices: 20.7 us -> 21.6 us
    ppermute x16, waiting for transfers between devices: 30.4 us -> 28.7 us  [trade(): return lax.ppermute(value, axis, [(i, i ^ bit) for i in range(size)])]
    unnamed x17 -> x15, local copies, waits for them, and re-layouts: 3.92 us -> 2.93 us
    ppermute x16, starting transfers between devices: 14.9 us -> 15.8 us  [trade(): return lax.ppermute(value, axis, [(i, i ^ bit) for i in range(size)])]
  transfers between devices with their start and end apart: 19 -> 19, of which waited for: 11 -> 13; matrix products, arithmetic and copies ran while one was open for 2% -> 2% of each run, Pallas kernels for 29% -> 29%
where the time goes in v6:
time: 87.3 us; the launch traced here: 87 us
  Pallas kernels  30.9 us (35%)
  waiting for transfers between devices  30.2 us (35%)
  starting transfers between devices  21.6 us (25%)
  local copies, waits for them, and re-layouts  2.95 us (3%)
  between operations  0.88 us (1%)
    ppermute x16, waiting for transfers between devices, trade(): return lax.ppermute(value, axis, [(i, i ^ bit) for i in range(size)])  28.7 us
    ppermute x16, starting transfers between devices, trade(): return lax.ppermute(value, axis, [(i, i ^ bit) for i in range(size)])  15.8 us
    pallas_call x3, Pallas kernels, stage(): pl.pallas_call(stage_kernel, out_shape=tuple((pltpu.VMEM(w.shape, w.dtype...  8.11 us
    ppermute x3, starting transfers between devices, cross(): return lax.ppermute(value, 'req', pairs)  5.83 us
    pallas_call x2, Pallas kernels, extend_attention(): pl.pallas_call(functools.partial(chunk_kernel, blocks=2 * kv_local), out_...  5.36 us
    pallas_call x2, Pallas kernels, feed_forward(): pl.pallas_call(functools.partial(mlp_kernel, second=len(other) > 0), out_...  4.76 us
    pallas_call x2, Pallas kernels, finish_attention(): pl.pallas_call(functools.partial(finish_kernel, half=half, kv_local=kv_lo...  4.58 us
    pallas_call x1, Pallas kernels, start_attention(): pl.pallas_call(functools.partial(local_kernel, chunks=len(pools)), out_sh...  3.77 us
  transfers between devices with their start and end apart: 19, of which 13 were waited for; matrix products, arithmetic and copies ran while one was open for 2% of the time, Pallas kernels for 29%

profile of v6, /device:TPU:0, one launch (start us, length us, event | category | flops | bytes accessed | tf_op | source)
XLA Modules:
  0.0 87.0 jit_solution(8497647022123870650)
XLA Ops:
  0.6 1.1 %pool_rows.1.refs_0_ = bf16[512,384]{1,0:T(8,128)(2,1)S(1)} custom-call(s32[32]{0:T(128)} %node_hbm.1, s32[32]{0:T(128)} %rank_hbm.1, s32[8]{0:T(128)} %length_hbm.1, s32[6]{0:T(128)} %root_hbm.1, bf16[32,16,320]{2,1,0:T(8,128)(2,1)} %pool_hbm.1), custom_call_target="tpu_custom_call" | custom-call | tf_op jit(solution)/shard_map/pool_rows/pallas_call | solution.py:128
  1.7 0.5 collective-permute-start.1
  2.2 2.6 %collective-permute-start = (bf16[512,384]{1,0:T(8,128)(2,1)S(1)}, bf16[512,384]{1,0:T(8,128)(2,1)S(1)}, u32[]{:S(2)}, u32[]{:S(2)}) collective-permute-start(bf16[512,384]{1,0:T(8,128)(2,1)S(1)} %pool_rows.1.refs_0_), channel_id=1, source_target_pairs={{0,8},{4,20},{8,0},{12,28},{16,24},{20,4},{24,16},{28,12},{1,9},{5... | collective-permute-start | bytes 1179656 | tf_op jit(solution)/shard_map/ppermute | solution.py:495
  4.8 1.5 %collective-permute-start.3 = (bf16[512,384]{1,0:T(8,128)(2,1)S(1)}, bf16[512,384]{1,0:T(8,128)(2,1)S(1)}, u32[]{:S(2)}, u32[]{:S(2)}) collective-permute-start(bf16[512,384]{1,0:T(8,128)(2,1)S(1)} %pool_rows.1.refs_0_), channel_id=1, source_target_pairs={{0,16},{4,12},{8,24},{12,4},{16,0},{20,28},{24,8},{28,20},{1,17},{... | collective-permute-start | bytes 1179656 | tf_op jit(solution)/shard_map/ppermute | solution.py:495
  6.3 1.0 %copy.24.keyval_ref = bf16[128,320]{1,0:T(8,128)(2,1)S(1)} copy(bf16[128,320]{0,1:T(8,128)(2,1)} %param.21) | data formatting | bytes 163840 | tf_op args[1]
  7.3 1.0 %copy-done.3 = bf16[16,32,320]{2,1,0:T(8,128)(2,1)S(1)} copy-done((bf16[16,32,320]{2,1,0:T(8,128)(2,1)S(1)}, bf16[16,32,320]{2,1,0:T(8,128)(2,1)}, u32[]{:S(2)}) %copy-start.3) | copy-done | bytes 327704
  8.3 0.9 %copy-done.4 = bf16[128,640]{1,0:T(8,128)(2,1)S(1)} copy-done((bf16[128,640]{1,0:T(8,128)(2,1)S(1)}, bf16[128,640]{1,0:T(8,128)(2,1)}, u32[]{:S(2)}) %copy-start.4) | copy-done | bytes 163864
  9.2 3.8 %attend_local.1 = (bf16[1024,256]{1,0:T(8,128)(2,1)S(1)}, f32[1024,256]{1,0:T(8,128)S(1)}) custom-call(s32[1,16]{1,0:T(1,128)} %count_hbm.1, s32[16]{0:T(128)} %mid_hbm.1, s32[16]{0:T(128)} %leaf_len_hbm.1, bf16[128,640]{1,0:T(8,128)(2,1)S(1)} %copy-done.4, bf16[128,320]{1,0:T(8,128)(2,1)S(1)} %copy.24.keyval_ref, bf16[16,32,320]{2,1,0:T(8,128)(2,1)S(1)} %copy-done.3, ...), custom_call_target="tpu_custom_call" | custom-call | flops 1744830464 | bytes 2097152 | tf_op jit(solution)/shard_map/attend_local/pallas_call | solution.py:242
  13.0 0.6 collective-permute-done.refs_2_
  13.6 0.9 %collective-permute-done.3.refs_3_ = bf16[512,384]{1,0:T(8,128)(2,1)S(1)} collective-permute-done((bf16[512,384]{1,0:T(8,128)(2,1)S(1)}, bf16[512,384]{1,0:T(8,128)(2,1)S(1)}, u32[]{:S(2)}, u32[]{:S(2)}) %collective-permute-start.3) | collective-permute-done | bytes 393248 | tf_op jit(solution)/shard_map/ppermute | solution.py:495
  14.5 0.1 collective-permute-start.4
  14.7 0.4 collective-permute-start.5
  15.0 1.8 %collective-permute-start.2 = (bf16[512,384]{1,0:T(8,128)(2,1)S(1)}, bf16[512,384]{1,0:T(8,128)(2,1)S(1)}, u32[]{:S(2)}, u32[]{:S(2)}) collective-permute-start(bf16[512,384]{1,0:T(8,128)(2,1)S(1)} %collective-permute-done.refs_2_), channel_id=1, source_target_pairs={{0,16},{4,12},{8,24},{12,4},{16,0},{20,28},{24,8},{28,20},{1,17},{... | collective-permute-start | bytes 1179656 | tf_op jit(solution)/shard_map/ppermute | solution.py:495
  16.8 3.6 %attend_pages.2.refs_1_ = f32[1024,256]{1,0:T(8,128)S(1)} custom-call(bf16[1024,256]{1,0:T(8,128)(2,1)S(1)} %get-tuple-element.48.refs_0_, f32[1024,256]{1,0:T(8,128)S(1)} %get-tuple-element.50.refs_1_, bf16[512,384]{1,0:T(8,128)(2,1)S(1)} %collective-permute-done.refs_2_, bf16[512,384]{1,0:T(8,128)(2,1)S(1)} %collective-permute-done.3.refs_3_, ...), custom_call_target="tpu_custom_call" | custom-call | flops 2147483648 | bytes 2097152 | tf_op jit(solution)/shard_map/attend_pages/pallas_call | solution.py:281
  20.4 2.5 %stage.3.refs_5_ = bf16[896,2560]{1,0:T(8,128)(2,1)S(1)} custom-call(bf16[896,2560]{1,0:T(8,128)(2,1)} %refs_0_), custom_call_target="tpu_custom_call" | custom-call | bytes 4587520 | tf_op jit(solution)/shard_map/stage/pallas_call | solution.py:372
  22.9 0.2 collective-permute-start.6
  23.1 1.8 %attend_pages.3.refs_1_ = f32[1024,256]{1,0:T(8,128)S(1)} custom-call(bf16[1024,256]{1,0:T(8,128)(2,1)S(1)} %get-tuple-element.48.refs_0_, f32[1024,256]{1,0:T(8,128)S(1)} %attend_pages.2.refs_1_, bf16[512,384]{1,0:T(8,128)(2,1)S(1)} %collective-permute-done.2.refs_2_), custom_call_target="tpu_custom_call" | custom-call | flops 536870912 | bytes 2097152 | tf_op jit(solution)/shard_map/attend_pages/pallas_call | solution.py:281
  24.9 2.1 %attend_finish.2 = (bf16[64,640]{1,0:T(8,128)(2,1)S(1)}, bf16[64,1280]{1,0:T(8,128)(2,1)S(1)}) custom-call(bf16[1024,256]{1,0:T(8,128)(2,1)S(1)} %get-tuple-element.48.refs_0_, f32[1024,256]{1,0:T(8,128)S(1)} %attend_pages.3.refs_1_, bf16[512,384]{1,0:T(8,128)(2,1)S(1)} %collective-permute-done.6.refs_2_, bf16[640,2560]{1,0:T(8,128)(2,1)S(1)} %copy-done), custom_call_target="tpu_custom_call" | custom-call | flops 536870912 | bytes 1048576 | tf_op jit(solution)/shard_map/attend_finish/pallas_call | solution.py:345
  27.0 2.1 %collective-permute-start.7 = (bf16[64,1280]{1,0:T(8,128)(2,1)S(1)}, bf16[64,1280]{1,0:T(8,128)(2,1)S(1)}, u32[]{:S(2)}, u32[]{:S(2)}) collective-permute-start(bf16[64,1280]{1,0:T(8,128)(2,1)S(1)} %get-tuple-element.61), channel_id=1, source_target_pairs={{0,1},{1,0},{2,3},{3,2},{4,5},{5,4},{6,7},{7,6},{8,9},{9,8},{10,11... | collective-permute-start | bytes 491528 | tf_op jit(solution)/shard_map/ppermute | solution.py:489
  29.2 2.5 %attend_finish.3 = (bf16[128,640]{1,0:T(8,128)(2,1)}, bf16[64,1280]{1,0:T(8,128)(2,1)S(1)}, f32[64,1280]{1,0:T(8,128)S(1)}, f32[64,1280]{1,0:T(8,128)S(1)}, bf16...) custom-call(bf16[1024,256]{1,0:T(8,128)(2,1)S(1)} %get-tuple-element.48.refs_0_, ...), custom_call_target="tpu_custom_call" | custom-call | flops 536870912 | bytes 1048576 | tf_op jit(solution)/shard_map/attend_finish/pallas_call | solution.py:345
  31.6 0.1 collective-permute-start.10
  31.7 2.0 %collective-permute-done.7 = bf16[64,1280]{1,0:T(8,128)(2,1)S(1)} collective-permute-done((bf16[64,1280]{1,0:T(8,128)(2,1)S(1)}, bf16[64,1280]{1,0:T(8,128)(2,1)S(1)}, u32[]{:S(2)}, u32[]{:S(2)}) %collective-permute-start.7) | collective-permute-done | bytes 163872 | tf_op jit(solution)/shard_map/ppermute | solution.py:489
  33.7 2.8 %collective-permute-start.8 = (bf16[64,1280]{1,0:T(8,128)(2,1)S(1)}, bf16[64,1280]{1,0:T(8,128)(2,1)S(1)}, u32[]{:S(2)}, u32[]{:S(2)}) collective-permute-start(bf16[64,1280]{1,0:T(8,128)(2,1)S(1)} %add_convert_fusion.7), channel_id=1, source_target_pairs={{0,2},{1,3},{2,0},{3,1},{4,6},{5,7},{6,4},{7,5},{8,10},{9,11},{10,... | collective-permute-start | bytes 491528 | tf_op jit(solution)/shard_map/ppermute | solution.py:489
  36.5 3.6 %collective-permute-done.10 = bf16[64,1280]{1,0:T(8,128)(2,1)S(1)} collective-permute-done((bf16[64,1280]{1,0:T(8,128)(2,1)S(1)}, bf16[64,1280]{1,0:T(8,128)(2,1)S(1)}, u32[]{:S(2)}, u32[]{:S(2)}) %collective-permute-start.10) | collective-permute-done | bytes 163872 | tf_op jit(solution)/shard_map/ppermute | solution.py:489
  40.1 1.3 %collective-permute-start.11 = (bf16[64,1280]{1,0:T(8,128)(2,1)S(1)}, bf16[64,1280]{1,0:T(8,128)(2,1)S(1)}, u32[]{:S(2)}, u32[]{:S(2)}) collective-permute-start(bf16[64,1280]{1,0:T(8,128)(2,1)S(1)} %add_convert_fusion.5), channel_id=1, source_target_pairs={{0,2},{1,3},{2,0},{3,1},{4,6},{5,7},{6,4},{7,5},{8,10},{9,11},{10,... | collective-permute-start | bytes 491528 | tf_op jit(solution)/shard_map/ppermute | solution.py:489
  41.5 3.7 %stage.4 = (bf16[2560,896]{1,0:T(8,128)(2,1)S(1)}, bf16[2560,896]{1,0:T(8,128)(2,1)S(1)}) custom-call(bf16[2560,896]{1,0:T(8,128)(2,1)} %refs_0_.1, bf16[2560,896]{1,0:T(8,128)(2,1)} %refs_1_), custom_call_target="tpu_custom_call" | custom-call | bytes 9175040 | tf_op jit(solution)/shard_map/stage/pallas_call | solution.py:372
  45.2 3.2 %collective-permute-done.8 = bf16[64,1280]{1,0:T(8,128)(2,1)S(1)} collective-permute-done((bf16[64,1280]{1,0:T(8,128)(2,1)S(1)}, bf16[64,1280]{1,0:T(8,128)(2,1)S(1)}, u32[]{:S(2)}, u32[]{:S(2)}) %collective-permute-start.8) | collective-permute-done | bytes 163872 | tf_op jit(solution)/shard_map/ppermute | solution.py:489
  48.4 0.3 collective-permute-start.9
  48.7 2.4 %collective-permute-done.11 = bf16[64,1280]{1,0:T(8,128)(2,1)S(1)} collective-permute-done((bf16[64,1280]{1,0:T(8,128)(2,1)S(1)}, bf16[64,1280]{1,0:T(8,128)(2,1)S(1)}, u32[]{:S(2)}, u32[]{:S(2)}) %collective-permute-start.11) | collective-permute-done | bytes 163872 | tf_op jit(solution)/shard_map/ppermute | solution.py:489
  51.1 0.5 collective-permute-start.12
  51.7 2.3 %feed_forward.2 = (bf16[64,896]{1,0:T(8,128)(2,1)S(1)}, bf16[64,1280]{1,0:T(8,128)(2,1)S(1)}) custom-call(bf16[64,1280]{1,0:T(8,128)(2,1)S(1)} %add_convert_fusion.6.refs_0_, bf16[64,1280]{1,0:T(8,128)(2,1)S(1)} %add_convert_fusion.4.refs_1_, bf16[1,2560]{1,0:T(2,128)(2,1)S(1)} %reshape.16.refs_2_, bf16[2560,896]{1,0:T(8,128)(2,1)S(1)} %get-tuple-element.71.refs_3_, ...), custom_call_target="tpu_custom_call" | custom-call | flops 880803840 | bytes 13762560 | tf_op jit(solution)/shard_map/feed_forward/pallas_call | solution.py:410
  53.9 1.6 %collective-permute-start.13 = (bf16[64,1280]{1,0:T(8,128)(2,1)S(1)}, bf16[64,1280]{1,0:T(8,128)(2,1)S(1)}, u32[]{:S(2)}, u32[]{:S(2)}) collective-permute-start(bf16[64,1280]{1,0:T(8,128)(2,1)S(1)} %get-tuple-element.77), channel_id=1, source_target_pairs={{0,1},{1,0},{2,3},{3,2},{4,5},{5,4},{6,7},{7,6},{8,9},{9,8},{10,11... | collective-permute-start | bytes 491528 | tf_op jit(solution)/shard_map/ppermute | solution.py:489
  55.6 0.1 collective-permute-done.9.refs_0_
  55.6 3.5 %collective-permute-done.12.refs_1_ = bf16[64,1280]{1,0:T(8,128)(2,1)S(1)} collective-permute-done((bf16[64,1280]{1,0:T(8,128)(2,1)S(1)}, bf16[64,1280]{1,0:T(8,128)(2,1)S(1)}, u32[]{:S(2)}, u32[]{:S(2)}) %collective-permute-start.12) | collective-permute-done | bytes 163872 | tf_op jit(solution)/shard_map/ppermute | solution.py:489
  59.2 2.5 %feed_forward.3 = (bf16[64,1280]{1,0:T(8,128)(2,1)S(1)}, f32[64,1280]{1,0:T(8,128)S(1)}, f32[64,1280]{1,0:T(8,128)S(1)}) custom-call(bf16[64,1280]{1,0:T(8,128)(2,1)S(1)} %collective-permute-done.9.refs_0_, bf16[64,1280]{1,0:T(8,128)(2,1)S(1)} %collective-permute-done.12.refs_1_, bf16[1,2560]{1,0:T(2,128)(2,1)S(1)} %reshape.16.refs_2_, ...), custom_call_target="tpu_custom_call" | custom-call | flops 880803840 | bytes 13762560 | tf_op jit(solution)/shard_map/feed_forward/pallas_call | solution.py:410
  61.6 0.1 collective-permute-start.14
  61.8 3.6 %collective-permute-start.17 = (bf16[64,1280]{1,0:T(8,128)(2,1)S(1)}, bf16[64,1280]{1,0:T(8,128)(2,1)S(1)}, u32[]{:S(2)}, u32[]{:S(2)}) collective-permute-start(bf16[64,1280]{1,0:T(8,128)(2,1)S(1)} %add_convert_fusion.3), channel_id=1, source_target_pairs={{0,2},{1,3},{2,0},{3,1},{4,6},{5,7},{6,4},{7,5},{8,10},{9,11},{10,... | collective-permute-start | bytes 491528 | tf_op jit(solution)/shard_map/ppermute | solution.py:489
  65.4 3.4 %collective-permute-done.14 = bf16[64,1280]{1,0:T(8,128)(2,1)S(1)} collective-permute-done((bf16[64,1280]{1,0:T(8,128)(2,1)S(1)}, bf16[64,1280]{1,0:T(8,128)(2,1)S(1)}, u32[]{:S(2)}, u32[]{:S(2)}) %collective-permute-start.14) | collective-permute-done | bytes 163872 | tf_op jit(solution)/shard_map/ppermute | solution.py:489
  68.9 1.6 %collective-permute-start.15 = (bf16[64,1280]{1,0:T(8,128)(2,1)S(1)}, bf16[64,1280]{1,0:T(8,128)(2,1)S(1)}, u32[]{:S(2)}, u32[]{:S(2)}) collective-permute-start(bf16[64,1280]{1,0:T(8,128)(2,1)S(1)} %add_convert_fusion.2), channel_id=1, source_target_pairs={{0,2},{1,3},{2,0},{3,1},{4,6},{5,7},{6,4},{7,5},{8,10},{9,11},{10,... | collective-permute-start | bytes 491528 | tf_op jit(solution)/shard_map/ppermute | solution.py:489
  70.5 1.9 %stage.5.refs_3_ = bf16[2560,640]{1,0:T(8,128)(2,1)S(1)} custom-call(bf16[2560,640]{1,0:T(8,128)(2,1)} %refs_0_.2), custom_call_target="tpu_custom_call" | custom-call | bytes 3276800 | tf_op jit(solution)/shard_map/stage/pallas_call | solution.py:372
  72.4 4.4 %collective-permute-done.17 = bf16[64,1280]{1,0:T(8,128)(2,1)S(1)} collective-permute-done((bf16[64,1280]{1,0:T(8,128)(2,1)S(1)}, bf16[64,1280]{1,0:T(8,128)(2,1)S(1)}, u32[]{:S(2)}, u32[]{:S(2)}) %collective-permute-start.17) | collective-permute-done | bytes 163872 | tf_op jit(solution)/shard_map/ppermute | solution.py:489
  76.9 0.1 collective-permute-start.18
  76.9 1.7 %collective-permute-done.15 = bf16[64,1280]{1,0:T(8,128)(2,1)S(1)} collective-permute-done((bf16[64,1280]{1,0:T(8,128)(2,1)S(1)}, bf16[64,1280]{1,0:T(8,128)(2,1)S(1)}, u32[]{:S(2)}, u32[]{:S(2)}) %collective-permute-start.15) | collective-permute-done | bytes 163872 | tf_op jit(solution)/shard_map/ppermute | solution.py:489
  78.7 0.5 collective-permute-start.16
  79.2 1.2 %next_layer.2 = (bf16[64,640]{1,0:T(8,128)(2,1)S(1)}, bf16[320,64]{1,0:T(8,128)(2,1)S(1)}) custom-call(bf16[64,1280]{1,0:T(8,128)(2,1)S(1)} %add_convert_fusion.1.refs_0_.refs_7_, bf16[64,1280]{1,0:T(8,128)(2,1)S(1)} %add_convert_fusion.refs_1_.refs_8_, bf16[1,2560]{1,0:T(2,128)(2,1)S(1)} %reshape.17.refs_2_, bf16[2560,640]{1,0:T(8,128)(2,1)S(1)} %stage.5.refs_3_, ...), custom_call_target="tpu_custom_call" | custom-call | flops 314572800 | bytes 4915200 | tf_op jit(solution)/shard_map/next_layer/pallas_call | solution.py:472
  80.4 2.8 %collective-permute-done.18.refs_1_ = bf16[64,1280]{1,0:T(8,128)(2,1)S(1)} collective-permute-done((bf16[64,1280]{1,0:T(8,128)(2,1)S(1)}, bf16[64,1280]{1,0:T(8,128)(2,1)S(1)}, u32[]{:S(2)}, u32[]{:S(2)}) %collective-permute-start.18) | collective-permute-done | bytes 163872 | tf_op jit(solution)/shard_map/ppermute | solution.py:489
  83.2 1.8 %collective-permute-done.16.refs_0_ = bf16[64,1280]{1,0:T(8,128)(2,1)S(1)} collective-permute-done((bf16[64,1280]{1,0:T(8,128)(2,1)S(1)}, bf16[64,1280]{1,0:T(8,128)(2,1)S(1)}, u32[]{:S(2)}, u32[]{:S(2)}) %collective-permute-start.16) | collective-permute-done | bytes 163872 | tf_op jit(solution)/shard_map/ppermute | solution.py:489
  84.9 2.1 %next_layer.3 = (bf16[128,640]{1,0:T(8,128)(2,1)}, bf16[320,128]{1,0:T(8,128)(2,1)}, bf16[32,2560]{1,0:T(8,128)(2,1)}) custom-call(bf16[64,1280]{1,0:T(8,128)(2,1)S(1)} %collective-permute-done.16.refs_0_, bf16[64,1280]{1,0:T(8,128)(2,1)S(1)} %collective-permute-done.18.refs_1_, bf16[1,2560]{1,0:T(2,128)(2,1)S(1)} %reshape.17.refs_2_, ...), custom_call_target="tpu_custom_call" | custom-call | flops 314572800 | bytes 4915200 | tf_op jit(solution)/shard_map/next_layer/pallas_call | solution.py:472
  (28 shorter events, 0.5 us)
Async XLA Ops:
  1.7 5.6 %collective-permute-start.1 = (bf16[512,384]{1,0:T(8,128)(2,1)S(1)}, bf16[512,384]{1,0:T(8,128)(2,1)S(1)}, u32[]{:S(2)}, u32[]{:S(2)}) collective-permute-start(bf16[512,384]{1,0:T(8,128)(2,1)S(1)} %pool_rows.1.refs_0_), channel_id=1, source_target_pairs={{0,4},{4,0},{8,12},{12,8},{16,20},{20,16},{24,28},{28,24},{1,5},{5... | collective-permute-start | bytes 1179656 | tf_op jit(solution)/shard_map/ppermute | solution.py:489
  2.2 11.4 %collective-permute-start = (bf16[512,384]{1,0:T(8,128)(2,1)S(1)}, bf16[512,384]{1,0:T(8,128)(2,1)S(1)}, u32[]{:S(2)}, u32[]{:S(2)}) collective-permute-start(bf16[512,384]{1,0:T(8,128)(2,1)S(1)} %pool_rows.1.refs_0_), channel_id=1, source_target_pairs={{0,8},{4,20},{8,0},{12,28},{16,24},{20,4},{24,16},{28,12},{1,9},{5... | collective-permute-start | bytes 1179656 | tf_op jit(solution)/shard_map/ppermute | solution.py:495
  4.8 9.7 %collective-permute-start.3 = (bf16[512,384]{1,0:T(8,128)(2,1)S(1)}, bf16[512,384]{1,0:T(8,128)(2,1)S(1)}, u32[]{:S(2)}, u32[]{:S(2)}) collective-permute-start(bf16[512,384]{1,0:T(8,128)(2,1)S(1)} %pool_rows.1.refs_0_), channel_id=1, source_target_pairs={{0,16},{4,12},{8,24},{12,4},{16,0},{20,28},{24,8},{28,20},{1,17},{... | collective-permute-start | bytes 1179656 | tf_op jit(solution)/shard_map/ppermute | solution.py:495
  7.3 1.0 %copy-start.3 = (bf16[16,32,320]{2,1,0:T(8,128)(2,1)S(1)}, bf16[16,32,320]{2,1,0:T(8,128)(2,1)}, u32[]{:S(2)}) copy-start(bf16[16,32,320]{2,1,0:T(8,128)(2,1)} %leaf_ref.1) | copy-start | bytes 983044
  8.3 0.9 %copy-start.4 = (bf16[128,640]{1,0:T(8,128)(2,1)S(1)}, bf16[128,640]{1,0:T(8,128)(2,1)}, u32[]{:S(2)}) copy-start(bf16[128,640]{1,0:T(8,128)(2,1)} %query_ref.1) | copy-start | bytes 491524
  14.5 2.3 %collective-permute-start.4 = (bf16[512,384]{1,0:T(8,128)(2,1)S(1)}, bf16[512,384]{1,0:T(8,128)(2,1)S(1)}, u32[]{:S(2)}, u32[]{:S(2)}) collective-permute-start(bf16[512,384]{1,0:T(8,128)(2,1)S(1)} %collective-permute-done.refs_2_), channel_id=1, source_target_pairs={{0,4},{4,0},{8,12},{12,8},{16,20},{20,16},{24,28},{28,24},{1,5},{5... | collective-permute-start | bytes 1179656 | tf_op jit(solution)/shard_map/ppermute | solution.py:489
  14.7 2.2 %collective-permute-start.5 = (bf16[512,384]{1,0:T(8,128)(2,1)S(1)}, bf16[512,384]{1,0:T(8,128)(2,1)S(1)}, u32[]{:S(2)}, u32[]{:S(2)}) collective-permute-start(bf16[512,384]{1,0:T(8,128)(2,1)S(1)} %collective-permute-done.3.refs_3_), channel_id=1, source_target_pairs={{0,4},{4,0},{8,12},{12,8},{16,20},{20,16},{24,28},{28,24},{1,5},{5... | collective-permute-start | bytes 1179656 | tf_op jit(solution)/shard_map/ppermute | solution.py:489
  15.0 7.8 %collective-permute-start.2 = (bf16[512,384]{1,0:T(8,128)(2,1)S(1)}, bf16[512,384]{1,0:T(8,128)(2,1)S(1)}, u32[]{:S(2)}, u32[]{:S(2)}) collective-permute-start(bf16[512,384]{1,0:T(8,128)(2,1)S(1)} %collective-permute-done.refs_2_), channel_id=1, source_target_pairs={{0,16},{4,12},{8,24},{12,4},{16,0},{20,28},{24,8},{28,20},{1,17},{... | collective-permute-start | bytes 1179656 | tf_op jit(solution)/shard_map/ppermute | solution.py:495
  20.4 4.5 %copy-start = (bf16[640,2560]{1,0:T(8,128)(2,1)S(1)}, bf16[640,2560]{1,0:T(8,128)(2,1)}, u32[]{:S(2)}) copy-start(bf16[640,2560]{1,0:T(8,128)(2,1)} %refs_3_.3) | copy-start | bytes 9830404
  22.9 6.3 %copy-start.5 = (bf16[2560]{0:T(1024)(128)(2,1)S(1)}, bf16[2560]{0:T(1024)(128)(2,1)}, u32[]{:S(2)}) copy-start(bf16[2560]{0:T(1024)(128)(2,1)} %param.33) | copy-start | bytes 15364
  22.9 6.3 %copy-start.2 = (bf16[128,2560]{1,0:T(8,128)(2,1)S(1)}, bf16[128,2560]{1,0:T(8,128)(2,1)}, u32[]{:S(2)}) copy-start(bf16[128,2560]{1,0:T(8,128)(2,1)} %refs_5_.1) | copy-start | bytes 1966084
  22.9 2.0 %collective-permute-start.6 = (bf16[512,384]{1,0:T(8,128)(2,1)S(1)}, bf16[512,384]{1,0:T(8,128)(2,1)S(1)}, u32[]{:S(2)}, u32[]{:S(2)}) collective-permute-start(bf16[512,384]{1,0:T(8,128)(2,1)S(1)} %collective-permute-done.2.refs_2_), channel_id=1, source_target_pairs={{0,4},{4,0},{8,12},{12,8},{16,20},{20,16},{24,28},{28,24},{1,5},{5... | collective-permute-start | bytes 1179656 | tf_op jit(solution)/shard_map/ppermute | solution.py:489
  27.0 6.7 %collective-permute-start.7 = (bf16[64,1280]{1,0:T(8,128)(2,1)S(1)}, bf16[64,1280]{1,0:T(8,128)(2,1)S(1)}, u32[]{:S(2)}, u32[]{:S(2)}) collective-permute-start(bf16[64,1280]{1,0:T(8,128)(2,1)S(1)} %get-tuple-element.61), channel_id=1, source_target_pairs={{0,1},{1,0},{2,3},{3,2},{4,5},{5,4},{6,7},{7,6},{8,9},{9,8},{10,11... | collective-permute-start | bytes 491528 | tf_op jit(solution)/shard_map/ppermute | solution.py:489
  31.6 8.5 %collective-permute-start.10 = (bf16[64,1280]{1,0:T(8,128)(2,1)S(1)}, bf16[64,1280]{1,0:T(8,128)(2,1)S(1)}, u32[]{:S(2)}, u32[]{:S(2)}) collective-permute-start(bf16[64,1280]{1,0:T(8,128)(2,1)S(1)} %get-tuple-element.64), channel_id=1, source_target_pairs={{0,1},{1,0},{2,3},{3,2},{4,5},{5,4},{6,7},{7,6},{8,9},{9,8},{10,11... | collective-permute-start | bytes 491528 | tf_op jit(solution)/shard_map/ppermute | solution.py:489
  33.7 14.6 %collective-permute-start.8 = (bf16[64,1280]{1,0:T(8,128)(2,1)S(1)}, bf16[64,1280]{1,0:T(8,128)(2,1)S(1)}, u32[]{:S(2)}, u32[]{:S(2)}) collective-permute-start(bf16[64,1280]{1,0:T(8,128)(2,1)S(1)} %add_convert_fusion.7), channel_id=1, source_target_pairs={{0,2},{1,3},{2,0},{3,1},{4,6},{5,7},{6,4},{7,5},{8,10},{9,11},{10,... | collective-permute-start | bytes 491528 | tf_op jit(solution)/shard_map/ppermute | solution.py:489
  40.1 10.9 %collective-permute-start.11 = (bf16[64,1280]{1,0:T(8,128)(2,1)S(1)}, bf16[64,1280]{1,0:T(8,128)(2,1)S(1)}, u32[]{:S(2)}, u32[]{:S(2)}) collective-permute-start(bf16[64,1280]{1,0:T(8,128)(2,1)S(1)} %add_convert_fusion.5), channel_id=1, source_target_pairs={{0,2},{1,3},{2,0},{3,1},{4,6},{5,7},{6,4},{7,5},{8,10},{9,11},{10,... | collective-permute-start | bytes 491528 | tf_op jit(solution)/shard_map/ppermute | solution.py:489
  48.4 7.2 %collective-permute-start.9 = (bf16[64,1280]{1,0:T(8,128)(2,1)S(1)}, bf16[64,1280]{1,0:T(8,128)(2,1)S(1)}, u32[]{:S(2)}, u32[]{:S(2)}) collective-permute-start(bf16[64,1280]{1,0:T(8,128)(2,1)S(1)} %add_convert_fusion.6.refs_0_), channel_id=1, source_target_pairs={{0,1},{1,0},{2,3},{3,2},{4,5},{5,4},{6,7},{7,6},{8,9},{9,8},{10,11... | collective-permute-start | bytes 491528 | tf_op jit(solution)/shard_map/ppermute | solution.py:489
  51.1 8.0 %collective-permute-start.12 = (bf16[64,1280]{1,0:T(8,128)(2,1)S(1)}, bf16[64,1280]{1,0:T(8,128)(2,1)S(1)}, u32[]{:S(2)}, u32[]{:S(2)}) collective-permute-start(bf16[64,1280]{1,0:T(8,128)(2,1)S(1)} %add_convert_fusion.4.refs_1_), channel_id=1, source_target_pairs={{0,1},{1,0},{2,3},{3,2},{4,5},{5,4},{6,7},{7,6},{8,9},{9,8},{10,11... | collective-permute-start | bytes 491528 | tf_op jit(solution)/shard_map/ppermute | solution.py:489
  53.9 7.8 %collective-permute-start.13 = (bf16[64,1280]{1,0:T(8,128)(2,1)S(1)}, bf16[64,1280]{1,0:T(8,128)(2,1)S(1)}, u32[]{:S(2)}, u32[]{:S(2)}) collective-permute-start(bf16[64,1280]{1,0:T(8,128)(2,1)S(1)} %get-tuple-element.77), channel_id=1, source_target_pairs={{0,1},{1,0},{2,3},{3,2},{4,5},{5,4},{6,7},{7,6},{8,9},{9,8},{10,11... | collective-permute-start | bytes 491528 | tf_op jit(solution)/shard_map/ppermute | solution.py:489
  61.6 7.2 %collective-permute-start.14 = (bf16[64,1280]{1,0:T(8,128)(2,1)S(1)}, bf16[64,1280]{1,0:T(8,128)(2,1)S(1)}, u32[]{:S(2)}, u32[]{:S(2)}) collective-permute-start(bf16[64,1280]{1,0:T(8,128)(2,1)S(1)} %get-tuple-element.78), channel_id=1, source_target_pairs={{0,1},{1,0},{2,3},{3,2},{4,5},{5,4},{6,7},{7,6},{8,9},{9,8},{10,11... | collective-permute-start | bytes 491528 | tf_op jit(solution)/shard_map/ppermute | solution.py:489
  61.7 17.4 %copy-start.6 = (bf16[2560]{0:T(1024)(128)(2,1)S(1)}, bf16[2560]{0:T(1024)(128)(2,1)}, u32[]{:S(2)}) copy-start(bf16[2560]{0:T(1024)(128)(2,1)} %param.37) | copy-start | bytes 15364
  61.7 17.5 %copy-start.1 = (bf16[2560,320]{0,1:T(8,128)(2,1)S(1)}, bf16[2560,320]{0,1:T(8,128)(2,1)}, u32[]{:S(2)}) copy-start(bf16[2560,320]{0,1:T(8,128)(2,1)} %param.39) | copy-start | bytes 4915204
  61.8 15.0 %collective-permute-start.17 = (bf16[64,1280]{1,0:T(8,128)(2,1)S(1)}, bf16[64,1280]{1,0:T(8,128)(2,1)S(1)}, u32[]{:S(2)}, u32[]{:S(2)}) collective-permute-start(bf16[64,1280]{1,0:T(8,128)(2,1)S(1)} %add_convert_fusion.3), channel_id=1, source_target_pairs={{0,2},{1,3},{2,0},{3,1},{4,6},{5,7},{6,4},{7,5},{8,10},{9,11},{10,... | collective-permute-start | bytes 491528 | tf_op jit(solution)/shard_map/ppermute | solution.py:489
  68.9 9.7 %collective-permute-start.15 = (bf16[64,1280]{1,0:T(8,128)(2,1)S(1)}, bf16[64,1280]{1,0:T(8,128)(2,1)S(1)}, u32[]{:S(2)}, u32[]{:S(2)}) collective-permute-start(bf16[64,1280]{1,0:T(8,128)(2,1)S(1)} %add_convert_fusion.2), channel_id=1, source_target_pairs={{0,2},{1,3},{2,0},{3,1},{4,6},{5,7},{6,4},{7,5},{8,10},{9,11},{10,... | collective-permute-start | bytes 491528 | tf_op jit(solution)/shard_map/ppermute | solution.py:489
  76.9 6.3 %collective-permute-start.18 = (bf16[64,1280]{1,0:T(8,128)(2,1)S(1)}, bf16[64,1280]{1,0:T(8,128)(2,1)S(1)}, u32[]{:S(2)}, u32[]{:S(2)}) collective-permute-start(bf16[64,1280]{1,0:T(8,128)(2,1)S(1)} %add_convert_fusion.refs_1_.refs_8_), channel_id=1, source_target_pairs={{0,1},{1,0},{2,3},{3,2},{4,5},{5,4},{6,7},{7,6},{8,9},{9,8},{10,11... | collective-permute-start | bytes 491528 | tf_op jit(solution)/shard_map/ppermute | solution.py:489
  78.7 6.3 %collective-permute-start.16 = (bf16[64,1280]{1,0:T(8,128)(2,1)S(1)}, bf16[64,1280]{1,0:T(8,128)(2,1)S(1)}, u32[]{:S(2)}, u32[]{:S(2)}) collective-permute-start(bf16[64,1280]{1,0:T(8,128)(2,1)S(1)} %add_convert_fusion.1.refs_0_.refs_7_), channel_id=1, source_target_pairs={{0,1},{1,0},{2,3},{3,2},{4,5},{5,4},{6,7},{7,6},{8,9},{9,8},{10,11... | collective-permute-start | bytes 491528 | tf_op jit(solution)/shard_map/ppermute | solution.py:489

commit v7 on v6

--- a/solution.py
+++ b/solution.py
@@ -507,12 +507,6 @@
     return (mine + wide(got)).astype(bf16)
 
 
-def pairs_in_turn(mine, got, weights):
-    last = add_pair(mine[-1], got[-1])
-    _, rest, weights = lax.optimization_barrier((last, got[:-1], weights))
-    return [*each(add_pair, mine[:-1], rest), last], weights
-
-
 def add_rows(pair, rows, got):
     return (wide(rows) + (wide(pair) + wide(got))).astype(bf16)
 
@@ -558,10 +552,6 @@
         first, second = lax.optimization_barrier((first, second))
         near = [first, second, trade(first, "req", 1), trade(second, "req", 1)]
         state = extend_attention(aug, state, near, kv_local)
-        state, down_weight = lax.optimization_barrier((state, down_weight))
-        corner, state, down_weight = lax.optimization_barrier(
-            (corner, state, *stage([down_weight]))
-        )
         corner_other = trade(corner, "req", 1)
         state = extend_attention(aug, state, [corner], kv_local)
         pools = [corner_other]
@@ -590,13 +580,11 @@
     depth = residual_in.shape[1]
     if lax.axis_size("tp") == 4:
         got = trades(theirs_proj, 1)
-        pair, (gate_weight, up_weight) = pairs_in_turn(
-            mine_proj[::-1], got[::-1], (gate_weight, up_weight)
-        )
-        pair = pair[::-1]
+        lead = add_pair(mine_proj[0], got[0])
+        _, *mlp = lax.optimization_barrier((lead, gate_weight, up_weight, down_weight))
+        got[1:], *mlp = lax.optimization_barrier((got[1:], *stage(mlp)))
+        pair = [lead, *each(add_pair, mine_proj[1:], got[1:])]
         got = trades(pair, 2)
-        got[-1], *staged = lax.optimization_barrier((got[-1], *stage([gate_weight, up_weight])))
-        mlp = (*staged, down_weight)
         mixed_mine = each(add_rows, pair, res_mine, got)
         mixed_theirs = trades(mixed_mine, 1)
         hidden, last = feed_forward(mixed_mine, norm_gain, *mlp)
@@ -604,9 +592,11 @@
         result = feed_forward(mixed_theirs, norm_gain, *mlp, [hidden])
         got = [*trades(result[: PIECES - 1], 1), last]
         mlp_theirs = result[PIECES - 1 :]
-        pair, (query_weight,) = pairs_in_turn(mlp_theirs, got, (query_weight,))
+        lead = add_pair(mlp_theirs[-1], got[-1])
+        _, query_weight = lax.optimization_barrier((lead, query_weight))
+        got[:-1], query_weight = lax.optimization_barrier((got[:-1], *stage([query_weight])))
+        pair = [*each(add_pair, mlp_theirs[:-1], got[:-1]), lead]
         got = trades(pair, 2)
-        got[-1], query_weight = lax.optimization_barrier((got[-1], *stage([query_weight])))
         layer_theirs = each(add_rows, pair, mixed_theirs, got)
         layer_mine = trades(layer_theirs, 1)
     else:

time: 87.3 us -> 91.8 us (1.052)
  waiting for transfers between devices: 30.2 us -> 33.7 us
  starting transfers between devices: 21.6 us -> 23.8 us
  Pallas kernels: 30.9 us -> 29.8 us
    ppermute x3, waiting for transfers between devices: 1.51 us -> 5.86 us  [cross(): return lax.ppermute(value, 'req', pairs)]
    ppermute x16, starting transfers between devices: 15.8 us -> 17.1 us  [trade(): return lax.ppermute(value, axis, [(i, i ^ bit) for i in range(size)])]
    pallas_call x3 -> x2, Pallas kernels: 8.11 us -> 6.96 us  [stage(): pl.pallas_call(stage_kernel, out_shape=tuple((pltpu.VMEM(w.shape, w.dtype...]
  transfers between devices with their start and end apart: 19 -> 19, of which waited for: 13 -> 12; matrix products, arithmetic and copies ran while one was open for 2% -> 2% of each run, Pallas kernels for 29% -> 27%
where the time goes in v7:
time: 91.8 us; the launch traced here: 91.5 us
  waiting for transfers between devices  33.7 us (37%)
  Pallas kernels  29.8 us (32%)
  starting transfers between devices  23.8 us (26%)
  local copies, waits for them, and re-layouts  2.94 us (3%)
    ppermute x16, waiting for transfers between devices, trade(): return lax.ppermute(value, axis, [(i, i ^ bit) for i in range(size)])  27.9 us
    ppermute x16, starting transfers between devices, trade(): return lax.ppermute(value, axis, [(i, i ^ bit) for i in range(size)])  17.1 us
    pallas_call x2, Pallas kernels, stage(): pl.pallas_call(stage_kernel, out_shape=tuple((pltpu.VMEM(w.shape, w.dtype...  6.96 us
    ppermute x3, starting transfers between devices, cross(): return lax.ppermute(value, 'req', pairs)  6.72 us
    ppermute x3, waiting for transfers between devices, cross(): return lax.ppermute(value, 'req', pairs)  5.86 us
    pallas_call x2, Pallas kernels, extend_attention(): pl.pallas_call(functools.partial(chunk_kernel, blocks=2 * kv_local), out_...  5.37 us
    pallas_call x2, Pallas kernels, feed_forward(): pl.pallas_call(functools.partial(mlp_kernel, second=len(other) > 0), out_...  4.79 us
    pallas_call x2, Pallas kernels, finish_attention(): pl.pallas_call(functools.partial(finish_kernel, half=half, kv_local=kv_lo...  4.56 us
  transfers between devices with their start and end apart: 19, of which 12 were waited for; matrix products, arithmetic and copies ran while one was open for 2% of the time, Pallas kernels for 27%

profile of v7, /device:TPU:0, one launch (start us, length us, event | category | flops | bytes accessed | tf_op | source)
XLA Modules:
  0.0 91.5 jit_solution(11390294094328578890)
XLA Ops:
  0.6 1.1 %pool_rows.1.refs_0_ = bf16[512,384]{1,0:T(8,128)(2,1)S(1)} custom-call(s32[32]{0:T(128)} %node_hbm.1, s32[32]{0:T(128)} %rank_hbm.1, s32[8]{0:T(128)} %length_hbm.1, s32[6]{0:T(128)} %root_hbm.1, bf16[32,16,320]{2,1,0:T(8,128)(2,1)} %pool_hbm.1), custom_call_target="tpu_custom_call" | custom-call | tf_op jit(solution)/shard_map/pool_rows/pallas_call | solution.py:128
  1.7 0.5 collective-permute-start.1
  2.2 2.6 %collective-permute-start = (bf16[512,384]{1,0:T(8,128)(2,1)S(1)}, bf16[512,384]{1,0:T(8,128)(2,1)S(1)}, u32[]{:S(2)}, u32[]{:S(2)}) collective-permute-start(bf16[512,384]{1,0:T(8,128)(2,1)S(1)} %pool_rows.1.refs_0_), channel_id=1, source_target_pairs={{0,8},{4,20},{8,0},{12,28},{16,24},{20,4},{24,16},{28,12},{1,9},{5... | collective-permute-start | bytes 1179656 | tf_op jit(solution)/shard_map/ppermute | solution.py:495
  4.8 1.5 %collective-permute-start.2 = (bf16[512,384]{1,0:T(8,128)(2,1)S(1)}, bf16[512,384]{1,0:T(8,128)(2,1)S(1)}, u32[]{:S(2)}, u32[]{:S(2)}) collective-permute-start(bf16[512,384]{1,0:T(8,128)(2,1)S(1)} %pool_rows.1.refs_0_), channel_id=1, source_target_pairs={{0,16},{4,12},{8,24},{12,4},{16,0},{20,28},{24,8},{28,20},{1,17},{... | collective-permute-start | bytes 1179656 | tf_op jit(solution)/shard_map/ppermute | solution.py:495
  6.3 1.0 %copy.24.keyval_ref = bf16[128,320]{1,0:T(8,128)(2,1)S(1)} copy(bf16[128,320]{0,1:T(8,128)(2,1)} %param.21) | data formatting | bytes 163840 | tf_op args[1]
  7.3 1.0 %copy-done.3 = bf16[16,32,320]{2,1,0:T(8,128)(2,1)S(1)} copy-done((bf16[16,32,320]{2,1,0:T(8,128)(2,1)S(1)}, bf16[16,32,320]{2,1,0:T(8,128)(2,1)}, u32[]{:S(2)}) %copy-start.3) | copy-done | bytes 327704
  8.3 0.9 copy-done.4
  9.2 3.8 %attend_local.1 = (bf16[1024,256]{1,0:T(8,128)(2,1)S(1)}, f32[1024,256]{1,0:T(8,128)S(1)}) custom-call(s32[1,16]{1,0:T(1,128)} %count_hbm.1, s32[16]{0:T(128)} %mid_hbm.1, s32[16]{0:T(128)} %leaf_len_hbm.1, bf16[128,640]{1,0:T(8,128)(2,1)S(1)} %copy-done.4, bf16[128,320]{1,0:T(8,128)(2,1)S(1)} %copy.24.keyval_ref, bf16[16,32,320]{2,1,0:T(8,128)(2,1)S(1)} %copy-done.3, ...), custom_call_target="tpu_custom_call" | custom-call | flops 1744830464 | bytes 2097152 | tf_op jit(solution)/shard_map/attend_local/pallas_call | solution.py:242
  13.0 0.6 collective-permute-done.refs_2_
  13.7 2.6 %collective-permute-start.5 = (bf16[512,384]{1,0:T(8,128)(2,1)S(1)}, bf16[512,384]{1,0:T(8,128)(2,1)S(1)}, u32[]{:S(2)}, u32[]{:S(2)}) collective-permute-start(bf16[512,384]{1,0:T(8,128)(2,1)S(1)} %collective-permute-done.refs_2_), channel_id=1, source_target_pairs={{0,16},{4,12},{8,24},{12,4},{16,0},{20,28},{24,8},{28,20},{1,17},{... | collective-permute-start | bytes 1179656 | tf_op jit(solution)/shard_map/ppermute | solution.py:495
  16.3 0.5 collective-permute-start.4
  16.8 5.2 %collective-permute-done.5.refs_2_ = bf16[512,384]{1,0:T(8,128)(2,1)S(1)} collective-permute-done((bf16[512,384]{1,0:T(8,128)(2,1)S(1)}, bf16[512,384]{1,0:T(8,128)(2,1)S(1)}, u32[]{:S(2)}, u32[]{:S(2)}) %collective-permute-start.5) | collective-permute-done | bytes 393248 | tf_op jit(solution)/shard_map/ppermute | solution.py:495
  22.1 3.6 %attend_pages.2.refs_1_ = f32[1024,256]{1,0:T(8,128)S(1)} custom-call(bf16[1024,256]{1,0:T(8,128)(2,1)S(1)} %get-tuple-element.44.refs_0_, f32[1024,256]{1,0:T(8,128)S(1)} %get-tuple-element.45.refs_1_, bf16[512,384]{1,0:T(8,128)(2,1)S(1)} %collective-permute-done.refs_2_, bf16[512,384]{1,0:T(8,128)(2,1)S(1)} %collective-permute-done.2.refs_3_, ...), custom_call_target="tpu_custom_call" | custom-call | flops 2147483648 | bytes 2097152 | tf_op jit(solution)/shard_map/attend_pages/pallas_call | solution.py:281
  25.6 1.8 %attend_pages.3.refs_1_ = f32[1024,256]{1,0:T(8,128)S(1)} custom-call(bf16[1024,256]{1,0:T(8,128)(2,1)S(1)} %get-tuple-element.44.refs_0_, f32[1024,256]{1,0:T(8,128)S(1)} %attend_pages.2.refs_1_, bf16[512,384]{1,0:T(8,128)(2,1)S(1)} %collective-permute-done.5.refs_2_), custom_call_target="tpu_custom_call" | custom-call | flops 536870912 | bytes 2097152 | tf_op jit(solution)/shard_map/attend_pages/pallas_call | solution.py:281
  27.5 2.1 %attend_finish.2 = (bf16[64,640]{1,0:T(8,128)(2,1)S(1)}, bf16[64,1280]{1,0:T(8,128)(2,1)S(1)}) custom-call(bf16[1024,256]{1,0:T(8,128)(2,1)S(1)} %get-tuple-element.44.refs_0_, f32[1024,256]{1,0:T(8,128)S(1)} %attend_pages.3.refs_1_, bf16[512,384]{1,0:T(8,128)(2,1)S(1)} %collective-permute-done.6.refs_2_, bf16[640,2560]{1,0:T(8,128)(2,1)S(1)} %copy-done), custom_call_target="tpu_custom_call" | custom-call | flops 536870912 | bytes 1048576 | tf_op jit(solution)/shard_map/attend_finish/pallas_call | solution.py:345
  29.6 2.0 %collective-permute-start.7 = (bf16[64,1280]{1,0:T(8,128)(2,1)S(1)}, bf16[64,1280]{1,0:T(8,128)(2,1)S(1)}, u32[]{:S(2)}, u32[]{:S(2)}) collective-permute-start(bf16[64,1280]{1,0:T(8,128)(2,1)S(1)} %get-tuple-element.53), channel_id=1, source_target_pairs={{0,1},{1,0},{2,3},{3,2},{4,5},{5,4},{6,7},{7,6},{8,9},{9,8},{10,11... | collective-permute-start | bytes 491528 | tf_op jit(solution)/shard_map/ppermute | solution.py:489
  31.6 2.5 %attend_finish.3 = (bf16[128,640]{1,0:T(8,128)(2,1)}, bf16[64,1280]{1,0:T(8,128)(2,1)S(1)}, f32[64,1280]{1,0:T(8,128)S(1)}, f32[64,1280]{1,0:T(8,128)S(1)}, bf16...) custom-call(bf16[1024,256]{1,0:T(8,128)(2,1)S(1)} %get-tuple-element.44.refs_0_, ...), custom_call_target="tpu_custom_call" | custom-call | flops 536870912 | bytes 1048576 | tf_op jit(solution)/shard_map/attend_finish/pallas_call | solution.py:345
  34.1 0.1 collective-permute-start.10
  34.2 2.2 %collective-permute-done.7 = bf16[64,1280]{1,0:T(8,128)(2,1)S(1)} collective-permute-done((bf16[64,1280]{1,0:T(8,128)(2,1)S(1)}, bf16[64,1280]{1,0:T(8,128)(2,1)S(1)}, u32[]{:S(2)}, u32[]{:S(2)}) %collective-permute-start.7) | collective-permute-done | bytes 163872 | tf_op jit(solution)/shard_map/ppermute | solution.py:489
  36.5 2.8 %collective-permute-start.8 = (bf16[64,1280]{1,0:T(8,128)(2,1)S(1)}, bf16[64,1280]{1,0:T(8,128)(2,1)S(1)}, u32[]{:S(2)}, u32[]{:S(2)}) collective-permute-start(bf16[64,1280]{1,0:T(8,128)(2,1)S(1)} %add_convert_fusion.7), channel_id=1, source_target_pairs={{0,2},{1,3},{2,0},{3,1},{4,6},{5,7},{6,4},{7,5},{8,10},{9,11},{10,... | collective-permute-start | bytes 491528 | tf_op jit(solution)/shard_map/ppermute | solution.py:489
  39.3 5.0 %stage.2 = (bf16[2560,896]{1,0:T(8,128)(2,1)S(1)}, bf16[2560,896]{1,0:T(8,128)(2,1)S(1)}, bf16[896,2560]{1,0:T(8,128)(2,1)S(1)}) custom-call(bf16[2560,896]{1,0:T(8,128)(2,1)} %refs_0_, bf16[2560,896]{1,0:T(8,128)(2,1)} %refs_1_, bf16[896,2560]{1,0:T(8,128)(2,1)} %refs_2_), custom_call_target="tpu_custom_call" | custom-call | bytes 13762560 | tf_op jit(solution)/shard_map/stage/pallas_call | solution.py:372
  44.4 0.2 collective-permute-start.11
  44.6 2.3 %collective-permute-done.8 = bf16[64,1280]{1,0:T(8,128)(2,1)S(1)} collective-permute-done((bf16[64,1280]{1,0:T(8,128)(2,1)S(1)}, bf16[64,1280]{1,0:T(8,128)(2,1)S(1)}, u32[]{:S(2)}, u32[]{:S(2)}) %collective-permute-start.8) | collective-permute-done | bytes 163872 | tf_op jit(solution)/shard_map/ppermute | solution.py:489
  47.0 0.1 add_convert_fusion.6.refs_0_
  47.1 4.4 %collective-permute-start.9 = (bf16[64,1280]{1,0:T(8,128)(2,1)S(1)}, bf16[64,1280]{1,0:T(8,128)(2,1)S(1)}, u32[]{:S(2)}, u32[]{:S(2)}) collective-permute-start(bf16[64,1280]{1,0:T(8,128)(2,1)S(1)} %add_convert_fusion.6.refs_0_), channel_id=1, source_target_pairs={{0,1},{1,0},{2,3},{3,2},{4,5},{5,4},{6,7},{7,6},{8,9},{9,8},{10,11... | collective-permute-start | bytes 491528 | tf_op jit(solution)/shard_map/ppermute | solution.py:489
  51.5 3.1 %collective-permute-done.11 = bf16[64,1280]{1,0:T(8,128)(2,1)S(1)} collective-permute-done((bf16[64,1280]{1,0:T(8,128)(2,1)S(1)}, bf16[64,1280]{1,0:T(8,128)(2,1)S(1)}, u32[]{:S(2)}, u32[]{:S(2)}) %collective-permute-start.11) | collective-permute-done | bytes 163872 | tf_op jit(solution)/shard_map/ppermute | solution.py:489
  54.5 0.1 add_convert_fusion.4.refs_1_
  54.6 0.3 collective-permute-start.12
  54.9 2.3 %feed_forward.2 = (bf16[64,896]{1,0:T(8,128)(2,1)S(1)}, bf16[64,1280]{1,0:T(8,128)(2,1)S(1)}) custom-call(bf16[64,1280]{1,0:T(8,128)(2,1)S(1)} %add_convert_fusion.6.refs_0_, bf16[64,1280]{1,0:T(8,128)(2,1)S(1)} %add_convert_fusion.4.refs_1_, bf16[1,2560]{1,0:T(2,128)(2,1)S(1)} %reshape.16.refs_2_, bf16[2560,896]{1,0:T(8,128)(2,1)S(1)} %get-tuple-element.64.refs_3_, ...), custom_call_target="tpu_custom_call" | custom-call | flops 880803840 | bytes 13762560 | tf_op jit(solution)/shard_map/feed_forward/pallas_call | solution.py:410
  57.2 1.9 %collective-permute-start.14 = (bf16[64,1280]{1,0:T(8,128)(2,1)S(1)}, bf16[64,1280]{1,0:T(8,128)(2,1)S(1)}, u32[]{:S(2)}, u32[]{:S(2)}) collective-permute-start(bf16[64,1280]{1,0:T(8,128)(2,1)S(1)} %get-tuple-element.71), channel_id=1, source_target_pairs={{0,1},{1,0},{2,3},{3,2},{4,5},{5,4},{6,7},{7,6},{8,9},{9,8},{10,11... | collective-permute-start | bytes 491528 | tf_op jit(solution)/shard_map/ppermute | solution.py:489
  59.0 2.8 %collective-permute-done.12.refs_1_ = bf16[64,1280]{1,0:T(8,128)(2,1)S(1)} collective-permute-done((bf16[64,1280]{1,0:T(8,128)(2,1)S(1)}, bf16[64,1280]{1,0:T(8,128)(2,1)S(1)}, u32[]{:S(2)}, u32[]{:S(2)}) %collective-permute-start.12) | collective-permute-done | bytes 163872 | tf_op jit(solution)/shard_map/ppermute | solution.py:489
  61.8 2.5 %feed_forward.3 = (bf16[64,1280]{1,0:T(8,128)(2,1)S(1)}, f32[64,1280]{1,0:T(8,128)S(1)}, f32[64,1280]{1,0:T(8,128)S(1)}) custom-call(bf16[64,1280]{1,0:T(8,128)(2,1)S(1)} %collective-permute-done.9.refs_0_, bf16[64,1280]{1,0:T(8,128)(2,1)S(1)} %collective-permute-done.12.refs_1_, bf16[1,2560]{1,0:T(2,128)(2,1)S(1)} %reshape.16.refs_2_, ...), custom_call_target="tpu_custom_call" | custom-call | flops 880803840 | bytes 13762560 | tf_op jit(solution)/shard_map/feed_forward/pallas_call | solution.py:410
  64.3 0.1 collective-permute-start.13
  64.4 0.6 collective-permute-done.14
  65.0 3.1 %collective-permute-start.17 = (bf16[64,1280]{1,0:T(8,128)(2,1)S(1)}, bf16[64,1280]{1,0:T(8,128)(2,1)S(1)}, u32[]{:S(2)}, u32[]{:S(2)}) collective-permute-start(bf16[64,1280]{1,0:T(8,128)(2,1)S(1)} %add_convert_fusion.3), channel_id=1, source_target_pairs={{0,2},{1,3},{2,0},{3,1},{4,6},{5,7},{6,4},{7,5},{8,10},{9,11},{10,... | collective-permute-start | bytes 491528 | tf_op jit(solution)/shard_map/ppermute | solution.py:489
  68.1 1.9 %stage.3.refs_3_ = bf16[2560,640]{1,0:T(8,128)(2,1)S(1)} custom-call(bf16[2560,640]{1,0:T(8,128)(2,1)} %refs_0_.1), custom_call_target="tpu_custom_call" | custom-call | bytes 3276800 | tf_op jit(solution)/shard_map/stage/pallas_call | solution.py:372
  70.1 2.9 %collective-permute-done.13 = bf16[64,1280]{1,0:T(8,128)(2,1)S(1)} collective-permute-done((bf16[64,1280]{1,0:T(8,128)(2,1)S(1)}, bf16[64,1280]{1,0:T(8,128)(2,1)S(1)}, u32[]{:S(2)}, u32[]{:S(2)}) %collective-permute-start.13) | collective-permute-done | bytes 163872 | tf_op jit(solution)/shard_map/ppermute | solution.py:489
  73.0 0.2 collective-permute-start.15
  73.2 6.0 %collective-permute-done.17 = bf16[64,1280]{1,0:T(8,128)(2,1)S(1)} collective-permute-done((bf16[64,1280]{1,0:T(8,128)(2,1)S(1)}, bf16[64,1280]{1,0:T(8,128)(2,1)S(1)}, u32[]{:S(2)}, u32[]{:S(2)}) %collective-permute-start.17) | collective-permute-done | bytes 163872 | tf_op jit(solution)/shard_map/ppermute | solution.py:489
  79.2 0.1 add_convert_fusion.refs_1_.refs_8_
  79.3 0.6 collective-permute-start.18
  79.9 2.6 %collective-permute-done.15 = bf16[64,1280]{1,0:T(8,128)(2,1)S(1)} collective-permute-done((bf16[64,1280]{1,0:T(8,128)(2,1)S(1)}, bf16[64,1280]{1,0:T(8,128)(2,1)S(1)}, u32[]{:S(2)}, u32[]{:S(2)}) %collective-permute-start.15) | collective-permute-done | bytes 163872 | tf_op jit(solution)/shard_map/ppermute | solution.py:489
  82.5 0.1 add_convert_fusion.1.refs_0_.refs_7_
  82.6 0.3 collective-permute-start.16
  82.9 1.2 %next_layer.2 = (bf16[64,640]{1,0:T(8,128)(2,1)S(1)}, bf16[320,64]{1,0:T(8,128)(2,1)S(1)}) custom-call(bf16[64,1280]{1,0:T(8,128)(2,1)S(1)} %add_convert_fusion.1.refs_0_.refs_7_, bf16[64,1280]{1,0:T(8,128)(2,1)S(1)} %add_convert_fusion.refs_1_.refs_8_, bf16[1,2560]{1,0:T(2,128)(2,1)S(1)} %reshape.17.refs_2_, bf16[2560,640]{1,0:T(8,128)(2,1)S(1)} %stage.3.refs_3_, ...), custom_call_target="tpu_custom_call" | custom-call | flops 314572800 | bytes 4915200 | tf_op jit(solution)/shard_map/next_layer/pallas_call | solution.py:472
  84.1 2.4 %collective-permute-done.18.refs_1_ = bf16[64,1280]{1,0:T(8,128)(2,1)S(1)} collective-permute-done((bf16[64,1280]{1,0:T(8,128)(2,1)S(1)}, bf16[64,1280]{1,0:T(8,128)(2,1)S(1)}, u32[]{:S(2)}, u32[]{:S(2)}) %collective-permute-start.18) | collective-permute-done | bytes 163872 | tf_op jit(solution)/shard_map/ppermute | solution.py:489
  86.5 2.9 %collective-permute-done.16.refs_0_ = bf16[64,1280]{1,0:T(8,128)(2,1)S(1)} collective-permute-done((bf16[64,1280]{1,0:T(8,128)(2,1)S(1)}, bf16[64,1280]{1,0:T(8,128)(2,1)S(1)}, u32[]{:S(2)}, u32[]{:S(2)}) %collective-permute-start.16) | collective-permute-done | bytes 163872 | tf_op jit(solution)/shard_map/ppermute | solution.py:489
  89.4 2.1 %next_layer.3 = (bf16[128,640]{1,0:T(8,128)(2,1)}, bf16[320,128]{1,0:T(8,128)(2,1)}, bf16[32,2560]{1,0:T(8,128)(2,1)}) custom-call(bf16[64,1280]{1,0:T(8,128)(2,1)S(1)} %collective-permute-done.16.refs_0_, bf16[64,1280]{1,0:T(8,128)(2,1)S(1)} %collective-permute-done.18.refs_1_, bf16[1,2560]{1,0:T(2,128)(2,1)S(1)} %reshape.17.refs_2_, ...), custom_call_target="tpu_custom_call" | custom-call | flops 314572800 | bytes 4915200 | tf_op jit(solution)/shard_map/next_layer/pallas_call | solution.py:472
  (27 shorter events, 0.2 us)
Async XLA Ops:
  1.7 5.6 %collective-permute-start.1 = (bf16[512,384]{1,0:T(8,128)(2,1)S(1)}, bf16[512,384]{1,0:T(8,128)(2,1)S(1)}, u32[]{:S(2)}, u32[]{:S(2)}) collective-permute-start(bf16[512,384]{1,0:T(8,128)(2,1)S(1)} %pool_rows.1.refs_0_), channel_id=1, source_target_pairs={{0,4},{4,0},{8,12},{12,8},{16,20},{20,16},{24,28},{28,24},{1,5},{5... | collective-permute-start | bytes 1179656 | tf_op jit(solution)/shard_map/ppermute | solution.py:489
  2.2 11.4 %collective-permute-start = (bf16[512,384]{1,0:T(8,128)(2,1)S(1)}, bf16[512,384]{1,0:T(8,128)(2,1)S(1)}, u32[]{:S(2)}, u32[]{:S(2)}) collective-permute-start(bf16[512,384]{1,0:T(8,128)(2,1)S(1)} %pool_rows.1.refs_0_), channel_id=1, source_target_pairs={{0,8},{4,20},{8,0},{12,28},{16,24},{20,4},{24,16},{28,12},{1,9},{5... | collective-permute-start | bytes 1179656 | tf_op jit(solution)/shard_map/ppermute | solution.py:495
  4.8 11.5 %collective-permute-start.2 = (bf16[512,384]{1,0:T(8,128)(2,1)S(1)}, bf16[512,384]{1,0:T(8,128)(2,1)S(1)}, u32[]{:S(2)}, u32[]{:S(2)}) collective-permute-start(bf16[512,384]{1,0:T(8,128)(2,1)S(1)} %pool_rows.1.refs_0_), channel_id=1, source_target_pairs={{0,16},{4,12},{8,24},{12,4},{16,0},{20,28},{24,8},{28,20},{1,17},{... | collective-permute-start | bytes 1179656 | tf_op jit(solution)/shard_map/ppermute | solution.py:495
  7.3 1.0 %copy-start.3 = (bf16[16,32,320]{2,1,0:T(8,128)(2,1)S(1)}, bf16[16,32,320]{2,1,0:T(8,128)(2,1)}, u32[]{:S(2)}) copy-start(bf16[16,32,320]{2,1,0:T(8,128)(2,1)} %leaf_ref.1) | copy-start | bytes 983044
  8.3 0.9 %copy-start.4 = (bf16[128,640]{1,0:T(8,128)(2,1)S(1)}, bf16[128,640]{1,0:T(8,128)(2,1)}, u32[]{:S(2)}) copy-start(bf16[128,640]{1,0:T(8,128)(2,1)} %query_ref.1) | copy-start | bytes 491524
  13.6 13.8 %copy-start = (bf16[640,2560]{1,0:T(8,128)(2,1)S(1)}, bf16[640,2560]{1,0:T(8,128)(2,1)}, u32[]{:S(2)}) copy-start(bf16[640,2560]{1,0:T(8,128)(2,1)} %refs_3_.3) | copy-start | bytes 9830404
  13.7 8.4 %collective-permute-start.5 = (bf16[512,384]{1,0:T(8,128)(2,1)S(1)}, bf16[512,384]{1,0:T(8,128)(2,1)S(1)}, u32[]{:S(2)}, u32[]{:S(2)}) collective-permute-start(bf16[512,384]{1,0:T(8,128)(2,1)S(1)} %collective-permute-done.refs_2_), channel_id=1, source_target_pairs={{0,16},{4,12},{8,24},{12,4},{16,0},{20,28},{24,8},{28,20},{1,17},{... | collective-permute-start | bytes 1179656 | tf_op jit(solution)/shard_map/ppermute | solution.py:495
  16.3 5.8 %collective-permute-start.3 = (bf16[512,384]{1,0:T(8,128)(2,1)S(1)}, bf16[512,384]{1,0:T(8,128)(2,1)S(1)}, u32[]{:S(2)}, u32[]{:S(2)}) collective-permute-start(bf16[512,384]{1,0:T(8,128)(2,1)S(1)} %collective-permute-done.refs_2_), channel_id=1, source_target_pairs={{0,4},{4,0},{8,12},{12,8},{16,20},{20,16},{24,28},{28,24},{1,5},{5... | collective-permute-start | bytes 1179656 | tf_op jit(solution)/shard_map/ppermute | solution.py:489
  16.3 5.8 %collective-permute-start.4 = (bf16[512,384]{1,0:T(8,128)(2,1)S(1)}, bf16[512,384]{1,0:T(8,128)(2,1)S(1)}, u32[]{:S(2)}, u32[]{:S(2)}) collective-permute-start(bf16[512,384]{1,0:T(8,128)(2,1)S(1)} %collective-permute-done.2.refs_3_), channel_id=1, source_target_pairs={{0,4},{4,0},{8,12},{12,8},{16,20},{20,16},{24,28},{28,24},{1,5},{5... | collective-permute-start | bytes 1179656 | tf_op jit(solution)/shard_map/ppermute | solution.py:489
  22.0 5.4 %collective-permute-start.6 = (bf16[512,384]{1,0:T(8,128)(2,1)S(1)}, bf16[512,384]{1,0:T(8,128)(2,1)S(1)}, u32[]{:S(2)}, u32[]{:S(2)}) collective-permute-start(bf16[512,384]{1,0:T(8,128)(2,1)S(1)} %collective-permute-done.5.refs_2_), channel_id=1, source_target_pairs={{0,4},{4,0},{8,12},{12,8},{16,20},{20,16},{24,28},{28,24},{1,5},{5... | collective-permute-start | bytes 1179656 | tf_op jit(solution)/shard_map/ppermute | solution.py:489
  25.6 6.0 %copy-start.5 = (bf16[2560]{0:T(1024)(128)(2,1)S(1)}, bf16[2560]{0:T(1024)(128)(2,1)}, u32[]{:S(2)}) copy-start(bf16[2560]{0:T(1024)(128)(2,1)} %param.33) | copy-start | bytes 15364
  25.6 6.0 %copy-start.2 = (bf16[128,2560]{1,0:T(8,128)(2,1)S(1)}, bf16[128,2560]{1,0:T(8,128)(2,1)}, u32[]{:S(2)}) copy-start(bf16[128,2560]{1,0:T(8,128)(2,1)} %refs_5_.1) | copy-start | bytes 1966084
  29.6 6.9 %collective-permute-start.7 = (bf16[64,1280]{1,0:T(8,128)(2,1)S(1)}, bf16[64,1280]{1,0:T(8,128)(2,1)S(1)}, u32[]{:S(2)}, u32[]{:S(2)}) collective-permute-start(bf16[64,1280]{1,0:T(8,128)(2,1)S(1)} %get-tuple-element.53), channel_id=1, source_target_pairs={{0,1},{1,0},{2,3},{3,2},{4,5},{5,4},{6,7},{7,6},{8,9},{9,8},{10,11... | collective-permute-start | bytes 491528 | tf_op jit(solution)/shard_map/ppermute | solution.py:489
  34.1 10.3 %collective-permute-start.10 = (bf16[64,1280]{1,0:T(8,128)(2,1)S(1)}, bf16[64,1280]{1,0:T(8,128)(2,1)S(1)}, u32[]{:S(2)}, u32[]{:S(2)}) collective-permute-start(bf16[64,1280]{1,0:T(8,128)(2,1)S(1)} %get-tuple-element.56), channel_id=1, source_target_pairs={{0,1},{1,0},{2,3},{3,2},{4,5},{5,4},{6,7},{7,6},{8,9},{9,8},{10,11... | collective-permute-start | bytes 491528 | tf_op jit(solution)/shard_map/ppermute | solution.py:489
  36.5 10.5 %collective-permute-start.8 = (bf16[64,1280]{1,0:T(8,128)(2,1)S(1)}, bf16[64,1280]{1,0:T(8,128)(2,1)S(1)}, u32[]{:S(2)}, u32[]{:S(2)}) collective-permute-start(bf16[64,1280]{1,0:T(8,128)(2,1)S(1)} %add_convert_fusion.7), channel_id=1, source_target_pairs={{0,2},{1,3},{2,0},{3,1},{4,6},{5,7},{6,4},{7,5},{8,10},{9,11},{10,... | collective-permute-start | bytes 491528 | tf_op jit(solution)/shard_map/ppermute | solution.py:489
  44.4 10.1 %collective-permute-start.11 = (bf16[64,1280]{1,0:T(8,128)(2,1)S(1)}, bf16[64,1280]{1,0:T(8,128)(2,1)S(1)}, u32[]{:S(2)}, u32[]{:S(2)}) collective-permute-start(bf16[64,1280]{1,0:T(8,128)(2,1)S(1)} %add_convert_fusion.5), channel_id=1, source_target_pairs={{0,2},{1,3},{2,0},{3,1},{4,6},{5,7},{6,4},{7,5},{8,10},{9,11},{10,... | collective-permute-start | bytes 491528 | tf_op jit(solution)/shard_map/ppermute | solution.py:489
  47.1 12.0 %collective-permute-start.9 = (bf16[64,1280]{1,0:T(8,128)(2,1)S(1)}, bf16[64,1280]{1,0:T(8,128)(2,1)S(1)}, u32[]{:S(2)}, u32[]{:S(2)}) collective-permute-start(bf16[64,1280]{1,0:T(8,128)(2,1)S(1)} %add_convert_fusion.6.refs_0_), channel_id=1, source_target_pairs={{0,1},{1,0},{2,3},{3,2},{4,5},{5,4},{6,7},{7,6},{8,9},{9,8},{10,11... | collective-permute-start | bytes 491528 | tf_op jit(solution)/shard_map/ppermute | solution.py:489
  54.6 7.2 %collective-permute-start.12 = (bf16[64,1280]{1,0:T(8,128)(2,1)S(1)}, bf16[64,1280]{1,0:T(8,128)(2,1)S(1)}, u32[]{:S(2)}, u32[]{:S(2)}) collective-permute-start(bf16[64,1280]{1,0:T(8,128)(2,1)S(1)} %add_convert_fusion.4.refs_1_), channel_id=1, source_target_pairs={{0,1},{1,0},{2,3},{3,2},{4,5},{5,4},{6,7},{7,6},{8,9},{9,8},{10,11... | collective-permute-start | bytes 491528 | tf_op jit(solution)/shard_map/ppermute | solution.py:489
  57.2 7.8 %collective-permute-start.14 = (bf16[64,1280]{1,0:T(8,128)(2,1)S(1)}, bf16[64,1280]{1,0:T(8,128)(2,1)S(1)}, u32[]{:S(2)}, u32[]{:S(2)}) collective-permute-start(bf16[64,1280]{1,0:T(8,128)(2,1)S(1)} %get-tuple-element.71), channel_id=1, source_target_pairs={{0,1},{1,0},{2,3},{3,2},{4,5},{5,4},{6,7},{7,6},{8,9},{9,8},{10,11... | collective-permute-start | bytes 491528 | tf_op jit(solution)/shard_map/ppermute | solution.py:489
  64.3 8.7 %collective-permute-start.13 = (bf16[64,1280]{1,0:T(8,128)(2,1)S(1)}, bf16[64,1280]{1,0:T(8,128)(2,1)S(1)}, u32[]{:S(2)}, u32[]{:S(2)}) collective-permute-start(bf16[64,1280]{1,0:T(8,128)(2,1)S(1)} %get-tuple-element.69), channel_id=1, source_target_pairs={{0,1},{1,0},{2,3},{3,2},{4,5},{5,4},{6,7},{7,6},{8,9},{9,8},{10,11... | collective-permute-start | bytes 491528 | tf_op jit(solution)/shard_map/ppermute | solution.py:489
  65.0 17.9 %copy-start.6 = (bf16[2560]{0:T(1024)(128)(2,1)S(1)}, bf16[2560]{0:T(1024)(128)(2,1)}, u32[]{:S(2)}) copy-start(bf16[2560]{0:T(1024)(128)(2,1)} %param.37) | copy-start | bytes 15364
  65.0 17.9 %copy-start.1 = (bf16[2560,320]{0,1:T(8,128)(2,1)S(1)}, bf16[2560,320]{0,1:T(8,128)(2,1)}, u32[]{:S(2)}) copy-start(bf16[2560,320]{0,1:T(8,128)(2,1)} %param.39) | copy-start | bytes 4915204
  65.0 14.2 %collective-permute-start.17 = (bf16[64,1280]{1,0:T(8,128)(2,1)S(1)}, bf16[64,1280]{1,0:T(8,128)(2,1)S(1)}, u32[]{:S(2)}, u32[]{:S(2)}) collective-permute-start(bf16[64,1280]{1,0:T(8,128)(2,1)S(1)} %add_convert_fusion.3), channel_id=1, source_target_pairs={{0,2},{1,3},{2,0},{3,1},{4,6},{5,7},{6,4},{7,5},{8,10},{9,11},{10,... | collective-permute-start | bytes 491528 | tf_op jit(solution)/shard_map/ppermute | solution.py:489
  73.0 9.5 %collective-permute-start.15 = (bf16[64,1280]{1,0:T(8,128)(2,1)S(1)}, bf16[64,1280]{1,0:T(8,128)(2,1)S(1)}, u32[]{:S(2)}, u32[]{:S(2)}) collective-permute-start(bf16[64,1280]{1,0:T(8,128)(2,1)S(1)} %add_convert_fusion.2), channel_id=1, source_target_pairs={{0,2},{1,3},{2,0},{3,1},{4,6},{5,7},{6,4},{7,5},{8,10},{9,11},{10,... | collective-permute-start | bytes 491528 | tf_op jit(solution)/shard_map/ppermute | solution.py:489
  79.3 7.2 %collective-permute-start.18 = (bf16[64,1280]{1,0:T(8,128)(2,1)S(1)}, bf16[64,1280]{1,0:T(8,128)(2,1)S(1)}, u32[]{:S(2)}, u32[]{:S(2)}) collective-permute-start(bf16[64,1280]{1,0:T(8,128)(2,1)S(1)} %add_convert_fusion.refs_1_.refs_8_), channel_id=1, source_target_pairs={{0,1},{1,0},{2,3},{3,2},{4,5},{5,4},{6,7},{7,6},{8,9},{9,8},{10,11... | collective-permute-start | bytes 491528 | tf_op jit(solution)/shard_map/ppermute | solution.py:489
  82.6 6.9 %collective-permute-start.16 = (bf16[64,1280]{1,0:T(8,128)(2,1)S(1)}, bf16[64,1280]{1,0:T(8,128)(2,1)S(1)}, u32[]{:S(2)}, u32[]{:S(2)}) collective-permute-start(bf16[64,1280]{1,0:T(8,128)(2,1)S(1)} %add_convert_fusion.1.refs_0_.refs_7_), channel_id=1, source_target_pairs={{0,1},{1,0},{2,3},{3,2},{4,5},{5,4},{6,7},{7,6},{8,9},{9,8},{10,11... | collective-permute-start | bytes 491528 | tf_op jit(solution)/shard_map/ppermute | solution.py:489

commit v8 on v6

--- a/solution.py
+++ b/solution.py
@@ -383,15 +383,60 @@
     )(*in_hbm(weights))
 
 
-def mlp_kernel(*refs, second):
+def gained(rows, gain_ref, k):
+    return (wide(rows) * wide(gain_ref[:, piece(gain_ref.shape[1], k)])).astype(bf16)
+
+
+def inverse_rms(row_refs):
+    squares = [jnp.sum(wide(ref[...]) ** 2, axis=-1, keepdims=True) for ref in row_refs]
+    depth = sum(ref.shape[1] for ref in row_refs)
+    return lax.rsqrt(sum(squares) / depth + EPSILON)
+
+
+def times(rows, weight_ref, k):
+    weight = weight_ref[piece(weight_ref.shape[0], k), :]
+    return jnp.dot(rows, weight, preferred_element_type=f32)
+
+
+def early_kernel(rows_ref, gain_ref, *refs):
+    rows = gained(rows_ref[...], gain_ref, 0)
+    count = len(refs) // 2
+    for weight_ref, out_ref in zip(refs[:count], refs[count:]):
+        out_ref[...] = times(rows, weight_ref, 0)
+
+
+def early_products(rows, gain, weights):
+    count = rows.shape[0]
+    shapes = [jax.ShapeDtypeStruct((count, w.shape[1]), f32) for w in weights]
+    return pl.pallas_call(
+        early_kernel,
+        out_shape=tuple(shapes),
+        in_specs=[VMEM] * (2 + len(weights)),
+        out_specs=(VMEM,) * len(weights),
+        compiler_params=PARAMS,
+        cost_estimate=pl.CostEstimate(
+            flops=sum(w.size for w in weights) * count,
+            bytes_accessed=sum(w.size for w in weights),
+            transcendentals=0,
+        ),
+        name="early_piece",
+    )(rows, gain.reshape(1, -1), *in_vmem(weights))
+
+
+def mlp_kernel(*refs, second, early):
     row_refs, (gain_ref, gate_ref, up_ref, down_ref) = refs[:PIECES], refs[PIECES : PIECES + 4]
     refs = refs[PIECES + 4 :]
+    sums = [0.0, 0.0]
+    if early:
+        sums, refs = [ref[...] for ref in refs[:2]], refs[2:]
     if second:
         project(refs[1:PIECES], refs[0][...], down_ref, range(PIECES - 1))
-    normed = normalized(joined(row_refs), gain_ref[...])
-    gate = jnp.dot(normed, gate_ref[...], preferred_element_type=f32)
-    upward = jnp.dot(normed, up_ref[...], preferred_element_type=f32)
-    hidden = (jax.nn.silu(gate) * upward).astype(bf16)
+    scale = inverse_rms(row_refs)
+    for k in range(early, PIECES):
+        rows = gained(row_refs[k][...], gain_ref, k)
+        sums = [item + times(rows, ref, k) for item, ref in zip(sums, (gate_ref, up_ref))]
+    gate, upward = sums
+    hidden = (jax.nn.silu(gate * scale) * (upward * scale)).astype(bf16)
     if second:
         project(refs[PIECES:], hidden, down_ref, range(PIECES))
     else:
@@ -399,7 +444,7 @@
         project(refs[1:], hidden, down_ref, [PIECES - 1])
 
 
-def feed_forward(rows, gain, gate_weight, up_weight, down_weight, other=()):
+def feed_forward(rows, early, gain, gate_weight, up_weight, down_weight, other=()):
     count = rows[0].shape[0]
     depth, width = gate_weight.shape
     sent = pieces_of(count, depth, bf16)
@@ -408,16 +453,22 @@
     else:
         shapes = (jax.ShapeDtypeStruct((count, width), bf16), sent[-1])
     return pl.pallas_call(
-        functools.partial(mlp_kernel, second=len(other) > 0),
+        functools.partial(mlp_kernel, second=len(other) > 0, early=min(len(early), 1)),
         out_shape=shapes,
-        in_specs=[VMEM] * (PIECES + 4 + len(other)),
+        in_specs=[VMEM] * (PIECES + 4 + len(early) + len(other)),
         out_specs=(VMEM,) * len(shapes),
         compiler_params=PARAMS,
         cost_estimate=pl.CostEstimate(
             flops=6 * count * depth * width, bytes_accessed=6 * depth * width, transcendentals=0
         ),
         name="feed_forward",
-    )(*rows, gain.reshape(1, depth), *in_vmem((gate_weight, up_weight, down_weight)), *other)
+    )(
+        *rows,
+        gain.reshape(1, depth),
+        *in_vmem((gate_weight, up_weight, down_weight)),
+        *early,
+        *other,
+    )
 
 
 def next_kernel(*refs, half):
@@ -599,9 +650,11 @@
         mlp = (*staged, down_weight)
         mixed_mine = each(add_rows, pair, res_mine, got)
         mixed_theirs = trades(mixed_mine, 1)
-        hidden, last = feed_forward(mixed_mine, norm_gain, *mlp)
+        hidden, last = feed_forward(mixed_mine, (), norm_gain, *mlp)
         last = trade(last, "tp", 1)
-        result = feed_forward(mixed_theirs, norm_gain, *mlp, [hidden])
+        early = early_products(mixed_theirs[0], norm_gain, mlp[:2])
+        _, mixed_theirs[1:] = lax.optimization_barrier((early, mixed_theirs[1:]))
+        result = feed_forward(mixed_theirs, early, norm_gain, *mlp, [hidden])
         got = [*trades(result[: PIECES - 1], 1), last]
         mlp_theirs = result[PIECES - 1 :]
         pair, (query_weight,) = pairs_in_turn(mlp_theirs, got, (query_weight,))
@@ -626,8 +679,8 @@
             for h in range(2)
         ]
         mlp_weights = (gate_weight, up_weight, down_weight)
-        hidden, last = feed_forward(mixed_halves[0], norm_gain, *mlp_weights)
-        result = feed_forward(mixed_halves[1], norm_gain, *mlp_weights, [hidden])
+        hidden, last = feed_forward(mixed_halves[0], (), norm_gain, *mlp_weights)
+        result = feed_forward(mixed_halves[1], (), norm_gain, *mlp_weights, [hidden])
         halves = [[*result[: PIECES - 1], last], result[PIECES - 1 :]]
         mlp = [jnp.concatenate([wide(item) for item in half], axis=1) for half in halves]
         mlp = lax.psum(jnp.concatenate(mlp, axis=0), "tp")

time: 87.3 us -> 87.1 us (level)
    pallas_call x2 -> x3, Pallas kernels: 4.76 us -> 4.88 us  [the longest x2 4.07 us: feed_forward(): pl.pallas_call(functools.partial(mlp_kernel, second=len(other) > 0, early...]
  transfers between devices with their start and end apart: 19 -> 19, of which waited for: 13 -> 14; matrix products, arithmetic and copies ran while one was open for 2% -> 2% of each run, Pallas kernels for 29% -> 30%
where the time goes in v8:
time: 87.1 us; the launch traced here: 86.8 us
  Pallas kernels  31 us (36%)
  waiting for transfers between devices  29.8 us (34%)
  starting transfers between devices  21.8 us (25%)
  local copies, waits for them, and re-layouts  2.94 us (3%)
    ppermute x16, waiting for transfers between devices, trade(): return lax.ppermute(value, axis, [(i, i ^ bit) for i in range(size)])  28.3 us
    ppermute x16, starting transfers between devices, trade(): return lax.ppermute(value, axis, [(i, i ^ bit) for i in range(size)])  15.9 us
    pallas_call x3, Pallas kernels, stage(): pl.pallas_call(stage_kernel, out_shape=tuple((pltpu.VMEM(w.shape, w.dtype...  8.11 us
    ppermute x3, starting transfers between devices, cross(): return lax.ppermute(value, 'req', pairs)  5.83 us
    pallas_call x2, Pallas kernels, extend_attention(): pl.pallas_call(functools.partial(chunk_kernel, blocks=2 * kv_local), out_...  5.36 us
    pallas_call x2, Pallas kernels, finish_attention(): pl.pallas_call(functools.partial(finish_kernel, half=half, kv_local=kv_lo...  4.57 us
    pallas_call x2, Pallas kernels, feed_forward(): pl.pallas_call(functools.partial(mlp_kernel, second=len(other) > 0, early...  4.07 us
    pallas_call x1, Pallas kernels, start_attention(): pl.pallas_call(functools.partial(local_kernel, chunks=len(pools)), out_sh...  3.77 us
  transfers between devices with their start and end apart: 19, of which 14 were waited for; matrix products, arithmetic and copies ran while one was open for 2% of the time, Pallas kernels for 30%

profile of v8, /device:TPU:0, one launch (start us, length us, event | category | flops | bytes accessed | tf_op | source)
XLA Modules:
  0.0 86.8 jit_solution(15321208486699196866)
XLA Ops:
  0.6 1.1 %pool_rows.1.refs_0_ = bf16[512,384]{1,0:T(8,128)(2,1)S(1)} custom-call(s32[32]{0:T(128)} %node_hbm.1, s32[32]{0:T(128)} %rank_hbm.1, s32[8]{0:T(128)} %length_hbm.1, s32[6]{0:T(128)} %root_hbm.1, bf16[32,16,320]{2,1,0:T(8,128)(2,1)} %pool_hbm.1), custom_call_target="tpu_custom_call" | custom-call | tf_op jit(solution)/shard_map/pool_rows/pallas_call | solution.py:128
  1.7 0.5 collective-permute-start.1
  2.2 2.6 %collective-permute-start = (bf16[512,384]{1,0:T(8,128)(2,1)S(1)}, bf16[512,384]{1,0:T(8,128)(2,1)S(1)}, u32[]{:S(2)}, u32[]{:S(2)}) collective-permute-start(bf16[512,384]{1,0:T(8,128)(2,1)S(1)} %pool_rows.1.refs_0_), channel_id=1, source_target_pairs={{0,8},{4,20},{8,0},{12,28},{16,24},{20,4},{24,16},{28,12},{1,9},{5... | collective-permute-start | bytes 1179656 | tf_op jit(solution)/shard_map/ppermute | solution.py:546
  4.8 1.5 %collective-permute-start.3 = (bf16[512,384]{1,0:T(8,128)(2,1)S(1)}, bf16[512,384]{1,0:T(8,128)(2,1)S(1)}, u32[]{:S(2)}, u32[]{:S(2)}) collective-permute-start(bf16[512,384]{1,0:T(8,128)(2,1)S(1)} %pool_rows.1.refs_0_), channel_id=1, source_target_pairs={{0,16},{4,12},{8,24},{12,4},{16,0},{20,28},{24,8},{28,20},{1,17},{... | collective-permute-start | bytes 1179656 | tf_op jit(solution)/shard_map/ppermute | solution.py:546
  6.3 1.0 %copy.24.keyval_ref = bf16[128,320]{1,0:T(8,128)(2,1)S(1)} copy(bf16[128,320]{0,1:T(8,128)(2,1)} %param.21) | data formatting | bytes 163840 | tf_op args[1]
  7.3 1.0 %copy-done.3 = bf16[16,32,320]{2,1,0:T(8,128)(2,1)S(1)} copy-done((bf16[16,32,320]{2,1,0:T(8,128)(2,1)S(1)}, bf16[16,32,320]{2,1,0:T(8,128)(2,1)}, u32[]{:S(2)}) %copy-start.3) | copy-done | bytes 327704
  8.3 0.9 %copy-done.4 = bf16[128,640]{1,0:T(8,128)(2,1)S(1)} copy-done((bf16[128,640]{1,0:T(8,128)(2,1)S(1)}, bf16[128,640]{1,0:T(8,128)(2,1)}, u32[]{:S(2)}) %copy-start.4) | copy-done | bytes 163864
  9.2 3.8 %attend_local.1 = (bf16[1024,256]{1,0:T(8,128)(2,1)S(1)}, f32[1024,256]{1,0:T(8,128)S(1)}) custom-call(s32[1,16]{1,0:T(1,128)} %count_hbm.1, s32[16]{0:T(128)} %mid_hbm.1, s32[16]{0:T(128)} %leaf_len_hbm.1, bf16[128,640]{1,0:T(8,128)(2,1)S(1)} %copy-done.4, bf16[128,320]{1,0:T(8,128)(2,1)S(1)} %copy.24.keyval_ref, bf16[16,32,320]{2,1,0:T(8,128)(2,1)S(1)} %copy-done.3, ...), custom_call_target="tpu_custom_call" | custom-call | flops 1744830464 | bytes 2097152 | tf_op jit(solution)/shard_map/attend_local/pallas_call | solution.py:242
  13.0 0.6 collective-permute-done.refs_2_
  13.6 0.9 %collective-permute-done.3.refs_3_ = bf16[512,384]{1,0:T(8,128)(2,1)S(1)} collective-permute-done((bf16[512,384]{1,0:T(8,128)(2,1)S(1)}, bf16[512,384]{1,0:T(8,128)(2,1)S(1)}, u32[]{:S(2)}, u32[]{:S(2)}) %collective-permute-start.3) | collective-permute-done | bytes 393248 | tf_op jit(solution)/shard_map/ppermute | solution.py:546
  14.5 0.1 collective-permute-start.4
  14.7 0.4 collective-permute-start.5
  15.0 1.8 %collective-permute-start.2 = (bf16[512,384]{1,0:T(8,128)(2,1)S(1)}, bf16[512,384]{1,0:T(8,128)(2,1)S(1)}, u32[]{:S(2)}, u32[]{:S(2)}) collective-permute-start(bf16[512,384]{1,0:T(8,128)(2,1)S(1)} %collective-permute-done.refs_2_), channel_id=1, source_target_pairs={{0,16},{4,12},{8,24},{12,4},{16,0},{20,28},{24,8},{28,20},{1,17},{... | collective-permute-start | bytes 1179656 | tf_op jit(solution)/shard_map/ppermute | solution.py:546
  16.8 3.6 %attend_pages.2.refs_1_ = f32[1024,256]{1,0:T(8,128)S(1)} custom-call(bf16[1024,256]{1,0:T(8,128)(2,1)S(1)} %get-tuple-element.51.refs_0_, f32[1024,256]{1,0:T(8,128)S(1)} %get-tuple-element.53.refs_1_, bf16[512,384]{1,0:T(8,128)(2,1)S(1)} %collective-permute-done.refs_2_, bf16[512,384]{1,0:T(8,128)(2,1)S(1)} %collective-permute-done.3.refs_3_, ...), custom_call_target="tpu_custom_call" | custom-call | flops 2147483648 | bytes 2097152 | tf_op jit(solution)/shard_map/attend_pages/pallas_call | solution.py:281
  20.4 2.5 %stage.3.refs_5_ = bf16[896,2560]{1,0:T(8,128)(2,1)S(1)} custom-call(bf16[896,2560]{1,0:T(8,128)(2,1)} %refs_0_), custom_call_target="tpu_custom_call" | custom-call | bytes 4587520 | tf_op jit(solution)/shard_map/stage/pallas_call | solution.py:372
  22.9 0.2 collective-permute-start.6
  23.1 1.8 %attend_pages.3.refs_1_ = f32[1024,256]{1,0:T(8,128)S(1)} custom-call(bf16[1024,256]{1,0:T(8,128)(2,1)S(1)} %get-tuple-element.51.refs_0_, f32[1024,256]{1,0:T(8,128)S(1)} %attend_pages.2.refs_1_, bf16[512,384]{1,0:T(8,128)(2,1)S(1)} %collective-permute-done.2.refs_2_), custom_call_target="tpu_custom_call" | custom-call | flops 536870912 | bytes 2097152 | tf_op jit(solution)/shard_map/attend_pages/pallas_call | solution.py:281
  24.9 2.1 %attend_finish.2 = (bf16[64,640]{1,0:T(8,128)(2,1)S(1)}, bf16[64,1280]{1,0:T(8,128)(2,1)S(1)}) custom-call(bf16[1024,256]{1,0:T(8,128)(2,1)S(1)} %get-tuple-element.51.refs_0_, f32[1024,256]{1,0:T(8,128)S(1)} %attend_pages.3.refs_1_, bf16[512,384]{1,0:T(8,128)(2,1)S(1)} %collective-permute-done.6.refs_2_, bf16[640,2560]{1,0:T(8,128)(2,1)S(1)} %copy-done), custom_call_target="tpu_custom_call" | custom-call | flops 536870912 | bytes 1048576 | tf_op jit(solution)/shard_map/attend_finish/pallas_call | solution.py:345
  27.0 2.1 %collective-permute-start.7 = (bf16[64,1280]{1,0:T(8,128)(2,1)S(1)}, bf16[64,1280]{1,0:T(8,128)(2,1)S(1)}, u32[]{:S(2)}, u32[]{:S(2)}) collective-permute-start(bf16[64,1280]{1,0:T(8,128)(2,1)S(1)} %get-tuple-element.64), channel_id=1, source_target_pairs={{0,1},{1,0},{2,3},{3,2},{4,5},{5,4},{6,7},{7,6},{8,9},{9,8},{10,11... | collective-permute-start | bytes 491528 | tf_op jit(solution)/shard_map/ppermute | solution.py:540
  29.1 2.5 %attend_finish.3 = (bf16[128,640]{1,0:T(8,128)(2,1)}, bf16[64,1280]{1,0:T(8,128)(2,1)S(1)}, f32[64,1280]{1,0:T(8,128)S(1)}, f32[64,1280]{1,0:T(8,128)S(1)}, bf16...) custom-call(bf16[1024,256]{1,0:T(8,128)(2,1)S(1)} %get-tuple-element.51.refs_0_, ...), custom_call_target="tpu_custom_call" | custom-call | flops 536870912 | bytes 1048576 | tf_op jit(solution)/shard_map/attend_finish/pallas_call | solution.py:345
  31.6 0.1 collective-permute-start.10
  31.7 2.0 %collective-permute-done.7 = bf16[64,1280]{1,0:T(8,128)(2,1)S(1)} collective-permute-done((bf16[64,1280]{1,0:T(8,128)(2,1)S(1)}, bf16[64,1280]{1,0:T(8,128)(2,1)S(1)}, u32[]{:S(2)}, u32[]{:S(2)}) %collective-permute-start.7) | collective-permute-done | bytes 163872 | tf_op jit(solution)/shard_map/ppermute | solution.py:540
  33.7 2.8 %collective-permute-start.8 = (bf16[64,1280]{1,0:T(8,128)(2,1)S(1)}, bf16[64,1280]{1,0:T(8,128)(2,1)S(1)}, u32[]{:S(2)}, u32[]{:S(2)}) collective-permute-start(bf16[64,1280]{1,0:T(8,128)(2,1)S(1)} %add_convert_fusion.7), channel_id=1, source_target_pairs={{0,2},{1,3},{2,0},{3,1},{4,6},{5,7},{6,4},{7,5},{8,10},{9,11},{10,... | collective-permute-start | bytes 491528 | tf_op jit(solution)/shard_map/ppermute | solution.py:540
  36.5 3.5 %collective-permute-done.10 = bf16[64,1280]{1,0:T(8,128)(2,1)S(1)} collective-permute-done((bf16[64,1280]{1,0:T(8,128)(2,1)S(1)}, bf16[64,1280]{1,0:T(8,128)(2,1)S(1)}, u32[]{:S(2)}, u32[]{:S(2)}) %collective-permute-start.10) | collective-permute-done | bytes 163872 | tf_op jit(solution)/shard_map/ppermute | solution.py:540
  40.1 1.4 %collective-permute-start.11 = (bf16[64,1280]{1,0:T(8,128)(2,1)S(1)}, bf16[64,1280]{1,0:T(8,128)(2,1)S(1)}, u32[]{:S(2)}, u32[]{:S(2)}) collective-permute-start(bf16[64,1280]{1,0:T(8,128)(2,1)S(1)} %add_convert_fusion.5), channel_id=1, source_target_pairs={{0,2},{1,3},{2,0},{3,1},{4,6},{5,7},{6,4},{7,5},{8,10},{9,11},{10,... | collective-permute-start | bytes 491528 | tf_op jit(solution)/shard_map/ppermute | solution.py:540
  41.4 3.7 %stage.4 = (bf16[2560,896]{1,0:T(8,128)(2,1)S(1)}, bf16[2560,896]{1,0:T(8,128)(2,1)S(1)}) custom-call(bf16[2560,896]{1,0:T(8,128)(2,1)} %refs_0_.1, bf16[2560,896]{1,0:T(8,128)(2,1)} %refs_1_), custom_call_target="tpu_custom_call" | custom-call | bytes 9175040 | tf_op jit(solution)/shard_map/stage/pallas_call | solution.py:372
  45.2 3.2 %collective-permute-done.8 = bf16[64,1280]{1,0:T(8,128)(2,1)S(1)} collective-permute-done((bf16[64,1280]{1,0:T(8,128)(2,1)S(1)}, bf16[64,1280]{1,0:T(8,128)(2,1)S(1)}, u32[]{:S(2)}, u32[]{:S(2)}) %collective-permute-start.8) | collective-permute-done | bytes 163872 | tf_op jit(solution)/shard_map/ppermute | solution.py:540
  48.4 0.3 collective-permute-start.9
  48.7 2.3 %collective-permute-done.11 = bf16[64,1280]{1,0:T(8,128)(2,1)S(1)} collective-permute-done((bf16[64,1280]{1,0:T(8,128)(2,1)S(1)}, bf16[64,1280]{1,0:T(8,128)(2,1)S(1)}, u32[]{:S(2)}, u32[]{:S(2)}) %collective-permute-start.11) | collective-permute-done | bytes 163872 | tf_op jit(solution)/shard_map/ppermute | solution.py:540
  51.1 0.5 collective-permute-start.12
  51.7 2.1 %feed_forward.2 = (bf16[64,896]{1,0:T(8,128)(2,1)S(1)}, bf16[64,1280]{1,0:T(8,128)(2,1)S(1)}) custom-call(bf16[64,1280]{1,0:T(8,128)(2,1)S(1)} %add_convert_fusion.6.refs_0_, bf16[64,1280]{1,0:T(8,128)(2,1)S(1)} %add_convert_fusion.4.refs_1_, bf16[1,2560]{1,0:T(2,128)(2,1)S(1)} %reshape.13.gain_ref.refs_2_, ...), custom_call_target="tpu_custom_call" | custom-call | flops 880803840 | bytes 13762560 | tf_op jit(solution)/shard_map/feed_forward/pallas_call | solution.py:455
  53.7 1.6 %collective-permute-start.13 = (bf16[64,1280]{1,0:T(8,128)(2,1)S(1)}, bf16[64,1280]{1,0:T(8,128)(2,1)S(1)}, u32[]{:S(2)}, u32[]{:S(2)}) collective-permute-start(bf16[64,1280]{1,0:T(8,128)(2,1)S(1)} %get-tuple-element.83), channel_id=1, source_target_pairs={{0,1},{1,0},{2,3},{3,2},{4,5},{5,4},{6,7},{7,6},{8,9},{9,8},{10,11... | collective-permute-start | bytes 491528 | tf_op jit(solution)/shard_map/ppermute | solution.py:540
  55.4 0.3 collective-permute-done.9.rows_ref.refs_0_
  55.6 0.8 early_piece.1
  56.5 2.7 %collective-permute-done.12.refs_1_ = bf16[64,1280]{1,0:T(8,128)(2,1)S(1)} collective-permute-done((bf16[64,1280]{1,0:T(8,128)(2,1)S(1)}, bf16[64,1280]{1,0:T(8,128)(2,1)S(1)}, u32[]{:S(2)}, u32[]{:S(2)}) %collective-permute-start.12) | collective-permute-done | bytes 163872 | tf_op jit(solution)/shard_map/ppermute | solution.py:540
  59.2 2.0 %feed_forward.3 = (bf16[64,1280]{1,0:T(8,128)(2,1)S(1)}, f32[64,1280]{1,0:T(8,128)S(1)}, f32[64,1280]{1,0:T(8,128)S(1)}) custom-call(bf16[64,1280]{1,0:T(8,128)(2,1)S(1)} %collective-permute-done.9.rows_ref.refs_0_, bf16[64,1280]{1,0:T(8,128)(2,1)S(1)} %collective-permute-done.12.refs_1_, bf16[1,2560]{1,0:T(2,128)(2,1)S(1)} %reshape.13.gain_ref.refs_2_, ...), custom_call_target="tpu_custom_call" | custom-call | flops 880803840 | bytes 13762560 | tf_op jit(solution)/shard_map/feed_forward/pallas_call | solution.py:455
  61.2 0.2 collective-permute-done.13
  61.5 3.4 %collective-permute-start.17 = (bf16[64,1280]{1,0:T(8,128)(2,1)S(1)}, bf16[64,1280]{1,0:T(8,128)(2,1)S(1)}, u32[]{:S(2)}, u32[]{:S(2)}) collective-permute-start(bf16[64,1280]{1,0:T(8,128)(2,1)S(1)} %add_convert_fusion.3), channel_id=1, source_target_pairs={{0,2},{1,3},{2,0},{3,1},{4,6},{5,7},{6,4},{7,5},{8,10},{9,11},{10,... | collective-permute-start | bytes 491528 | tf_op jit(solution)/shard_map/ppermute | solution.py:540
  64.9 3.4 %collective-permute-done.14 = bf16[64,1280]{1,0:T(8,128)(2,1)S(1)} collective-permute-done((bf16[64,1280]{1,0:T(8,128)(2,1)S(1)}, bf16[64,1280]{1,0:T(8,128)(2,1)S(1)}, u32[]{:S(2)}, u32[]{:S(2)}) %collective-permute-start.14) | collective-permute-done | bytes 163872 | tf_op jit(solution)/shard_map/ppermute | solution.py:540
  68.4 1.6 %collective-permute-start.15 = (bf16[64,1280]{1,0:T(8,128)(2,1)S(1)}, bf16[64,1280]{1,0:T(8,128)(2,1)S(1)}, u32[]{:S(2)}, u32[]{:S(2)}) collective-permute-start(bf16[64,1280]{1,0:T(8,128)(2,1)S(1)} %add_convert_fusion.2), channel_id=1, source_target_pairs={{0,2},{1,3},{2,0},{3,1},{4,6},{5,7},{6,4},{7,5},{8,10},{9,11},{10,... | collective-permute-start | bytes 491528 | tf_op jit(solution)/shard_map/ppermute | solution.py:540
  70.0 1.9 %stage.5.refs_3_ = bf16[2560,640]{1,0:T(8,128)(2,1)S(1)} custom-call(bf16[2560,640]{1,0:T(8,128)(2,1)} %refs_0_.2), custom_call_target="tpu_custom_call" | custom-call | bytes 3276800 | tf_op jit(solution)/shard_map/stage/pallas_call | solution.py:372
  72.0 4.4 %collective-permute-done.17 = bf16[64,1280]{1,0:T(8,128)(2,1)S(1)} collective-permute-done((bf16[64,1280]{1,0:T(8,128)(2,1)S(1)}, bf16[64,1280]{1,0:T(8,128)(2,1)S(1)}, u32[]{:S(2)}, u32[]{:S(2)}) %collective-permute-start.17) | collective-permute-done | bytes 163872 | tf_op jit(solution)/shard_map/ppermute | solution.py:540
  76.5 1.7 %collective-permute-done.15 = bf16[64,1280]{1,0:T(8,128)(2,1)S(1)} collective-permute-done((bf16[64,1280]{1,0:T(8,128)(2,1)S(1)}, bf16[64,1280]{1,0:T(8,128)(2,1)S(1)}, u32[]{:S(2)}, u32[]{:S(2)}) %collective-permute-start.15) | collective-permute-done | bytes 163872 | tf_op jit(solution)/shard_map/ppermute | solution.py:540
  78.2 0.8 collective-permute-start.16
  79.0 1.2 %next_layer.2 = (bf16[64,640]{1,0:T(8,128)(2,1)S(1)}, bf16[320,64]{1,0:T(8,128)(2,1)S(1)}) custom-call(bf16[64,1280]{1,0:T(8,128)(2,1)S(1)} %add_convert_fusion.1.refs_0_.refs_7_, bf16[64,1280]{1,0:T(8,128)(2,1)S(1)} %add_convert_fusion.refs_1_.refs_8_, bf16[1,2560]{1,0:T(2,128)(2,1)S(1)} %reshape.18.refs_2_, bf16[2560,640]{1,0:T(8,128)(2,1)S(1)} %stage.5.refs_3_, ...), custom_call_target="tpu_custom_call" | custom-call | flops 314572800 | bytes 4915200 | tf_op jit(solution)/shard_map/next_layer/pallas_call | solution.py:523
  80.2 2.8 %collective-permute-done.18.refs_1_ = bf16[64,1280]{1,0:T(8,128)(2,1)S(1)} collective-permute-done((bf16[64,1280]{1,0:T(8,128)(2,1)S(1)}, bf16[64,1280]{1,0:T(8,128)(2,1)S(1)}, u32[]{:S(2)}, u32[]{:S(2)}) %collective-permute-start.18) | collective-permute-done | bytes 163872 | tf_op jit(solution)/shard_map/ppermute | solution.py:540
  83.0 1.8 %collective-permute-done.16.refs_0_ = bf16[64,1280]{1,0:T(8,128)(2,1)S(1)} collective-permute-done((bf16[64,1280]{1,0:T(8,128)(2,1)S(1)}, bf16[64,1280]{1,0:T(8,128)(2,1)S(1)}, u32[]{:S(2)}, u32[]{:S(2)}) %collective-permute-start.16) | collective-permute-done | bytes 163872 | tf_op jit(solution)/shard_map/ppermute | solution.py:540
  84.8 2.1 %next_layer.3 = (bf16[128,640]{1,0:T(8,128)(2,1)}, bf16[320,128]{1,0:T(8,128)(2,1)}, bf16[32,2560]{1,0:T(8,128)(2,1)}) custom-call(bf16[64,1280]{1,0:T(8,128)(2,1)S(1)} %collective-permute-done.16.refs_0_, bf16[64,1280]{1,0:T(8,128)(2,1)S(1)} %collective-permute-done.18.refs_1_, bf16[1,2560]{1,0:T(2,128)(2,1)S(1)} %reshape.18.refs_2_, ...), custom_call_target="tpu_custom_call" | custom-call | flops 314572800 | bytes 4915200 | tf_op jit(solution)/shard_map/next_layer/pallas_call | solution.py:523
  (29 shorter events, 0.6 us)
Async XLA Ops:
  1.7 5.6 %collective-permute-start.1 = (bf16[512,384]{1,0:T(8,128)(2,1)S(1)}, bf16[512,384]{1,0:T(8,128)(2,1)S(1)}, u32[]{:S(2)}, u32[]{:S(2)}) collective-permute-start(bf16[512,384]{1,0:T(8,128)(2,1)S(1)} %pool_rows.1.refs_0_), channel_id=1, source_target_pairs={{0,4},{4,0},{8,12},{12,8},{16,20},{20,16},{24,28},{28,24},{1,5},{5... | collective-permute-start | bytes 1179656 | tf_op jit(solution)/shard_map/ppermute | solution.py:540
  2.2 11.4 %collective-permute-start = (bf16[512,384]{1,0:T(8,128)(2,1)S(1)}, bf16[512,384]{1,0:T(8,128)(2,1)S(1)}, u32[]{:S(2)}, u32[]{:S(2)}) collective-permute-start(bf16[512,384]{1,0:T(8,128)(2,1)S(1)} %pool_rows.1.refs_0_), channel_id=1, source_target_pairs={{0,8},{4,20},{8,0},{12,28},{16,24},{20,4},{24,16},{28,12},{1,9},{5... | collective-permute-start | bytes 1179656 | tf_op jit(solution)/shard_map/ppermute | solution.py:546
  4.8 9.7 %collective-permute-start.3 = (bf16[512,384]{1,0:T(8,128)(2,1)S(1)}, bf16[512,384]{1,0:T(8,128)(2,1)S(1)}, u32[]{:S(2)}, u32[]{:S(2)}) collective-permute-start(bf16[512,384]{1,0:T(8,128)(2,1)S(1)} %pool_rows.1.refs_0_), channel_id=1, source_target_pairs={{0,16},{4,12},{8,24},{12,4},{16,0},{20,28},{24,8},{28,20},{1,17},{... | collective-permute-start | bytes 1179656 | tf_op jit(solution)/shard_map/ppermute | solution.py:546
  7.3 1.0 %copy-start.3 = (bf16[16,32,320]{2,1,0:T(8,128)(2,1)S(1)}, bf16[16,32,320]{2,1,0:T(8,128)(2,1)}, u32[]{:S(2)}) copy-start(bf16[16,32,320]{2,1,0:T(8,128)(2,1)} %leaf_ref.1) | copy-start | bytes 983044
  8.3 0.9 %copy-start.4 = (bf16[128,640]{1,0:T(8,128)(2,1)S(1)}, bf16[128,640]{1,0:T(8,128)(2,1)}, u32[]{:S(2)}) copy-start(bf16[128,640]{1,0:T(8,128)(2,1)} %query_ref.1) | copy-start | bytes 491524
  14.5 2.3 %collective-permute-start.4 = (bf16[512,384]{1,0:T(8,128)(2,1)S(1)}, bf16[512,384]{1,0:T(8,128)(2,1)S(1)}, u32[]{:S(2)}, u32[]{:S(2)}) collective-permute-start(bf16[512,384]{1,0:T(8,128)(2,1)S(1)} %collective-permute-done.refs_2_), channel_id=1, source_target_pairs={{0,4},{4,0},{8,12},{12,8},{16,20},{20,16},{24,28},{28,24},{1,5},{5... | collective-permute-start | bytes 1179656 | tf_op jit(solution)/shard_map/ppermute | solution.py:540
  14.7 2.2 %collective-permute-start.5 = (bf16[512,384]{1,0:T(8,128)(2,1)S(1)}, bf16[512,384]{1,0:T(8,128)(2,1)S(1)}, u32[]{:S(2)}, u32[]{:S(2)}) collective-permute-start(bf16[512,384]{1,0:T(8,128)(2,1)S(1)} %collective-permute-done.3.refs_3_), channel_id=1, source_target_pairs={{0,4},{4,0},{8,12},{12,8},{16,20},{20,16},{24,28},{28,24},{1,5},{5... | collective-permute-start | bytes 1179656 | tf_op jit(solution)/shard_map/ppermute | solution.py:540
  15.0 7.8 %collective-permute-start.2 = (bf16[512,384]{1,0:T(8,128)(2,1)S(1)}, bf16[512,384]{1,0:T(8,128)(2,1)S(1)}, u32[]{:S(2)}, u32[]{:S(2)}) collective-permute-start(bf16[512,384]{1,0:T(8,128)(2,1)S(1)} %collective-permute-done.refs_2_), channel_id=1, source_target_pairs={{0,16},{4,12},{8,24},{12,4},{16,0},{20,28},{24,8},{28,20},{1,17},{... | collective-permute-start | bytes 1179656 | tf_op jit(solution)/shard_map/ppermute | solution.py:546
  20.4 4.5 %copy-start = (bf16[640,2560]{1,0:T(8,128)(2,1)S(1)}, bf16[640,2560]{1,0:T(8,128)(2,1)}, u32[]{:S(2)}) copy-start(bf16[640,2560]{1,0:T(8,128)(2,1)} %refs_3_.3) | copy-start | bytes 9830404
  22.9 6.3 %copy-start.2 = (bf16[128,2560]{1,0:T(8,128)(2,1)S(1)}, bf16[128,2560]{1,0:T(8,128)(2,1)}, u32[]{:S(2)}) copy-start(bf16[128,2560]{1,0:T(8,128)(2,1)} %refs_5_.1) | copy-start | bytes 1966084
  22.9 2.0 %collective-permute-start.6 = (bf16[512,384]{1,0:T(8,128)(2,1)S(1)}, bf16[512,384]{1,0:T(8,128)(2,1)S(1)}, u32[]{:S(2)}, u32[]{:S(2)}) collective-permute-start(bf16[512,384]{1,0:T(8,128)(2,1)S(1)} %collective-permute-done.2.refs_2_), channel_id=1, source_target_pairs={{0,4},{4,0},{8,12},{12,8},{16,20},{20,16},{24,28},{28,24},{1,5},{5... | collective-permute-start | bytes 1179656 | tf_op jit(solution)/shard_map/ppermute | solution.py:540
  27.0 6.7 %collective-permute-start.7 = (bf16[64,1280]{1,0:T(8,128)(2,1)S(1)}, bf16[64,1280]{1,0:T(8,128)(2,1)S(1)}, u32[]{:S(2)}, u32[]{:S(2)}) collective-permute-start(bf16[64,1280]{1,0:T(8,128)(2,1)S(1)} %get-tuple-element.64), channel_id=1, source_target_pairs={{0,1},{1,0},{2,3},{3,2},{4,5},{5,4},{6,7},{7,6},{8,9},{9,8},{10,11... | collective-permute-start | bytes 491528 | tf_op jit(solution)/shard_map/ppermute | solution.py:540
  31.6 8.4 %collective-permute-start.10 = (bf16[64,1280]{1,0:T(8,128)(2,1)S(1)}, bf16[64,1280]{1,0:T(8,128)(2,1)S(1)}, u32[]{:S(2)}, u32[]{:S(2)}) collective-permute-start(bf16[64,1280]{1,0:T(8,128)(2,1)S(1)} %get-tuple-element.66), channel_id=1, source_target_pairs={{0,1},{1,0},{2,3},{3,2},{4,5},{5,4},{6,7},{7,6},{8,9},{9,8},{10,11... | collective-permute-start | bytes 491528 | tf_op jit(solution)/shard_map/ppermute | solution.py:540
  33.7 14.7 %collective-permute-start.8 = (bf16[64,1280]{1,0:T(8,128)(2,1)S(1)}, bf16[64,1280]{1,0:T(8,128)(2,1)S(1)}, u32[]{:S(2)}, u32[]{:S(2)}) collective-permute-start(bf16[64,1280]{1,0:T(8,128)(2,1)S(1)} %add_convert_fusion.7), channel_id=1, source_target_pairs={{0,2},{1,3},{2,0},{3,1},{4,6},{5,7},{6,4},{7,5},{8,10},{9,11},{10,... | collective-permute-start | bytes 491528 | tf_op jit(solution)/shard_map/ppermute | solution.py:540
  40.0 11.6 %copy-start.5 = (bf16[2560]{0:T(1024)(128)(2,1)S(1)}, bf16[2560]{0:T(1024)(128)(2,1)}, u32[]{:S(2)}) copy-start(bf16[2560]{0:T(1024)(128)(2,1)} %param.33) | copy-start | bytes 15364
  40.1 11.0 %collective-permute-start.11 = (bf16[64,1280]{1,0:T(8,128)(2,1)S(1)}, bf16[64,1280]{1,0:T(8,128)(2,1)S(1)}, u32[]{:S(2)}, u32[]{:S(2)}) collective-permute-start(bf16[64,1280]{1,0:T(8,128)(2,1)S(1)} %add_convert_fusion.5), channel_id=1, source_target_pairs={{0,2},{1,3},{2,0},{3,1},{4,6},{5,7},{6,4},{7,5},{8,10},{9,11},{10,... | collective-permute-start | bytes 491528 | tf_op jit(solution)/shard_map/ppermute | solution.py:540
  48.4 7.2 %collective-permute-start.9 = (bf16[64,1280]{1,0:T(8,128)(2,1)S(1)}, bf16[64,1280]{1,0:T(8,128)(2,1)S(1)}, u32[]{:S(2)}, u32[]{:S(2)}) collective-permute-start(bf16[64,1280]{1,0:T(8,128)(2,1)S(1)} %add_convert_fusion.6.refs_0_), channel_id=1, source_target_pairs={{0,1},{1,0},{2,3},{3,2},{4,5},{5,4},{6,7},{7,6},{8,9},{9,8},{10,11... | collective-permute-start | bytes 491528 | tf_op jit(solution)/shard_map/ppermute | solution.py:540
  51.1 8.0 %collective-permute-start.12 = (bf16[64,1280]{1,0:T(8,128)(2,1)S(1)}, bf16[64,1280]{1,0:T(8,128)(2,1)S(1)}, u32[]{:S(2)}, u32[]{:S(2)}) collective-permute-start(bf16[64,1280]{1,0:T(8,128)(2,1)S(1)} %add_convert_fusion.4.refs_1_), channel_id=1, source_target_pairs={{0,1},{1,0},{2,3},{3,2},{4,5},{5,4},{6,7},{7,6},{8,9},{9,8},{10,11... | collective-permute-start | bytes 491528 | tf_op jit(solution)/shard_map/ppermute | solution.py:540
  53.7 7.7 %collective-permute-start.13 = (bf16[64,1280]{1,0:T(8,128)(2,1)S(1)}, bf16[64,1280]{1,0:T(8,128)(2,1)S(1)}, u32[]{:S(2)}, u32[]{:S(2)}) collective-permute-start(bf16[64,1280]{1,0:T(8,128)(2,1)S(1)} %get-tuple-element.83), channel_id=1, source_target_pairs={{0,1},{1,0},{2,3},{3,2},{4,5},{5,4},{6,7},{7,6},{8,9},{9,8},{10,11... | collective-permute-start | bytes 491528 | tf_op jit(solution)/shard_map/ppermute | solution.py:540
  61.2 7.2 %collective-permute-start.14 = (bf16[64,1280]{1,0:T(8,128)(2,1)S(1)}, bf16[64,1280]{1,0:T(8,128)(2,1)S(1)}, u32[]{:S(2)}, u32[]{:S(2)}) collective-permute-start(bf16[64,1280]{1,0:T(8,128)(2,1)S(1)} %get-tuple-element.84), channel_id=1, source_target_pairs={{0,1},{1,0},{2,3},{3,2},{4,5},{5,4},{6,7},{7,6},{8,9},{9,8},{10,11... | collective-permute-start | bytes 491528 | tf_op jit(solution)/shard_map/ppermute | solution.py:540
  61.5 17.5 %copy-start.6 = (bf16[2560]{0:T(1024)(128)(2,1)S(1)}, bf16[2560]{0:T(1024)(128)(2,1)}, u32[]{:S(2)}) copy-start(bf16[2560]{0:T(1024)(128)(2,1)} %param.37) | copy-start | bytes 15364
  61.5 17.5 %copy-start.1 = (bf16[2560,320]{0,1:T(8,128)(2,1)S(1)}, bf16[2560,320]{0,1:T(8,128)(2,1)}, u32[]{:S(2)}) copy-start(bf16[2560,320]{0,1:T(8,128)(2,1)} %param.39) | copy-start | bytes 4915204
  61.5 14.8 %collective-permute-start.17 = (bf16[64,1280]{1,0:T(8,128)(2,1)S(1)}, bf16[64,1280]{1,0:T(8,128)(2,1)S(1)}, u32[]{:S(2)}, u32[]{:S(2)}) collective-permute-start(bf16[64,1280]{1,0:T(8,128)(2,1)S(1)} %add_convert_fusion.3), channel_id=1, source_target_pairs={{0,2},{1,3},{2,0},{3,1},{4,6},{5,7},{6,4},{7,5},{8,10},{9,11},{10,... | collective-permute-start | bytes 491528 | tf_op jit(solution)/shard_map/ppermute | solution.py:540
  68.4 9.8 %collective-permute-start.15 = (bf16[64,1280]{1,0:T(8,128)(2,1)S(1)}, bf16[64,1280]{1,0:T(8,128)(2,1)S(1)}, u32[]{:S(2)}, u32[]{:S(2)}) collective-permute-start(bf16[64,1280]{1,0:T(8,128)(2,1)S(1)} %add_convert_fusion.2), channel_id=1, source_target_pairs={{0,2},{1,3},{2,0},{3,1},{4,6},{5,7},{6,4},{7,5},{8,10},{9,11},{10,... | collective-permute-start | bytes 491528 | tf_op jit(solution)/shard_map/ppermute | solution.py:540
  76.4 6.6 %collective-permute-start.18 = (bf16[64,1280]{1,0:T(8,128)(2,1)S(1)}, bf16[64,1280]{1,0:T(8,128)(2,1)S(1)}, u32[]{:S(2)}, u32[]{:S(2)}) collective-permute-start(bf16[64,1280]{1,0:T(8,128)(2,1)S(1)} %add_convert_fusion.refs_1_.refs_8_), channel_id=1, source_target_pairs={{0,1},{1,0},{2,3},{3,2},{4,5},{5,4},{6,7},{7,6},{8,9},{9,8},{10,11... | collective-permute-start | bytes 491528 | tf_op jit(solution)/shard_map/ppermute | solution.py:540
  78.2 6.6 %collective-permute-start.16 = (bf16[64,1280]{1,0:T(8,128)(2,1)S(1)}, bf16[64,1280]{1,0:T(8,128)(2,1)S(1)}, u32[]{:S(2)}, u32[]{:S(2)}) collective-permute-start(bf16[64,1280]{1,0:T(8,128)(2,1)S(1)} %add_convert_fusion.1.refs_0_.refs_7_), channel_id=1, source_target_pairs={{0,1},{1,0},{2,3},{3,2},{4,5},{5,4},{6,7},{7,6},{8,9},{9,8},{10,11... | collective-permute-start | bytes 491528 | tf_op jit(solution)/shard_map/ppermute | solution.py:540

commit v9 on v8

--- a/solution.py
+++ b/solution.py
@@ -393,34 +393,34 @@
     return lax.rsqrt(sum(squares) / depth + EPSILON)
 
 
-def times(rows, weight_ref, k):
+def times(rows, weight_ref, k, flipped=False):
+    if flipped:
+        return scores_of(weight_ref[:, piece(weight_ref.shape[1], k)], rows)
     weight = weight_ref[piece(weight_ref.shape[0], k), :]
     return jnp.dot(rows, weight, preferred_element_type=f32)
 
 
-def early_kernel(rows_ref, gain_ref, *refs):
-    rows = gained(rows_ref[...], gain_ref, 0)
-    count = len(refs) // 2
-    for weight_ref, out_ref in zip(refs[:count], refs[count:]):
-        out_ref[...] = times(rows, weight_ref, 0)
-
-
-def early_products(rows, gain, weights):
+def early_kernel(rows_ref, gain_ref, *refs, k, flips):
+    rows = gained(rows_ref[...], gain_ref, k)
+    count = len(flips)
+    for weight_ref, out_ref, flipped in zip(refs[:count], refs[count:], flips):
+        out_ref[...] = times(rows, weight_ref, k, flipped)
+
+
+def early_products(rows, gain, weights, k=0, flips=(False, False)):
     count = rows.shape[0]
-    shapes = [jax.ShapeDtypeStruct((count, w.shape[1]), f32) for w in weights]
+    shapes = [
+        jax.ShapeDtypeStruct((w.shape[0], count) if flipped else (count, w.shape[1]), f32)
+        for w, flipped in zip(weights, flips)
+    ]
     return pl.pallas_call(
-        early_kernel,
+        functools.partial(early_kernel, k=k, flips=flips),
         out_shape=tuple(shapes),
         in_specs=[VMEM] * (2 + len(weights)),
         out_specs=(VMEM,) * len(weights),
         compiler_params=PARAMS,
-        cost_estimate=pl.CostEstimate(
-            flops=sum(w.size for w in weights) * count,
-            bytes_accessed=sum(w.size for w in weights),
-            transcendentals=0,
-        ),
         name="early_piece",
-    )(rows, gain.reshape(1, -1), *in_vmem(weights))
+    )(rows, gain.reshape(1, -1), *weights)
 
 
 def mlp_kernel(*refs, second, early):
@@ -474,11 +474,20 @@
 def next_kernel(*refs, half):
     row_refs, refs = refs[:PIECES], refs[PIECES:]
     gain_ref, query_ref, keyval_ref = refs[:3]
-    rows = joined(row_refs)
-    normed = normalized(rows, gain_ref[...])
-    query = jnp.dot(normed, query_ref[...], preferred_element_type=f32).astype(bf16)
-    keyval = scores_of(keyval_ref[...], normed).astype(bf16)
-    if not half:
+    if half:
+        query, keyval = refs[3][...], refs[4][...]
+        refs = (*refs[:3], *refs[5:])
+        for k in range(PIECES - 1):
+            rows = gained(row_refs[k][...], gain_ref, k)
+            query = query + times(rows, query_ref, k)
+            keyval = keyval + times(rows, keyval_ref, k, True)
+        scale = inverse_rms(row_refs)
+        across = jnp.broadcast_to(scale, (scale.shape[0], LANES)).T[0:1, :]
+        query, keyval = (query * scale).astype(bf16), (keyval * across).astype(bf16)
+    else:
+        normed = normalized(joined(row_refs), gain_ref[...])
+        query = jnp.dot(normed, query_ref[...], preferred_element_type=f32).astype(bf16)
+        keyval = scores_of(keyval_ref[...], normed).astype(bf16)
         query_out, keyval_out = refs[3:]
         query_out[...] = query
         keyval_out[...] = keyval
@@ -508,7 +517,7 @@
     for k in range(PIECES):
         ours = row_refs[k][pl.ds(at, share), :]
         others = refs[5 + k][pl.ds(at, share), :]
-        residual_out[:, piece(rows.shape[1], k)] = jnp.where(held, ours, others)
+        residual_out[:, piece(residual_out.shape[1], k)] = jnp.where(held, ours, others)
 
 
 def next_projections(rows, gain, query_weight, keyval_weight, other):
@@ -690,8 +699,10 @@
         layer_theirs = [lax.dynamic_slice_in_dim(item, theirs, part, 0) for item in layer]
     weights = (next_gain, query_weight, keyval_weight.T)
     other = next_projections(layer_theirs, *weights, ())
+    _, arrived = lax.optimization_barrier((other, layer_mine[-1]))
+    early = early_products(arrived, next_gain, weights[1:], PIECES - 1, (False, True))
     next_query, next_keyval, residual_out = next_projections(
-        layer_mine, *weights, (*other, *layer_theirs)
+        layer_mine, *weights, (*early, *other, *layer_theirs)
     )
     return (attention, residual_out, next_query, next_keyval.T)
 

time: 87.1 us -> 86.5 us (level)
  transfers between devices with their start and end apart: 19 -> 19, of which waited for: 14 -> 14; matrix products, arithmetic and copies ran while one was open for 2% -> 2% of each run, Pallas kernels for 30% -> 31%
where the time goes in v9:
time: 86.5 us; the launch traced here: 86.3 us
  Pallas kernels  31.1 us (36%)
  waiting for transfers between devices  29.2 us (34%)
  starting transfers between devices  21.8 us (25%)
  local copies, waits for them, and re-layouts  2.94 us (3%)
    ppermute x16, waiting for transfers between devices, trade(): return lax.ppermute(value, axis, [(i, i ^ bit) for i in range(size)])  27.7 us
    ppermute x16, starting transfers between devices, trade(): return lax.ppermute(value, axis, [(i, i ^ bit) for i in range(size)])  15.9 us
    pallas_call x3, Pallas kernels, stage(): pl.pallas_call(stage_kernel, out_shape=tuple((pltpu.VMEM(w.shape, w.dtype...  8.11 us
    ppermute x3, starting transfers between devices, cross(): return lax.ppermute(value, 'req', pairs)  5.83 us
    pallas_call x2, Pallas kernels, extend_attention(): pl.pallas_call(functools.partial(chunk_kernel, blocks=2 * kv_local), out_...  5.36 us
    pallas_call x2, Pallas kernels, finish_attention(): pl.pallas_call(functools.partial(finish_kernel, half=half, kv_local=kv_lo...  4.57 us
    pallas_call x2, Pallas kernels, feed_forward(): pl.pallas_call(functools.partial(mlp_kernel, second=len(other) > 0, early...  4.07 us
    pallas_call x1, Pallas kernels, start_attention(): pl.pallas_call(functools.partial(local_kernel, chunks=len(pools)), out_sh...  3.77 us
  transfers between devices with their start and end apart: 19, of which 14 were waited for; matrix products, arithmetic and copies ran while one was open for 2% of the time, Pallas kernels for 31%

profile of v9, /device:TPU:0, one launch (start us, length us, event | category | flops | bytes accessed | tf_op | source)
XLA Modules:
  0.0 86.3 jit_solution(12610387712067099138)
XLA Ops:
  0.6 1.1 %pool_rows.1.refs_0_ = bf16[512,384]{1,0:T(8,128)(2,1)S(1)} custom-call(s32[32]{0:T(128)} %node_hbm.1, s32[32]{0:T(128)} %rank_hbm.1, s32[8]{0:T(128)} %length_hbm.1, s32[6]{0:T(128)} %root_hbm.1, bf16[32,16,320]{2,1,0:T(8,128)(2,1)} %pool_hbm.1), custom_call_target="tpu_custom_call" | custom-call | tf_op jit(solution)/shard_map/pool_rows/pallas_call | solution.py:128
  1.7 0.5 collective-permute-start.1
  2.2 2.6 %collective-permute-start = (bf16[512,384]{1,0:T(8,128)(2,1)S(1)}, bf16[512,384]{1,0:T(8,128)(2,1)S(1)}, u32[]{:S(2)}, u32[]{:S(2)}) collective-permute-start(bf16[512,384]{1,0:T(8,128)(2,1)S(1)} %pool_rows.1.refs_0_), channel_id=1, source_target_pairs={{0,8},{4,20},{8,0},{12,28},{16,24},{20,4},{24,16},{28,12},{1,9},{5... | collective-permute-start | bytes 1179656 | tf_op jit(solution)/shard_map/ppermute | solution.py:555
  4.8 1.5 %collective-permute-start.3 = (bf16[512,384]{1,0:T(8,128)(2,1)S(1)}, bf16[512,384]{1,0:T(8,128)(2,1)S(1)}, u32[]{:S(2)}, u32[]{:S(2)}) collective-permute-start(bf16[512,384]{1,0:T(8,128)(2,1)S(1)} %pool_rows.1.refs_0_), channel_id=1, source_target_pairs={{0,16},{4,12},{8,24},{12,4},{16,0},{20,28},{24,8},{28,20},{1,17},{... | collective-permute-start | bytes 1179656 | tf_op jit(solution)/shard_map/ppermute | solution.py:555
  6.3 1.0 %copy.24.keyval_ref = bf16[128,320]{1,0:T(8,128)(2,1)S(1)} copy(bf16[128,320]{0,1:T(8,128)(2,1)} %param.21) | data formatting | bytes 163840 | tf_op args[1]
  7.3 1.0 %copy-done.3 = bf16[16,32,320]{2,1,0:T(8,128)(2,1)S(1)} copy-done((bf16[16,32,320]{2,1,0:T(8,128)(2,1)S(1)}, bf16[16,32,320]{2,1,0:T(8,128)(2,1)}, u32[]{:S(2)}) %copy-start.3) | copy-done | bytes 327704
  8.3 0.9 %copy-done.4 = bf16[128,640]{1,0:T(8,128)(2,1)S(1)} copy-done((bf16[128,640]{1,0:T(8,128)(2,1)S(1)}, bf16[128,640]{1,0:T(8,128)(2,1)}, u32[]{:S(2)}) %copy-start.4) | copy-done | bytes 163864
  9.2 3.8 %attend_local.1 = (bf16[1024,256]{1,0:T(8,128)(2,1)S(1)}, f32[1024,256]{1,0:T(8,128)S(1)}) custom-call(s32[1,16]{1,0:T(1,128)} %count_hbm.1, s32[16]{0:T(128)} %mid_hbm.1, s32[16]{0:T(128)} %leaf_len_hbm.1, bf16[128,640]{1,0:T(8,128)(2,1)S(1)} %copy-done.4, bf16[128,320]{1,0:T(8,128)(2,1)S(1)} %copy.24.keyval_ref, bf16[16,32,320]{2,1,0:T(8,128)(2,1)S(1)} %copy-done.3, ...), custom_call_target="tpu_custom_call" | custom-call | flops 1744830464 | bytes 2097152 | tf_op jit(solution)/shard_map/attend_local/pallas_call | solution.py:242
  13.0 0.6 collective-permute-done.refs_2_
  13.6 0.9 %collective-permute-done.3.refs_3_ = bf16[512,384]{1,0:T(8,128)(2,1)S(1)} collective-permute-done((bf16[512,384]{1,0:T(8,128)(2,1)S(1)}, bf16[512,384]{1,0:T(8,128)(2,1)S(1)}, u32[]{:S(2)}, u32[]{:S(2)}) %collective-permute-start.3) | collective-permute-done | bytes 393248 | tf_op jit(solution)/shard_map/ppermute | solution.py:555
  14.5 0.1 collective-permute-start.4
  14.7 0.4 collective-permute-start.5
  15.0 1.8 %collective-permute-start.2 = (bf16[512,384]{1,0:T(8,128)(2,1)S(1)}, bf16[512,384]{1,0:T(8,128)(2,1)S(1)}, u32[]{:S(2)}, u32[]{:S(2)}) collective-permute-start(bf16[512,384]{1,0:T(8,128)(2,1)S(1)} %collective-permute-done.refs_2_), channel_id=1, source_target_pairs={{0,16},{4,12},{8,24},{12,4},{16,0},{20,28},{24,8},{28,20},{1,17},{... | collective-permute-start | bytes 1179656 | tf_op jit(solution)/shard_map/ppermute | solution.py:555
  16.8 3.6 %attend_pages.2.refs_1_ = f32[1024,256]{1,0:T(8,128)S(1)} custom-call(bf16[1024,256]{1,0:T(8,128)(2,1)S(1)} %get-tuple-element.54.refs_0_, f32[1024,256]{1,0:T(8,128)S(1)} %get-tuple-element.56.refs_1_, bf16[512,384]{1,0:T(8,128)(2,1)S(1)} %collective-permute-done.refs_2_, bf16[512,384]{1,0:T(8,128)(2,1)S(1)} %collective-permute-done.3.refs_3_, ...), custom_call_target="tpu_custom_call" | custom-call | flops 2147483648 | bytes 2097152 | tf_op jit(solution)/shard_map/attend_pages/pallas_call | solution.py:281
  20.4 2.5 %stage.3.refs_5_ = bf16[896,2560]{1,0:T(8,128)(2,1)S(1)} custom-call(bf16[896,2560]{1,0:T(8,128)(2,1)} %refs_0_), custom_call_target="tpu_custom_call" | custom-call | bytes 4587520 | tf_op jit(solution)/shard_map/stage/pallas_call | solution.py:372
  22.9 0.2 collective-permute-start.6
  23.1 1.8 %attend_pages.3.refs_1_ = f32[1024,256]{1,0:T(8,128)S(1)} custom-call(bf16[1024,256]{1,0:T(8,128)(2,1)S(1)} %get-tuple-element.54.refs_0_, f32[1024,256]{1,0:T(8,128)S(1)} %attend_pages.2.refs_1_, bf16[512,384]{1,0:T(8,128)(2,1)S(1)} %collective-permute-done.2.refs_2_), custom_call_target="tpu_custom_call" | custom-call | flops 536870912 | bytes 2097152 | tf_op jit(solution)/shard_map/attend_pages/pallas_call | solution.py:281
  24.9 2.1 %attend_finish.2 = (bf16[64,640]{1,0:T(8,128)(2,1)S(1)}, bf16[64,1280]{1,0:T(8,128)(2,1)S(1)}) custom-call(bf16[1024,256]{1,0:T(8,128)(2,1)S(1)} %get-tuple-element.54.refs_0_, f32[1024,256]{1,0:T(8,128)S(1)} %attend_pages.3.refs_1_, bf16[512,384]{1,0:T(8,128)(2,1)S(1)} %collective-permute-done.6.refs_2_, bf16[640,2560]{1,0:T(8,128)(2,1)S(1)} %copy-done.1), custom_call_target="tpu_custom_call" | custom-call | flops 536870912 | bytes 1048576 | tf_op jit(solution)/shard_map/attend_finish/pallas_call | solution.py:345
  27.0 2.1 %collective-permute-start.7 = (bf16[64,1280]{1,0:T(8,128)(2,1)S(1)}, bf16[64,1280]{1,0:T(8,128)(2,1)S(1)}, u32[]{:S(2)}, u32[]{:S(2)}) collective-permute-start(bf16[64,1280]{1,0:T(8,128)(2,1)S(1)} %get-tuple-element.67), channel_id=1, source_target_pairs={{0,1},{1,0},{2,3},{3,2},{4,5},{5,4},{6,7},{7,6},{8,9},{9,8},{10,11... | collective-permute-start | bytes 491528 | tf_op jit(solution)/shard_map/ppermute | solution.py:549
  29.1 2.5 %attend_finish.3 = (bf16[128,640]{1,0:T(8,128)(2,1)}, bf16[64,1280]{1,0:T(8,128)(2,1)S(1)}, f32[64,1280]{1,0:T(8,128)S(1)}, f32[64,1280]{1,0:T(8,128)S(1)}, bf16...) custom-call(bf16[1024,256]{1,0:T(8,128)(2,1)S(1)} %get-tuple-element.54.refs_0_, ...), custom_call_target="tpu_custom_call" | custom-call | flops 536870912 | bytes 1048576 | tf_op jit(solution)/shard_map/attend_finish/pallas_call | solution.py:345
  31.7 2.0 %collective-permute-done.7 = bf16[64,1280]{1,0:T(8,128)(2,1)S(1)} collective-permute-done((bf16[64,1280]{1,0:T(8,128)(2,1)S(1)}, bf16[64,1280]{1,0:T(8,128)(2,1)S(1)}, u32[]{:S(2)}, u32[]{:S(2)}) %collective-permute-start.7) | collective-permute-done | bytes 163872 | tf_op jit(solution)/shard_map/ppermute | solution.py:549
  33.7 2.8 %collective-permute-start.8 = (bf16[64,1280]{1,0:T(8,128)(2,1)S(1)}, bf16[64,1280]{1,0:T(8,128)(2,1)S(1)}, u32[]{:S(2)}, u32[]{:S(2)}) collective-permute-start(bf16[64,1280]{1,0:T(8,128)(2,1)S(1)} %add_convert_fusion.7), channel_id=1, source_target_pairs={{0,2},{1,3},{2,0},{3,1},{4,6},{5,7},{6,4},{7,5},{8,10},{9,11},{10,... | collective-permute-start | bytes 491528 | tf_op jit(solution)/shard_map/ppermute | solution.py:549
  36.5 3.5 %collective-permute-done.10 = bf16[64,1280]{1,0:T(8,128)(2,1)S(1)} collective-permute-done((bf16[64,1280]{1,0:T(8,128)(2,1)S(1)}, bf16[64,1280]{1,0:T(8,128)(2,1)S(1)}, u32[]{:S(2)}, u32[]{:S(2)}) %collective-permute-start.10) | collective-permute-done | bytes 163872 | tf_op jit(solution)/shard_map/ppermute | solution.py:549
  40.1 1.4 %collective-permute-start.11 = (bf16[64,1280]{1,0:T(8,128)(2,1)S(1)}, bf16[64,1280]{1,0:T(8,128)(2,1)S(1)}, u32[]{:S(2)}, u32[]{:S(2)}) collective-permute-start(bf16[64,1280]{1,0:T(8,128)(2,1)S(1)} %add_convert_fusion.5), channel_id=1, source_target_pairs={{0,2},{1,3},{2,0},{3,1},{4,6},{5,7},{6,4},{7,5},{8,10},{9,11},{10,... | collective-permute-start | bytes 491528 | tf_op jit(solution)/shard_map/ppermute | solution.py:549
  41.4 3.7 %stage.4 = (bf16[2560,896]{1,0:T(8,128)(2,1)S(1)}, bf16[2560,896]{1,0:T(8,128)(2,1)S(1)}) custom-call(bf16[2560,896]{1,0:T(8,128)(2,1)} %refs_0_.1, bf16[2560,896]{1,0:T(8,128)(2,1)} %refs_1_), custom_call_target="tpu_custom_call" | custom-call | bytes 9175040 | tf_op jit(solution)/shard_map/stage/pallas_call | solution.py:372
  45.2 3.2 %collective-permute-done.8 = bf16[64,1280]{1,0:T(8,128)(2,1)S(1)} collective-permute-done((bf16[64,1280]{1,0:T(8,128)(2,1)S(1)}, bf16[64,1280]{1,0:T(8,128)(2,1)S(1)}, u32[]{:S(2)}, u32[]{:S(2)}) %collective-permute-start.8) | collective-permute-done | bytes 163872 | tf_op jit(solution)/shard_map/ppermute | solution.py:549
  48.4 0.2 collective-permute-start.9
  48.7 2.4 %collective-permute-done.11 = bf16[64,1280]{1,0:T(8,128)(2,1)S(1)} collective-permute-done((bf16[64,1280]{1,0:T(8,128)(2,1)S(1)}, bf16[64,1280]{1,0:T(8,128)(2,1)S(1)}, u32[]{:S(2)}, u32[]{:S(2)}) %collective-permute-start.11) | collective-permute-done | bytes 163872 | tf_op jit(solution)/shard_map/ppermute | solution.py:549
  51.1 0.5 collective-permute-start.12
  51.7 2.1 %feed_forward.2 = (bf16[64,896]{1,0:T(8,128)(2,1)S(1)}, bf16[64,1280]{1,0:T(8,128)(2,1)S(1)}) custom-call(bf16[64,1280]{1,0:T(8,128)(2,1)S(1)} %add_convert_fusion.6.refs_0_, bf16[64,1280]{1,0:T(8,128)(2,1)S(1)} %add_convert_fusion.4.refs_1_, bf16[1,2560]{1,0:T(2,128)(2,1)S(1)} %reshape.14.gain_ref.refs_2_, ...), custom_call_target="tpu_custom_call" | custom-call | flops 880803840 | bytes 13762560 | tf_op jit(solution)/shard_map/feed_forward/pallas_call | solution.py:455
  53.7 1.6 %collective-permute-start.13 = (bf16[64,1280]{1,0:T(8,128)(2,1)S(1)}, bf16[64,1280]{1,0:T(8,128)(2,1)S(1)}, u32[]{:S(2)}, u32[]{:S(2)}) collective-permute-start(bf16[64,1280]{1,0:T(8,128)(2,1)S(1)} %get-tuple-element.86), channel_id=1, source_target_pairs={{0,1},{1,0},{2,3},{3,2},{4,5},{5,4},{6,7},{7,6},{8,9},{9,8},{10,11... | collective-permute-start | bytes 491528 | tf_op jit(solution)/shard_map/ppermute | solution.py:549
  55.4 0.3 collective-permute-done.9.rows_ref.refs_0_
  55.6 0.8 early_piece.2
  56.5 2.7 %collective-permute-done.12.refs_1_ = bf16[64,1280]{1,0:T(8,128)(2,1)S(1)} collective-permute-done((bf16[64,1280]{1,0:T(8,128)(2,1)S(1)}, bf16[64,1280]{1,0:T(8,128)(2,1)S(1)}, u32[]{:S(2)}, u32[]{:S(2)}) %collective-permute-start.12) | collective-permute-done | bytes 163872 | tf_op jit(solution)/shard_map/ppermute | solution.py:549
  59.2 2.0 %feed_forward.3 = (bf16[64,1280]{1,0:T(8,128)(2,1)S(1)}, f32[64,1280]{1,0:T(8,128)S(1)}, f32[64,1280]{1,0:T(8,128)S(1)}) custom-call(bf16[64,1280]{1,0:T(8,128)(2,1)S(1)} %collective-permute-done.9.rows_ref.refs_0_, bf16[64,1280]{1,0:T(8,128)(2,1)S(1)} %collective-permute-done.12.refs_1_, bf16[1,2560]{1,0:T(2,128)(2,1)S(1)} %reshape.14.gain_ref.refs_2_, ...), custom_call_target="tpu_custom_call" | custom-call | flops 880803840 | bytes 13762560 | tf_op jit(solution)/shard_map/feed_forward/pallas_call | solution.py:455
  61.2 0.2 collective-permute-done.13
  61.5 3.4 %collective-permute-start.17 = (bf16[64,1280]{1,0:T(8,128)(2,1)S(1)}, bf16[64,1280]{1,0:T(8,128)(2,1)S(1)}, u32[]{:S(2)}, u32[]{:S(2)}) collective-permute-start(bf16[64,1280]{1,0:T(8,128)(2,1)S(1)} %add_convert_fusion.3), channel_id=1, source_target_pairs={{0,2},{1,3},{2,0},{3,1},{4,6},{5,7},{6,4},{7,5},{8,10},{9,11},{10,... | collective-permute-start | bytes 491528 | tf_op jit(solution)/shard_map/ppermute | solution.py:549
  64.9 3.4 %collective-permute-done.14 = bf16[64,1280]{1,0:T(8,128)(2,1)S(1)} collective-permute-done((bf16[64,1280]{1,0:T(8,128)(2,1)S(1)}, bf16[64,1280]{1,0:T(8,128)(2,1)S(1)}, u32[]{:S(2)}, u32[]{:S(2)}) %collective-permute-start.14) | collective-permute-done | bytes 163872 | tf_op jit(solution)/shard_map/ppermute | solution.py:549
  68.4 1.6 %collective-permute-start.15 = (bf16[64,1280]{1,0:T(8,128)(2,1)S(1)}, bf16[64,1280]{1,0:T(8,128)(2,1)S(1)}, u32[]{:S(2)}, u32[]{:S(2)}) collective-permute-start(bf16[64,1280]{1,0:T(8,128)(2,1)S(1)} %add_convert_fusion.2), channel_id=1, source_target_pairs={{0,2},{1,3},{2,0},{3,1},{4,6},{5,7},{6,4},{7,5},{8,10},{9,11},{10,... | collective-permute-start | bytes 491528 | tf_op jit(solution)/shard_map/ppermute | solution.py:549
  70.0 1.9 %stage.5.refs_3_.refs_0_ = bf16[2560,640]{1,0:T(8,128)(2,1)S(1)} custom-call(bf16[2560,640]{1,0:T(8,128)(2,1)} %refs_0_.2), custom_call_target="tpu_custom_call" | custom-call | bytes 3276800 | tf_op jit(solution)/shard_map/stage/pallas_call | solution.py:372
  72.0 4.4 %collective-permute-done.17 = bf16[64,1280]{1,0:T(8,128)(2,1)S(1)} collective-permute-done((bf16[64,1280]{1,0:T(8,128)(2,1)S(1)}, bf16[64,1280]{1,0:T(8,128)(2,1)S(1)}, u32[]{:S(2)}, u32[]{:S(2)}) %collective-permute-start.17) | collective-permute-done | bytes 163872 | tf_op jit(solution)/shard_map/ppermute | solution.py:549
  76.5 1.7 %collective-permute-done.15 = bf16[64,1280]{1,0:T(8,128)(2,1)S(1)} collective-permute-done((bf16[64,1280]{1,0:T(8,128)(2,1)S(1)}, bf16[64,1280]{1,0:T(8,128)(2,1)S(1)}, u32[]{:S(2)}, u32[]{:S(2)}) %collective-permute-start.15) | collective-permute-done | bytes 163872 | tf_op jit(solution)/shard_map/ppermute | solution.py:549
  78.2 0.8 collective-permute-start.16
  79.0 1.2 %next_layer.2 = (bf16[64,640]{1,0:T(8,128)(2,1)S(1)}, bf16[320,64]{1,0:T(8,128)(2,1)S(1)}) custom-call(bf16[64,1280]{1,0:T(8,128)(2,1)S(1)} %add_convert_fusion.1.refs_0_.refs_9_, bf16[64,1280]{1,0:T(8,128)(2,1)S(1)} %add_convert_fusion.refs_1_.refs_10_, bf16[1,2560]{1,0:T(2,128)(2,1)S(1)} %reshape.15.refs_2_.gain_ref, ...), custom_call_target="tpu_custom_call" | custom-call | flops 314572800 | bytes 4915200 | tf_op jit(solution)/shard_map/next_layer/pallas_call | solution.py:532
  80.2 2.8 %collective-permute-done.18.rows_ref.refs_1_ = bf16[64,1280]{1,0:T(8,128)(2,1)S(1)} collective-permute-done((bf16[64,1280]{1,0:T(8,128)(2,1)S(1)}, bf16[64,1280]{1,0:T(8,128)(2,1)S(1)}, u32[]{:S(2)}, u32[]{:S(2)}) %collective-permute-start.18) | collective-permute-done | bytes 163872 | tf_op jit(solution)/shard_map/ppermute | solution.py:549
  83.0 0.6 early_piece.3
  83.6 1.1 %collective-permute-done.16.refs_0_ = bf16[64,1280]{1,0:T(8,128)(2,1)S(1)} collective-permute-done((bf16[64,1280]{1,0:T(8,128)(2,1)S(1)}, bf16[64,1280]{1,0:T(8,128)(2,1)S(1)}, u32[]{:S(2)}, u32[]{:S(2)}) %collective-permute-start.16) | collective-permute-done | bytes 163872 | tf_op jit(solution)/shard_map/ppermute | solution.py:549
  84.8 1.5 %next_layer.3 = (bf16[128,640]{1,0:T(8,128)(2,1)}, bf16[320,128]{1,0:T(8,128)(2,1)}, bf16[32,2560]{1,0:T(8,128)(2,1)}) custom-call(bf16[64,1280]{1,0:T(8,128)(2,1)S(1)} %collective-permute-done.16.refs_0_, bf16[64,1280]{1,0:T(8,128)(2,1)S(1)} %collective-permute-done.18.rows_ref.refs_1_, bf16[1,2560]{1,0:T(2,128)(2,1)S(1)} %reshape.15.refs_2_.gain_ref, ...), custom_call_target="tpu_custom_call" | custom-call | flops 314572800 | bytes 4915200 | tf_op jit(solution)/shard_map/next_layer/pallas_call | solution.py:532
  (30 shorter events, 0.7 us)
Async XLA Ops:
  1.7 5.6 %collective-permute-start.1 = (bf16[512,384]{1,0:T(8,128)(2,1)S(1)}, bf16[512,384]{1,0:T(8,128)(2,1)S(1)}, u32[]{:S(2)}, u32[]{:S(2)}) collective-permute-start(bf16[512,384]{1,0:T(8,128)(2,1)S(1)} %pool_rows.1.refs_0_), channel_id=1, source_target_pairs={{0,4},{4,0},{8,12},{12,8},{16,20},{20,16},{24,28},{28,24},{1,5},{5... | collective-permute-start | bytes 1179656 | tf_op jit(solution)/shard_map/ppermute | solution.py:549
  2.2 11.4 %collective-permute-start = (bf16[512,384]{1,0:T(8,128)(2,1)S(1)}, bf16[512,384]{1,0:T(8,128)(2,1)S(1)}, u32[]{:S(2)}, u32[]{:S(2)}) collective-permute-start(bf16[512,384]{1,0:T(8,128)(2,1)S(1)} %pool_rows.1.refs_0_), channel_id=1, source_target_pairs={{0,8},{4,20},{8,0},{12,28},{16,24},{20,4},{24,16},{28,12},{1,9},{5... | collective-permute-start | bytes 1179656 | tf_op jit(solution)/shard_map/ppermute | solution.py:555
  4.8 9.7 %collective-permute-start.3 = (bf16[512,384]{1,0:T(8,128)(2,1)S(1)}, bf16[512,384]{1,0:T(8,128)(2,1)S(1)}, u32[]{:S(2)}, u32[]{:S(2)}) collective-permute-start(bf16[512,384]{1,0:T(8,128)(2,1)S(1)} %pool_rows.1.refs_0_), channel_id=1, source_target_pairs={{0,16},{4,12},{8,24},{12,4},{16,0},{20,28},{24,8},{28,20},{1,17},{... | collective-permute-start | bytes 1179656 | tf_op jit(solution)/shard_map/ppermute | solution.py:555
  7.3 1.0 %copy-start.3 = (bf16[16,32,320]{2,1,0:T(8,128)(2,1)S(1)}, bf16[16,32,320]{2,1,0:T(8,128)(2,1)}, u32[]{:S(2)}) copy-start(bf16[16,32,320]{2,1,0:T(8,128)(2,1)} %leaf_ref.1) | copy-start | bytes 983044
  8.3 0.9 %copy-start.4 = (bf16[128,640]{1,0:T(8,128)(2,1)S(1)}, bf16[128,640]{1,0:T(8,128)(2,1)}, u32[]{:S(2)}) copy-start(bf16[128,640]{1,0:T(8,128)(2,1)} %query_ref.1) | copy-start | bytes 491524
  14.5 2.3 %collective-permute-start.4 = (bf16[512,384]{1,0:T(8,128)(2,1)S(1)}, bf16[512,384]{1,0:T(8,128)(2,1)S(1)}, u32[]{:S(2)}, u32[]{:S(2)}) collective-permute-start(bf16[512,384]{1,0:T(8,128)(2,1)S(1)} %collective-permute-done.refs_2_), channel_id=1, source_target_pairs={{0,4},{4,0},{8,12},{12,8},{16,20},{20,16},{24,28},{28,24},{1,5},{5... | collective-permute-start | bytes 1179656 | tf_op jit(solution)/shard_map/ppermute | solution.py:549
  14.7 2.2 %collective-permute-start.5 = (bf16[512,384]{1,0:T(8,128)(2,1)S(1)}, bf16[512,384]{1,0:T(8,128)(2,1)S(1)}, u32[]{:S(2)}, u32[]{:S(2)}) collective-permute-start(bf16[512,384]{1,0:T(8,128)(2,1)S(1)} %collective-permute-done.3.refs_3_), channel_id=1, source_target_pairs={{0,4},{4,0},{8,12},{12,8},{16,20},{20,16},{24,28},{28,24},{1,5},{5... | collective-permute-start | bytes 1179656 | tf_op jit(solution)/shard_map/ppermute | solution.py:549
  15.0 7.8 %collective-permute-start.2 = (bf16[512,384]{1,0:T(8,128)(2,1)S(1)}, bf16[512,384]{1,0:T(8,128)(2,1)S(1)}, u32[]{:S(2)}, u32[]{:S(2)}) collective-permute-start(bf16[512,384]{1,0:T(8,128)(2,1)S(1)} %collective-permute-done.refs_2_), channel_id=1, source_target_pairs={{0,16},{4,12},{8,24},{12,4},{16,0},{20,28},{24,8},{28,20},{1,17},{... | collective-permute-start | bytes 1179656 | tf_op jit(solution)/shard_map/ppermute | solution.py:555
  20.4 4.5 %copy-start.1 = (bf16[640,2560]{1,0:T(8,128)(2,1)S(1)}, bf16[640,2560]{1,0:T(8,128)(2,1)}, u32[]{:S(2)}) copy-start(bf16[640,2560]{1,0:T(8,128)(2,1)} %refs_3_.3) | copy-start | bytes 9830404
  22.9 6.3 %copy-start.2 = (bf16[128,2560]{1,0:T(8,128)(2,1)S(1)}, bf16[128,2560]{1,0:T(8,128)(2,1)}, u32[]{:S(2)}) copy-start(bf16[128,2560]{1,0:T(8,128)(2,1)} %refs_5_.1) | copy-start | bytes 1966084
  22.9 2.0 %collective-permute-start.6 = (bf16[512,384]{1,0:T(8,128)(2,1)S(1)}, bf16[512,384]{1,0:T(8,128)(2,1)S(1)}, u32[]{:S(2)}, u32[]{:S(2)}) collective-permute-start(bf16[512,384]{1,0:T(8,128)(2,1)S(1)} %collective-permute-done.2.refs_2_), channel_id=1, source_target_pairs={{0,4},{4,0},{8,12},{12,8},{16,20},{20,16},{24,28},{28,24},{1,5},{5... | collective-permute-start | bytes 1179656 | tf_op jit(solution)/shard_map/ppermute | solution.py:549
  27.0 6.7 %collective-permute-start.7 = (bf16[64,1280]{1,0:T(8,128)(2,1)S(1)}, bf16[64,1280]{1,0:T(8,128)(2,1)S(1)}, u32[]{:S(2)}, u32[]{:S(2)}) collective-permute-start(bf16[64,1280]{1,0:T(8,128)(2,1)S(1)} %get-tuple-element.67), channel_id=1, source_target_pairs={{0,1},{1,0},{2,3},{3,2},{4,5},{5,4},{6,7},{7,6},{8,9},{9,8},{10,11... | collective-permute-start | bytes 491528 | tf_op jit(solution)/shard_map/ppermute | solution.py:549
  31.6 8.4 %collective-permute-start.10 = (bf16[64,1280]{1,0:T(8,128)(2,1)S(1)}, bf16[64,1280]{1,0:T(8,128)(2,1)S(1)}, u32[]{:S(2)}, u32[]{:S(2)}) collective-permute-start(bf16[64,1280]{1,0:T(8,128)(2,1)S(1)} %get-tuple-element.69), channel_id=1, source_target_pairs={{0,1},{1,0},{2,3},{3,2},{4,5},{5,4},{6,7},{7,6},{8,9},{9,8},{10,11... | collective-permute-start | bytes 491528 | tf_op jit(solution)/shard_map/ppermute | solution.py:549
  33.7 14.7 %collective-permute-start.8 = (bf16[64,1280]{1,0:T(8,128)(2,1)S(1)}, bf16[64,1280]{1,0:T(8,128)(2,1)S(1)}, u32[]{:S(2)}, u32[]{:S(2)}) collective-permute-start(bf16[64,1280]{1,0:T(8,128)(2,1)S(1)} %add_convert_fusion.7), channel_id=1, source_target_pairs={{0,2},{1,3},{2,0},{3,1},{4,6},{5,7},{6,4},{7,5},{8,10},{9,11},{10,... | collective-permute-start | bytes 491528 | tf_op jit(solution)/shard_map/ppermute | solution.py:549
  40.0 11.6 %copy-start.5 = (bf16[2560]{0:T(1024)(128)(2,1)S(1)}, bf16[2560]{0:T(1024)(128)(2,1)}, u32[]{:S(2)}) copy-start(bf16[2560]{0:T(1024)(128)(2,1)} %param.33) | copy-start | bytes 15364
  40.1 11.0 %collective-permute-start.11 = (bf16[64,1280]{1,0:T(8,128)(2,1)S(1)}, bf16[64,1280]{1,0:T(8,128)(2,1)S(1)}, u32[]{:S(2)}, u32[]{:S(2)}) collective-permute-start(bf16[64,1280]{1,0:T(8,128)(2,1)S(1)} %add_convert_fusion.5), channel_id=1, source_target_pairs={{0,2},{1,3},{2,0},{3,1},{4,6},{5,7},{6,4},{7,5},{8,10},{9,11},{10,... | collective-permute-start | bytes 491528 | tf_op jit(solution)/shard_map/ppermute | solution.py:549
  48.4 7.2 %collective-permute-start.9 = (bf16[64,1280]{1,0:T(8,128)(2,1)S(1)}, bf16[64,1280]{1,0:T(8,128)(2,1)S(1)}, u32[]{:S(2)}, u32[]{:S(2)}) collective-permute-start(bf16[64,1280]{1,0:T(8,128)(2,1)S(1)} %add_convert_fusion.6.refs_0_), channel_id=1, source_target_pairs={{0,1},{1,0},{2,3},{3,2},{4,5},{5,4},{6,7},{7,6},{8,9},{9,8},{10,11... | collective-permute-start | bytes 491528 | tf_op jit(solution)/shard_map/ppermute | solution.py:549
  51.1 8.0 %collective-permute-start.12 = (bf16[64,1280]{1,0:T(8,128)(2,1)S(1)}, bf16[64,1280]{1,0:T(8,128)(2,1)S(1)}, u32[]{:S(2)}, u32[]{:S(2)}) collective-permute-start(bf16[64,1280]{1,0:T(8,128)(2,1)S(1)} %add_convert_fusion.4.refs_1_), channel_id=1, source_target_pairs={{0,1},{1,0},{2,3},{3,2},{4,5},{5,4},{6,7},{7,6},{8,9},{9,8},{10,11... | collective-permute-start | bytes 491528 | tf_op jit(solution)/shard_map/ppermute | solution.py:549
  53.7 7.7 %collective-permute-start.13 = (bf16[64,1280]{1,0:T(8,128)(2,1)S(1)}, bf16[64,1280]{1,0:T(8,128)(2,1)S(1)}, u32[]{:S(2)}, u32[]{:S(2)}) collective-permute-start(bf16[64,1280]{1,0:T(8,128)(2,1)S(1)} %get-tuple-element.86), channel_id=1, source_target_pairs={{0,1},{1,0},{2,3},{3,2},{4,5},{5,4},{6,7},{7,6},{8,9},{9,8},{10,11... | collective-permute-start | bytes 491528 | tf_op jit(solution)/shard_map/ppermute | solution.py:549
  61.2 7.2 %collective-permute-start.14 = (bf16[64,1280]{1,0:T(8,128)(2,1)S(1)}, bf16[64,1280]{1,0:T(8,128)(2,1)S(1)}, u32[]{:S(2)}, u32[]{:S(2)}) collective-permute-start(bf16[64,1280]{1,0:T(8,128)(2,1)S(1)} %get-tuple-element.87), channel_id=1, source_target_pairs={{0,1},{1,0},{2,3},{3,2},{4,5},{5,4},{6,7},{7,6},{8,9},{9,8},{10,11... | collective-permute-start | bytes 491528 | tf_op jit(solution)/shard_map/ppermute | solution.py:549
  61.5 17.5 %copy-start.6 = (bf16[2560]{0:T(1024)(128)(2,1)S(1)}, bf16[2560]{0:T(1024)(128)(2,1)}, u32[]{:S(2)}) copy-start(bf16[2560]{0:T(1024)(128)(2,1)} %param.37) | copy-start | bytes 15364
  61.5 17.5 %copy-start = (bf16[2560,320]{0,1:T(8,128)(2,1)S(1)}, bf16[2560,320]{0,1:T(8,128)(2,1)}, u32[]{:S(2)}) copy-start(bf16[2560,320]{0,1:T(8,128)(2,1)} %param.39) | copy-start | bytes 4915204
  61.5 14.8 %collective-permute-start.17 = (bf16[64,1280]{1,0:T(8,128)(2,1)S(1)}, bf16[64,1280]{1,0:T(8,128)(2,1)S(1)}, u32[]{:S(2)}, u32[]{:S(2)}) collective-permute-start(bf16[64,1280]{1,0:T(8,128)(2,1)S(1)} %add_convert_fusion.3), channel_id=1, source_target_pairs={{0,2},{1,3},{2,0},{3,1},{4,6},{5,7},{6,4},{7,5},{8,10},{9,11},{10,... | collective-permute-start | bytes 491528 | tf_op jit(solution)/shard_map/ppermute | solution.py:549
  68.4 9.8 %collective-permute-start.15 = (bf16[64,1280]{1,0:T(8,128)(2,1)S(1)}, bf16[64,1280]{1,0:T(8,128)(2,1)S(1)}, u32[]{:S(2)}, u32[]{:S(2)}) collective-permute-start(bf16[64,1280]{1,0:T(8,128)(2,1)S(1)} %add_convert_fusion.2), channel_id=1, source_target_pairs={{0,2},{1,3},{2,0},{3,1},{4,6},{5,7},{6,4},{7,5},{8,10},{9,11},{10,... | collective-permute-start | bytes 491528 | tf_op jit(solution)/shard_map/ppermute | solution.py:549
  76.4 6.6 %collective-permute-start.18 = (bf16[64,1280]{1,0:T(8,128)(2,1)S(1)}, bf16[64,1280]{1,0:T(8,128)(2,1)S(1)}, u32[]{:S(2)}, u32[]{:S(2)}) collective-permute-start(bf16[64,1280]{1,0:T(8,128)(2,1)S(1)} %add_convert_fusion.refs_1_.refs_10_), channel_id=1, source_target_pairs={{0,1},{1,0},{2,3},{3,2},{4,5},{5,4},{6,7},{7,6},{8,9},{9,8},{10,11... | collective-permute-start | bytes 491528 | tf_op jit(solution)/shard_map/ppermute | solution.py:549
  78.2 6.6 %collective-permute-start.16 = (bf16[64,1280]{1,0:T(8,128)(2,1)S(1)}, bf16[64,1280]{1,0:T(8,128)(2,1)S(1)}, u32[]{:S(2)}, u32[]{:S(2)}) collective-permute-start(bf16[64,1280]{1,0:T(8,128)(2,1)S(1)} %add_convert_fusion.1.refs_0_.refs_9_), channel_id=1, source_target_pairs={{0,1},{1,0},{2,3},{3,2},{4,5},{5,4},{6,7},{7,6},{8,9},{9,8},{10,11... | collective-permute-start | bytes 491528 | tf_op jit(solution)/shard_map/ppermute | solution.py:549

commit v10 on v9

--- a/solution.py
+++ b/solution.py
@@ -70,12 +70,13 @@
 
 
 def piece(width, k):
-    step = width // PIECES
-    return slice(k * step, (k + 1) * step)
+    cut = width * 9 // 20
+    return slice(cut, width) if k else slice(0, cut)
 
 
 def pieces_of(rows, width, dtype):
-    return tuple(jax.ShapeDtypeStruct((rows, width // PIECES), dtype) for _ in range(PIECES))
+    places = [piece(width, k) for k in range(PIECES)]
+    return tuple(jax.ShapeDtypeStruct((rows, p.stop - p.start), dtype) for p in places)
 
 
 def joined(refs):
@@ -306,7 +307,7 @@
     if half:
         send_refs, proj_refs = proj_refs[: PIECES - 1], proj_refs[PIECES - 1 :]
         proj_refs, res_refs = proj_refs[:PIECES], proj_refs[PIECES:]
-        project(send_refs, rest[0][...], weight_ref, range(1, PIECES))
+        project(send_refs, rest[0][...], weight_ref, range(PIECES - 1))
     group = width // (kv_local * HD)
     size = group * part
     for c in range(kv_local):
@@ -329,7 +330,7 @@
             res_ref[...] = rest[1][pl.ds(mine, part), piece(rest[1].shape[1], k)]
     else:
         att_ref[...] = mine_ref[...]
-    project(proj_refs, mine_ref[...], weight_ref, range(PIECES if half else 1))
+    project(proj_refs, mine_ref[...], weight_ref, range(PIECES) if half else [PIECES - 1])
 
 
 def finish_attention(aug, state, pools, out_weight, half, kv_local, rows, other):
@@ -400,27 +401,37 @@
     return jnp.dot(rows, weight, preferred_element_type=f32)
 
 
-def early_kernel(rows_ref, gain_ref, *refs, k, flips):
-    rows = gained(rows_ref[...], gain_ref, k)
+def early_kernel(*refs, k, flips, terms):
+    row_refs, (gain_ref, *refs) = refs[:terms], refs[terms:]
+    rows = row_refs[0][...]
+    if terms > 1:
+        rows = add_rows(rows, row_refs[1][...], row_refs[2][...])
+        refs[len(flips)][...] = rows
+        refs = (*refs[: len(flips)], *refs[len(flips) + 1 :])
+    rows = gained(rows, gain_ref, k)
     count = len(flips)
     for weight_ref, out_ref, flipped in zip(refs[:count], refs[count:], flips):
         out_ref[...] = times(rows, weight_ref, k, flipped)
 
 
 def early_products(rows, gain, weights, k=0, flips=(False, False)):
+    terms = rows if isinstance(rows, tuple) else (rows,)
+    rows = terms[0]
     count = rows.shape[0]
     shapes = [
         jax.ShapeDtypeStruct((w.shape[0], count) if flipped else (count, w.shape[1]), f32)
         for w, flipped in zip(weights, flips)
     ]
+    if len(terms) > 1:
+        shapes.insert(0, jax.ShapeDtypeStruct(rows.shape, bf16))
     return pl.pallas_call(
-        functools.partial(early_kernel, k=k, flips=flips),
+        functools.partial(early_kernel, k=k, flips=flips, terms=len(terms)),
         out_shape=tuple(shapes),
-        in_specs=[VMEM] * (2 + len(weights)),
-        out_specs=(VMEM,) * len(weights),
+        in_specs=[VMEM] * (len(terms) + 1 + len(weights)),
+        out_specs=(VMEM,) * len(shapes),
         compiler_params=PARAMS,
         name="early_piece",
-    )(rows, gain.reshape(1, -1), *weights)
+    )(*terms, gain.reshape(1, -1), *weights)
 
 
 def mlp_kernel(*refs, second, early):
@@ -432,7 +443,7 @@
     if second:
         project(refs[1:PIECES], refs[0][...], down_ref, range(PIECES - 1))
     scale = inverse_rms(row_refs)
-    for k in range(early, PIECES):
+    for k in range(PIECES - early):
         rows = gained(row_refs[k][...], gain_ref, k)
         sums = [item + times(rows, ref, k) for item, ref in zip(sums, (gate_ref, up_ref))]
     gate, upward = sums
@@ -642,7 +653,7 @@
     attention, *mine_proj = finish_attention(
         aug, state, pools, out_weight, 1, kv_local, rows, (theirs_att, residual_in)
     )
-    theirs_proj = theirs_proj + mine_proj[: PIECES - 1]
+    theirs_proj = mine_proj[: PIECES - 1] + theirs_proj
     mine_proj, res_mine = mine_proj[PIECES - 1 : -PIECES], mine_proj[-PIECES:]
 
     mine = half_start(rows, 1)
@@ -650,19 +661,19 @@
     depth = residual_in.shape[1]
     if lax.axis_size("tp") == 4:
         got = trades(theirs_proj, 1)
-        pair, (gate_weight, up_weight) = pairs_in_turn(
-            mine_proj[::-1], got[::-1], (gate_weight, up_weight)
-        )
-        pair = pair[::-1]
+        pair, (gate_weight, up_weight) = pairs_in_turn(mine_proj, got, (gate_weight, up_weight))
         got = trades(pair, 2)
         got[-1], *staged = lax.optimization_barrier((got[-1], *stage([gate_weight, up_weight])))
         mlp = (*staged, down_weight)
-        mixed_mine = each(add_rows, pair, res_mine, got)
+        lead, *early = early_products(
+            (pair[-1], res_mine[-1], got[-1]), norm_gain, mlp[:2], PIECES - 1
+        )
+        mixed_mine = [*each(add_rows, pair[:-1], res_mine[:-1], got[:-1]), lead]
         mixed_theirs = trades(mixed_mine, 1)
-        hidden, last = feed_forward(mixed_mine, (), norm_gain, *mlp)
+        hidden, last = feed_forward(mixed_mine, early, norm_gain, *mlp)
         last = trade(last, "tp", 1)
-        early = early_products(mixed_theirs[0], norm_gain, mlp[:2])
-        _, mixed_theirs[1:] = lax.optimization_barrier((early, mixed_theirs[1:]))
+        early = early_products(mixed_theirs[-1], norm_gain, mlp[:2], PIECES - 1)
+        _, mixed_theirs[:-1] = lax.optimization_barrier((early, mixed_theirs[:-1]))
         result = feed_forward(mixed_theirs, early, norm_gain, *mlp, [hidden])
         got = [*trades(result[: PIECES - 1], 1), last]
         mlp_theirs = result[PIECES - 1 :]

time: 86.5 us -> 87.2 us (level)
  starting transfers between devices: 21.8 us -> 23 us
    ppermute x16, starting transfers between devices: 15.9 us -> 17.1 us  [trade(): return lax.ppermute(value, axis, [(i, i ^ bit) for i in range(size)])]
    pallas_call x2 -> x3, Pallas kernels: 1.41 us -> 2.52 us  [early_products(): pl.pallas_call(functools.partial(early_kernel, k=k, flips=flips, terms=le...]
where the time goes in v10:
time: 87.2 us; the launch traced here: 87 us
  Pallas kernels  31.3 us (36%)
  waiting for transfers between devices  28.6 us (33%)
  starting transfers between devices  23 us (26%)
  local copies, waits for them, and re-layouts  2.94 us (3%)
    ppermute x16, waiting for transfers between devices, trade(): return lax.ppermute(value, axis, [(i, i ^ bit) for i in range(size)])  27 us
    ppermute x16, starting transfers between devices, trade(): return lax.ppermute(value, axis, [(i, i ^ bit) for i in range(size)])  17.1 us
    pallas_call x3, Pallas kernels, stage(): pl.pallas_call(stage_kernel, out_shape=tuple((pltpu.VMEM(w.shape, w.dtype...  8.12 us
    ppermute x3, starting transfers between devices, cross(): return lax.ppermute(value, 'req', pairs)  5.83 us
    pallas_call x2, Pallas kernels, extend_attention(): pl.pallas_call(functools.partial(chunk_kernel, blocks=2 * kv_local), out_...  5.36 us
    pallas_call x2, Pallas kernels, finish_attention(): pl.pallas_call(functools.partial(finish_kernel, half=half, kv_local=kv_lo...  4.53 us
    pallas_call x1, Pallas kernels, start_attention(): pl.pallas_call(functools.partial(local_kernel, chunks=len(pools)), out_sh...  3.77 us
    pallas_call x2, Pallas kernels, feed_forward(): pl.pallas_call(functools.partial(mlp_kernel, second=len(other) > 0, early...  3.28 us
  transfers between devices with their start and end apart: 19, of which 14 were waited for; matrix products, arithmetic and copies ran while one was open for 2% of the time, Pallas kernels for 31%

profile of v10, /device:TPU:0, one launch (start us, length us, event | category | flops | bytes accessed | tf_op | source)
XLA Modules:
  0.0 87.0 jit_solution(4096632934708095480)
XLA Ops:
  0.6 1.1 %pool_rows.1.refs_0_ = bf16[512,384]{1,0:T(8,128)(2,1)S(1)} custom-call(s32[32]{0:T(128)} %node_hbm.1, s32[32]{0:T(128)} %rank_hbm.1, s32[8]{0:T(128)} %length_hbm.1, s32[6]{0:T(128)} %root_hbm.1, bf16[32,16,320]{2,1,0:T(8,128)(2,1)} %pool_hbm.1), custom_call_target="tpu_custom_call" | custom-call | tf_op jit(solution)/shard_map/pool_rows/pallas_call | solution.py:129
  1.7 0.5 collective-permute-start.1
  2.2 2.6 %collective-permute-start = (bf16[512,384]{1,0:T(8,128)(2,1)S(1)}, bf16[512,384]{1,0:T(8,128)(2,1)S(1)}, u32[]{:S(2)}, u32[]{:S(2)}) collective-permute-start(bf16[512,384]{1,0:T(8,128)(2,1)S(1)} %pool_rows.1.refs_0_), channel_id=1, source_target_pairs={{0,8},{4,20},{8,0},{12,28},{16,24},{20,4},{24,16},{28,12},{1,9},{5... | collective-permute-start | bytes 1179656 | tf_op jit(solution)/shard_map/ppermute | solution.py:566
  4.8 1.5 %collective-permute-start.3 = (bf16[512,384]{1,0:T(8,128)(2,1)S(1)}, bf16[512,384]{1,0:T(8,128)(2,1)S(1)}, u32[]{:S(2)}, u32[]{:S(2)}) collective-permute-start(bf16[512,384]{1,0:T(8,128)(2,1)S(1)} %pool_rows.1.refs_0_), channel_id=1, source_target_pairs={{0,16},{4,12},{8,24},{12,4},{16,0},{20,28},{24,8},{28,20},{1,17},{... | collective-permute-start | bytes 1179656 | tf_op jit(solution)/shard_map/ppermute | solution.py:566
  6.3 1.0 %copy.24.keyval_ref = bf16[128,320]{1,0:T(8,128)(2,1)S(1)} copy(bf16[128,320]{0,1:T(8,128)(2,1)} %param.21) | data formatting | bytes 163840 | tf_op args[1]
  7.3 1.0 %copy-done.3 = bf16[16,32,320]{2,1,0:T(8,128)(2,1)S(1)} copy-done((bf16[16,32,320]{2,1,0:T(8,128)(2,1)S(1)}, bf16[16,32,320]{2,1,0:T(8,128)(2,1)}, u32[]{:S(2)}) %copy-start.3) | copy-done | bytes 327704
  8.3 0.9 %copy-done.4 = bf16[128,640]{1,0:T(8,128)(2,1)S(1)} copy-done((bf16[128,640]{1,0:T(8,128)(2,1)S(1)}, bf16[128,640]{1,0:T(8,128)(2,1)}, u32[]{:S(2)}) %copy-start.4) | copy-done | bytes 163864
  9.2 3.8 %attend_local.1 = (bf16[1024,256]{1,0:T(8,128)(2,1)S(1)}, f32[1024,256]{1,0:T(8,128)S(1)}) custom-call(s32[1,16]{1,0:T(1,128)} %count_hbm.1, s32[16]{0:T(128)} %mid_hbm.1, s32[16]{0:T(128)} %leaf_len_hbm.1, bf16[128,640]{1,0:T(8,128)(2,1)S(1)} %copy-done.4, bf16[128,320]{1,0:T(8,128)(2,1)S(1)} %copy.24.keyval_ref, bf16[16,32,320]{2,1,0:T(8,128)(2,1)S(1)} %copy-done.3, ...), custom_call_target="tpu_custom_call" | custom-call | flops 1744830464 | bytes 2097152 | tf_op jit(solution)/shard_map/attend_local/pallas_call | solution.py:243
  13.0 0.6 collective-permute-done.refs_2_
  13.6 0.9 %collective-permute-done.3.refs_3_ = bf16[512,384]{1,0:T(8,128)(2,1)S(1)} collective-permute-done((bf16[512,384]{1,0:T(8,128)(2,1)S(1)}, bf16[512,384]{1,0:T(8,128)(2,1)S(1)}, u32[]{:S(2)}, u32[]{:S(2)}) %collective-permute-start.3) | collective-permute-done | bytes 393248 | tf_op jit(solution)/shard_map/ppermute | solution.py:566
  14.7 0.4 collective-permute-start.5
  15.0 1.8 %collective-permute-start.2 = (bf16[512,384]{1,0:T(8,128)(2,1)S(1)}, bf16[512,384]{1,0:T(8,128)(2,1)S(1)}, u32[]{:S(2)}, u32[]{:S(2)}) collective-permute-start(bf16[512,384]{1,0:T(8,128)(2,1)S(1)} %collective-permute-done.refs_2_), channel_id=1, source_target_pairs={{0,16},{4,12},{8,24},{12,4},{16,0},{20,28},{24,8},{28,20},{1,17},{... | collective-permute-start | bytes 1179656 | tf_op jit(solution)/shard_map/ppermute | solution.py:566
  16.8 3.6 %attend_pages.2.refs_1_ = f32[1024,256]{1,0:T(8,128)S(1)} custom-call(bf16[1024,256]{1,0:T(8,128)(2,1)S(1)} %get-tuple-element.57.refs_0_, f32[1024,256]{1,0:T(8,128)S(1)} %get-tuple-element.59.refs_1_, bf16[512,384]{1,0:T(8,128)(2,1)S(1)} %collective-permute-done.refs_2_, bf16[512,384]{1,0:T(8,128)(2,1)S(1)} %collective-permute-done.3.refs_3_, ...), custom_call_target="tpu_custom_call" | custom-call | flops 2147483648 | bytes 2097152 | tf_op jit(solution)/shard_map/attend_pages/pallas_call | solution.py:282
  20.4 2.5 %stage.3.refs_5_ = bf16[896,2560]{1,0:T(8,128)(2,1)S(1)} custom-call(bf16[896,2560]{1,0:T(8,128)(2,1)} %refs_0_), custom_call_target="tpu_custom_call" | custom-call | bytes 4587520 | tf_op jit(solution)/shard_map/stage/pallas_call | solution.py:373
  23.1 1.8 %attend_pages.3.refs_1_ = f32[1024,256]{1,0:T(8,128)S(1)} custom-call(bf16[1024,256]{1,0:T(8,128)(2,1)S(1)} %get-tuple-element.57.refs_0_, f32[1024,256]{1,0:T(8,128)S(1)} %attend_pages.2.refs_1_, bf16[512,384]{1,0:T(8,128)(2,1)S(1)} %collective-permute-done.2.refs_2_), custom_call_target="tpu_custom_call" | custom-call | flops 536870912 | bytes 2097152 | tf_op jit(solution)/shard_map/attend_pages/pallas_call | solution.py:282
  24.9 1.9 %attend_finish.2 = (bf16[64,640]{1,0:T(8,128)(2,1)S(1)}, bf16[64,1408]{1,0:T(8,128)(2,1)S(1)}) custom-call(bf16[1024,256]{1,0:T(8,128)(2,1)S(1)} %get-tuple-element.57.refs_0_, f32[1024,256]{1,0:T(8,128)S(1)} %attend_pages.3.refs_1_, bf16[512,384]{1,0:T(8,128)(2,1)S(1)} %collective-permute-done.6.refs_2_, bf16[640,2560]{1,0:T(8,128)(2,1)S(1)} %copy-done.1), custom_call_target="tpu_custom_call" | custom-call | flops 536870912 | bytes 1048576 | tf_op jit(solution)/shard_map/attend_finish/pallas_call | solution.py:346
  26.9 2.1 %collective-permute-start.7 = (bf16[64,1408]{1,0:T(8,128)(2,1)S(1)}, bf16[64,1408]{1,0:T(8,128)(2,1)S(1)}, u32[]{:S(2)}, u32[]{:S(2)}) collective-permute-start(bf16[64,1408]{1,0:T(8,128)(2,1)S(1)} %get-tuple-element.69), channel_id=1, source_target_pairs={{0,1},{1,0},{2,3},{3,2},{4,5},{5,4},{6,7},{7,6},{8,9},{9,8},{10,11... | collective-permute-start | bytes 540680 | tf_op jit(solution)/shard_map/ppermute | solution.py:560
  28.9 2.6 %attend_finish.3 = (bf16[128,640]{1,0:T(8,128)(2,1)}, bf16[64,1152]{1,0:T(8,128)(2,1)S(1)}, f32[64,1152]{1,0:T(8,128)S(1)}, f32[64,1408]{1,0:T(8,128)S(1)}, bf16...) custom-call(bf16[1024,256]{1,0:T(8,128)(2,1)S(1)} %get-tuple-element.57.refs_0_, ...), custom_call_target="tpu_custom_call" | custom-call | flops 536870912 | bytes 1048576 | tf_op jit(solution)/shard_map/attend_finish/pallas_call | solution.py:346
  31.6 2.2 %collective-permute-done.7 = bf16[64,1408]{1,0:T(8,128)(2,1)S(1)} collective-permute-done((bf16[64,1408]{1,0:T(8,128)(2,1)S(1)}, bf16[64,1408]{1,0:T(8,128)(2,1)S(1)}, u32[]{:S(2)}, u32[]{:S(2)}) %collective-permute-start.7) | collective-permute-done | bytes 180256 | tf_op jit(solution)/shard_map/ppermute | solution.py:560
  33.9 2.8 %collective-permute-start.8 = (bf16[64,1408]{1,0:T(8,128)(2,1)S(1)}, bf16[64,1408]{1,0:T(8,128)(2,1)S(1)}, u32[]{:S(2)}, u32[]{:S(2)}) collective-permute-start(bf16[64,1408]{1,0:T(8,128)(2,1)S(1)} %add_convert_fusion.2.refs_0_), channel_id=1, source_target_pairs={{0,2},{1,3},{2,0},{3,1},{4,6},{5,7},{6,4},{7,5},{8,10},{9,11},{10,... | collective-permute-start | bytes 540680 | tf_op jit(solution)/shard_map/ppermute | solution.py:560
  36.7 1.8 %collective-permute-done.9 = bf16[64,1152]{1,0:T(8,128)(2,1)S(1)} collective-permute-done((bf16[64,1152]{1,0:T(8,128)(2,1)S(1)}, bf16[64,1152]{1,0:T(8,128)(2,1)S(1)}, u32[]{:S(2)}, u32[]{:S(2)}) %collective-permute-start.9) | collective-permute-done | bytes 147488 | tf_op jit(solution)/shard_map/ppermute | solution.py:560
  38.5 2.5 %collective-permute-start.11 = (bf16[64,1152]{1,0:T(8,128)(2,1)S(1)}, bf16[64,1152]{1,0:T(8,128)(2,1)S(1)}, u32[]{:S(2)}, u32[]{:S(2)}) collective-permute-start(bf16[64,1152]{1,0:T(8,128)(2,1)S(1)} %add_convert_fusion.6), channel_id=1, source_target_pairs={{0,2},{1,3},{2,0},{3,1},{4,6},{5,7},{6,4},{7,5},{8,10},{9,11},{10,... | collective-permute-start | bytes 442376 | tf_op jit(solution)/shard_map/ppermute | solution.py:560
  41.1 3.7 %stage.4 = (bf16[2560,896]{1,0:T(8,128)(2,1)S(1)}, bf16[2560,896]{1,0:T(8,128)(2,1)S(1)}) custom-call(bf16[2560,896]{1,0:T(8,128)(2,1)} %refs_0_.1, bf16[2560,896]{1,0:T(8,128)(2,1)} %refs_1_), custom_call_target="tpu_custom_call" | custom-call | bytes 9175040 | tf_op jit(solution)/shard_map/stage/pallas_call | solution.py:373
  44.8 4.4 %collective-permute-done.8.refs_2_ = bf16[64,1408]{1,0:T(8,128)(2,1)S(1)} collective-permute-done((bf16[64,1408]{1,0:T(8,128)(2,1)S(1)}, bf16[64,1408]{1,0:T(8,128)(2,1)S(1)}, u32[]{:S(2)}, u32[]{:S(2)}) %collective-permute-start.8) | collective-permute-done | bytes 180256 | tf_op jit(solution)/shard_map/ppermute | solution.py:560
  49.2 0.9 %early_piece.3 = (bf16[64,1408]{1,0:T(8,128)(2,1)S(1)}, f32[64,896]{1,0:T(8,128)S(1)}, f32[64,896]{1,0:T(8,128)S(1)}) custom-call(bf16[64,1408]{1,0:T(8,128)(2,1)S(1)} %add_convert_fusion.2.refs_0_, bf16[64,1408]{1,0:T(8,128)(2,1)S(1)} %get-tuple-element.70.refs_1_, bf16[64,1408]{1,0:T(8,128)(2,1)S(1)} %collective-permute-done.8.refs_2_, ...), custom_call_target="tpu_custom_call" | custom-call | tf_op jit(solution)/shard_map/early_piece/pallas_call | solution.py:427
  50.2 1.0 %collective-permute-done.11 = bf16[64,1152]{1,0:T(8,128)(2,1)S(1)} collective-permute-done((bf16[64,1152]{1,0:T(8,128)(2,1)S(1)}, bf16[64,1152]{1,0:T(8,128)(2,1)S(1)}, u32[]{:S(2)}, u32[]{:S(2)}) %collective-permute-start.11) | collective-permute-done | bytes 147488 | tf_op jit(solution)/shard_map/ppermute | solution.py:560
  51.3 1.1 %collective-permute-start.12 = (bf16[64,1152]{1,0:T(8,128)(2,1)S(1)}, bf16[64,1152]{1,0:T(8,128)(2,1)S(1)}, u32[]{:S(2)}, u32[]{:S(2)}) collective-permute-start(bf16[64,1152]{1,0:T(8,128)(2,1)S(1)} %add_convert_fusion.5.refs_0_), channel_id=1, source_target_pairs={{0,1},{1,0},{2,3},{3,2},{4,5},{5,4},{6,7},{7,6},{8,9},{9,8},{10,11... | collective-permute-start | bytes 442376 | tf_op jit(solution)/shard_map/ppermute | solution.py:560
  52.4 1.3 %feed_forward.2 = (bf16[64,896]{1,0:T(8,128)(2,1)S(1)}, bf16[64,1408]{1,0:T(8,128)(2,1)S(1)}) custom-call(bf16[64,1152]{1,0:T(8,128)(2,1)S(1)} %add_convert_fusion.5.refs_0_, bf16[64,1408]{1,0:T(8,128)(2,1)S(1)} %get-tuple-element.79.refs_1_, bf16[1,2560]{1,0:T(2,128)(2,1)S(1)} %reshape.15.refs_3_.refs_1_.refs_2_, ...), custom_call_target="tpu_custom_call" | custom-call | flops 880803840 | bytes 13762560 | tf_op jit(solution)/shard_map/feed_forward/pallas_call | solution.py:466
  53.7 1.0 %collective-permute-start.13 = (bf16[64,1408]{1,0:T(8,128)(2,1)S(1)}, bf16[64,1408]{1,0:T(8,128)(2,1)S(1)}, u32[]{:S(2)}, u32[]{:S(2)}) collective-permute-start(bf16[64,1408]{1,0:T(8,128)(2,1)S(1)} %get-tuple-element.92), channel_id=1, source_target_pairs={{0,1},{1,0},{2,3},{3,2},{4,5},{5,4},{6,7},{7,6},{8,9},{9,8},{10,11... | collective-permute-start | bytes 540680 | tf_op jit(solution)/shard_map/ppermute | solution.py:560
  54.7 2.9 %collective-permute-done.10.refs_0_.refs_1_ = bf16[64,1408]{1,0:T(8,128)(2,1)S(1)} collective-permute-done((bf16[64,1408]{1,0:T(8,128)(2,1)S(1)}, bf16[64,1408]{1,0:T(8,128)(2,1)S(1)}, u32[]{:S(2)}, u32[]{:S(2)}) %collective-permute-start.10) | collective-permute-done | bytes 180256 | tf_op jit(solution)/shard_map/ppermute | solution.py:560
  57.6 0.9 %early_piece.4 = (f32[64,896]{1,0:T(8,128)S(1)}, f32[64,896]{1,0:T(8,128)S(1)}) custom-call(bf16[64,1408]{1,0:T(8,128)(2,1)S(1)} %collective-permute-done.10.refs_0_.refs_1_, bf16[1,2560]{1,0:T(2,128)(2,1)S(1)} %reshape.15.refs_3_.refs_1_.refs_2_, bf16[2560,896]{1,0:T(8,128)(2,1)S(1)} %get-tuple-element.77.refs_4_.refs_2_.refs_3_, ...), custom_call_target="tpu_custom_call" | custom-call | tf_op jit(solution)/shard_map/early_piece/pallas_call | solution.py:427
  58.5 1.6 %collective-permute-done.12.refs_0_ = bf16[64,1152]{1,0:T(8,128)(2,1)S(1)} collective-permute-done((bf16[64,1152]{1,0:T(8,128)(2,1)S(1)}, bf16[64,1152]{1,0:T(8,128)(2,1)S(1)}, u32[]{:S(2)}, u32[]{:S(2)}) %collective-permute-start.12) | collective-permute-done | bytes 147488 | tf_op jit(solution)/shard_map/ppermute | solution.py:560
  60.1 2.0 %feed_forward.3 = (bf16[64,1152]{1,0:T(8,128)(2,1)S(1)}, f32[64,1152]{1,0:T(8,128)S(1)}, f32[64,1408]{1,0:T(8,128)S(1)}) custom-call(bf16[64,1152]{1,0:T(8,128)(2,1)S(1)} %collective-permute-done.12.refs_0_, bf16[64,1408]{1,0:T(8,128)(2,1)S(1)} %collective-permute-done.10.refs_0_.refs_1_, bf16[1,2560]{1,0:T(2,128)(2,1)S(1)} %reshape.15.refs_3_.refs_1_.refs_2_, ...), custom_call_target="tpu_custom_call" | custom-call | flops 880803840 | bytes 13762560 | tf_op jit(solution)/shard_map/feed_forward/pallas_call | solution.py:466
  62.1 0.7 collective-permute-start.14
  62.8 0.6 collective-permute-done.13
  63.5 2.4 %collective-permute-start.17 = (bf16[64,1408]{1,0:T(8,128)(2,1)S(1)}, bf16[64,1408]{1,0:T(8,128)(2,1)S(1)}, u32[]{:S(2)}, u32[]{:S(2)}) collective-permute-start(bf16[64,1408]{1,0:T(8,128)(2,1)S(1)} %add_convert_fusion.1), channel_id=1, source_target_pairs={{0,2},{1,3},{2,0},{3,1},{4,6},{5,7},{6,4},{7,5},{8,10},{9,11},{10,... | collective-permute-start | bytes 540680 | tf_op jit(solution)/shard_map/ppermute | solution.py:560
  65.8 2.1 %collective-permute-done.14 = bf16[64,1152]{1,0:T(8,128)(2,1)S(1)} collective-permute-done((bf16[64,1152]{1,0:T(8,128)(2,1)S(1)}, bf16[64,1152]{1,0:T(8,128)(2,1)S(1)}, u32[]{:S(2)}, u32[]{:S(2)}) %collective-permute-start.14) | collective-permute-done | bytes 147488 | tf_op jit(solution)/shard_map/ppermute | solution.py:560
  68.0 1.9 %stage.5.refs_3_.refs_2_ = bf16[2560,640]{1,0:T(8,128)(2,1)S(1)} custom-call(bf16[2560,640]{1,0:T(8,128)(2,1)} %refs_0_.2), custom_call_target="tpu_custom_call" | custom-call | bytes 3276800 | tf_op jit(solution)/shard_map/stage/pallas_call | solution.py:373
  69.9 1.9 %collective-permute-start.15 = (bf16[64,1152]{1,0:T(8,128)(2,1)S(1)}, bf16[64,1152]{1,0:T(8,128)(2,1)S(1)}, u32[]{:S(2)}, u32[]{:S(2)}) collective-permute-start(bf16[64,1152]{1,0:T(8,128)(2,1)S(1)} %add_convert_fusion.4), channel_id=1, source_target_pairs={{0,2},{1,3},{2,0},{3,1},{4,6},{5,7},{6,4},{7,5},{8,10},{9,11},{10,... | collective-permute-start | bytes 442376 | tf_op jit(solution)/shard_map/ppermute | solution.py:560
  71.9 5.3 %collective-permute-done.17 = bf16[64,1408]{1,0:T(8,128)(2,1)S(1)} collective-permute-done((bf16[64,1408]{1,0:T(8,128)(2,1)S(1)}, bf16[64,1408]{1,0:T(8,128)(2,1)S(1)}, u32[]{:S(2)}, u32[]{:S(2)}) %collective-permute-start.17) | collective-permute-done | bytes 180256 | tf_op jit(solution)/shard_map/ppermute | solution.py:560
  77.3 0.5 collective-permute-start.18
  77.7 1.3 %collective-permute-done.15 = bf16[64,1152]{1,0:T(8,128)(2,1)S(1)} collective-permute-done((bf16[64,1152]{1,0:T(8,128)(2,1)S(1)}, bf16[64,1152]{1,0:T(8,128)(2,1)S(1)}, u32[]{:S(2)}, u32[]{:S(2)}) %collective-permute-start.15) | collective-permute-done | bytes 147488 | tf_op jit(solution)/shard_map/ppermute | solution.py:560
  79.1 0.7 collective-permute-start.16
  79.8 1.2 %next_layer.2 = (bf16[64,640]{1,0:T(8,128)(2,1)S(1)}, bf16[320,64]{1,0:T(8,128)(2,1)S(1)}) custom-call(bf16[64,1152]{1,0:T(8,128)(2,1)S(1)} %add_convert_fusion.3.refs_0_.refs_9_, bf16[64,1408]{1,0:T(8,128)(2,1)S(1)} %add_convert_fusion.refs_1_.refs_10_, bf16[1,2560]{1,0:T(2,128)(2,1)S(1)} %reshape.16.refs_2_.refs_1_, ...), custom_call_target="tpu_custom_call" | custom-call | flops 314572800 | bytes 4915200 | tf_op jit(solution)/shard_map/next_layer/pallas_call | solution.py:543
  81.0 2.9 %collective-permute-done.18.refs_0_.refs_1_ = bf16[64,1408]{1,0:T(8,128)(2,1)S(1)} collective-permute-done((bf16[64,1408]{1,0:T(8,128)(2,1)S(1)}, bf16[64,1408]{1,0:T(8,128)(2,1)S(1)}, u32[]{:S(2)}, u32[]{:S(2)}) %collective-permute-start.18) | collective-permute-done | bytes 180256 | tf_op jit(solution)/shard_map/ppermute | solution.py:560
  83.9 0.7 early_piece.5
  84.6 0.9 %collective-permute-done.16.refs_0_ = bf16[64,1152]{1,0:T(8,128)(2,1)S(1)} collective-permute-done((bf16[64,1152]{1,0:T(8,128)(2,1)S(1)}, bf16[64,1152]{1,0:T(8,128)(2,1)S(1)}, u32[]{:S(2)}, u32[]{:S(2)}) %collective-permute-start.16) | collective-permute-done | bytes 147488 | tf_op jit(solution)/shard_map/ppermute | solution.py:560
  85.5 1.5 %next_layer.3 = (bf16[128,640]{1,0:T(8,128)(2,1)}, bf16[320,128]{1,0:T(8,128)(2,1)}, bf16[32,2560]{1,0:T(8,128)(2,1)}) custom-call(bf16[64,1152]{1,0:T(8,128)(2,1)S(1)} %collective-permute-done.16.refs_0_, bf16[64,1408]{1,0:T(8,128)(2,1)S(1)} %collective-permute-done.18.refs_0_.refs_1_, bf16[1,2560]{1,0:T(2,128)(2,1)S(1)} %reshape.16.refs_2_.refs_1_, ...), custom_call_target="tpu_custom_call" | custom-call | flops 314572800 | bytes 4915200 | tf_op jit(solution)/shard_map/next_layer/pallas_call | solution.py:543
  (30 shorter events, 0.9 us)
Async XLA Ops:
  1.7 5.6 %collective-permute-start.1 = (bf16[512,384]{1,0:T(8,128)(2,1)S(1)}, bf16[512,384]{1,0:T(8,128)(2,1)S(1)}, u32[]{:S(2)}, u32[]{:S(2)}) collective-permute-start(bf16[512,384]{1,0:T(8,128)(2,1)S(1)} %pool_rows.1.refs_0_), channel_id=1, source_target_pairs={{0,4},{4,0},{8,12},{12,8},{16,20},{20,16},{24,28},{28,24},{1,5},{5... | collective-permute-start | bytes 1179656 | tf_op jit(solution)/shard_map/ppermute | solution.py:560
  2.2 11.4 %collective-permute-start = (bf16[512,384]{1,0:T(8,128)(2,1)S(1)}, bf16[512,384]{1,0:T(8,128)(2,1)S(1)}, u32[]{:S(2)}, u32[]{:S(2)}) collective-permute-start(bf16[512,384]{1,0:T(8,128)(2,1)S(1)} %pool_rows.1.refs_0_), channel_id=1, source_target_pairs={{0,8},{4,20},{8,0},{12,28},{16,24},{20,4},{24,16},{28,12},{1,9},{5... | collective-permute-start | bytes 1179656 | tf_op jit(solution)/shard_map/ppermute | solution.py:566
  4.8 9.7 %collective-permute-start.3 = (bf16[512,384]{1,0:T(8,128)(2,1)S(1)}, bf16[512,384]{1,0:T(8,128)(2,1)S(1)}, u32[]{:S(2)}, u32[]{:S(2)}) collective-permute-start(bf16[512,384]{1,0:T(8,128)(2,1)S(1)} %pool_rows.1.refs_0_), channel_id=1, source_target_pairs={{0,16},{4,12},{8,24},{12,4},{16,0},{20,28},{24,8},{28,20},{1,17},{... | collective-permute-start | bytes 1179656 | tf_op jit(solution)/shard_map/ppermute | solution.py:566
  7.3 1.0 %copy-start.3 = (bf16[16,32,320]{2,1,0:T(8,128)(2,1)S(1)}, bf16[16,32,320]{2,1,0:T(8,128)(2,1)}, u32[]{:S(2)}) copy-start(bf16[16,32,320]{2,1,0:T(8,128)(2,1)} %leaf_ref.1) | copy-start | bytes 983044
  8.3 0.9 %copy-start.4 = (bf16[128,640]{1,0:T(8,128)(2,1)S(1)}, bf16[128,640]{1,0:T(8,128)(2,1)}, u32[]{:S(2)}) copy-start(bf16[128,640]{1,0:T(8,128)(2,1)} %query_ref.1) | copy-start | bytes 491524
  14.5 2.3 %collective-permute-start.4 = (bf16[512,384]{1,0:T(8,128)(2,1)S(1)}, bf16[512,384]{1,0:T(8,128)(2,1)S(1)}, u32[]{:S(2)}, u32[]{:S(2)}) collective-permute-start(bf16[512,384]{1,0:T(8,128)(2,1)S(1)} %collective-permute-done.refs_2_), channel_id=1, source_target_pairs={{0,4},{4,0},{8,12},{12,8},{16,20},{20,16},{24,28},{28,24},{1,5},{5... | collective-permute-start | bytes 1179656 | tf_op jit(solution)/shard_map/ppermute | solution.py:560
  14.7 2.2 %collective-permute-start.5 = (bf16[512,384]{1,0:T(8,128)(2,1)S(1)}, bf16[512,384]{1,0:T(8,128)(2,1)S(1)}, u32[]{:S(2)}, u32[]{:S(2)}) collective-permute-start(bf16[512,384]{1,0:T(8,128)(2,1)S(1)} %collective-permute-done.3.refs_3_), channel_id=1, source_target_pairs={{0,4},{4,0},{8,12},{12,8},{16,20},{20,16},{24,28},{28,24},{1,5},{5... | collective-permute-start | bytes 1179656 | tf_op jit(solution)/shard_map/ppermute | solution.py:560
  15.0 7.8 %collective-permute-start.2 = (bf16[512,384]{1,0:T(8,128)(2,1)S(1)}, bf16[512,384]{1,0:T(8,128)(2,1)S(1)}, u32[]{:S(2)}, u32[]{:S(2)}) collective-permute-start(bf16[512,384]{1,0:T(8,128)(2,1)S(1)} %collective-permute-done.refs_2_), channel_id=1, source_target_pairs={{0,16},{4,12},{8,24},{12,4},{16,0},{20,28},{24,8},{28,20},{1,17},{... | collective-permute-start | bytes 1179656 | tf_op jit(solution)/shard_map/ppermute | solution.py:566
  20.4 4.5 %copy-start.1 = (bf16[640,2560]{1,0:T(8,128)(2,1)S(1)}, bf16[640,2560]{1,0:T(8,128)(2,1)}, u32[]{:S(2)}) copy-start(bf16[640,2560]{1,0:T(8,128)(2,1)} %refs_3_.3) | copy-start | bytes 9830404
  22.9 6.1 %copy-start.2 = (bf16[128,2560]{1,0:T(8,128)(2,1)S(1)}, bf16[128,2560]{1,0:T(8,128)(2,1)}, u32[]{:S(2)}) copy-start(bf16[128,2560]{1,0:T(8,128)(2,1)} %refs_5_.1) | copy-start | bytes 1966084
  22.9 2.0 %collective-permute-start.6 = (bf16[512,384]{1,0:T(8,128)(2,1)S(1)}, bf16[512,384]{1,0:T(8,128)(2,1)S(1)}, u32[]{:S(2)}, u32[]{:S(2)}) collective-permute-start(bf16[512,384]{1,0:T(8,128)(2,1)S(1)} %collective-permute-done.2.refs_2_), channel_id=1, source_target_pairs={{0,4},{4,0},{8,12},{12,8},{16,20},{20,16},{24,28},{28,24},{1,5},{5... | collective-permute-start | bytes 1179656 | tf_op jit(solution)/shard_map/ppermute | solution.py:560
  26.8 14.2 %copy-start.5 = (bf16[2560]{0:T(1024)(128)(2,1)S(1)}, bf16[2560]{0:T(1024)(128)(2,1)}, u32[]{:S(2)}) copy-start(bf16[2560]{0:T(1024)(128)(2,1)} %param.33) | copy-start | bytes 15364
  26.9 7.0 %collective-permute-start.7 = (bf16[64,1408]{1,0:T(8,128)(2,1)S(1)}, bf16[64,1408]{1,0:T(8,128)(2,1)S(1)}, u32[]{:S(2)}, u32[]{:S(2)}) collective-permute-start(bf16[64,1408]{1,0:T(8,128)(2,1)S(1)} %get-tuple-element.69), channel_id=1, source_target_pairs={{0,1},{1,0},{2,3},{3,2},{4,5},{5,4},{6,7},{7,6},{8,9},{9,8},{10,11... | collective-permute-start | bytes 540680 | tf_op jit(solution)/shard_map/ppermute | solution.py:560
  31.6 6.9 %collective-permute-start.9 = (bf16[64,1152]{1,0:T(8,128)(2,1)S(1)}, bf16[64,1152]{1,0:T(8,128)(2,1)S(1)}, u32[]{:S(2)}, u32[]{:S(2)}) collective-permute-start(bf16[64,1152]{1,0:T(8,128)(2,1)S(1)} %get-tuple-element.71), channel_id=1, source_target_pairs={{0,1},{1,0},{2,3},{3,2},{4,5},{5,4},{6,7},{7,6},{8,9},{9,8},{10,11... | collective-permute-start | bytes 442376 | tf_op jit(solution)/shard_map/ppermute | solution.py:560
  33.9 15.3 %collective-permute-start.8 = (bf16[64,1408]{1,0:T(8,128)(2,1)S(1)}, bf16[64,1408]{1,0:T(8,128)(2,1)S(1)}, u32[]{:S(2)}, u32[]{:S(2)}) collective-permute-start(bf16[64,1408]{1,0:T(8,128)(2,1)S(1)} %add_convert_fusion.2.refs_0_), channel_id=1, source_target_pairs={{0,2},{1,3},{2,0},{3,1},{4,6},{5,7},{6,4},{7,5},{8,10},{9,11},{10,... | collective-permute-start | bytes 540680 | tf_op jit(solution)/shard_map/ppermute | solution.py:560
  38.5 12.7 %collective-permute-start.11 = (bf16[64,1152]{1,0:T(8,128)(2,1)S(1)}, bf16[64,1152]{1,0:T(8,128)(2,1)S(1)}, u32[]{:S(2)}, u32[]{:S(2)}) collective-permute-start(bf16[64,1152]{1,0:T(8,128)(2,1)S(1)} %add_convert_fusion.6), channel_id=1, source_target_pairs={{0,2},{1,3},{2,0},{3,1},{4,6},{5,7},{6,4},{7,5},{8,10},{9,11},{10,... | collective-permute-start | bytes 442376 | tf_op jit(solution)/shard_map/ppermute | solution.py:560
  50.2 7.4 %collective-permute-start.10 = (bf16[64,1408]{1,0:T(8,128)(2,1)S(1)}, bf16[64,1408]{1,0:T(8,128)(2,1)S(1)}, u32[]{:S(2)}, u32[]{:S(2)}) collective-permute-start(bf16[64,1408]{1,0:T(8,128)(2,1)S(1)} %get-tuple-element.79.refs_1_), channel_id=1, source_target_pairs={{0,1},{1,0},{2,3},{3,2},{4,5},{5,4},{6,7},{7,6},{8,9},{9,8},{10,11... | collective-permute-start | bytes 540680 | tf_op jit(solution)/shard_map/ppermute | solution.py:560
  51.3 8.8 %collective-permute-start.12 = (bf16[64,1152]{1,0:T(8,128)(2,1)S(1)}, bf16[64,1152]{1,0:T(8,128)(2,1)S(1)}, u32[]{:S(2)}, u32[]{:S(2)}) collective-permute-start(bf16[64,1152]{1,0:T(8,128)(2,1)S(1)} %add_convert_fusion.5.refs_0_), channel_id=1, source_target_pairs={{0,1},{1,0},{2,3},{3,2},{4,5},{5,4},{6,7},{7,6},{8,9},{9,8},{10,11... | collective-permute-start | bytes 442376 | tf_op jit(solution)/shard_map/ppermute | solution.py:560
  53.7 9.7 %collective-permute-start.13 = (bf16[64,1408]{1,0:T(8,128)(2,1)S(1)}, bf16[64,1408]{1,0:T(8,128)(2,1)S(1)}, u32[]{:S(2)}, u32[]{:S(2)}) collective-permute-start(bf16[64,1408]{1,0:T(8,128)(2,1)S(1)} %get-tuple-element.92), channel_id=1, source_target_pairs={{0,1},{1,0},{2,3},{3,2},{4,5},{5,4},{6,7},{7,6},{8,9},{9,8},{10,11... | collective-permute-start | bytes 540680 | tf_op jit(solution)/shard_map/ppermute | solution.py:560
  62.1 5.9 %collective-permute-start.14 = (bf16[64,1152]{1,0:T(8,128)(2,1)S(1)}, bf16[64,1152]{1,0:T(8,128)(2,1)S(1)}, u32[]{:S(2)}, u32[]{:S(2)}) collective-permute-start(bf16[64,1152]{1,0:T(8,128)(2,1)S(1)} %get-tuple-element.93), channel_id=1, source_target_pairs={{0,1},{1,0},{2,3},{3,2},{4,5},{5,4},{6,7},{7,6},{8,9},{9,8},{10,11... | collective-permute-start | bytes 442376 | tf_op jit(solution)/shard_map/ppermute | solution.py:560
  63.4 16.3 %copy-start.6 = (bf16[2560]{0:T(1024)(128)(2,1)S(1)}, bf16[2560]{0:T(1024)(128)(2,1)}, u32[]{:S(2)}) copy-start(bf16[2560]{0:T(1024)(128)(2,1)} %param.37) | copy-start | bytes 15364
  63.4 16.4 %copy-start = (bf16[2560,320]{0,1:T(8,128)(2,1)S(1)}, bf16[2560,320]{0,1:T(8,128)(2,1)}, u32[]{:S(2)}) copy-start(bf16[2560,320]{0,1:T(8,128)(2,1)} %param.39) | copy-start | bytes 4915204
  63.5 13.7 %collective-permute-start.17 = (bf16[64,1408]{1,0:T(8,128)(2,1)S(1)}, bf16[64,1408]{1,0:T(8,128)(2,1)S(1)}, u32[]{:S(2)}, u32[]{:S(2)}) collective-permute-start(bf16[64,1408]{1,0:T(8,128)(2,1)S(1)} %add_convert_fusion.1), channel_id=1, source_target_pairs={{0,2},{1,3},{2,0},{3,1},{4,6},{5,7},{6,4},{7,5},{8,10},{9,11},{10,... | collective-permute-start | bytes 540680 | tf_op jit(solution)/shard_map/ppermute | solution.py:560
  69.9 9.1 %collective-permute-start.15 = (bf16[64,1152]{1,0:T(8,128)(2,1)S(1)}, bf16[64,1152]{1,0:T(8,128)(2,1)S(1)}, u32[]{:S(2)}, u32[]{:S(2)}) collective-permute-start(bf16[64,1152]{1,0:T(8,128)(2,1)S(1)} %add_convert_fusion.4), channel_id=1, source_target_pairs={{0,2},{1,3},{2,0},{3,1},{4,6},{5,7},{6,4},{7,5},{8,10},{9,11},{10,... | collective-permute-start | bytes 442376 | tf_op jit(solution)/shard_map/ppermute | solution.py:560
  77.3 6.6 %collective-permute-start.18 = (bf16[64,1408]{1,0:T(8,128)(2,1)S(1)}, bf16[64,1408]{1,0:T(8,128)(2,1)S(1)}, u32[]{:S(2)}, u32[]{:S(2)}) collective-permute-start(bf16[64,1408]{1,0:T(8,128)(2,1)S(1)} %add_convert_fusion.refs_1_.refs_10_), channel_id=1, source_target_pairs={{0,1},{1,0},{2,3},{3,2},{4,5},{5,4},{6,7},{7,6},{8,9},{9,8},{10,11... | collective-permute-start | bytes 540680 | tf_op jit(solution)/shard_map/ppermute | solution.py:560
  79.1 6.4 %collective-permute-start.16 = (bf16[64,1152]{1,0:T(8,128)(2,1)S(1)}, bf16[64,1152]{1,0:T(8,128)(2,1)S(1)}, u32[]{:S(2)}, u32[]{:S(2)}) collective-permute-start(bf16[64,1152]{1,0:T(8,128)(2,1)S(1)} %add_convert_fusion.3.refs_0_.refs_9_), channel_id=1, source_target_pairs={{0,1},{1,0},{2,3},{3,2},{4,5},{5,4},{6,7},{7,6},{8,9},{9,8},{10,11... | collective-permute-start | bytes 442376 | tf_op jit(solution)/shard_map/ppermute | solution.py:560

commit v11 on v10

--- a/solution.py
+++ b/solution.py
@@ -70,7 +70,7 @@
 
 
 def piece(width, k):
-    cut = width * 9 // 20
+    cut = width * 2 // 5
     return slice(cut, width) if k else slice(0, cut)
 
 

time: 87.2 us -> 88.9 us (1.019)
  waiting for transfers between devices: 28.6 us -> 29.5 us
    ppermute x16, waiting for transfers between devices: 27 us -> 28 us  [trade(): return lax.ppermute(value, axis, [(i, i ^ bit) for i in range(size)])]
  transfers between devices with their start and end apart: 19 -> 19, of which waited for: 14 -> 14; matrix products, arithmetic and copies ran while one was open for 2% -> 1% of each run, Pallas kernels for 31% -> 31%
where the time goes in v11:
time: 88.9 us; the launch traced here: 88.6 us
  Pallas kernels  31.6 us (36%)
  waiting for transfers between devices  29.5 us (33%)
  starting transfers between devices  23.3 us (26%)
  local copies, waits for them, and re-layouts  2.94 us (3%)
    ppermute x16, waiting for transfers between devices, trade(): return lax.ppermute(value, axis, [(i, i ^ bit) for i in range(size)])  28 us
    ppermute x16, starting transfers between devices, trade(): return lax.ppermute(value, axis, [(i, i ^ bit) for i in range(size)])  17.5 us
    pallas_call x3, Pallas kernels, stage(): pl.pallas_call(stage_kernel, out_shape=tuple((pltpu.VMEM(w.shape, w.dtype...  8.11 us
    ppermute x3, starting transfers between devices, cross(): return lax.ppermute(value, 'req', pairs)  5.83 us
    pallas_call x2, Pallas kernels, extend_attention(): pl.pallas_call(functools.partial(chunk_kernel, blocks=2 * kv_local), out_...  5.36 us
    pallas_call x2, Pallas kernels, finish_attention(): pl.pallas_call(functools.partial(finish_kernel, half=half, kv_local=kv_lo...  4.79 us
    pallas_call x1, Pallas kernels, start_attention(): pl.pallas_call(functools.partial(local_kernel, chunks=len(pools)), out_sh...  3.77 us
    pallas_call x2, Pallas kernels, feed_forward(): pl.pallas_call(functools.partial(mlp_kernel, second=len(other) > 0, early...  3.14 us
  transfers between devices with their start and end apart: 19, of which 14 were waited for; matrix products, arithmetic and copies ran while one was open for 1% of the time, Pallas kernels for 31%

profile of v11, /device:TPU:0, one launch (start us, length us, event | category | flops | bytes accessed | tf_op | source)
XLA Modules:
  0.0 88.6 jit_solution(16786213286565912588)
XLA Ops:
  0.6 1.1 %pool_rows.1.refs_0_ = bf16[512,384]{1,0:T(8,128)(2,1)S(1)} custom-call(s32[32]{0:T(128)} %node_hbm.1, s32[32]{0:T(128)} %rank_hbm.1, s32[8]{0:T(128)} %length_hbm.1, s32[6]{0:T(128)} %root_hbm.1, bf16[32,16,320]{2,1,0:T(8,128)(2,1)} %pool_hbm.1), custom_call_target="tpu_custom_call" | custom-call | tf_op jit(solution)/shard_map/pool_rows/pallas_call | solution.py:129
  1.7 0.5 collective-permute-start.1
  2.2 2.6 %collective-permute-start = (bf16[512,384]{1,0:T(8,128)(2,1)S(1)}, bf16[512,384]{1,0:T(8,128)(2,1)S(1)}, u32[]{:S(2)}, u32[]{:S(2)}) collective-permute-start(bf16[512,384]{1,0:T(8,128)(2,1)S(1)} %pool_rows.1.refs_0_), channel_id=1, source_target_pairs={{0,8},{4,20},{8,0},{12,28},{16,24},{20,4},{24,16},{28,12},{1,9},{5... | collective-permute-start | bytes 1179656 | tf_op jit(solution)/shard_map/ppermute | solution.py:566
  4.8 1.5 %collective-permute-start.3 = (bf16[512,384]{1,0:T(8,128)(2,1)S(1)}, bf16[512,384]{1,0:T(8,128)(2,1)S(1)}, u32[]{:S(2)}, u32[]{:S(2)}) collective-permute-start(bf16[512,384]{1,0:T(8,128)(2,1)S(1)} %pool_rows.1.refs_0_), channel_id=1, source_target_pairs={{0,16},{4,12},{8,24},{12,4},{16,0},{20,28},{24,8},{28,20},{1,17},{... | collective-permute-start | bytes 1179656 | tf_op jit(solution)/shard_map/ppermute | solution.py:566
  6.3 1.0 %copy.24.keyval_ref = bf16[128,320]{1,0:T(8,128)(2,1)S(1)} copy(bf16[128,320]{0,1:T(8,128)(2,1)} %param.21) | data formatting | bytes 163840 | tf_op args[1]
  7.3 1.0 %copy-done.3 = bf16[16,32,320]{2,1,0:T(8,128)(2,1)S(1)} copy-done((bf16[16,32,320]{2,1,0:T(8,128)(2,1)S(1)}, bf16[16,32,320]{2,1,0:T(8,128)(2,1)}, u32[]{:S(2)}) %copy-start.3) | copy-done | bytes 327704
  8.3 0.9 %copy-done.4 = bf16[128,640]{1,0:T(8,128)(2,1)S(1)} copy-done((bf16[128,640]{1,0:T(8,128)(2,1)S(1)}, bf16[128,640]{1,0:T(8,128)(2,1)}, u32[]{:S(2)}) %copy-start.4) | copy-done | bytes 163864
  9.2 3.8 %attend_local.1 = (bf16[1024,256]{1,0:T(8,128)(2,1)S(1)}, f32[1024,256]{1,0:T(8,128)S(1)}) custom-call(s32[1,16]{1,0:T(1,128)} %count_hbm.1, s32[16]{0:T(128)} %mid_hbm.1, s32[16]{0:T(128)} %leaf_len_hbm.1, bf16[128,640]{1,0:T(8,128)(2,1)S(1)} %copy-done.4, bf16[128,320]{1,0:T(8,128)(2,1)S(1)} %copy.24.keyval_ref, bf16[16,32,320]{2,1,0:T(8,128)(2,1)S(1)} %copy-done.3, ...), custom_call_target="tpu_custom_call" | custom-call | flops 1744830464 | bytes 2097152 | tf_op jit(solution)/shard_map/attend_local/pallas_call | solution.py:243
  13.0 0.6 collective-permute-done.refs_2_
  13.6 0.9 collective-permute-done.3.refs_3_
  14.7 0.4 collective-permute-start.5
  15.0 1.8 %collective-permute-start.2 = (bf16[512,384]{1,0:T(8,128)(2,1)S(1)}, bf16[512,384]{1,0:T(8,128)(2,1)S(1)}, u32[]{:S(2)}, u32[]{:S(2)}) collective-permute-start(bf16[512,384]{1,0:T(8,128)(2,1)S(1)} %collective-permute-done.refs_2_), channel_id=1, source_target_pairs={{0,16},{4,12},{8,24},{12,4},{16,0},{20,28},{24,8},{28,20},{1,17},{... | collective-permute-start | bytes 1179656 | tf_op jit(solution)/shard_map/ppermute | solution.py:566
  16.8 3.6 %attend_pages.2.refs_1_ = f32[1024,256]{1,0:T(8,128)S(1)} custom-call(bf16[1024,256]{1,0:T(8,128)(2,1)S(1)} %get-tuple-element.57.refs_0_, f32[1024,256]{1,0:T(8,128)S(1)} %get-tuple-element.59.refs_1_, bf16[512,384]{1,0:T(8,128)(2,1)S(1)} %collective-permute-done.refs_2_, bf16[512,384]{1,0:T(8,128)(2,1)S(1)} %collective-permute-done.3.refs_3_, ...), custom_call_target="tpu_custom_call" | custom-call | flops 2147483648 | bytes 2097152 | tf_op jit(solution)/shard_map/attend_pages/pallas_call | solution.py:282
  20.4 2.5 %stage.3.refs_5_ = bf16[896,2560]{1,0:T(8,128)(2,1)S(1)} custom-call(bf16[896,2560]{1,0:T(8,128)(2,1)} %refs_0_), custom_call_target="tpu_custom_call" | custom-call | bytes 4587520 | tf_op jit(solution)/shard_map/stage/pallas_call | solution.py:373
  22.9 0.2 collective-permute-start.6
  23.1 1.8 %attend_pages.3.refs_1_ = f32[1024,256]{1,0:T(8,128)S(1)} custom-call(bf16[1024,256]{1,0:T(8,128)(2,1)S(1)} %get-tuple-element.57.refs_0_, f32[1024,256]{1,0:T(8,128)S(1)} %attend_pages.2.refs_1_, bf16[512,384]{1,0:T(8,128)(2,1)S(1)} %collective-permute-done.2.refs_2_), custom_call_target="tpu_custom_call" | custom-call | flops 536870912 | bytes 2097152 | tf_op jit(solution)/shard_map/attend_pages/pallas_call | solution.py:282
  24.9 1.9 %attend_finish.2 = (bf16[64,640]{1,0:T(8,128)(2,1)S(1)}, bf16[64,1536]{1,0:T(8,128)(2,1)S(1)}) custom-call(bf16[1024,256]{1,0:T(8,128)(2,1)S(1)} %get-tuple-element.57.refs_0_, f32[1024,256]{1,0:T(8,128)S(1)} %attend_pages.3.refs_1_, bf16[512,384]{1,0:T(8,128)(2,1)S(1)} %collective-permute-done.6.refs_2_, bf16[640,2560]{1,0:T(8,128)(2,1)S(1)} %copy-done.1), custom_call_target="tpu_custom_call" | custom-call | flops 536870912 | bytes 1048576 | tf_op jit(solution)/shard_map/attend_finish/pallas_call | solution.py:346
  26.9 2.1 %collective-permute-start.7 = (bf16[64,1536]{1,0:T(8,128)(2,1)S(1)}, bf16[64,1536]{1,0:T(8,128)(2,1)S(1)}, u32[]{:S(2)}, u32[]{:S(2)}) collective-permute-start(bf16[64,1536]{1,0:T(8,128)(2,1)S(1)} %get-tuple-element.69), channel_id=1, source_target_pairs={{0,1},{1,0},{2,3},{3,2},{4,5},{5,4},{6,7},{7,6},{8,9},{9,8},{10,11... | collective-permute-start | bytes 589832 | tf_op jit(solution)/shard_map/ppermute | solution.py:560
  29.0 2.8 %attend_finish.3 = (bf16[128,640]{1,0:T(8,128)(2,1)}, bf16[64,1024]{1,0:T(8,128)(2,1)S(1)}, f32[64,1024]{1,0:T(8,128)S(1)}, f32[64,1536]{1,0:T(8,128)S(1)}, bf16...) custom-call(bf16[1024,256]{1,0:T(8,128)(2,1)S(1)} %get-tuple-element.57.refs_0_, ...), custom_call_target="tpu_custom_call" | custom-call | flops 536870912 | bytes 1048576 | tf_op jit(solution)/shard_map/attend_finish/pallas_call | solution.py:346
  31.9 2.3 %collective-permute-done.7 = bf16[64,1536]{1,0:T(8,128)(2,1)S(1)} collective-permute-done((bf16[64,1536]{1,0:T(8,128)(2,1)S(1)}, bf16[64,1536]{1,0:T(8,128)(2,1)S(1)}, u32[]{:S(2)}, u32[]{:S(2)}) %collective-permute-start.7) | collective-permute-done | bytes 196640 | tf_op jit(solution)/shard_map/ppermute | solution.py:560
  34.3 2.8 %collective-permute-start.8 = (bf16[64,1536]{1,0:T(8,128)(2,1)S(1)}, bf16[64,1536]{1,0:T(8,128)(2,1)S(1)}, u32[]{:S(2)}, u32[]{:S(2)}) collective-permute-start(bf16[64,1536]{1,0:T(8,128)(2,1)S(1)} %add_convert_fusion.2.refs_0_), channel_id=1, source_target_pairs={{0,2},{1,3},{2,0},{3,1},{4,6},{5,7},{6,4},{7,5},{8,10},{9,11},{10,... | collective-permute-start | bytes 589832 | tf_op jit(solution)/shard_map/ppermute | solution.py:560
  37.0 0.1 collective-permute-done.9
  37.2 3.6 %collective-permute-start.11 = (bf16[64,1024]{1,0:T(8,128)(2,1)S(1)}, bf16[64,1024]{1,0:T(8,128)(2,1)S(1)}, u32[]{:S(2)}, u32[]{:S(2)}) collective-permute-start(bf16[64,1024]{1,0:T(8,128)(2,1)S(1)} %add_convert_fusion.6), channel_id=1, source_target_pairs={{0,2},{1,3},{2,0},{3,1},{4,6},{5,7},{6,4},{7,5},{8,10},{9,11},{10,... | collective-permute-start | bytes 393224 | tf_op jit(solution)/shard_map/ppermute | solution.py:560
  40.8 3.7 %stage.4 = (bf16[2560,896]{1,0:T(8,128)(2,1)S(1)}, bf16[2560,896]{1,0:T(8,128)(2,1)S(1)}) custom-call(bf16[2560,896]{1,0:T(8,128)(2,1)} %refs_0_.1, bf16[2560,896]{1,0:T(8,128)(2,1)} %refs_1_), custom_call_target="tpu_custom_call" | custom-call | bytes 9175040 | tf_op jit(solution)/shard_map/stage/pallas_call | solution.py:373
  44.5 5.3 %collective-permute-done.8.refs_2_ = bf16[64,1536]{1,0:T(8,128)(2,1)S(1)} collective-permute-done((bf16[64,1536]{1,0:T(8,128)(2,1)S(1)}, bf16[64,1536]{1,0:T(8,128)(2,1)S(1)}, u32[]{:S(2)}, u32[]{:S(2)}) %collective-permute-start.8) | collective-permute-done | bytes 196640 | tf_op jit(solution)/shard_map/ppermute | solution.py:560
  49.8 1.0 %early_piece.3 = (bf16[64,1536]{1,0:T(8,128)(2,1)S(1)}, f32[64,896]{1,0:T(8,128)S(1)}, f32[64,896]{1,0:T(8,128)S(1)}) custom-call(bf16[64,1536]{1,0:T(8,128)(2,1)S(1)} %add_convert_fusion.2.refs_0_, bf16[64,1536]{1,0:T(8,128)(2,1)S(1)} %get-tuple-element.70.refs_1_, bf16[64,1536]{1,0:T(8,128)(2,1)S(1)} %collective-permute-done.8.refs_2_, ...), custom_call_target="tpu_custom_call" | custom-call | tf_op jit(solution)/shard_map/early_piece/pallas_call | solution.py:427
  50.9 0.5 collective-permute-done.11
  51.5 1.5 %collective-permute-start.12 = (bf16[64,1024]{1,0:T(8,128)(2,1)S(1)}, bf16[64,1024]{1,0:T(8,128)(2,1)S(1)}, u32[]{:S(2)}, u32[]{:S(2)}) collective-permute-start(bf16[64,1024]{1,0:T(8,128)(2,1)S(1)} %add_convert_fusion.5.refs_0_), channel_id=1, source_target_pairs={{0,1},{1,0},{2,3},{3,2},{4,5},{5,4},{6,7},{7,6},{8,9},{9,8},{10,11... | collective-permute-start | bytes 393224 | tf_op jit(solution)/shard_map/ppermute | solution.py:560
  53.1 1.2 %feed_forward.2 = (bf16[64,896]{1,0:T(8,128)(2,1)S(1)}, bf16[64,1536]{1,0:T(8,128)(2,1)S(1)}) custom-call(bf16[64,1024]{1,0:T(8,128)(2,1)S(1)} %add_convert_fusion.5.refs_0_, bf16[64,1536]{1,0:T(8,128)(2,1)S(1)} %get-tuple-element.79.refs_1_, bf16[1,2560]{1,0:T(2,128)(2,1)S(1)} %reshape.15.refs_3_.refs_1_.refs_2_, ...), custom_call_target="tpu_custom_call" | custom-call | flops 880803840 | bytes 13762560 | tf_op jit(solution)/shard_map/feed_forward/pallas_call | solution.py:466
  54.3 0.6 collective-permute-start.13
  54.9 3.4 %collective-permute-done.10.refs_0_.refs_1_ = bf16[64,1536]{1,0:T(8,128)(2,1)S(1)} collective-permute-done((bf16[64,1536]{1,0:T(8,128)(2,1)S(1)}, bf16[64,1536]{1,0:T(8,128)(2,1)S(1)}, u32[]{:S(2)}, u32[]{:S(2)}) %collective-permute-start.10) | collective-permute-done | bytes 196640 | tf_op jit(solution)/shard_map/ppermute | solution.py:560
  58.4 1.0 %early_piece.4 = (f32[64,896]{1,0:T(8,128)S(1)}, f32[64,896]{1,0:T(8,128)S(1)}) custom-call(bf16[64,1536]{1,0:T(8,128)(2,1)S(1)} %collective-permute-done.10.refs_0_.refs_1_, bf16[1,2560]{1,0:T(2,128)(2,1)S(1)} %reshape.15.refs_3_.refs_1_.refs_2_, bf16[2560,896]{1,0:T(8,128)(2,1)S(1)} %get-tuple-element.77.refs_4_.refs_2_.refs_3_, ...), custom_call_target="tpu_custom_call" | custom-call | tf_op jit(solution)/shard_map/early_piece/pallas_call | solution.py:427
  59.4 1.2 %collective-permute-done.12.refs_0_ = bf16[64,1024]{1,0:T(8,128)(2,1)S(1)} collective-permute-done((bf16[64,1024]{1,0:T(8,128)(2,1)S(1)}, bf16[64,1024]{1,0:T(8,128)(2,1)S(1)}, u32[]{:S(2)}, u32[]{:S(2)}) %collective-permute-start.12) | collective-permute-done | bytes 131104 | tf_op jit(solution)/shard_map/ppermute | solution.py:560
  60.6 1.9 %feed_forward.3 = (bf16[64,1024]{1,0:T(8,128)(2,1)S(1)}, f32[64,1024]{1,0:T(8,128)S(1)}, f32[64,1536]{1,0:T(8,128)S(1)}) custom-call(bf16[64,1024]{1,0:T(8,128)(2,1)S(1)} %collective-permute-done.12.refs_0_, bf16[64,1536]{1,0:T(8,128)(2,1)S(1)} %collective-permute-done.10.refs_0_.refs_1_, bf16[1,2560]{1,0:T(2,128)(2,1)S(1)} %reshape.15.refs_3_.refs_1_.refs_2_, ...), custom_call_target="tpu_custom_call" | custom-call | flops 880803840 | bytes 13762560 | tf_op jit(solution)/shard_map/feed_forward/pallas_call | solution.py:466
  62.5 1.1 %collective-permute-start.14 = (bf16[64,1024]{1,0:T(8,128)(2,1)S(1)}, bf16[64,1024]{1,0:T(8,128)(2,1)S(1)}, u32[]{:S(2)}, u32[]{:S(2)}) collective-permute-start(bf16[64,1024]{1,0:T(8,128)(2,1)S(1)} %get-tuple-element.93), channel_id=1, source_target_pairs={{0,1},{1,0},{2,3},{3,2},{4,5},{5,4},{6,7},{7,6},{8,9},{9,8},{10,11... | collective-permute-start | bytes 393224 | tf_op jit(solution)/shard_map/ppermute | solution.py:560
  63.5 0.6 collective-permute-done.13
  64.1 2.3 %collective-permute-start.17 = (bf16[64,1536]{1,0:T(8,128)(2,1)S(1)}, bf16[64,1536]{1,0:T(8,128)(2,1)S(1)}, u32[]{:S(2)}, u32[]{:S(2)}) collective-permute-start(bf16[64,1536]{1,0:T(8,128)(2,1)S(1)} %add_convert_fusion.1), channel_id=1, source_target_pairs={{0,2},{1,3},{2,0},{3,1},{4,6},{5,7},{6,4},{7,5},{8,10},{9,11},{10,... | collective-permute-start | bytes 589832 | tf_op jit(solution)/shard_map/ppermute | solution.py:560
  66.4 3.0 %collective-permute-done.14 = bf16[64,1024]{1,0:T(8,128)(2,1)S(1)} collective-permute-done((bf16[64,1024]{1,0:T(8,128)(2,1)S(1)}, bf16[64,1024]{1,0:T(8,128)(2,1)S(1)}, u32[]{:S(2)}, u32[]{:S(2)}) %collective-permute-start.14) | collective-permute-done | bytes 131104 | tf_op jit(solution)/shard_map/ppermute | solution.py:560
  69.4 1.9 %stage.5.refs_3_.refs_2_ = bf16[2560,640]{1,0:T(8,128)(2,1)S(1)} custom-call(bf16[2560,640]{1,0:T(8,128)(2,1)} %refs_0_.2), custom_call_target="tpu_custom_call" | custom-call | bytes 3276800 | tf_op jit(solution)/shard_map/stage/pallas_call | solution.py:373
  71.4 1.3 %collective-permute-start.15 = (bf16[64,1024]{1,0:T(8,128)(2,1)S(1)}, bf16[64,1024]{1,0:T(8,128)(2,1)S(1)}, u32[]{:S(2)}, u32[]{:S(2)}) collective-permute-start(bf16[64,1024]{1,0:T(8,128)(2,1)S(1)} %add_convert_fusion.4), channel_id=1, source_target_pairs={{0,2},{1,3},{2,0},{3,1},{4,6},{5,7},{6,4},{7,5},{8,10},{9,11},{10,... | collective-permute-start | bytes 393224 | tf_op jit(solution)/shard_map/ppermute | solution.py:560
  72.7 6.1 %collective-permute-done.17 = bf16[64,1536]{1,0:T(8,128)(2,1)S(1)} collective-permute-done((bf16[64,1536]{1,0:T(8,128)(2,1)S(1)}, bf16[64,1536]{1,0:T(8,128)(2,1)S(1)}, u32[]{:S(2)}, u32[]{:S(2)}) %collective-permute-start.17) | collective-permute-done | bytes 196640 | tf_op jit(solution)/shard_map/ppermute | solution.py:560
  79.0 1.3 %collective-permute-done.15 = bf16[64,1024]{1,0:T(8,128)(2,1)S(1)} collective-permute-done((bf16[64,1024]{1,0:T(8,128)(2,1)S(1)}, bf16[64,1024]{1,0:T(8,128)(2,1)S(1)}, u32[]{:S(2)}, u32[]{:S(2)}) %collective-permute-start.15) | collective-permute-done | bytes 131104 | tf_op jit(solution)/shard_map/ppermute | solution.py:560
  80.3 0.8 collective-permute-start.16
  81.1 1.2 %next_layer.2 = (bf16[64,640]{1,0:T(8,128)(2,1)S(1)}, bf16[320,64]{1,0:T(8,128)(2,1)S(1)}) custom-call(bf16[64,1024]{1,0:T(8,128)(2,1)S(1)} %add_convert_fusion.3.refs_0_.refs_9_, bf16[64,1536]{1,0:T(8,128)(2,1)S(1)} %add_convert_fusion.refs_1_.refs_10_, bf16[1,2560]{1,0:T(2,128)(2,1)S(1)} %reshape.16.refs_2_.refs_1_, ...), custom_call_target="tpu_custom_call" | custom-call | flops 314572800 | bytes 4915200 | tf_op jit(solution)/shard_map/next_layer/pallas_call | solution.py:543
  82.3 3.5 %collective-permute-done.18.refs_0_.refs_1_ = bf16[64,1536]{1,0:T(8,128)(2,1)S(1)} collective-permute-done((bf16[64,1536]{1,0:T(8,128)(2,1)S(1)}, bf16[64,1536]{1,0:T(8,128)(2,1)S(1)}, u32[]{:S(2)}, u32[]{:S(2)}) %collective-permute-start.18) | collective-permute-done | bytes 196640 | tf_op jit(solution)/shard_map/ppermute | solution.py:560
  85.8 0.7 early_piece.5
  86.5 0.7 collective-permute-done.16.refs_0_
  87.2 1.4 %next_layer.3 = (bf16[128,640]{1,0:T(8,128)(2,1)}, bf16[320,128]{1,0:T(8,128)(2,1)}, bf16[32,2560]{1,0:T(8,128)(2,1)}) custom-call(bf16[64,1024]{1,0:T(8,128)(2,1)S(1)} %collective-permute-done.16.refs_0_, bf16[64,1536]{1,0:T(8,128)(2,1)S(1)} %collective-permute-done.18.refs_0_.refs_1_, bf16[1,2560]{1,0:T(2,128)(2,1)S(1)} %reshape.16.refs_2_.refs_1_, ...), custom_call_target="tpu_custom_call" | custom-call | flops 314572800 | bytes 4915200 | tf_op jit(solution)/shard_map/next_layer/pallas_call | solution.py:543
  (30 shorter events, 0.7 us)
Async XLA Ops:
  1.7 5.6 %collective-permute-start.1 = (bf16[512,384]{1,0:T(8,128)(2,1)S(1)}, bf16[512,384]{1,0:T(8,128)(2,1)S(1)}, u32[]{:S(2)}, u32[]{:S(2)}) collective-permute-start(bf16[512,384]{1,0:T(8,128)(2,1)S(1)} %pool_rows.1.refs_0_), channel_id=1, source_target_pairs={{0,4},{4,0},{8,12},{12,8},{16,20},{20,16},{24,28},{28,24},{1,5},{5... | collective-permute-start | bytes 1179656 | tf_op jit(solution)/shard_map/ppermute | solution.py:560
  2.2 11.4 %collective-permute-start = (bf16[512,384]{1,0:T(8,128)(2,1)S(1)}, bf16[512,384]{1,0:T(8,128)(2,1)S(1)}, u32[]{:S(2)}, u32[]{:S(2)}) collective-permute-start(bf16[512,384]{1,0:T(8,128)(2,1)S(1)} %pool_rows.1.refs_0_), channel_id=1, source_target_pairs={{0,8},{4,20},{8,0},{12,28},{16,24},{20,4},{24,16},{28,12},{1,9},{5... | collective-permute-start | bytes 1179656 | tf_op jit(solution)/shard_map/ppermute | solution.py:566
  4.8 9.7 %collective-permute-start.3 = (bf16[512,384]{1,0:T(8,128)(2,1)S(1)}, bf16[512,384]{1,0:T(8,128)(2,1)S(1)}, u32[]{:S(2)}, u32[]{:S(2)}) collective-permute-start(bf16[512,384]{1,0:T(8,128)(2,1)S(1)} %pool_rows.1.refs_0_), channel_id=1, source_target_pairs={{0,16},{4,12},{8,24},{12,4},{16,0},{20,28},{24,8},{28,20},{1,17},{... | collective-permute-start | bytes 1179656 | tf_op jit(solution)/shard_map/ppermute | solution.py:566
  7.3 1.0 %copy-start.3 = (bf16[16,32,320]{2,1,0:T(8,128)(2,1)S(1)}, bf16[16,32,320]{2,1,0:T(8,128)(2,1)}, u32[]{:S(2)}) copy-start(bf16[16,32,320]{2,1,0:T(8,128)(2,1)} %leaf_ref.1) | copy-start | bytes 983044
  8.3 0.9 %copy-start.4 = (bf16[128,640]{1,0:T(8,128)(2,1)S(1)}, bf16[128,640]{1,0:T(8,128)(2,1)}, u32[]{:S(2)}) copy-start(bf16[128,640]{1,0:T(8,128)(2,1)} %query_ref.1) | copy-start | bytes 491524
  14.5 2.3 %collective-permute-start.4 = (bf16[512,384]{1,0:T(8,128)(2,1)S(1)}, bf16[512,384]{1,0:T(8,128)(2,1)S(1)}, u32[]{:S(2)}, u32[]{:S(2)}) collective-permute-start(bf16[512,384]{1,0:T(8,128)(2,1)S(1)} %collective-permute-done.refs_2_), channel_id=1, source_target_pairs={{0,4},{4,0},{8,12},{12,8},{16,20},{20,16},{24,28},{28,24},{1,5},{5... | collective-permute-start | bytes 1179656 | tf_op jit(solution)/shard_map/ppermute | solution.py:560
  14.7 2.2 %collective-permute-start.5 = (bf16[512,384]{1,0:T(8,128)(2,1)S(1)}, bf16[512,384]{1,0:T(8,128)(2,1)S(1)}, u32[]{:S(2)}, u32[]{:S(2)}) collective-permute-start(bf16[512,384]{1,0:T(8,128)(2,1)S(1)} %collective-permute-done.3.refs_3_), channel_id=1, source_target_pairs={{0,4},{4,0},{8,12},{12,8},{16,20},{20,16},{24,28},{28,24},{1,5},{5... | collective-permute-start | bytes 1179656 | tf_op jit(solution)/shard_map/ppermute | solution.py:560
  15.0 7.8 %collective-permute-start.2 = (bf16[512,384]{1,0:T(8,128)(2,1)S(1)}, bf16[512,384]{1,0:T(8,128)(2,1)S(1)}, u32[]{:S(2)}, u32[]{:S(2)}) collective-permute-start(bf16[512,384]{1,0:T(8,128)(2,1)S(1)} %collective-permute-done.refs_2_), channel_id=1, source_target_pairs={{0,16},{4,12},{8,24},{12,4},{16,0},{20,28},{24,8},{28,20},{1,17},{... | collective-permute-start | bytes 1179656 | tf_op jit(solution)/shard_map/ppermute | solution.py:566
  20.4 4.5 %copy-start.1 = (bf16[640,2560]{1,0:T(8,128)(2,1)S(1)}, bf16[640,2560]{1,0:T(8,128)(2,1)}, u32[]{:S(2)}) copy-start(bf16[640,2560]{1,0:T(8,128)(2,1)} %refs_3_.3) | copy-start | bytes 9830404
  22.9 6.1 %copy-start.2 = (bf16[128,2560]{1,0:T(8,128)(2,1)S(1)}, bf16[128,2560]{1,0:T(8,128)(2,1)}, u32[]{:S(2)}) copy-start(bf16[128,2560]{1,0:T(8,128)(2,1)} %refs_5_.1) | copy-start | bytes 1966084
  22.9 2.0 %collective-permute-start.6 = (bf16[512,384]{1,0:T(8,128)(2,1)S(1)}, bf16[512,384]{1,0:T(8,128)(2,1)S(1)}, u32[]{:S(2)}, u32[]{:S(2)}) collective-permute-start(bf16[512,384]{1,0:T(8,128)(2,1)S(1)} %collective-permute-done.2.refs_2_), channel_id=1, source_target_pairs={{0,4},{4,0},{8,12},{12,8},{16,20},{20,16},{24,28},{28,24},{1,5},{5... | collective-permute-start | bytes 1179656 | tf_op jit(solution)/shard_map/ppermute | solution.py:560
  26.9 13.9 %copy-start.5 = (bf16[2560]{0:T(1024)(128)(2,1)S(1)}, bf16[2560]{0:T(1024)(128)(2,1)}, u32[]{:S(2)}) copy-start(bf16[2560]{0:T(1024)(128)(2,1)} %param.33) | copy-start | bytes 15364
  26.9 7.4 %collective-permute-start.7 = (bf16[64,1536]{1,0:T(8,128)(2,1)S(1)}, bf16[64,1536]{1,0:T(8,128)(2,1)S(1)}, u32[]{:S(2)}, u32[]{:S(2)}) collective-permute-start(bf16[64,1536]{1,0:T(8,128)(2,1)S(1)} %get-tuple-element.69), channel_id=1, source_target_pairs={{0,1},{1,0},{2,3},{3,2},{4,5},{5,4},{6,7},{7,6},{8,9},{9,8},{10,11... | collective-permute-start | bytes 589832 | tf_op jit(solution)/shard_map/ppermute | solution.py:560
  31.8 5.3 %collective-permute-start.9 = (bf16[64,1024]{1,0:T(8,128)(2,1)S(1)}, bf16[64,1024]{1,0:T(8,128)(2,1)S(1)}, u32[]{:S(2)}, u32[]{:S(2)}) collective-permute-start(bf16[64,1024]{1,0:T(8,128)(2,1)S(1)} %get-tuple-element.71), channel_id=1, source_target_pairs={{0,1},{1,0},{2,3},{3,2},{4,5},{5,4},{6,7},{7,6},{8,9},{9,8},{10,11... | collective-permute-start | bytes 393224 | tf_op jit(solution)/shard_map/ppermute | solution.py:560
  34.3 15.5 %collective-permute-start.8 = (bf16[64,1536]{1,0:T(8,128)(2,1)S(1)}, bf16[64,1536]{1,0:T(8,128)(2,1)S(1)}, u32[]{:S(2)}, u32[]{:S(2)}) collective-permute-start(bf16[64,1536]{1,0:T(8,128)(2,1)S(1)} %add_convert_fusion.2.refs_0_), channel_id=1, source_target_pairs={{0,2},{1,3},{2,0},{3,1},{4,6},{5,7},{6,4},{7,5},{8,10},{9,11},{10,... | collective-permute-start | bytes 589832 | tf_op jit(solution)/shard_map/ppermute | solution.py:560
  37.2 14.3 %collective-permute-start.11 = (bf16[64,1024]{1,0:T(8,128)(2,1)S(1)}, bf16[64,1024]{1,0:T(8,128)(2,1)S(1)}, u32[]{:S(2)}, u32[]{:S(2)}) collective-permute-start(bf16[64,1024]{1,0:T(8,128)(2,1)S(1)} %add_convert_fusion.6), channel_id=1, source_target_pairs={{0,2},{1,3},{2,0},{3,1},{4,6},{5,7},{6,4},{7,5},{8,10},{9,11},{10,... | collective-permute-start | bytes 393224 | tf_op jit(solution)/shard_map/ppermute | solution.py:560
  50.8 7.5 %collective-permute-start.10 = (bf16[64,1536]{1,0:T(8,128)(2,1)S(1)}, bf16[64,1536]{1,0:T(8,128)(2,1)S(1)}, u32[]{:S(2)}, u32[]{:S(2)}) collective-permute-start(bf16[64,1536]{1,0:T(8,128)(2,1)S(1)} %get-tuple-element.79.refs_1_), channel_id=1, source_target_pairs={{0,1},{1,0},{2,3},{3,2},{4,5},{5,4},{6,7},{7,6},{8,9},{9,8},{10,11... | collective-permute-start | bytes 589832 | tf_op jit(solution)/shard_map/ppermute | solution.py:560
  51.5 9.1 %collective-permute-start.12 = (bf16[64,1024]{1,0:T(8,128)(2,1)S(1)}, bf16[64,1024]{1,0:T(8,128)(2,1)S(1)}, u32[]{:S(2)}, u32[]{:S(2)}) collective-permute-start(bf16[64,1024]{1,0:T(8,128)(2,1)S(1)} %add_convert_fusion.5.refs_0_), channel_id=1, source_target_pairs={{0,1},{1,0},{2,3},{3,2},{4,5},{5,4},{6,7},{7,6},{8,9},{9,8},{10,11... | collective-permute-start | bytes 393224 | tf_op jit(solution)/shard_map/ppermute | solution.py:560
  54.3 9.8 %collective-permute-start.13 = (bf16[64,1536]{1,0:T(8,128)(2,1)S(1)}, bf16[64,1536]{1,0:T(8,128)(2,1)S(1)}, u32[]{:S(2)}, u32[]{:S(2)}) collective-permute-start(bf16[64,1536]{1,0:T(8,128)(2,1)S(1)} %get-tuple-element.92), channel_id=1, source_target_pairs={{0,1},{1,0},{2,3},{3,2},{4,5},{5,4},{6,7},{7,6},{8,9},{9,8},{10,11... | collective-permute-start | bytes 589832 | tf_op jit(solution)/shard_map/ppermute | solution.py:560
  62.5 7.0 %collective-permute-start.14 = (bf16[64,1024]{1,0:T(8,128)(2,1)S(1)}, bf16[64,1024]{1,0:T(8,128)(2,1)S(1)}, u32[]{:S(2)}, u32[]{:S(2)}) collective-permute-start(bf16[64,1024]{1,0:T(8,128)(2,1)S(1)} %get-tuple-element.93), channel_id=1, source_target_pairs={{0,1},{1,0},{2,3},{3,2},{4,5},{5,4},{6,7},{7,6},{8,9},{9,8},{10,11... | collective-permute-start | bytes 393224 | tf_op jit(solution)/shard_map/ppermute | solution.py:560
  64.1 17.0 %copy-start.6 = (bf16[2560]{0:T(1024)(128)(2,1)S(1)}, bf16[2560]{0:T(1024)(128)(2,1)}, u32[]{:S(2)}) copy-start(bf16[2560]{0:T(1024)(128)(2,1)} %param.37) | copy-start | bytes 15364
  64.1 17.0 %copy-start = (bf16[2560,320]{0,1:T(8,128)(2,1)S(1)}, bf16[2560,320]{0,1:T(8,128)(2,1)}, u32[]{:S(2)}) copy-start(bf16[2560,320]{0,1:T(8,128)(2,1)} %param.39) | copy-start | bytes 4915204
  64.1 14.7 %collective-permute-start.17 = (bf16[64,1536]{1,0:T(8,128)(2,1)S(1)}, bf16[64,1536]{1,0:T(8,128)(2,1)S(1)}, u32[]{:S(2)}, u32[]{:S(2)}) collective-permute-start(bf16[64,1536]{1,0:T(8,128)(2,1)S(1)} %add_convert_fusion.1), channel_id=1, source_target_pairs={{0,2},{1,3},{2,0},{3,1},{4,6},{5,7},{6,4},{7,5},{8,10},{9,11},{10,... | collective-permute-start | bytes 589832 | tf_op jit(solution)/shard_map/ppermute | solution.py:560
  71.4 8.8 %collective-permute-start.15 = (bf16[64,1024]{1,0:T(8,128)(2,1)S(1)}, bf16[64,1024]{1,0:T(8,128)(2,1)S(1)}, u32[]{:S(2)}, u32[]{:S(2)}) collective-permute-start(bf16[64,1024]{1,0:T(8,128)(2,1)S(1)} %add_convert_fusion.4), channel_id=1, source_target_pairs={{0,2},{1,3},{2,0},{3,1},{4,6},{5,7},{6,4},{7,5},{8,10},{9,11},{10,... | collective-permute-start | bytes 393224 | tf_op jit(solution)/shard_map/ppermute | solution.py:560
  78.9 6.9 %collective-permute-start.18 = (bf16[64,1536]{1,0:T(8,128)(2,1)S(1)}, bf16[64,1536]{1,0:T(8,128)(2,1)S(1)}, u32[]{:S(2)}, u32[]{:S(2)}) collective-permute-start(bf16[64,1536]{1,0:T(8,128)(2,1)S(1)} %add_convert_fusion.refs_1_.refs_10_), channel_id=1, source_target_pairs={{0,1},{1,0},{2,3},{3,2},{4,5},{5,4},{6,7},{7,6},{8,9},{9,8},{10,11... | collective-permute-start | bytes 589832 | tf_op jit(solution)/shard_map/ppermute | solution.py:560
  80.3 6.9 %collective-permute-start.16 = (bf16[64,1024]{1,0:T(8,128)(2,1)S(1)}, bf16[64,1024]{1,0:T(8,128)(2,1)S(1)}, u32[]{:S(2)}, u32[]{:S(2)}) collective-permute-start(bf16[64,1024]{1,0:T(8,128)(2,1)S(1)} %add_convert_fusion.3.refs_0_.refs_9_), channel_id=1, source_target_pairs={{0,1},{1,0},{2,3},{3,2},{4,5},{5,4},{6,7},{7,6},{8,9},{9,8},{10,11... | collective-permute-start | bytes 393224 | tf_op jit(solution)/shard_map/ppermute | solution.py:560
